TPU v7x, 32 devices: a whole 2x2x4 slice. The times are simulated.
32 devices in a mesh: fsdp: 16 (over z, y, core), seq: 2 (over x).
Axes of the slice: x: 2, y: 2, z: 4, core: 2. Of those that a mesh axis runs over, the one named last changes fastest.
Arguments:
- activations: bfloat16 [32, 736, 1152], P('fsdp', 'seq'), may hold values from -6 to 6
- group_image_count: int32 [16], P('fsdp'), may hold values from 1 to 2, as said below
- image_adapter_index: int32 [32], P('fsdp'), may hold values from 0 to 7
- lengths: int32 [32], P('fsdp'), may hold values from 644 to 736
- frozen: bfloat16 [2, 15269888], P(None, 'fsdp')
- attention_adapter_weights: bfloat16 [2, 8, 8, 16, 1152], replicated
- narrow_adapter_weights: bfloat16 [2, 2, 8, 16, 1152], replicated
- broad_adapter_weights: bfloat16 [2, 2, 8, 16, 4304], replicated
- cotangent: bfloat16 [32, 736, 1152], P('fsdp', 'seq'), may hold values from -6 to 6
Outputs:
- output: bfloat16 [32, 736, 1152], P('fsdp', 'seq')
- input_grad: float32 [32, 736, 1152], P('fsdp', 'seq')
- grad_attn: float32 [2, 8, 8, 16, 1152], replicated
- grad_narrow: float32 [2, 2, 8, 16, 1152], replicated
- grad_wide: float32 [2, 2, 8, 16, 4304], replicated
Inputs may be any that keep to these rules, and one draw needn't show every extreme that they name: `group_image_count`: the images of a group fill its first slots. Some group holds 2 images and some other group holds one.
All inputs are finite; a program needn't handle non-finite values.
Results may differ from a plain program's by a relative error of at most 0.025.
Values may be sent and summed in bfloat16 or wider, within the bound.
A program may use at most 448 MiB of HBM per device.

v0:
```python
import math

import jax
import jax.numpy as jnp
from jax import lax
from jax.sharding import PartitionSpec as P

D = 1152
HD = 72
FF = 4304


epsilon = 1e-06


def gelu_tanh(tensor):
    return (
        0.5
        * tensor
        * (1.0 + jnp.tanh(0.7978845608028654 * (tensor + 0.044715 * tensor * tensor * tensor)))
    )


def layer_norm(tensor, gain, offset):
    average = jnp.mean(tensor, axis=-1, keepdims=True)
    centred = tensor - average
    variance = jnp.mean(centred * centred, axis=-1, keepdims=True)
    return centred * lax.rsqrt(variance + epsilon) * gain + offset


def unpack(flat_weights):
    cut_qkv = D * 3 * D
    cut_out = cut_qkv + D * D
    cut_up = cut_out + D * FF
    cut_down = cut_up + FF * D
    w_qkv = flat_weights[:cut_qkv].reshape(D, 3 * D)
    output_weight = flat_weights[cut_qkv:cut_out].reshape(D, D)
    up_weight = flat_weights[cut_out:cut_up].reshape(D, FF)
    down_weight = flat_weights[cut_up:cut_down].reshape(FF, D)
    token_vectors = flat_weights[cut_down : cut_down + 8 * D].reshape(8, D)
    up_bias = flat_weights[cut_down + 8 * D : cut_down + 8 * D + FF]
    return (w_qkv, output_weight, up_weight, down_weight, token_vectors, up_bias)


def select_adapter_tables(select_adapter_rows, table):
    return jnp.einsum(
        "se,cerd->scrd", select_adapter_rows, table, preferred_element_type=jnp.float32
    ).astype(jnp.bfloat16)


def attend_forward(qkv_heads, valid_keys):
    seq_total = qkv_heads.shape[1]
    head_count = qkv_heads.shape[3] // HD
    ratio = 1.0 / math.sqrt(HD)

    def per_slot(inputs_slot):
        head_block, keys_valid = inputs_slot
        query = head_block[:, 0].reshape(seq_total, head_count, HD)
        key_block = head_block[:, 1].reshape(seq_total, head_count, HD)
        value_block = head_block[:, 2].reshape(seq_total, head_count, HD)
        scores = (
            jnp.einsum("qhd,khd->hqk", query, key_block, preferred_element_type=jnp.float32) * ratio
        )
        scores = jnp.where(keys_valid[None, None, :], scores, -1e30)
        highest = jnp.max(scores, axis=-1, keepdims=True)
        weights = jnp.exp(scores - highest)
        row_total = jnp.sum(weights, axis=-1, keepdims=True)
        probable = (weights / row_total).astype(jnp.bfloat16)
        attention_output = jnp.einsum(
            "hqk,khd->qhd", probable, value_block, preferred_element_type=jnp.float32
        )
        log_total = (highest + jnp.log(row_total))[..., 0]
        return (
            attention_output.reshape(seq_total, head_count * HD).astype(jnp.bfloat16),
            log_total,
        )

    return lax.map(per_slot, (qkv_heads, valid_keys))


def attend_backward(qkv_heads, log_totals, grad_heads, valid_keys):
    seq_total = qkv_heads.shape[1]
    head_count = qkv_heads.shape[3] // HD
    ratio = 1.0 / math.sqrt(HD)

    def per_slot(inputs_slot):
        head_block, log_block, grad_block, keys_valid = inputs_slot
        query = head_block[:, 0].reshape(seq_total, head_count, HD)
        key_block = head_block[:, 1].reshape(seq_total, head_count, HD)
        value_block = head_block[:, 2].reshape(seq_total, head_count, HD)
        scores = (
            jnp.einsum("qhd,khd->hqk", query, key_block, preferred_element_type=jnp.float32) * ratio
        )
        scores = jnp.where(keys_valid[None, None, :], scores, -1e30)
        probable = jnp.exp(scores - log_block[..., None])
        grad_rows = grad_block.reshape(seq_total, head_count, HD)
        d_probable = jnp.einsum(
            "qhd,khd->hqk", grad_rows, value_block, preferred_element_type=jnp.float32
        )
        d_value = jnp.einsum(
            "hqk,qhd->khd",
            probable.astype(jnp.bfloat16),
            grad_rows,
            preferred_element_type=jnp.float32,
        )
        row_delta = jnp.sum(probable * d_probable, axis=-1, keepdims=True)
        d_scores = (probable * (d_probable - row_delta)).astype(jnp.bfloat16)
        d_query = (
            jnp.einsum("hqk,khd->qhd", d_scores, key_block, preferred_element_type=jnp.float32)
            * ratio
        )
        d_key = (
            jnp.einsum("hqk,qhd->khd", d_scores, query, preferred_element_type=jnp.float32) * ratio
        )
        stacked = jnp.stack([d_query, d_key, d_value], axis=1)
        return stacked.reshape(seq_total, 3, head_count * HD).astype(jnp.bfloat16)

    return lax.map(per_slot, (qkv_heads, log_totals, grad_heads, valid_keys))


def local(
    activations,
    group_image_count,
    image_adapter_index,
    lengths,
    frozen,
    attention_adapter_weights,
    narrow_adapter_weights,
    broad_adapter_weights,
    cotangent,
):
    slot_count, local_len, model_width = activations.shape
    seq_parts = lax.axis_size("seq")
    seq_total = local_len * seq_parts
    layer_count = frozen.shape[0]
    offset = lax.axis_index("seq") * local_len
    local_positions = offset + jnp.arange(local_len, dtype=jnp.int32)
    is_live = jnp.arange(slot_count, dtype=jnp.int32) < group_image_count[0]
    row_valid = (local_positions[None, :] < lengths[:, None]) & is_live[:, None]
    row_mask = row_valid.astype(jnp.float32)[..., None]
    valid_keys = jnp.arange(seq_total, dtype=jnp.int32)[None, :] < lengths[:, None]
    adapter_choice_list = jnp.arange(attention_adapter_weights.shape[2], dtype=jnp.int32)
    select_adapter_rows = (image_adapter_index[:, None] == adapter_choice_list[None, :]).astype(
        jnp.bfloat16
    )
    select_wide = select_adapter_rows.astype(jnp.float32)
    hidden = activations.astype(jnp.float32) * row_mask
    stored = []
    for current_layer_index in range(layer_count):
        flat_weights = lax.all_gather(frozen[current_layer_index], "fsdp", axis=0, tiled=True)
        w_qkv, output_weight, up_weight, down_weight, token_vectors, up_bias = unpack(flat_weights)
        token_vectors = token_vectors.astype(jnp.float32)
        select_attention_adapters = select_adapter_tables(
            select_adapter_rows, attention_adapter_weights[current_layer_index]
        )
        select_narrow_adapters = select_adapter_tables(
            select_adapter_rows, narrow_adapter_weights[current_layer_index]
        )
        select_broad_adapters = select_adapter_tables(
            select_adapter_rows, broad_adapter_weights[current_layer_index]
        )
        normalized_input = layer_norm(hidden, token_vectors[0], token_vectors[1]).astype(
            jnp.bfloat16
        )
        inner_query_key_value = jnp.einsum(
            "zqx,zohx->zqoh",
            normalized_input,
            select_attention_adapters[:, 0:3],
            preferred_element_type=jnp.float32,
        ).astype(jnp.bfloat16)
        lifted = jnp.einsum(
            "slcr,scrd->slcd",
            inner_query_key_value,
            select_attention_adapters[:, 4:7],
            preferred_element_type=jnp.float32,
        )
        bias_qkv = jnp.stack([token_vectors[4], jnp.zeros_like(token_vectors[4]), token_vectors[5]])
        projected = jnp.dot(normalized_input, w_qkv, preferred_element_type=jnp.float32).reshape(
            slot_count, local_len, 3, model_width
        )
        qkv = (projected + bias_qkv + lifted).astype(jnp.bfloat16)
        qkv_heads = lax.all_to_all(qkv, "seq", split_axis=3, concat_axis=1, tiled=True)
        attended_heads, log_totals = attend_forward(qkv_heads, valid_keys)
        attention_output = lax.all_to_all(
            attended_heads, "seq", split_axis=1, concat_axis=2, tiled=True
        )
        inner_output = jnp.einsum(
            "mxb,mkb->mxk",
            attention_output,
            select_attention_adapters[:, 3],
            preferred_element_type=jnp.float32,
        ).astype(jnp.bfloat16)
        residual_branch = (
            jnp.dot(attention_output, output_weight, preferred_element_type=jnp.float32)
            + token_vectors[6]
            + jnp.einsum(
                "cgy,cyz->cgz",
                inner_output,
                select_attention_adapters[:, 7],
                preferred_element_type=jnp.float32,
            )
        )
        middle = hidden + residual_branch
        second_normalized_input = layer_norm(middle, token_vectors[2], token_vectors[3]).astype(
            jnp.bfloat16
        )
        inner_upward = jnp.einsum(
            "mxb,mkb->mxk",
            second_normalized_input,
            select_narrow_adapters[:, 0],
            preferred_element_type=jnp.float32,
        ).astype(jnp.bfloat16)
        gate_pre = (
            jnp.dot(second_normalized_input, up_weight, preferred_element_type=jnp.float32)
            + up_bias.astype(jnp.float32)
            + jnp.einsum(
                "slr,srf->slf",
                inner_upward,
                select_broad_adapters[:, 0],
                preferred_element_type=jnp.float32,
            )
        )
        gelu_applied = gelu_tanh(gate_pre).astype(jnp.bfloat16)
        inner_downward = jnp.einsum(
            "slf,srf->slr",
            gelu_applied,
            select_broad_adapters[:, 1],
            preferred_element_type=jnp.float32,
        ).astype(jnp.bfloat16)
        second_residual_branch = (
            jnp.dot(gelu_applied, down_weight, preferred_element_type=jnp.float32)
            + token_vectors[7]
            + jnp.einsum(
                "cgy,cyz->cgz",
                inner_downward,
                select_narrow_adapters[:, 1],
                preferred_element_type=jnp.float32,
            )
        )
        saved_weights = None
        stored.append(
            (
                hidden,
                normalized_input,
                inner_query_key_value,
                qkv_heads,
                log_totals,
                attention_output,
                inner_output,
                middle,
                second_normalized_input,
                inner_upward,
                gate_pre,
                gelu_applied,
                inner_downward,
                saved_weights,
            )
        )
        hidden = middle + second_residual_branch
    output = (hidden * row_mask).astype(jnp.bfloat16)
    gradient = cotangent.astype(jnp.float32) * row_mask
    collected = [None] * layer_count
    for current_layer_index in reversed(range(layer_count)):
        (
            layer_input,
            normalized_input,
            inner_query_key_value,
            qkv_heads,
            log_totals,
            attention_output,
            inner_output,
            middle,
            second_normalized_input,
            inner_upward,
            gate_pre,
            gelu_applied,
            inner_downward,
            saved_weights,
        ) = stored[current_layer_index]
        flat_weights = lax.all_gather(frozen[current_layer_index], "fsdp", axis=0, tiled=True)
        w_qkv, output_weight, up_weight, down_weight, token_vectors, up_bias = unpack(flat_weights)
        token_vectors = token_vectors.astype(jnp.float32)
        select_attention_adapters = select_adapter_tables(
            select_adapter_rows, attention_adapter_weights[current_layer_index]
        )
        select_narrow_adapters = select_adapter_tables(
            select_adapter_rows, narrow_adapter_weights[current_layer_index]
        )
        select_broad_adapters = select_adapter_tables(
            select_adapter_rows, broad_adapter_weights[current_layer_index]
        )
        residual_branch_gradient = gradient.astype(jnp.bfloat16)
        d_inner_down = jnp.einsum(
            "mxb,mkb->mxk",
            residual_branch_gradient,
            select_narrow_adapters[:, 1],
            preferred_element_type=jnp.float32,
        ).astype(jnp.bfloat16)
        up_second = jnp.einsum(
            "ikn,ikf->inf",
            inner_downward,
            residual_branch_gradient,
            preferred_element_type=jnp.float32,
        )
        d_activated = jnp.einsum(
            "vnz,jz->vnj", residual_branch_gradient, down_weight, preferred_element_type=jnp.float32
        ) + jnp.einsum(
            "slr,srf->slf",
            d_inner_down,
            select_broad_adapters[:, 1],
            preferred_element_type=jnp.float32,
        )
        down_second = jnp.einsum(
            "slr,slf->srf", d_inner_down, gelu_applied, preferred_element_type=jnp.float32
        )
        gelu_back = jax.vjp(gelu_tanh, gate_pre)[1]
        gate_gradient = gelu_back(d_activated)[0].astype(jnp.bfloat16)
        inner_upward_gradient = jnp.einsum(
            "slf,srf->slr",
            gate_gradient,
            select_broad_adapters[:, 0],
            preferred_element_type=jnp.float32,
        ).astype(jnp.bfloat16)
        up_first = jnp.einsum(
            "slr,slf->srf", inner_upward, gate_gradient, preferred_element_type=jnp.float32
        )
        d_normed_two = jnp.einsum(
            "ryi,ui->ryu", gate_gradient, up_weight, preferred_element_type=jnp.float32
        ) + jnp.einsum(
            "cgy,cyz->cgz",
            inner_upward_gradient,
            select_narrow_adapters[:, 0],
            preferred_element_type=jnp.float32,
        )
        down_first = jnp.einsum(
            "ikn,ikf->inf",
            inner_upward_gradient,
            second_normalized_input,
            preferred_element_type=jnp.float32,
        )
        norm_second = jax.vjp(
            lambda tensor: layer_norm(tensor, token_vectors[2], token_vectors[3]), middle
        )[1]
        d_middle = gradient + norm_second(d_normed_two)[0]
        output_gradient = d_middle.astype(jnp.bfloat16)
        inner_output_gradient = jnp.einsum(
            "mxb,mkb->mxk",
            output_gradient,
            select_attention_adapters[:, 7],
            preferred_element_type=jnp.float32,
        ).astype(jnp.bfloat16)
        upward_output = jnp.einsum(
            "ikn,ikf->inf", inner_output, output_gradient, preferred_element_type=jnp.float32
        )
        d_attended = (
            jnp.einsum(
                "xjo,fo->xjf", output_gradient, output_weight, preferred_element_type=jnp.float32
            )
            + jnp.einsum(
                "cgy,cyz->cgz",
                inner_output_gradient,
                select_attention_adapters[:, 3],
                preferred_element_type=jnp.float32,
            )
        ).astype(jnp.bfloat16)
        down_out = jnp.einsum(
            "ikn,ikf->inf",
            inner_output_gradient,
            attention_output,
            preferred_element_type=jnp.float32,
        )
        d_heads = lax.all_to_all(d_attended, "seq", split_axis=2, concat_axis=1, tiled=True)
        d_qkv_heads = attend_backward(qkv_heads, log_totals, d_heads, valid_keys)
        d_qkv = lax.all_to_all(d_qkv_heads, "seq", split_axis=1, concat_axis=3, tiled=True)
        inner_query_key_value_gradient = jnp.einsum(
            "slcd,scrd->slcr",
            d_qkv,
            select_attention_adapters[:, 4:7],
            preferred_element_type=jnp.float32,
        ).astype(jnp.bfloat16)
        up_qkv = jnp.einsum(
            "slcr,slcd->scrd", inner_query_key_value, d_qkv, preferred_element_type=jnp.float32
        )
        d_normed = jnp.einsum(
            "slcd,ecd->sle",
            d_qkv,
            w_qkv.reshape(model_width, 3, model_width),
            preferred_element_type=jnp.float32,
        ) + jnp.einsum(
            "japo,jpoh->jah",
            inner_query_key_value_gradient,
            select_attention_adapters[:, 0:3],
            preferred_element_type=jnp.float32,
        )
        down_qkv = jnp.einsum(
            "nwfh,nwk->nfhk",
            inner_query_key_value_gradient,
            normalized_input,
            preferred_element_type=jnp.float32,
        )
        norm_first = jax.vjp(
            lambda tensor: layer_norm(tensor, token_vectors[0], token_vectors[1]), layer_input
        )[1]
        gradient = d_middle + norm_first(d_normed)[0]
        slot_attn = jnp.concatenate(
            [down_qkv, down_out[:, None], up_qkv, upward_output[:, None]], axis=1
        )
        slot_narrow = jnp.stack([down_first, up_second], axis=1)
        slot_wide = jnp.stack([up_first, down_second], axis=1)
        layer_grads = (
            jnp.einsum("se,scrd->cerd", select_wide, slot_attn),
            jnp.einsum("se,scrd->cerd", select_wide, slot_narrow),
            jnp.einsum("se,scrd->cerd", select_wide, slot_wide),
        )
        collected[current_layer_index] = layer_grads
    grad_attn = jnp.stack([entry[0] for entry in collected], axis=0)
    grad_narrow = jnp.stack([entry[1] for entry in collected], axis=0)
    grad_wide = jnp.stack([entry[2] for entry in collected], axis=0)
    grad_attn, grad_narrow, grad_wide = lax.psum(
        (grad_attn, grad_narrow, grad_wide), ("fsdp", "seq")
    )
    input_grad = gradient * row_mask
    return (output, input_grad, grad_attn, grad_narrow, grad_wide)


def solution(mesh):
    in_specs = (
        P("fsdp", "seq", None),
        P("fsdp"),
        P("fsdp"),
        P("fsdp"),
        P(None, "fsdp"),
        P(),
        P(),
        P(),
        P("fsdp", "seq", None),
    )
    out_specs = (P("fsdp", "seq", None), P("fsdp", "seq", None), P(), P(), P())
    return jax.shard_map(local, mesh=mesh, in_specs=in_specs, out_specs=out_specs, check_vma=False)
```

profile of v0, /device:TPU:0, one launch (start us, length us, event | category | flops | bytes accessed | tf_op | source)
XLA Modules:
  0.0 3053.8 jit_solution(9712463732582530699)
XLA Ops:
  35.5 281.5 %all-gather.5.cloned.1.call-done = bf16[1,15269888]{1,0:T(2,128)(2,1)} async-done(((bf16[1,954368]{1,0:T(2,128)(2,1)}), bf16[1,15269888]{1,0:T(2,128)(2,1)}) %all-gather.5.cloned.1.call-update) | async-done | bytes 30539792 | tf_op jit(solution)/shard_map/all_gather | solution.py:150
  318.4 298.4 %all-gather.7.cloned.1.call-done = bf16[1,15269888]{1,0:T(2,128)(2,1)} async-done(((bf16[1,954368]{1,0:T(2,128)(2,1)}), bf16[1,15269888]{1,0:T(2,128)(2,1)}) %all-gather.7.cloned.1.call-update) | async-done | bytes 30539792 | tf_op jit(solution)/shard_map/all_gather | solution.py:150
  618.3 168.6 %slice_reduce_fusion.5 = bf16[3981312]{0:T(1024)(128)(2,1)} fusion(bf16[1,15269888]{1,0:T(2,128)(2,1)} %all-gather.5.cloned.1.call-done), kind=kLoop, calls=%fused_computation.71 | loop fusion | bytes 15925248 | tf_op jit(solution)/shard_map/slice | solution.py:36
  787.0 15.2 reshape.445
  820.6 14.1 fusion.43
  834.7 17.4 copy.358
  858.1 228.9 %slice_reduce_fusion.2 = (bf16[4958208]{0:T(1024)(128)(2,1)}, bf16[4958208]{0:T(1024)(128)(2,1)}) fusion(bf16[1,15269888]{1,0:T(2,128)(2,1)} %all-gather.5.cloned.1.call-done), kind=kLoop, calls=%fused_computation.60 | loop fusion | bytes 39665664 | tf_op jit(solution)/shard_map/slice | solution.py:39
  1087.0 168.7 %slice_reduce_fusion.4 = bf16[3981312]{0:T(1024)(128)(2,1)} fusion(bf16[1,15269888]{1,0:T(2,128)(2,1)} %all-gather.7.cloned.1.call-done), kind=kLoop, calls=%fused_computation.70 | loop fusion | bytes 15925248 | tf_op jit(solution)/shard_map/slice | solution.py:36
  1258.8 14.5 copy.360
  1285.3 59.1 %while.44 = (s32[]{:T(128)}, bf16[2,736,576]{1,2,0:T(8,128)(2,1)S(1)}, f32[2,8,736]{2,1,0:T(8,128)S(1)}, bf16[2,736,3,576]{1,3,2,0:T(8,128)(2,1)}, pred[2,736]{1,0:T(4,128)(4,1)S(1)}, /*index=5*/s32[]{:T(128)}) while((s32[]{:T(128)}, bf16[2,736,576]{1,2,0:T(8,128)(2,1)S(1)}, f32[2,8,736]{2,1,0:T(8,128)S(1)}, ...), condition=%wide.region_5.6_spmd, body=%wide.region_2.5_spmd.sunk | while | flops 1300488448 | bytes 67533496 | solution.py:78
  1353.6 53.0 %slice_reduce_fusion.7 = bf16[1327104]{0:T(1024)(128)(2,1)S(1)} fusion(bf16[1,15269888]{1,0:T(2,128)(2,1)} %all-gather.5.cloned.1.call-done), kind=kLoop, calls=%fused_computation.117 | loop fusion | bytes 5308416 | tf_op jit(solution)/shard_map/slice | solution.py:37
  1410.7 19.2 reshape.506
  1429.9 15.2 reshape.449
  1456.6 20.1 reshape.447
  1498.8 19.4 multiply_convert_fusion.7
  1553.7 17.4 copy.378
  1577.5 228.4 %slice_reduce_fusion = (bf16[4958208]{0:T(1024)(128)(2,1)}, bf16[4958208]{0:T(1024)(128)(2,1)}) fusion(bf16[1,15269888]{1,0:T(2,128)(2,1)} %all-gather.7.cloned.1.call-done), kind=kLoop, calls=%fused_computation.58 | loop fusion | bytes 39665664 | tf_op jit(solution)/shard_map/slice | solution.py:39
  1805.8 19.4 reshape.511
  1825.2 14.6 fusion.111
  1843.1 14.5 copy.380
  1869.5 59.3 %while.45 = (s32[]{:T(128)}, bf16[2,736,576]{1,2,0:T(8,128)(2,1)S(1)}, f32[2,8,736]{2,1,0:T(8,128)S(1)}, bf16[2,736,3,576]{1,3,2,0:T(8,128)(2,1)}, pred[2,736]{1,0:T(4,128)(4,1)S(1)}, /*index=5*/s32[]{:T(128)}) while((s32[]{:T(128)}, bf16[2,736,576]{1,2,0:T(8,128)(2,1)S(1)}, f32[2,8,736]{2,1,0:T(8,128)S(1)}, ...), condition=%wide.region_13.14_spmd, body=%wide.region_10.13_spmd.sunk | while | flops 1300488448 | bytes 67533496 | solution.py:78
  1938.0 52.9 %slice_reduce_fusion.6 = bf16[1327104]{0:T(1024)(128)(2,1)S(1)} fusion(bf16[1,15269888]{1,0:T(2,128)(2,1)} %all-gather.7.cloned.1.call-done), kind=kLoop, calls=%fused_computation.116 | loop fusion | bytes 5308416 | tf_op jit(solution)/shard_map/slice | solution.py:37
  1994.9 20.1 reshape.451
  2037.9 20.4 multiply_convert_fusion.6
  2058.3 14.7 fusion.37
  2080.6 15.8 multiply_reduce_fusion.5
  2114.3 16.7 reshape_reshape.6
  2143.1 103.4 %while.46 = (s32[]{:T(128)}, bf16[2,736,3,576]{1,3,2,0:T(8,128)(2,1)}, bf16[2,736,3,576]{1,3,2,0:T(8,128)(2,1)}, pred[2,736]{1,0:T(4,128)(4,1)S(1)}, f32[2,8,736...) while((s32[]{:T(128)}, bf16[2,736,3,576]{1,3,2,0:T(8,128)(2,1)}, ...), condition=%wide.region_20.21_spmd, body=%wide.region_18.20_spmd.sunk | while | flops 3194917120 | bytes 155722448 | solution.py:118
  2163.0 12.8 multiply_reduce_fusion.12
  2175.8 12.9 multiply_convert_fusion.14
  2227.3 12.9 multiply_convert_fusion.14
  2246.5 17.5 copy.404
  2283.2 50.9 %all-to-all-done.5 = bf16[2,736,3,576]{3,0,2,1:T(2,128)(2,1)} async-done(((bf16[2,736,3,576]{3,0,2,1:T(2,128)(2,1)}), bf16[2,736,3,576]{3,0,2,1:T(2,128)(2,1)}, u32[]{:S(2)}, u32[]{:S(2)}) %all-to-all-start.5) | async-done | bytes 5087264 | tf_op jit(solution)/shard_map/all_to_all | solution.py:374
  2334.1 17.7 copy.405
  2378.6 14.6 fusion.195
  2397.8 14.6 fusion.33
  2419.4 16.7 multiply_reduce_fusion.3
  2459.5 18.2 all-to-all-done.6
  2483.9 103.5 %while.47 = (s32[]{:T(128)}, bf16[2,736,3,576]{1,3,2,0:T(8,128)(2,1)}, bf16[2,736,3,576]{1,3,2,0:T(8,128)(2,1)}, pred[2,736]{1,0:T(4,128)(4,1)S(1)}, f32[2,8,736...) while((s32[]{:T(128)}, bf16[2,736,3,576]{1,3,2,0:T(8,128)(2,1)}, ...), condition=%wide.region_27.28_spmd, body=%wide.region_25.27_spmd.sunk | while | flops 3194917120 | bytes 155722448 | solution.py:118
  2516.5 12.9 multiply_convert_fusion.17
  2567.9 12.9 multiply_convert_fusion.17
  2587.4 17.5 copy.421
  2626.7 46.5 %all-to-all-done.7 = bf16[2,736,3,576]{3,0,2,1:T(2,128)(2,1)} async-done(((bf16[2,736,3,576]{3,0,2,1:T(2,128)(2,1)}), bf16[2,736,3,576]{3,0,2,1:T(2,128)(2,1)}, u32[]{:S(2)}, u32[]{:S(2)}) %all-to-all-start.7) | async-done | bytes 5087264 | tf_op jit(solution)/shard_map/all_to_all | solution.py:374
  2673.1 17.6 copy.422
  2702.9 17.0 reshape_reshape.7
  2720.0 13.1 convolution_add_fusion.6
  2737.4 12.9 multiply_reduce_fusion.2
  2755.4 274.3 %all-reduce.3.cloned.1.call-done = (f32[2,8,8,16,1152]{4,2,3,1,0:T(8,128)}, f32[2,2,8,16,1152]{4,2,3,1,0:T(8,128)}, f32[2,2,8,16,4304]{4,2,3,1,0:T(8,128)}) async-done(((f32[2,8,8,16,1152]{4,2,3,1,0:T(8,128)}, f32[2,2,8,16,1152]{4,2,3,1,0:T(8,128)}, f32[2,2,8,16,4304]{4,2,3,1,0:T(8,128)}), (f32[2,8,8,16,1152]{4,2,3,1,0:T(8,128)}, f32[2,2,8,16,1152]{4,2,3,1,0:T(8,128)}, ...) | async-done | bytes 20611088 | tf_op jit(solution)/shard_map/psum | solution.py:419
  (609 shorter events, 652.7 us)
Async XLA Ops:
  7.2 309.8 %all-gather.5.cloned.1.call-start = ((), (), s32[]{:S(2)}) async-start(), calls=%async_computation.8 | async-start | bytes 64897024 | tf_op jit(solution)/shard_map/all_gather | solution.py:150
  16.4 600.5 %all-gather.7.cloned.1.call-start = ((), (), s32[]{:S(2)}) async-start(), calls=%async_computation.9 | async-start | bytes 64897024 | tf_op jit(solution)/shard_map/all_gather | solution.py:150
  18.1 802.5 %copy-start.87 = (f32[2,368]{1,0:T(2,128)}, f32[2,368]{1,0:T(2,128)S(1)}, u32[]{:S(2)}) copy-start(f32[2,368]{1,0:T(2,128)S(1)} %and_convert_fusion) | copy-start | bytes 8836
  18.6 802.0 %copy-start.122 = (f32[2,368]{1,0:T(2,128)}, f32[2,368]{1,0:T(2,128)S(1)}, u32[]{:S(2)}) copy-start(f32[2,368]{1,0:T(2,128)S(1)} %broadcast_multiply_fusion.3) | copy-start | bytes 8836
  19.4 801.2 %copy-start.135 = (f32[2,368]{1,0:T(2,128)}, f32[2,368]{1,0:T(2,128)S(1)}, u32[]{:S(2)}) copy-start(f32[2,368]{1,0:T(2,128)S(1)} %fusion.177) | copy-start | bytes 8836
  33.1 780.6 %copy-start.60 = (bf16[2,3,16,1152]{3,0,2,1:T(2,128)(2,1)}, bf16[2,3,16,1152]{3,0,2,1:T(2,128)(2,1)S(1)}, u32[]{:S(2)}) copy-start(bf16[2,3,16,1152]{3,0,2,1:T(2,128)(2,1)S(1)} %get-tuple-element.258) | copy-start | bytes 663556
  33.1 781.6 %copy-start.50 = (bf16[2,3,16,1152]{3,0,2,1:T(2,128)(2,1)}, bf16[2,3,16,1152]{3,0,2,1:T(2,128)(2,1)S(1)}, u32[]{:S(2)}) copy-start(bf16[2,3,16,1152]{3,0,2,1:T(2,128)(2,1)S(1)} %get-tuple-element.257) | copy-start | bytes 663556
  318.4 502.2 %copy-start.155 = (f32[1152]{0:T(1024)}, f32[1152]{0:T(1024)S(1)}, u32[]{:S(2)}) copy-start(f32[1152]{0:T(1024)S(1)} %get-tuple-element.277) | copy-start | bytes 13828
  318.4 502.2 %copy-start.158 = (f32[1152]{0:T(1024)}, f32[1152]{0:T(1024)S(1)}, u32[]{:S(2)}) copy-start(f32[1152]{0:T(1024)S(1)} %get-tuple-element.278) | copy-start | bytes 13828
  852.1 403.5 %all-to-all-start = ((bf16[2,368,3,1152]{1,0,2,3:T(2,128)(2,1)}), bf16[2,368,3,1152]{1,0,2,3:T(2,128)(2,1)}, u32[]{:S(2)}, u32[]{:S(2)}) async-start(bf16[2,368,3,1152]{1,0,2,3:T(2,128)(2,1)} %copy.358), calls=%async_computation | async-start | bytes 10616832 | tf_op jit(solution)/shard_map/all_to_all | solution.py:182
  1348.8 128.7 %all-to-all-start.1 = ((bf16[2,736,576]{2,0,1:T(2,128)(2,1)}), bf16[2,736,576]{2,0,1:T(2,128)(2,1)}, u32[]{:S(2)}, u32[]{:S(2)}) async-start(bf16[2,736,576]{2,0,1:T(2,128)(2,1)} %copy.361), calls=%async_computation.1 | async-start | bytes 3768320 | tf_op jit(solution)/shard_map/all_to_all | solution.py:184
  1489.8 43.8 %copy-start.5 = (f32[2,368,1152]{2,1,0:T(8,128)}, f32[2,368,1152]{2,1,0:T(8,128)S(1)}, u32[]{:S(2)}) copy-start(f32[2,368,1152]{2,1,0:T(8,128)S(1)} %get-tuple-element.286) | copy-start | bytes 10174468
  1518.3 15.4 copy-start.21
  1521.2 12.4 copy-start.111
  1521.2 12.4 copy-start.75
  1571.1 268.7 %all-to-all-start.2 = ((bf16[2,368,3,1152]{1,0,2,3:T(2,128)(2,1)}), bf16[2,368,3,1152]{1,0,2,3:T(2,128)(2,1)}, u32[]{:S(2)}, u32[]{:S(2)}) async-start(bf16[2,368,3,1152]{1,0,2,3:T(2,128)(2,1)} %copy.378), calls=%async_computation.2 | async-start | bytes 10616832 | tf_op jit(solution)/shard_map/all_to_all | solution.py:182
  1805.8 19.4 copy-start.26
  1933.2 83.2 %all-to-all-start.3 = ((bf16[2,736,576]{2,0,1:T(2,128)(2,1)}), bf16[2,736,576]{2,0,1:T(2,128)(2,1)}, u32[]{:S(2)}, u32[]{:S(2)}) async-start(bf16[2,736,576]{2,0,1:T(2,128)(2,1)} %copy.381), calls=%async_computation.3 | async-start | bytes 3768320 | tf_op jit(solution)/shard_map/all_to_all | solution.py:184
  2028.6 67.8 %copy-start.6 = (f32[2,368,1152]{2,1,0:T(8,128)}, f32[2,368,1152]{2,1,0:T(8,128)S(1)}, u32[]{:S(2)}) copy-start(f32[2,368,1152]{2,1,0:T(8,128)S(1)} %get-tuple-element.292) | copy-start | bytes 10174468
  2037.8 20.4 copy-start.58
  2037.8 20.4 copy-start.115
  2080.6 15.8 copy-start.152
  2080.6 15.9 copy-start.144
  2110.6 26.3 all-to-all-start.4
  2114.3 16.7 copy-start.59
  2264.1 70.0 %all-to-all-start.5 = ((bf16[2,736,3,576]{3,0,2,1:T(2,128)(2,1)}), bf16[2,736,3,576]{3,0,2,1:T(2,128)(2,1)}, u32[]{:S(2)}, u32[]{:S(2)}) async-start(bf16[2,736,3,576]{3,0,2,1:T(2,128)(2,1)} %copy.404), calls=%async_computation.5 | async-start | bytes 11304960 | tf_op jit(solution)/shard_map/all_to_all | solution.py:374
  2334.1 17.7 copy-start.53
  2357.7 12.4 copy-start.150
  2357.7 12.4 copy-start.127
  2376.8 63.1 %copy-start.3 = (f32[2,368,1152]{2,1,0:T(8,128)}, f32[2,368,1152]{2,1,0:T(8,128)S(1)}, u32[]{:S(2)}) copy-start(f32[2,368,1152]{2,1,0:T(8,128)S(1)} %add_add_fusion.7) | copy-start | bytes 10174468
  2397.8 14.6 copy-start.46
  2419.4 16.7 copy-start.148
  2419.4 16.7 copy-start.138
  2452.8 24.9 all-to-all-start.6
  2604.9 68.2 %all-to-all-start.7 = ((bf16[2,736,3,576]{3,0,2,1:T(2,128)(2,1)}), bf16[2,736,3,576]{3,0,2,1:T(2,128)(2,1)}, u32[]{:S(2)}, u32[]{:S(2)}) async-start(bf16[2,736,3,576]{3,0,2,1:T(2,128)(2,1)} %copy.421), calls=%async_computation.7 | async-start | bytes 11304960 | tf_op jit(solution)/shard_map/all_to_all | solution.py:374
  2611.2 418.5 %all-reduce.3.cloned.1.call-start = ((), (), s32[]{:S(2)}) async-start(), calls=%async_computation.10 | async-start | bytes 41418752 | tf_op jit(solution)/shard_map/psum | solution.py:419
  2673.1 17.7 copy-start.51
  2702.9 17.0 copy-start.157
  2702.9 34.4 %slice-start = ((s8[5308416]{0:T(1024)(128)(4,1)}), s8[1114112]{0:T(1024)(128)(4,1)S(1)}, s32[]{:S(2)}) async-start(s8[5308416]{0:T(1024)(128)(4,1)} %bitcast.557), calls=%async_computation.11 | async-start | bytes 2228224
  2719.9 13.1 copy-start.7
  2719.9 13.1 copy-start.100
  2719.9 13.1 copy-start.110
  2719.9 17.4 slice-start.1
  2737.4 12.9 copy-start.146
  2737.4 14.2 copy-start.14
  3029.7 11.1 slice-start.6
  3029.7 11.1 slice-start.7
  3029.7 11.1 slice-start.8
  (138 other events, 491.2 us)
Sparse Core Ops, SparseCore 0:
  16.5 300.3 all-gather.4
  319.1 297.6 all-gather.6
  2703.0 326.5 all-reduce.2
where the time goes:
time: 3070 us; the launch traced here: 3050 us
  local copies, waits for them, and re-layouts  1350 us (44%)
  waiting for transfers between devices  970 us (32%)
  matrix products  533 us (17%)
  other arithmetic  136 us (4%)
  starting transfers between devices  41.9 us (1%)
    all_gather x2, waiting for transfers between devices, local(): lax.all_gather(frozen[current_layer_index], 'fsdp', axis=0, tiled=True)  580 us
    slice x2, local copies, waits for them, and re-layouts, unpack(): down_weight = flat_weights[cut_up:cut_down].reshape(FF, D)  457 us
    slice x2, local copies, waits for them, and re-layouts, unpack(): w_qkv = flat_weights[:cut_qkv].reshape(D, 3 * D)  337 us
    psum x1, waiting for transfers between devices, local(): lax.psum((grad_attn, grad_narrow, grad_wide), ('fsdp', 'seq'))  274 us
    slice x2, local copies, waits for them, and re-layouts, unpack(): output_weight = flat_weights[cut_qkv:cut_out].reshape(D, D)  106 us
    all_to_all x2, waiting for transfers between devices, local(): lax.all_to_all(d_qkv_heads, 'seq', split_axis=1, concat_axis=3, tiled=True)  97.3 us
    dot_general x8, matrix products, per_slot(): jnp.einsum('qhd,khd->hqk', query, key_block, preferred_element_type=jnp.f...  68.1 us
  transfers between devices with their start and end apart: 11, of which 6 were waited for; matrix products, arithmetic and copies ran while one was open for 32% of the time, Pallas kernels for 0%

commit v1 on v0

v1 whole, which is shorter than its diff:
```python
import functools
import math

import jax
import jax.numpy as jnp
from jax import lax
from jax.experimental import pallas as pl
from jax.experimental.pallas import tpu as pltpu
from jax.sharding import PartitionSpec as P

D = 1152
HD = 72
H = 16
FF = 4304
R = 16
LANES = 128
BF16 = jnp.bfloat16
F32 = jnp.float32
VMEM_LIMIT = 60 << 20
C2 = math.log2(math.e) / math.sqrt(HD)
SCALE = 1.0 / math.sqrt(HD)
NEG = -1e30
epsilon = 1e-06
CUT_OUT = 3 * D * D // LANES
CUT_UP = CUT_OUT + D * D // LANES
CUT_DOWN = CUT_UP + D * FF // LANES
CUT_VECTORS = CUT_DOWN + FF * D // LANES


def dot(a, b):
    return jnp.dot(a, b, preferred_element_type=F32)


def dot_t(a, b):
    return lax.dot_general(a, b, (((1,), (1,)), ((), ())), preferred_element_type=F32)


def dot_l(a, b):
    return lax.dot_general(a, b, (((0,), (0,)), ((), ())), preferred_element_type=F32)


def rows_aligned_kernel(panels, rows, in_ref, out_ref, wide):
    wide[...] = in_ref[...].astype(F32)
    for c in range(panels):
        out_ref[:, c * LANES : (c + 1) * LANES] = wide[pl.ds(c, rows, stride=panels), :].astype(BF16)


def rows_aligned(flat, start, count, panels, rows):
    step = rows * panels
    return pl.pallas_call(
        functools.partial(rows_aligned_kernel, panels, rows),
        grid=(pl.cdiv(count, rows),),
        in_specs=[
            pl.BlockSpec(
                (pl.Element(step), pl.Element(LANES)),
                lambda i: (pl.multiple_of(start + i * step, 16), 0),
            )
        ],
        out_specs=pl.BlockSpec((rows, panels * LANES), lambda i: (i, 0)),
        out_shape=jax.ShapeDtypeStruct((count, panels * LANES), BF16),
        scratch_shapes=[pltpu.VMEM((step, LANES), F32)],
        cost_estimate=pl.CostEstimate(
            flops=0, bytes_accessed=4 * count * panels * LANES, transcendentals=0
        ),
        compiler_params=pltpu.CompilerParams(vmem_limit_bytes=VMEM_LIMIT),
        name="weight_rows",
    )(flat)


PERIOD = 8
PERIOD_ROWS = PERIOD * FF // LANES


def rows_odd_kernel(rows, in_ref, out_ref, wide, turned):
    groups = rows // PERIOD
    panels = -(-FF // LANES)
    wide[...] = in_ref[...].astype(F32)
    lane = lax.broadcasted_iota(jnp.int32, (groups, LANES), 1)
    for j in range(PERIOD):
        first, shift = (FF * j) // LANES, (FF * j) % LANES
        held = wide[pl.ds(first, groups, stride=PERIOD_ROWS), :]
        for c in range(panels):
            after = min(first + c + 1, PERIOD_ROWS - 1)
            after = wide[pl.ds(after, groups, stride=PERIOD_ROWS), :]
            value = held
            if shift:
                value = jnp.where(
                    lane < LANES - shift,
                    pltpu.roll(held, LANES - shift, 1),
                    pltpu.roll(after, LANES - shift, 1),
                )
            held = after
            turned[pl.ds(c * rows + j, groups, stride=PERIOD), :] = value
    for c in range(panels):
        width = min(LANES, FF - c * LANES)
        out_ref[:, c * LANES : c * LANES + width] = turned[pl.ds(c * rows, rows), :][:, :width].astype(BF16)


def rows_odd(flat, start, count, rows):
    step = rows * FF // LANES
    return pl.pallas_call(
        functools.partial(rows_odd_kernel, rows),
        grid=(count // rows,),
        in_specs=[
            pl.BlockSpec(
                (pl.Element(step), pl.Element(LANES)),
                lambda i: (pl.multiple_of(start + i * step, 16), 0),
            )
        ],
        out_specs=pl.BlockSpec((rows, FF), lambda i: (i, 0)),
        out_shape=jax.ShapeDtypeStruct((count, FF), BF16),
        scratch_shapes=[
            pltpu.VMEM((step, LANES), F32),
            pltpu.VMEM((-(-FF // LANES) * rows, LANES), F32),
        ],
        cost_estimate=pl.CostEstimate(flops=0, bytes_accessed=4 * count * FF, transcendentals=0),
        compiler_params=pltpu.CompilerParams(vmem_limit_bytes=VMEM_LIMIT),
        name="weight_rows_odd",
    )(flat)


def unpack(flat):
    return (
        rows_aligned(flat, 0, D, 3 * D // LANES, 64),
        rows_aligned(flat, CUT_OUT, D, D // LANES, 192),
        rows_odd(flat, CUT_UP, D, 128),
        rows_aligned(flat, CUT_DOWN, FF, D // LANES, 288),
    )


def pad_lanes(x, extra=None):
    if extra is None:
        extra = jnp.zeros((x.shape[0], LANES - HD), x.dtype)
    return jnp.concatenate([x, extra], axis=1)


def first_lane(rows, value):
    lane = lax.broadcasted_iota(jnp.int32, (rows, LANES - HD), 1)
    return jnp.where(lane == 0, value, 0.0).astype(BF16)


def key_bias(rows, length):
    key = lax.broadcasted_iota(jnp.int32, (rows, LANES - HD), 0)
    return first_lane(rows, jnp.where(key < length, 0.0, NEG))


def attn_fwd_kernel(offset, len_ref, qkv_ref, kv_ref, o_ref, st_ref, q_s, k_s, v_s):
    if kv_ref is None:
        kv_ref = qkv_ref
    rows, keys = qkv_ref.shape[0], kv_ref.shape[0]
    one = first_lane(rows, F32(1.0))
    bias = key_bias(keys, len_ref[0])
    for h in range(H):
        q_s[h] = pad_lanes(qkv_ref[:, h * HD : (h + 1) * HD], one)
        k_s[h] = pad_lanes(kv_ref[:, offset + h * HD : offset + (h + 1) * HD], bias)
        v_s[h] = pad_lanes(kv_ref[:, offset + D + h * HD : offset + D + (h + 1) * HD])
    st_ref[...] = jnp.zeros_like(st_ref)
    lane = lax.broadcasted_iota(jnp.int32, (rows, LANES), 1)

    def body(h, carry):
        s = dot_t(q_s[h], k_s[h])
        m = jnp.max(s, axis=1, keepdims=True)
        p = jnp.exp2((s - m) * C2)
        total = jnp.sum(p, axis=1, keepdims=True)
        o = dot(p.astype(BF16), v_s[h])
        q_s[h] = (o * (1.0 / total)).astype(BF16)
        st_ref[...] = jnp.where(lane == h, m * C2 + jnp.log2(total), st_ref[...])
        return carry

    lax.fori_loop(0, H, body, 0)
    for h in range(H):
        o_ref[:, h * HD : (h + 1) * HD] = q_s[h][:, :HD]


def attn_fwd(length, qkv, kv=None):
    rows = qkv.shape[0]
    keys = rows if kv is None else kv.shape[0]
    vm = pl.BlockSpec(memory_space=pltpu.VMEM)
    if kv is None:
        kernel = lambda a, b, *rest: attn_fwd_kernel(D, a, b, None, *rest)
        operands = (length, qkv)
    else:
        kernel = functools.partial(attn_fwd_kernel, 0)
        operands = (length, qkv, kv)
    return pl.pallas_call(
        kernel,
        in_specs=[pl.BlockSpec(memory_space=pltpu.SMEM)] + [vm] * (len(operands) - 1),
        out_specs=[vm, vm],
        out_shape=[
            jax.ShapeDtypeStruct((rows, D), BF16),
            jax.ShapeDtypeStruct((rows, LANES), F32),
        ],
        scratch_shapes=[
            pltpu.VMEM((H, rows, LANES), BF16),
            pltpu.VMEM((H, keys, LANES), BF16),
            pltpu.VMEM((H, keys, LANES), BF16),
        ],
        cost_estimate=pl.CostEstimate(
            flops=H * rows * keys * 256 * 4, bytes_accessed=rows * D * 8, transcendentals=H * rows * keys
        ),
        compiler_params=pltpu.CompilerParams(vmem_limit_bytes=VMEM_LIMIT),
        name="attention_forward",
    )(*operands)


def attn_bwd_kernel(
    offset, len_ref, qkv_ref, kv_ref, do_ref, o_ref, st_ref, dq_ref, dkv_ref, q_s, k_s, v_s, do_s, st_t, dl_t
):
    if kv_ref is None:
        kv_ref, dkv_ref = qkv_ref, dq_ref
    rows, keys = qkv_ref.shape[0], kv_ref.shape[0]
    one = first_lane(rows, F32(1.0))
    bias = key_bias(keys, len_ref[0])
    lane = lax.broadcasted_iota(jnp.int32, (rows, LANES), 1)
    delta = jnp.zeros((rows, LANES), F32)
    for h in range(H):
        q_s[h] = pad_lanes(qkv_ref[:, h * HD : (h + 1) * HD], one)
        k_s[h] = pad_lanes(kv_ref[:, offset + h * HD : offset + (h + 1) * HD], bias)
        v_s[h] = pad_lanes(kv_ref[:, offset + D + h * HD : offset + D + (h + 1) * HD])
        do = do_ref[:, h * HD : (h + 1) * HD]
        do_s[h] = pad_lanes(do)
        o = o_ref[:, h * HD : (h + 1) * HD].astype(F32)
        d = jnp.sum(do.astype(F32) * o, axis=1, keepdims=True)
        delta = jnp.where(lane == h, d, delta)
    st_t[...] = st_ref[...].T
    dl_t[...] = delta.T

    def body(h, carry):
        q, k, do = q_s[h], k_s[h], do_s[h]
        p = jnp.exp2(dot_t(k, q) * C2 - st_t[pl.ds(h, 1), :])
        dv = dot(p.astype(BF16), do)
        dp = dot_t(v_s[h], do)
        ds = (p * (dp - dl_t[pl.ds(h, 1), :])).astype(BF16)
        dk = dot(ds, q)
        dq = dot(k.T, ds)
        v_s[h] = dv.astype(BF16)
        k_s[h] = (dk * SCALE).astype(BF16)
        q_s[h] = (dq * SCALE).astype(BF16).T
        return carry

    lax.fori_loop(0, H, body, 0)
    for h in range(H):
        dq_ref[:, h * HD : (h + 1) * HD] = q_s[h][:, :HD]
        dkv_ref[:, offset + h * HD : offset + (h + 1) * HD] = k_s[h][:, :HD]
        dkv_ref[:, offset + D + h * HD : offset + D + (h + 1) * HD] = v_s[h][:, :HD]


def attn_bwd(length, qkv, do, o, st, kv=None):
    rows = qkv.shape[0]
    keys = rows if kv is None else kv.shape[0]
    vm = pl.BlockSpec(memory_space=pltpu.VMEM)
    if kv is None:
        kernel = lambda a, b, c, d, e, f, *rest: attn_bwd_kernel(
            D, a, b, None, c, d, e, f, None, *rest
        )
        operands = (length, qkv, do, o, st)
        outs = [jax.ShapeDtypeStruct((rows, 3 * D), BF16)]
    else:
        kernel = functools.partial(attn_bwd_kernel, 0)
        operands = (length, qkv, kv, do, o, st)
        outs = [jax.ShapeDtypeStruct((rows, D), BF16), jax.ShapeDtypeStruct((keys, 2 * D), BF16)]
    return pl.pallas_call(
        kernel,
        in_specs=[pl.BlockSpec(memory_space=pltpu.SMEM)] + [vm] * (len(operands) - 1),
        out_specs=[vm] * len(outs),
        out_shape=outs,
        scratch_shapes=[
            pltpu.VMEM((H, rows, LANES), BF16),
            pltpu.VMEM((H, keys, LANES), BF16),
            pltpu.VMEM((H, keys, LANES), BF16),
            pltpu.VMEM((H, rows, LANES), BF16),
            pltpu.VMEM((LANES, rows), F32),
            pltpu.VMEM((LANES, rows), F32),
        ],
        cost_estimate=pl.CostEstimate(
            flops=H * rows * keys * 256 * 10, bytes_accessed=rows * D * 16, transcendentals=H * rows * keys
        ),
        compiler_params=pltpu.CompilerParams(vmem_limit_bytes=VMEM_LIMIT),
        name="attention_backward",
    )(*operands)


def gelu_tanh(tensor):
    return (
        0.5
        * tensor
        * (1.0 + jnp.tanh(0.7978845608028654 * (tensor + 0.044715 * tensor * tensor * tensor)))
    )


def layer_norm(tensor, gain, offset):
    average = jnp.mean(tensor, axis=-1, keepdims=True)
    centred = tensor - average
    variance = jnp.mean(centred * centred, axis=-1, keepdims=True)
    return centred * lax.rsqrt(variance + epsilon) * gain + offset


def local(
    activations,
    group_image_count,
    image_adapter_index,
    lengths,
    frozen,
    attention_adapter_weights,
    narrow_adapter_weights,
    broad_adapter_weights,
    cotangent,
):
    slots, local_len, _ = activations.shape
    seq_parts = lax.axis_size("seq")
    fsdp_parts = lax.axis_size("fsdp")
    device_count = seq_parts * fsdp_parts
    me = lax.axis_index("seq")
    seq_total = local_len * seq_parts
    layer_count = frozen.shape[0]
    adapters = attention_adapter_weights.shape[2]
    parts = seq_parts // slots
    slot = me // parts
    part = me % parts
    tokens = seq_total // parts
    groups = [[s * parts + p for p in range(parts)] for s in range(slots)]

    def to_image(v):
        if parts == 1 and slots == 2:
            mine = lax.dynamic_index_in_dim(v, slot, 0, keepdims=False)
            other = lax.dynamic_index_in_dim(v, 1 - slot, 0, keepdims=False)
            other = lax.ppermute(other, "seq", [(0, 1), (1, 0)])
            return jnp.where(
                slot == 0,
                jnp.concatenate([mine, other], 0),
                jnp.concatenate([other, mine], 0),
            )
        whole = lax.all_gather(v, "seq", axis=1, tiled=True)
        whole = lax.dynamic_index_in_dim(whole, slot, 0, keepdims=False)
        return lax.dynamic_slice_in_dim(whole, part * tokens, tokens, 0)

    def to_tokens(v):
        if parts == 1 and slots == 2:
            mine = lax.dynamic_slice_in_dim(v, slot * local_len, local_len, 0)
            other = lax.dynamic_slice_in_dim(v, (1 - slot) * local_len, local_len, 0)
            other = lax.ppermute(other, "seq", [(0, 1), (1, 0)])
            return jnp.where(slot == 0, jnp.stack([mine, other]), jnp.stack([other, mine]))
        whole = lax.all_gather(v, "seq", axis=0, tiled=True).reshape(slots, seq_total, -1)
        return lax.dynamic_slice_in_dim(whole, me * local_len, local_len, 1)

    length = lax.dynamic_slice_in_dim(lengths, slot, 1, 0)
    adapter = lax.dynamic_index_in_dim(image_adapter_index, slot, 0, keepdims=False)
    is_live = slot < group_image_count[0]
    positions = part * tokens + jnp.arange(tokens, dtype=jnp.int32)
    row_mask = ((positions < length[0]) & is_live).astype(F32)[:, None]
    adapter_of = lax.all_gather(adapter, ("fsdp", "seq"))
    choice = (
        jnp.arange(adapters, dtype=jnp.int32)[:, None] == adapter_of[None, :]
    ).astype(F32)

    def pick(table):
        return lax.dynamic_index_in_dim(table, adapter, 1, keepdims=False)

    hidden = to_image(activations).astype(F32) * row_mask
    stored = []
    weights = []
    for layer in range(layer_count):
        flat = lax.all_gather(frozen[layer].reshape(-1, LANES), "fsdp", axis=0, tiled=True)
        w_qkv, w_o, w_1, w_2 = unpack(flat)
        vectors = lax.slice_in_dim(flat, CUT_VECTORS, CUT_VECTORS + 106, axis=0).reshape(-1)
        vectors, b_1 = vectors[: 8 * D].reshape(8, D).astype(F32), vectors[8 * D : 8 * D + FF]
        b_1 = b_1.astype(F32)
        attn = pick(attention_adapter_weights[layer])
        narrow = pick(narrow_adapter_weights[layer])
        wide = pick(broad_adapter_weights[layer])
        weights.append((w_qkv, w_o, w_1, w_2, vectors, attn, narrow, wide))
        normed = layer_norm(hidden, vectors[0], vectors[1]).astype(BF16)
        inner_qkv = dot_t(normed, attn[0:3].reshape(3 * R, D)).astype(BF16)
        lifted = jnp.concatenate(
            [dot(inner_qkv[:, c * R : (c + 1) * R], attn[4 + c]) for c in range(3)], axis=1
        )
        bias_qkv = jnp.concatenate([vectors[4], jnp.zeros((D,), F32), vectors[5]])
        qkv = (dot(normed, w_qkv) + bias_qkv + lifted).astype(BF16)
        keys = None
        if parts > 1:
            keys = lax.all_gather(
                qkv[:, D:], "seq", axis=0, tiled=True, axis_index_groups=groups
            )
        attended, stats = attn_fwd(length, qkv, keys)
        inner_o = dot_t(attended, attn[3]).astype(BF16)
        middle = hidden + (dot(attended, w_o) + vectors[6] + dot(inner_o, attn[7]))
        normed_two = layer_norm(middle, vectors[2], vectors[3]).astype(BF16)
        inner_up = dot_t(normed_two, narrow[0]).astype(BF16)
        gate = dot(normed_two, w_1) + b_1 + dot(inner_up, wide[0])
        activated = gelu_tanh(gate).astype(BF16)
        inner_down = dot_t(activated, wide[1]).astype(BF16)
        stored.append(
            (
                hidden,
                normed,
                inner_qkv,
                qkv,
                keys,
                stats,
                attended,
                inner_o,
                middle,
                normed_two,
                inner_up,
                gate,
                activated,
                inner_down,
            )
        )
        hidden = middle + (dot(activated, w_2) + vectors[7] + dot(inner_down, narrow[1]))
    output = to_tokens((hidden * row_mask).astype(BF16))
    gradient = to_image(cotangent).astype(F32) * row_mask
    collected = [None] * layer_count
    for layer in reversed(range(layer_count)):
        (
            layer_input,
            normed,
            inner_qkv,
            qkv,
            keys,
            stats,
            attended,
            inner_o,
            middle,
            normed_two,
            inner_up,
            gate,
            activated,
            inner_down,
        ) = stored[layer]
        w_qkv, w_o, w_1, w_2, vectors, attn, narrow, wide = weights[layer]
        d_branch = gradient.astype(BF16)
        d_inner_down = dot_t(d_branch, narrow[1]).astype(BF16)
        up_second = dot_l(inner_down, d_branch)
        d_activated = dot_t(d_branch, w_2) + dot(d_inner_down, wide[1])
        down_second = dot_l(d_inner_down, activated)
        d_gate = jax.vjp(gelu_tanh, gate)[1](d_activated)[0].astype(BF16)
        d_inner_up = dot_t(d_gate, wide[0]).astype(BF16)
        up_first = dot_l(inner_up, d_gate)
        d_normed_two = dot_t(d_gate, w_1) + dot(d_inner_up, narrow[0])
        down_first = dot_l(d_inner_up, normed_two)
        norm_two = jax.vjp(lambda t: layer_norm(t, vectors[2], vectors[3]), middle)[1]
        d_middle = gradient + norm_two(d_normed_two)[0]
        d_out = d_middle.astype(BF16)
        d_inner_o = dot_t(d_out, attn[7]).astype(BF16)
        up_o = dot_l(inner_o, d_out)
        d_attended = (dot_t(d_out, w_o) + dot(d_inner_o, attn[3])).astype(BF16)
        down_o = dot_l(d_inner_o, attended)
        d_qkv = attn_bwd(length, qkv, d_attended, attended, stats, keys)
        if parts > 1:
            d_keys = lax.psum_scatter(
                d_qkv[1].astype(F32),
                "seq",
                scatter_dimension=0,
                tiled=True,
                axis_index_groups=groups,
            )
            d_qkv = jnp.concatenate([d_qkv[0], d_keys.astype(BF16)], axis=1)
        else:
            d_qkv = d_qkv[0]
        d_inner_qkv = jnp.concatenate(
            [dot_t(d_qkv[:, c * D : (c + 1) * D], attn[4 + c]) for c in range(3)], axis=1
        ).astype(BF16)
        up_qkv = jnp.stack(
            [
                dot_l(inner_qkv[:, c * R : (c + 1) * R], d_qkv[:, c * D : (c + 1) * D])
                for c in range(3)
            ]
        )
        d_normed = dot_t(d_qkv, w_qkv) + dot(d_inner_qkv, attn[0:3].reshape(3 * R, D))
        down_qkv = dot_l(d_inner_qkv, normed).reshape(3, R, D)
        norm_one = jax.vjp(lambda t: layer_norm(t, vectors[0], vectors[1]), layer_input)[1]
        gradient = d_middle + norm_one(d_normed)[0]
        rows_narrow = jnp.concatenate(
            [
                down_qkv.reshape(3 * R, D),
                down_o,
                up_qkv.reshape(3 * R, D),
                up_o,
                down_first,
                up_second,
            ]
        ).astype(BF16)
        rows_wide = jnp.concatenate([up_first, down_second]).astype(BF16)

        def total(rows):
            count, width = rows.shape
            share = -(-count // device_count)
            rows = jnp.pad(rows, ((0, share * device_count - count), (0, 0)))
            mine = lax.all_to_all(
                rows.reshape(device_count, share * width),
                ("fsdp", "seq"),
                split_axis=0,
                concat_axis=0,
                tiled=True,
            )
            mine = jnp.dot(choice, mine.astype(F32), precision=lax.Precision.HIGHEST)
            every = lax.all_gather(
                mine.astype(BF16).reshape(1, adapters, share, width), ("fsdp", "seq"), tiled=True
            )
            every = every.transpose(1, 0, 2, 3).reshape(adapters, device_count * share, width)
            every = every[:, :count].reshape(adapters, count // R, R, width)
            return every.transpose(1, 0, 2, 3).astype(F32)

        collected[layer] = (total(rows_narrow), total(rows_wide))
    grad_attn = jnp.stack([entry[0][0:8] for entry in collected], axis=0)
    grad_narrow = jnp.stack([entry[0][8:10] for entry in collected], axis=0)
    grad_wide = jnp.stack([entry[1] for entry in collected], axis=0)
    input_grad = to_tokens((gradient * row_mask).astype(BF16)).astype(F32)
    return (output, input_grad, grad_attn, grad_narrow, grad_wide)


def solution(mesh):
    in_specs = (
        P("fsdp", "seq", None),
        P("fsdp"),
        P("fsdp"),
        P("fsdp"),
        P(None, "fsdp"),
        P(),
        P(),
        P(),
        P("fsdp", "seq", None),
    )
    out_specs = (P("fsdp", "seq", None), P("fsdp", "seq", None), P(), P(), P())
    return jax.shard_map(local, mesh=mesh, in_specs=in_specs, out_specs=out_specs, check_vma=False)
```

time: 3070 us -> 1140 us (0.37)
  local copies, waits for them, and re-layouts: 1350 us -> 119 us
  waiting for transfers between devices: 970 us -> 267 us
  Pallas kernels: 0 us -> 249 us
  matrix products: 533 us -> 336 us
  other arithmetic: 136 us -> 47.6 us
  blocking collectives: 0 us -> 69.3 us
    slice x22 -> x6, local copies, waits for them, and re-layouts: 917 us -> 54.1 us  [the longest x1 43.3 us: local(): frozen[layer].reshape(-1, LANES)]
    all_gather x2 -> x6, waiting for transfers between devices: 580 us -> 232 us  [the longest x2 217 us: local(): lax.all_gather(frozen[layer].reshape(-1, LANES), 'fsdp', axis=0, tiled=True)]
    psum x1 -> x0, waiting for transfers between devices: 274 us -> none  [local(): lax.psum((grad_attn, grad_narrow, grad_wide), ('fsdp', 'seq'))]
    pallas_call x0 -> x12, Pallas kernels: none -> 249 us  [the longest x2 90.1 us: attn_bwd(): pl.pallas_call(kernel, in_specs=[pl.BlockSpec(memory_space=pltpu.SMEM)] +...]
    dot_general x104 -> x80, matrix products: 533 us -> 336 us  [the longest x28 178 us: dot(): return jnp.dot(a, b, preferred_element_type=F32)]
    reshape x10 -> x2, local copies, waits for them, and re-layouts: 140 us -> 1.5 us  [local(): lax.slice_in_dim(flat, CUT_VECTORS, CUT_VECTORS + 106, axis=0).reshape(-1)]
    all_to_all x16 -> x0, local copies, waits for them, and re-layouts: 114 us -> none  [the longest x6 59.1 us: local(): lax.all_to_all(qkv, 'seq', split_axis=3, concat_axis=1, tiled=True)]
    all_to_all x8 -> x4, waiting for transfers between devices: 116 us -> 16.2 us  [total(): lax.all_to_all(rows.reshape(device_count, share * width), ('fsdp', 'seq')...]
  transfers between devices with their start and end apart: 11 -> 14, of which waited for: 6 -> 5; matrix products, arithmetic and copies ran while one was open for 32% -> 16% of each run, Pallas kernels for 0% -> 4%
where the time goes in v1:
time: 1140 us; the launch traced here: 1130 us
  matrix products  336 us (29%)
  waiting for transfers between devices  267 us (23%)
  Pallas kernels  249 us (22%)
  local copies, waits for them, and re-layouts  119 us (10%)
  blocking collectives  69.3 us (6%)
  other arithmetic  47.6 us (4%)
  starting transfers between devices  25.3 us (2%)
  between operations  18.7 us (2%)
    all_gather x2, waiting for transfers between devices, local(): lax.all_gather(frozen[layer].reshape(-1, LANES), 'fsdp', axis=0, tiled=True)  217 us
    dot_general x28, matrix products, dot(): return jnp.dot(a, b, preferred_element_type=F32)  178 us
    dot_general x28, matrix products, dot_t(): lax.dot_general(a, b, (((1,), (1,)), ((), ())), preferred_element_type=F32)  126 us
    pallas_call x2, Pallas kernels, attn_bwd(): pl.pallas_call(kernel, in_specs=[pl.BlockSpec(memory_space=pltpu.SMEM)] +...  90.1 us
    unnamed x1, blocking collectives  69.3 us
    pallas_call x2, Pallas kernels, attn_fwd(): pl.pallas_call(kernel, in_specs=[pl.BlockSpec(memory_space=pltpu.SMEM)] +...  66.4 us
    pallas_call x6, Pallas kernels, rows_aligned(): pl.pallas_call(functools.partial(rows_aligned_kernel, panels, rows), grid...  65.1 us
    unnamed x267, local copies, waits for them, and re-layouts  45.3 us
  transfers between devices with their start and end apart: 14, of which 5 were waited for; matrix products, arithmetic and copies ran while one was open for 16% of the time, Pallas kernels for 4%

profile of v1, /device:TPU:0, one launch (start us, length us, event | category | flops | bytes accessed | tf_op | source)
XLA Modules:
  0.0 1131.9 jit_solution(3216138991949257326)
XLA Ops:
  7.2 43.3 %slice_reduce_fusion = (bf16[954368]{0:T(1024)(128)(2,1)}, bf16[954368]{0:T(1024)(128)(2,1)}) fusion(bf16[2,954368]{1,0:T(2,128)(2,1)} %param.13), kind=kLoop, calls=%fused_computation.69 | loop fusion | bytes 7634944 | tf_op jit(solution)/shard_map/slice | solution.py:363
  59.8 69.3 %all-reduce = s32[32]{0:T(128)} all-reduce(s32[32]{0:T(128)S(1)} %dynamic-update-slice), channel_id=1, replica_groups=mesh['fsdp'=16,'seq'=2] {'fsdp','seq'}, use_global_device_ids=true, to_apply=%add | all-reduce | flops 32 | bytes 256
  135.1 6.5 fusion.179
  146.8 61.5 %all-gather.9.cloned.1.call-done.in_ref = bf16[119296,128]{1,0:T(8,128)(2,1)} async-done(((bf16[7456,128]{1,0:T(8,128)(2,1)}), bf16[119296,128]{1,0:T(8,128)(2,1)}) %all-gather.9.cloned.1.call-update) | async-done | bytes 30539792 | tf_op jit(solution)/shard_map/all_gather | solution.py:363
  209.7 155.1 %all-gather.11.cloned.1.call-done.in_ref = bf16[119296,128]{1,0:T(8,128)(2,1)} async-done(((bf16[7456,128]{1,0:T(8,128)(2,1)}), bf16[119296,128]{1,0:T(8,128)(2,1)}) %all-gather.11.cloned.1.call-update) | async-done | bytes 30539792 | tf_op jit(solution)/shard_map/all_gather | solution.py:363
  380.8 13.5 %weight_rows.6 = bf16[1152,3456]{1,0:T(8,128)(2,1)} custom-call(bf16[119296,128]{1,0:T(8,128)(2,1)} %all-gather.9.cloned.1.call-done.in_ref), custom_call_target="tpu_custom_call" | custom-call | bytes 15925248 | tf_op jit(solution)/shard_map/weight_rows/pallas_call | solution.py:50
  394.2 14.0 %fusion.12.b = bf16[736,3456]{1,0:T(8,128)(2,1)} fusion(f32[736,1152]{1,0:T(8,128)} %fusion.98, f32[736,1152]{1,0:T(8,128)} %fusion.97, f32[736,1152]{1,0:T(8,128)} %fusion.96, bf16[736,1152]{1,0:T(8,128)(2,1)S(1)} %add_convert_fusion.3, bf16[1152,3456]{1,0:T(8,128)(2,1)} %weight_rows.6, f32[3456]{0:T(1024)S(1)} %get-tuple-element.69), kind=kOutput, calls=%fused_computation.25 | convolution fusion | flops 5873209344 | bytes 24933888 | tf_op jit(solution)/shard_map/dot_general | solution.py:31
  408.2 33.0 %attention_forward.2 = (bf16[736,1152]{1,0:T(8,128)(2,1)}, f32[736,128]{1,0:T(8,128)}) custom-call(s32[1]{0:T(128)} %dynamic_slice.55.a, bf16[736,3456]{1,0:T(8,128)(2,1)} %fusion.12.b), custom_call_target="tpu_custom_call" | custom-call | flops 8875147264 | bytes 6782976 | tf_op jit(solution)/shard_map/attention_forward/pallas_call | solution.py:185
  443.3 5.5 weight_rows.7
  448.8 4.5 convolution_add_fusion.11
  459.5 13.6 %weight_rows_odd.2 = bf16[1152,4304]{1,0:T(8,128)(2,1)} custom-call(bf16[119296,128]{1,0:T(8,128)(2,1)} %all-gather.9.cloned.1.call-done.in_ref), custom_call_target="tpu_custom_call" | custom-call | bytes 19832832 | tf_op jit(solution)/shard_map/weight_rows_odd/pallas_call | solution.py:101
  473.1 12.2 %fusion.184 = f32[736,4304]{1,0:T(8,128)S(1)} fusion(bf16[736,1152]{1,0:T(8,128)(2,1)} %copy-done.27, bf16[1152,4304]{1,0:T(8,128)(2,1)} %weight_rows_odd.2), kind=kOutput, calls=%fused_computation.348 | convolution fusion | flops 7298482176 | bytes 24283136 | tf_op jit(solution)/shard_map/dot_general | solution.py:31
  485.4 8.8 multiply_convert_fusion.1
  499.5 13.7 %weight_rows.8 = bf16[4304,1152]{1,0:T(8,128)(2,1)} custom-call(bf16[119296,128]{1,0:T(8,128)(2,1)} %all-gather.9.cloned.1.call-done.in_ref), custom_call_target="tpu_custom_call" | custom-call | bytes 19832832 | tf_op jit(solution)/shard_map/weight_rows/pallas_call | solution.py:50
  513.2 12.9 %convolution_add_fusion.13 = f32[736,1152]{1,0:T(8,128)S(1)} fusion(bf16[736,4304]{1,0:T(8,128)(2,1)} %copy-done.14, bf16[4304,1152]{1,0:T(8,128)(2,1)} %weight_rows.8, f32[1152]{0:T(1024)S(1)} %get-tuple-element.60), kind=kOutput, calls=%fused_computation.72 | convolution fusion | flops 7299330048 | bytes 19648000 | tf_op jit(solution)/shard_map/dot_general | solution.py:31
  540.4 13.4 %weight_rows.9 = bf16[1152,3456]{1,0:T(8,128)(2,1)} custom-call(bf16[119296,128]{1,0:T(8,128)(2,1)} %all-gather.11.cloned.1.call-done.in_ref), custom_call_target="tpu_custom_call" | custom-call | bytes 15925248 | tf_op jit(solution)/shard_map/weight_rows/pallas_call | solution.py:50
  553.9 13.6 %fusion.13.b = bf16[736,3456]{1,0:T(8,128)(2,1)} fusion(f32[736,1152]{1,0:T(8,128)} %fusion.101, f32[736,1152]{1,0:T(8,128)} %fusion.100, f32[736,1152]{1,0:T(8,128)} %fusion.99, bf16[736,1152]{1,0:T(8,128)(2,1)S(1)} %add_convert_fusion.1, bf16[1152,3456]{1,0:T(8,128)(2,1)} %weight_rows.9, f32[3456]{0:T(1024)S(1)} %get-tuple-element.68), kind=kOutput, calls=%fused_computation.27 | convolution fusion | flops 5873209344 | bytes 24933888 | tf_op jit(solution)/shard_map/dot_general | solution.py:31
  567.5 33.4 %attention_forward.3 = (bf16[736,1152]{1,0:T(8,128)(2,1)}, f32[736,128]{1,0:T(8,128)}) custom-call(s32[1]{0:T(128)} %dynamic_slice.55.a, bf16[736,3456]{1,0:T(8,128)(2,1)} %fusion.13.b), custom_call_target="tpu_custom_call" | custom-call | flops 8875147264 | bytes 6782976 | tf_op jit(solution)/shard_map/attention_forward/pallas_call | solution.py:185
  602.9 5.5 weight_rows.10
  608.4 4.5 convolution_add_fusion.10
  618.4 13.7 %weight_rows_odd.3 = bf16[1152,4304]{1,0:T(8,128)(2,1)} custom-call(bf16[119296,128]{1,0:T(8,128)(2,1)} %all-gather.11.cloned.1.call-done.in_ref), custom_call_target="tpu_custom_call" | custom-call | bytes 19832832 | tf_op jit(solution)/shard_map/weight_rows_odd/pallas_call | solution.py:101
  632.1 12.0 %fusion.185 = f32[736,4304]{1,0:T(8,128)S(1)} fusion(bf16[736,1152]{1,0:T(8,128)(2,1)} %copy-done.25, bf16[1152,4304]{1,0:T(8,128)(2,1)} %weight_rows_odd.3), kind=kOutput, calls=%fused_computation.349 | convolution fusion | flops 7298482176 | bytes 24283136 | tf_op jit(solution)/shard_map/dot_general | solution.py:31
  644.1 10.4 multiply_convert_fusion
  654.5 13.5 %weight_rows.11 = bf16[4304,1152]{1,0:T(8,128)(2,1)} custom-call(bf16[119296,128]{1,0:T(8,128)(2,1)} %all-gather.11.cloned.1.call-done.in_ref), custom_call_target="tpu_custom_call" | custom-call | bytes 19832832 | tf_op jit(solution)/shard_map/weight_rows/pallas_call | solution.py:50
  668.0 16.9 %fusion.172 = f32[736,4304]{1,0:T(8,128)} fusion(bf16[4304,1152]{1,0:T(8,128)(2,1)} %weight_rows.11, f32[736]{0:T(1024)S(1)} %copy-done.68, bf16[368,1152]{1,0:T(8,128)(2,1)} %copy-done.48, bf16[368,1152]{1,0:T(8,128)(2,1)} %copy-done.36, pred[]{:T(512)S(6)} %eq.10), kind=kOutput, calls=%fused_computation.337 | convolution fusion | flops 7308656640 | bytes 24286080 | tf_op jit(solution)/shard_map/dot_general | solution.py:35
  684.9 17.1 %fusion.7 = bf16[736,4304]{1,0:T(8,128)(2,1)} fusion(f32[736,4304]{1,0:T(8,128)} %get-tuple-element.79, f32[736,4304]{1,0:T(8,128)} %fusion.172, bf16[736,16]{0,1:T(8,128)(2,1)S(1)} %copy-done.108, bf16[1,2,8,16,4304]{4,3,2,1,0:T(8,128)(2,1)} %get-tuple-element.40, s32[]{:T(128)S(6)} %add.362, s32[]{:T(128)S(6)} %select_n.67), kind=kOutput, calls=%fused_computation.15 | convolution fusion | flops 180561408 | bytes 32122888 | tf_op jit(solution)/shard_map/dot_general | solution.py:31
  702.0 12.9 %fusion.186 = f32[736,1152]{1,0:T(8,128)S(1)} fusion(bf16[736,4304]{1,0:T(8,128)(2,1)} %fusion.7, bf16[1152,4304]{1,0:T(8,128)(2,1)} %weight_rows_odd.3), kind=kOutput, calls=%fused_computation.350 | convolution fusion | flops 7298482176 | bytes 19643392 | tf_op jit(solution)/shard_map/dot_general | solution.py:35
  714.9 4.7 convolution_convert_fusion.30
  733.8 44.9 %attention_backward.2 = bf16[736,3456]{1,0:T(8,128)(2,1)} custom-call(s32[1]{0:T(128)} %dynamic_slice.55.a, bf16[736,3456]{1,0:T(8,128)(2,1)} %fusion.13.b, bf16[736,1152]{1,0:T(8,128)(2,1)} %fusion.30.c, bf16[736,1152]{1,0:T(8,128)(2,1)} %get-tuple-element.10.d, f32[736,128]{1,0:T(8,128)} %get-tuple-element.11.e), custom_call_target="tpu_custom_call" | custom-call | flops 22187868160 | bytes 13565952 | tf_op jit(solution)/shard_map/attention_backward/pallas_call | solution.py:262
  778.7 10.4 fusion.188
  801.3 14.8 %fusion.168 = f32[736,4304]{1,0:T(8,128)} fusion(bf16[4304,1152]{1,0:T(8,128)(2,1)} %weight_rows.8, f32[736,1152]{1,0:T(8,128)S(1)} %add_add_fusion.7), kind=kOutput, calls=%fused_computation.335 | convolution fusion | flops 7299330048 | bytes 25978880 | tf_op jit(solution)/shard_map/dot_general | solution.py:35
  820.1 4.6 all-to-all-start.3
  824.8 17.2 %fusion.3 = bf16[736,4304]{1,0:T(8,128)(2,1)} fusion(f32[736,4304]{1,0:T(8,128)} %get-tuple-element.73, f32[736,4304]{1,0:T(8,128)} %fusion.168, bf16[736,16]{0,1:T(8,128)(2,1)S(1)} %copy-done.81, bf16[1,2,8,16,4304]{4,3,2,1,0:T(8,128)(2,1)} %get-tuple-element.41, s32[]{:T(128)S(6)} %add.362, s32[]{:T(128)S(6)} %select_n.67), kind=kOutput, calls=%fused_computation.11 | convolution fusion | flops 180561408 | bytes 32122888 | tf_op jit(solution)/shard_map/dot_general | solution.py:31
  842.0 14.7 %fusion.189 = f32[736,1152]{1,0:T(8,128)} fusion(bf16[736,4304]{1,0:T(8,128)(2,1)} %fusion.3, bf16[1152,4304]{1,0:T(8,128)(2,1)} %weight_rows_odd.2), kind=kOutput, calls=%fused_computation.353 | convolution fusion | flops 7298482176 | bytes 19643392 | tf_op jit(solution)/shard_map/dot_general | solution.py:35
  863.3 5.9 all-to-all-start.2
  869.5 4.8 convolution_convert_fusion.27
  890.0 45.2 %attention_backward.3 = bf16[736,3456]{1,0:T(8,128)(2,1)} custom-call(s32[1]{0:T(128)} %dynamic_slice.55.a, bf16[736,3456]{1,0:T(8,128)(2,1)} %fusion.12.b, bf16[736,1152]{1,0:T(8,128)(2,1)} %fusion.31.c, bf16[736,1152]{1,0:T(8,128)(2,1)} %get-tuple-element.9.d, f32[736,128]{1,0:T(8,128)} %get-tuple-element.12.e), custom_call_target="tpu_custom_call" | custom-call | flops 22187868160 | bytes 13565952 | tf_op jit(solution)/shard_map/attention_backward/pallas_call | solution.py:262
  952.9 4.4 reduce.5
  959.5 5.9 all-to-all-start
  965.4 16.2 %all-to-all-done = bf16[32,2,2880]{2,1,0:T(2,128)(2,1)} async-done(((bf16[32,2,2880]{2,1,0:T(2,128)(2,1)}), bf16[32,2,2880]{2,1,0:T(2,128)(2,1)}, u32[]{:S(2)}, u32[]{:S(2)}) %all-to-all-start) | async-done | bytes 368672 | tf_op jit(solution)/shard_map/all_to_all | solution.py:490
  997.6 4.7 convolution_convert_fusion.32
  1005.5 4.4 reduce.4
  1015.5 13.0 %convolution_add_fusion.12 = f32[736,1152]{1,0:T(8,128)S(1)} fusion(bf16[736,4304]{1,0:T(8,128)(2,1)} %get-tuple-element.78, bf16[4304,1152]{1,0:T(8,128)(2,1)} %weight_rows.11, f32[1152]{0:T(1024)S(1)} %copy-done.116), kind=kOutput, calls=%fused_computation.71 | convolution fusion | flops 7299330048 | bytes 19648000 | tf_op jit(solution)/shard_map/dot_general | solution.py:31
  1038.7 10.4 fusion.191
  1059.0 18.0 %collective-permute-done.3 = bf16[368,1152]{1,0:T(8,128)(2,1)S(1)} collective-permute-done((bf16[368,1152]{1,0:T(8,128)(2,1)S(1)}, bf16[368,1152]{1,0:T(8,128)(2,1)S(1)}, u32[]{:S(2)}, u32[]{:S(2)}) %collective-permute-start.3) | collective-permute-done | bytes 847904 | tf_op jit(solution)/shard_map/ppermute | solution.py:341
  1088.0 4.8 convert_element_type.293
  1092.8 15.2 %all-gather.15.cloned.1.call-done = bf16[32,8,5,1152]{3,1,2,0:T(8,128)(2,1)} async-done(((bf16[1,8,5,1152]{3,1,2,0:T(8,128)(2,1)}), bf16[32,8,5,1152]{3,1,2,0:T(8,128)(2,1)}) %all-gather.15.cloned.1.call-update) | async-done | bytes 2949136 | tf_op jit(solution)/shard_map/all_gather | solution.py:498
  1117.5 5.4 copy.34
  (426 shorter events, 209.5 us)
Async XLA Ops:
  7.2 201.2 %all-gather.9.cloned.1.call-start = ((), (), s32[]{:S(2)}) async-start(), calls=%async_computation.4 | async-start | bytes 32448512 | tf_op jit(solution)/shard_map/all_gather | solution.py:363
  50.5 314.3 %all-gather.11.cloned.1.call-start = ((), (), s32[]{:S(2)}) async-start(), calls=%async_computation.5 | async-start | bytes 32448512 | tf_op jit(solution)/shard_map/all_gather | solution.py:363
  51.9 77.8 %copy-start.121 = (s32[2]{0:T(128)S(1)}, s32[2]{0:T(128)}, u32[]{:S(2)}) copy-start(s32[2]{0:T(128)} %param.12) | copy-start | bytes 28
  53.0 314.4 %copy-start.18 = (bf16[368,1152]{1,0:T(8,128)(2,1)}, bf16[368,1152]{1,0:T(8,128)(2,1)S(1)}, u32[]{:S(2)}) copy-start(bf16[368,1152]{1,0:T(8,128)(2,1)S(1)} %get-tuple-element.49) | copy-start | bytes 2543620
  53.0 90.8 %collective-permute-start = (bf16[368,1152]{1,0:T(8,128)(2,1)}, bf16[368,1152]{1,0:T(8,128)(2,1)S(1)}, u32[]{:S(2)}, u32[]{:S(2)}) collective-permute-start(bf16[368,1152]{1,0:T(8,128)(2,1)} %get-tuple-element.48), channel_id=1, source_target_pairs={{0,1},{1,0},{2,3},{3,2},{4,5},{5,4},{6,7},{7,6},{8,9},{9,8},{10,11... | collective-permute-start | bytes 2543624 | tf_op jit(solution)/shard_map/ppermute | solution.py:327
  59.7 85.7 %copy-start.36 = (bf16[368,1152]{1,0:T(8,128)(2,1)}, bf16[368,1152]{1,0:T(8,128)(2,1)S(1)}, u32[]{:S(2)}) copy-start(bf16[368,1152]{1,0:T(8,128)(2,1)S(1)} %get-tuple-element.44) | copy-start | bytes 2543620
  59.7 85.7 %collective-permute-start.2 = (bf16[368,1152]{1,0:T(8,128)(2,1)}, bf16[368,1152]{1,0:T(8,128)(2,1)S(1)}, u32[]{:S(2)}, u32[]{:S(2)}) collective-permute-start(bf16[368,1152]{1,0:T(8,128)(2,1)} %get-tuple-element.45), channel_id=1, source_target_pairs={{0,1},{1,0},{2,3},{3,2},{4,5},{5,4},{6,7},{7,6},{8,9},{9,8},{10,11... | collective-permute-start | bytes 2543624 | tf_op jit(solution)/shard_map/ppermute | solution.py:327
  135.1 394.4 %copy-start.58 = (bf16[1,3,1,16,1152]{4,3,2,1,0:T(8,128)(2,1)}, bf16[1,3,1,16,1152]{4,3,2,1,0:T(8,128)(2,1)S(1)}, u32[]{:S(2)}) copy-start(bf16[1,3,1,16,1152]{4,3,2,1,0:T(8,128)(2,1)S(1)} %constant_dynamic-slice_fusion) | copy-start | bytes 331780
  142.2 311.1 %copy-start.67 = (f32[736]{0:T(1024)}, f32[736]{0:T(1024)S(1)}, u32[]{:S(2)}) copy-start(f32[736]{0:T(1024)S(1)} %fusion.153) | copy-start | bytes 8836
  143.8 223.7 %copy-start.33 = (bf16[368,1152]{1,0:T(8,128)(2,1)}, bf16[368,1152]{1,0:T(8,128)(2,1)S(1)}, u32[]{:S(2)}) copy-start(bf16[368,1152]{1,0:T(8,128)(2,1)S(1)} %collective-permute-done) | copy-start | bytes 2543620
  144.4 223.0 %copy-start.91 = (f32[736]{0:T(1024)}, f32[736]{0:T(1024)S(1)}, u32[]{:S(2)}) copy-start(f32[736]{0:T(1024)S(1)} %broadcast_multiply_fusion.3) | copy-start | bytes 8836
  145.4 222.1 %copy-start.97 = (f32[736]{0:T(1024)}, f32[736]{0:T(1024)S(1)}, u32[]{:S(2)}) copy-start(f32[736]{0:T(1024)S(1)} %fusion.154) | copy-start | bytes 8836
  366.1 162.1 %copy-start.86 = (f32[1152]{0:T(1024)}, f32[1152]{0:T(1024)S(1)}, u32[]{:S(2)}) copy-start(f32[1152]{0:T(1024)S(1)} %get-tuple-element.59) | copy-start | bytes 13828
  367.5 88.4 %copy-start.88 = (f32[1152]{0:T(1024)}, f32[1152]{0:T(1024)S(1)}, u32[]{:S(2)}) copy-start(f32[1152]{0:T(1024)S(1)} %get-tuple-element.62) | copy-start | bytes 13828
  369.7 24.6 %copy-start.23 = (bf16[736,1152]{1,0:T(8,128)(2,1)}, bf16[736,1152]{1,0:T(8,128)(2,1)S(1)}, u32[]{:S(2)}) copy-start(bf16[736,1152]{1,0:T(8,128)(2,1)S(1)} %add_convert_fusion.3) | copy-start | bytes 5087236
  455.3 70.8 %copy-start.5 = (f32[736,1152]{1,0:T(8,128)}, f32[736,1152]{1,0:T(8,128)S(1)}, u32[]{:S(2)}) copy-start(f32[736,1152]{1,0:T(8,128)S(1)} %get-tuple-element.71) | copy-start | bytes 10174468
  459.5 25.8 %copy-start.84 = (bf16[736,16]{0,1:T(8,128)(2,1)}, bf16[736,16]{0,1:T(8,128)(2,1)S(1)}, u32[]{:S(2)}) copy-start(bf16[736,16]{0,1:T(8,128)(2,1)S(1)} %convolution_convert_fusion.36) | copy-start | bytes 70660
  473.1 12.2 %copy-start.115 = (f32[4304]{0:T(1024)S(1)}, f32[4304]{0:T(1024)}, u32[]{:S(2)}) copy-start(f32[4304]{0:T(1024)} %slice_convert_fusion.3) | copy-start | bytes 51652
  499.5 26.6 %copy-start.71 = (bf16[736,16]{0,1:T(8,128)(2,1)}, bf16[736,16]{0,1:T(8,128)(2,1)S(1)}, u32[]{:S(2)}) copy-start(bf16[736,16]{0,1:T(8,128)(2,1)S(1)} %convolution_convert_fusion.35) | copy-start | bytes 70660
  529.5 24.4 %copy-start.21 = (bf16[736,1152]{1,0:T(8,128)(2,1)}, bf16[736,1152]{1,0:T(8,128)(2,1)S(1)}, u32[]{:S(2)}) copy-start(bf16[736,1152]{1,0:T(8,128)(2,1)S(1)} %add_convert_fusion.1) | copy-start | bytes 5087236
  614.5 108.8 %copy-start = (f32[736,1152]{1,0:T(8,128)}, f32[736,1152]{1,0:T(8,128)S(1)}, u32[]{:S(2)}) copy-start(f32[736,1152]{1,0:T(8,128)S(1)} %get-tuple-element.77) | copy-start | bytes 10174468
  654.5 13.5 %copy-start.68 = (f32[736]{0:T(1024)S(1)}, f32[736]{0:T(1024)}, u32[]{:S(2)}) copy-start(f32[736]{0:T(1024)} %copy-done.67) | copy-start | bytes 8836
  668.0 16.9 %copy-start.108 = (bf16[736,16]{0,1:T(8,128)(2,1)S(1)}, bf16[736,16]{0,1:T(8,128)(2,1)}, u32[]{:S(2)}) copy-start(bf16[736,16]{0,1:T(8,128)(2,1)} %convolution_convert_fusion.31) | copy-start | bytes 70660
  797.1 19.0 %slice-start = ((s8[6406144]{0:T(1024)(128)(4,1)}), s8[4194304]{0:T(1024)(128)(4,1)S(1)}, s32[]{:S(2)}) async-start(s8[6406144]{0:T(1024)(128)(4,1)} %bitcast.296), calls=%async_computation.10 | async-start | bytes 8388608
  799.3 16.9 %copy-start.7 = (f32[736,1152]{1,0:T(8,128)}, f32[736,1152]{1,0:T(8,128)S(1)}, u32[]{:S(2)}) copy-start(f32[736,1152]{1,0:T(8,128)S(1)} %add_add_fusion.7) | copy-start | bytes 10174468
  801.3 14.8 %slice-start.1 = ((s8[6406144]{0:T(1024)(128)(4,1)}), s8[2211840]{0:T(1024)(128)(4,1)S(1)}, s32[]{:S(2)}) async-start(s8[6406144]{0:T(1024)(128)(4,1)} %bitcast.296), calls=%async_computation.11 | async-start | bytes 4423680
  816.2 40.5 %slice-start.2 = ((s8[6406144]{0:T(1024)(128)(4,1)}), s8[2211840]{0:T(1024)(128)(4,1)S(1)}, s32[]{:S(2)}) async-start(s8[6406144]{0:T(1024)(128)(4,1)} %bitcast.298), calls=%async_computation.12 | async-start | bytes 4423680
  820.1 40.4 %all-to-all-start.3 = ((bf16[32,2,2152]{2,1,0:T(2,128)(2,1)}), bf16[32,2,2152]{2,1,0:T(2,128)(2,1)S(1)}, u32[]{:S(2)}, u32[]{:S(2)}) async-start(bf16[32,2,2152]{2,1,0:T(2,128)(2,1)} %reshape.369), calls=%async_computation.3 | async-start | bytes 557056 | tf_op jit(solution)/shard_map/all_to_all | solution.py:490
  824.7 254.4 %all-gather.19.cloned.1.call-start = ((), (), s32[]{:S(2)}) async-start(), calls=%async_computation.9 | async-start | bytes 2297856 | tf_op jit(solution)/shard_map/all_gather | solution.py:498
  824.8 31.9 %slice-start.3 = ((s8[6406144]{0:T(1024)(128)(4,1)}), s8[4194304]{0:T(1024)(128)(4,1)S(1)}, s32[]{:S(2)}) async-start(s8[6406144]{0:T(1024)(128)(4,1)} %bitcast.298), calls=%async_computation.13 | async-start | bytes 8388608
  863.3 23.6 %all-to-all-start.2 = ((bf16[32,2,2152]{2,1,0:T(2,128)(2,1)}), bf16[32,2,2152]{2,1,0:T(2,128)(2,1)}, u32[]{:S(2)}, u32[]{:S(2)}) async-start(bf16[32,2,2152]{2,1,0:T(2,128)(2,1)} %reshape.371), calls=%async_computation.2 | async-start | bytes 557056 | tf_op jit(solution)/shard_map/all_to_all | solution.py:490
  869.3 211.8 %all-gather.17.cloned.1.call-start = ((), (), s32[]{:S(2)}) async-start(), calls=%async_computation.8 | async-start | bytes 2297856 | tf_op jit(solution)/shard_map/all_gather | solution.py:498
  890.0 45.2 %copy-start.64 = (bf16[736,48]{0,1:T(8,128)(2,1)S(1)}, bf16[736,48]{0,1:T(8,128)(2,1)}, u32[]{:S(2)}) copy-start(bf16[736,48]{0,1:T(8,128)(2,1)} %copy-done.63) | copy-start | bytes 211972
  951.1 36.1 %copy-start.62 = (bf16[736,48]{0,1:T(8,128)(2,1)S(1)}, bf16[736,48]{0,1:T(8,128)(2,1)}, u32[]{:S(2)}) copy-start(bf16[736,48]{0,1:T(8,128)(2,1)} %copy-done.61) | copy-start | bytes 211972
  959.5 22.1 %all-to-all-start = ((bf16[32,2,2880]{2,1,0:T(2,128)(2,1)}), bf16[32,2,2880]{2,1,0:T(2,128)(2,1)}, u32[]{:S(2)}, u32[]{:S(2)}) async-start(bf16[32,2,2880]{2,1,0:T(2,128)(2,1)} %reshape.367), calls=%async_computation | async-start | bytes 753664 | tf_op jit(solution)/shard_map/all_to_all | solution.py:490
  965.3 122.6 %all-gather.13.cloned.1.call-start = ((), (), s32[]{:S(2)}) async-start(), calls=%async_computation.6 | async-start | bytes 3041280 | tf_op jit(solution)/shard_map/all_gather | solution.py:498
  1003.7 11.8 %copy-start.116 = (f32[1152]{0:T(1024)S(1)}, f32[1152]{0:T(1024)}, u32[]{:S(2)}) copy-start(f32[1152]{0:T(1024)} %get-tuple-element.52) | copy-start | bytes 13828
  1012.1 21.1 %all-to-all-start.1 = ((bf16[32,2,2880]{2,1,0:T(2,128)(2,1)}), bf16[32,2,2880]{2,1,0:T(2,128)(2,1)}, u32[]{:S(2)}, u32[]{:S(2)}) async-start(bf16[32,2,2880]{2,1,0:T(2,128)(2,1)} %reshape.365), calls=%async_computation.1 | async-start | bytes 753664 | tf_op jit(solution)/shard_map/all_to_all | solution.py:490
  1015.4 92.5 %all-gather.15.cloned.1.call-start = ((), (), s32[]{:S(2)}) async-start(), calls=%async_computation.7 | async-start | bytes 3041280 | tf_op jit(solution)/shard_map/all_gather | solution.py:498
  1015.5 13.0 %copy-start.1 = (f32[736,1152]{1,0:T(8,128)S(1)}, f32[736,1152]{1,0:T(8,128)}, u32[]{:S(2)}) copy-start(f32[736,1152]{1,0:T(8,128)} %copy-done) | copy-start | bytes 10174468
  1031.4 24.0 %collective-permute-start.1 = (bf16[368,1152]{1,0:T(8,128)(2,1)}, bf16[368,1152]{1,0:T(8,128)(2,1)}, u32[]{:S(2)}, u32[]{:S(2)}) collective-permute-start(bf16[368,1152]{1,0:T(8,128)(2,1)} %get-tuple-element.47), channel_id=1, source_target_pairs={{0,1},{1,0},{2,3},{3,2},{4,5},{5,4},{6,7},{7,6},{8,9},{9,8},{10,11... | collective-permute-start | bytes 2543624 | tf_op jit(solution)/shard_map/ppermute | solution.py:341
  1038.6 10.5 copy-start.20
  1038.6 10.5 copy-start.35
  1038.6 10.5 copy-start.66
  1038.7 10.5 copy-start.92
  1038.7 10.5 copy-start.106
  1038.7 10.5 copy-start.110
  1055.0 21.9 %collective-permute-start.3 = (bf16[368,1152]{1,0:T(8,128)(2,1)S(1)}, bf16[368,1152]{1,0:T(8,128)(2,1)S(1)}, u32[]{:S(2)}, u32[]{:S(2)}) collective-permute-start(bf16[368,1152]{1,0:T(8,128)(2,1)S(1)} %get-tuple-element.43), channel_id=1, source_target_pairs={{0,1},{1,0},{2,3},{3,2},{4,5},{5,4},{6,7},{7,6},{8,9},{9,8},{10,11... | collective-permute-start | bytes 2543624 | tf_op jit(solution)/shard_map/ppermute | solution.py:341
  (92 other events, 376.4 us)
Sparse Core Ops, SparseCore 0:
  50.6 157.6 all-gather.8
  210.5 154.2 all-gather.10
  861.8 58.6 all-gather.18
  923.3 59.3 all-gather.16
  987.2 59.7 all-gather.12
  1049.8 58.0 all-gather.14

commit v2 on v1

--- a/solution.py
+++ b/solution.py
@@ -16,6 +16,7 @@
 LANES = 128
 BF16 = jnp.bfloat16
 F32 = jnp.float32
+MESH = pl.DeviceIdType.MESH
 VMEM_LIMIT = 60 << 20
 C2 = math.log2(math.e) / math.sqrt(HD)
 SCALE = 1.0 / math.sqrt(HD)
@@ -280,6 +281,220 @@
     )(*operands)
 
 
+def gather_kernel(
+    src, out, stage, local_sem, z_recv, y_recv, b_recv, h_recv, c_recv_own, c_recv_z, c_recv_y, c_recv_b, c_recv_h,
+    up_send, down_send, y_send, b_send, h_send, c_send_own, c_send_z, c_send_y, c_send_b, c_send_h,
+):
+    rows = src.shape[0]
+    unit = rows // 6 // 16 * 16 + 16
+    sizes = [unit, unit, rows // 2 - 2 * unit, rows // 2 - 2 * unit, unit]
+    begins = [0, unit, 2 * unit, rows // 2, rows - 2 * unit]
+    x = lax.axis_index("seq")
+    f = lax.axis_index("fsdp")
+    z, y, c = f // 4, (f // 2) % 2, f % 2
+
+    def place(zb, yb, j, side, cb=None):
+        owner = (zb * 2 + yb) * 2 + (c if cb is None else cb)
+        begin = jnp.where(side == 0, begins[j], rows - begins[j] - sizes[j])
+        return pl.multiple_of(owner * rows + begin, 16), sizes[j]
+
+    def view(spot):
+        return out.at[pl.ds(spot[0], spot[1]), :]
+
+    def device(zb, yb, cb, xb):
+        return ((zb * 2 + yb) * 2 + cb, xb)
+
+    up, down = device(z + 1, y, c, x), device(z - 1, y, c, x)
+    beside, across, mate = device(z, 1 - y, c, x), device(z, y, c, 1 - x), device(z, y, 1 - c, x)
+
+    def copy(spot, send, recv, to, source=None):
+        return pltpu.make_async_remote_copy(
+            src_ref=view(spot) if source is None else source,
+            dst_ref=view(spot),
+            send_sem=send,
+            recv_sem=recv,
+            device_id=to,
+            device_id_type=MESH,
+        )
+
+    def arrived(spot, recv):
+        copy(spot, local_sem.at[1], recv, mate).wait_recv()
+
+    barrier = pltpu.get_barrier_semaphore()
+    for to in (beside, across, mate):
+        pl.semaphore_signal(barrier, inc=1, device_id=to, device_id_type=MESH)
+
+    @pl.when(z < 3)
+    def _():
+        pl.semaphore_signal(barrier, inc=1, device_id=up, device_id_type=MESH)
+
+    @pl.when(z > 0)
+    def _():
+        pl.semaphore_signal(barrier, inc=1, device_id=down, device_id_type=MESH)
+
+    pl.semaphore_wait(barrier, 3 + jnp.where(z < 3, 1, 0) + jnp.where(z > 0, 1, 0))
+
+    def own(j):
+        begin = jnp.where(x == 0, begins[j], rows - begins[j] - sizes[j])
+        return src.at[pl.ds(pl.multiple_of(begin, 16), sizes[j]), :]
+
+    whole = (pl.multiple_of(f * rows, 16), rows)
+    for j in range(5):
+        spot = place(z, y, j, x)
+
+        @pl.when(z < 3)
+        def _():
+            copy(spot, up_send.at[z, j], z_recv.at[z, j], up, own(j)).start()
+
+        @pl.when(z > 0)
+        def _():
+            copy(spot, down_send.at[z, j], z_recv.at[z, j], down, own(j)).start()
+
+        if j < 3:
+            copy(spot, y_send.at[z, j], y_recv.at[z, j], beside, own(j)).start()
+    copy(whole, c_send_own.at[0], c_recv_own.at[0], mate, src).start()
+    fetch = pltpu.make_async_copy(src, stage, local_sem.at[0])
+    fetch.start()
+    fetch.wait()
+    keep = pltpu.make_async_copy(stage, view(whole), local_sem.at[0])
+    keep.start()
+
+    def z_event(d, j):
+        def flow(zb, onward, to, sends):
+            spot = place(zb, y, j, x)
+            arrived(spot, z_recv.at[zb, j])
+
+            @pl.when(onward)
+            def _():
+                copy(spot, sends.at[zb, j], z_recv.at[zb, j], to).start()
+
+            if j == 0:
+                copy(spot, b_send.at[zb], b_recv.at[zb], across).start()
+            if j < 3:
+                copy(spot, y_send.at[zb, j], y_recv.at[zb, j], beside).start()
+            copy(spot, c_send_z.at[zb, j], c_recv_z.at[zb, j], mate).start()
+
+        @pl.when(z - d >= 0)
+        def _():
+            flow(z - d, z < 3, up, up_send)
+
+        @pl.when(z + d <= 3)
+        def _():
+            flow(z + d, z > 0, down, down_send)
+
+    def each(d, act):
+        if d == 0:
+            act(z)
+            return
+
+        @pl.when(z - d >= 0)
+        def _():
+            act(z - d)
+
+        @pl.when(z + d <= 3)
+        def _():
+            act(z + d)
+
+    def y_event(d, j):
+        def act(zb):
+            spot = place(zb, 1 - y, j, x)
+            arrived(spot, y_recv.at[zb, j])
+            copy(spot, h_send.at[zb, j], h_recv.at[zb, j], across).start()
+            copy(spot, c_send_y.at[zb, j], c_recv_y.at[zb, j], mate).start()
+
+        each(d, act)
+
+    def b_event(d):
+        def act(zb):
+            spot = place(zb, y, 0, 1 - x)
+            arrived(spot, b_recv.at[zb])
+            copy(spot, c_send_b.at[zb], c_recv_b.at[zb], mate).start()
+
+        each(d, act)
+
+    def h_event(d, j):
+        def act(zb):
+            spot = place(zb, 1 - y, j, 1 - x)
+            arrived(spot, h_recv.at[zb, j])
+            copy(spot, c_send_h.at[zb, j], c_recv_h.at[zb, j], mate).start()
+
+        each(d, act)
+
+    events = []
+    for d in range(4):
+        for j in range(5):
+            at = (d - 1) * 5 + j + 1 if d else 0
+            if d:
+                events.append((at, functools.partial(z_event, d, j)))
+                if j == 0:
+                    events.append((at + 2, functools.partial(b_event, d)))
+            if j < 3:
+                ready = at + 1.5 if d else j + 1
+                events.append((ready, functools.partial(y_event, d, j)))
+                events.append((ready + 2, functools.partial(h_event, d, j)))
+    for _, event in sorted(events, key=lambda e: e[0]):
+        event()
+    keep.wait()
+    other = 1 - c
+
+    def core_spot(zb, yb, j, side):
+        return place(zb, yb, j, side, other)
+
+    arrived((pl.multiple_of(((z * 2 + y) * 2 + other) * rows, 16), rows), c_recv_own.at[0])
+    copy(whole, c_send_own.at[0], c_recv_own.at[0], mate).wait_send()
+    for d in range(4):
+        def drain(zb, d=d):
+            for j in range(5):
+                if d:
+                    arrived(core_spot(zb, y, j, x), c_recv_z.at[zb, j])
+                    copy(place(zb, y, j, x), c_send_z.at[zb, j], c_recv_z.at[zb, j], mate).wait_send()
+                if j < 3:
+                    arrived(core_spot(zb, 1 - y, j, x), c_recv_y.at[zb, j])
+                    arrived(core_spot(zb, 1 - y, j, 1 - x), c_recv_h.at[zb, j])
+                    spot = place(zb, 1 - y, j, x)
+                    copy(spot, c_send_y.at[zb, j], c_recv_y.at[zb, j], mate).wait_send()
+                    copy(spot, h_send.at[zb, j], h_recv.at[zb, j], across).wait_send()
+                    spot = place(zb, 1 - y, j, 1 - x)
+                    copy(spot, c_send_h.at[zb, j], c_recv_h.at[zb, j], mate).wait_send()
+                    spot = place(zb, y, j, x)
+                    copy(spot, y_send.at[zb, j], y_recv.at[zb, j], beside).wait_send()
+            if d:
+                arrived(core_spot(zb, y, 0, 1 - x), c_recv_b.at[zb])
+                spot = place(zb, y, 0, 1 - x)
+                copy(spot, c_send_b.at[zb], c_recv_b.at[zb], mate).wait_send()
+                spot = place(zb, y, 0, x)
+                copy(spot, b_send.at[zb], b_recv.at[zb], across).wait_send()
+
+        each(d, drain)
+        for j in range(5):
+            @pl.when(jnp.logical_and(z - d >= 0, z < 3))
+            def _():
+                zb = z - d
+                copy(place(zb, y, j, x), up_send.at[zb, j], z_recv.at[zb, j], up).wait_send()
+
+            @pl.when(jnp.logical_and(z + d <= 3, z > 0))
+            def _():
+                zb = z + d
+                copy(place(zb, y, j, x), down_send.at[zb, j], z_recv.at[zb, j], down).wait_send()
+
+
+def gather_blocks(shard, collective_id):
+    rows = shard.shape[0]
+    dma = pltpu.SemaphoreType.DMA
+    core = [dma((1,)), dma((4, 5)), dma((4, 3)), dma((4,)), dma((4, 3))]
+    return pl.pallas_call(
+        gather_kernel,
+        in_specs=[pl.BlockSpec(memory_space=pl.ANY)],
+        out_specs=pl.BlockSpec(memory_space=pl.ANY),
+        out_shape=jax.ShapeDtypeStruct((16 * rows, LANES), BF16),
+        scratch_shapes=[pltpu.VMEM((rows, LANES), BF16), dma((2,))]
+        + [dma((4, 5)), dma((4, 3)), dma((4,)), dma((4, 3))] + core
+        + [dma((4, 5)), dma((4, 5)), dma((4, 3)), dma((4,)), dma((4, 3))] + core,
+        compiler_params=pltpu.CompilerParams(collective_id=collective_id, has_side_effects=True, vmem_limit_bytes=16 << 20),
+        name="gather_blocks",
+    )(shard)
+
+
 def gelu_tanh(tensor):
     return (
         0.5
@@ -348,19 +563,18 @@
     is_live = slot < group_image_count[0]
     positions = part * tokens + jnp.arange(tokens, dtype=jnp.int32)
     row_mask = ((positions < length[0]) & is_live).astype(F32)[:, None]
-    adapter_of = lax.all_gather(adapter, ("fsdp", "seq"))
-    choice = (
-        jnp.arange(adapters, dtype=jnp.int32)[:, None] == adapter_of[None, :]
-    ).astype(F32)
-
     def pick(table):
         return lax.dynamic_index_in_dim(table, adapter, 1, keepdims=False)
 
+    shards = lax.optimization_barrier(frozen.reshape(layer_count, -1, LANES))
     hidden = to_image(activations).astype(F32) * row_mask
     stored = []
     weights = []
     for layer in range(layer_count):
-        flat = lax.all_gather(frozen[layer].reshape(-1, LANES), "fsdp", axis=0, tiled=True)
+        if (fsdp_parts, seq_parts) == (16, 2):
+            flat = gather_blocks(shards[layer], 0)
+        else:
+            flat = lax.all_gather(shards[layer], "fsdp", axis=0, tiled=True)
         w_qkv, w_o, w_1, w_2 = unpack(flat)
         vectors = lax.slice_in_dim(flat, CUT_VECTORS, CUT_VECTORS + 106, axis=0).reshape(-1)
         vectors, b_1 = vectors[: 8 * D].reshape(8, D).astype(F32), vectors[8 * D : 8 * D + FF]
@@ -483,26 +697,31 @@
         ).astype(BF16)
         rows_wide = jnp.concatenate([up_first, down_second]).astype(BF16)
 
-        def total(rows):
-            count, width = rows.shape
-            share = -(-count // device_count)
-            rows = jnp.pad(rows, ((0, share * device_count - count), (0, 0)))
-            mine = lax.all_to_all(
-                rows.reshape(device_count, share * width),
-                ("fsdp", "seq"),
-                split_axis=0,
-                concat_axis=0,
-                tiled=True,
-            )
-            mine = jnp.dot(choice, mine.astype(F32), precision=lax.Precision.HIGHEST)
-            every = lax.all_gather(
-                mine.astype(BF16).reshape(1, adapters, share, width), ("fsdp", "seq"), tiled=True
-            )
-            every = every.transpose(1, 0, 2, 3).reshape(adapters, device_count * share, width)
-            every = every[:, :count].reshape(adapters, count // R, R, width)
-            return every.transpose(1, 0, 2, 3).astype(F32)
-
-        collected[layer] = (total(rows_narrow), total(rows_wide))
+        def shares(rows):
+            share = -(-rows.shape[0] // device_count)
+            rows = jnp.pad(rows, ((0, share * device_count - rows.shape[0]), (0, 0)))
+            return rows.reshape(device_count, share * rows.shape[1])
+
+        terms = [shares(rows_narrow), shares(rows_wide)]
+        used = terms[0].shape[1] + terms[1].shape[1]
+        label = jnp.broadcast_to(adapter.astype(BF16), (device_count, -used % LANES + LANES))
+        terms = lax.all_to_all(
+            jnp.concatenate(terms + [label], axis=1),
+            ("fsdp", "seq"),
+            split_axis=0,
+            concat_axis=0,
+            tiled=True,
+        )
+        choice = jnp.arange(adapters, dtype=F32)[:, None] == terms[:, used].astype(F32)[None, :]
+        sums = jnp.dot(choice.astype(F32), terms.astype(F32), precision=lax.Precision.HIGHEST)
+        sums = lax.all_gather(sums.astype(BF16), ("fsdp", "seq")).transpose(1, 0, 2)
+        split = -(-10 * R // device_count) * D
+
+        def table(part, count, width):
+            part = part.reshape(adapters, -1, width)[:, : count * R]
+            return part.reshape(adapters, count, R, width).transpose(1, 0, 2, 3).astype(F32)
+
+        collected[layer] = (table(sums[:, :, :split], 10, D), table(sums[:, :, split:used], 2, FF))
     grad_attn = jnp.stack([entry[0][0:8] for entry in collected], axis=0)
     grad_narrow = jnp.stack([entry[0][8:10] for entry in collected], axis=0)
     grad_wide = jnp.stack([entry[1] for entry in collected], axis=0)

time: 1140 us -> 1110 us (0.974)
  Pallas kernels: 249 us -> 510 us
  waiting for transfers between devices: 267 us -> 45.8 us
  blocking collectives: 69.3 us -> 21.9 us
  starting transfers between devices: 25.3 us -> 8.89 us
    pallas_call x0 -> x2, Pallas kernels: none -> 261 us  [gather_blocks(): pl.pallas_call(gather_kernel, in_specs=[pl.BlockSpec(memory_space=pl.ANY)...]
    all_gather x6 -> x2, waiting for transfers between devices: 232 us -> 0.01 us  [local(): sums = lax.all_gather(sums.astype(BF16), ('fsdp', 'seq')).transpose(1, 0, 2)]
    unnamed x1 -> x0, blocking collectives: 69.3 us -> none
    slice x1 -> x2, local copies, waits for them, and re-layouts: 43.3 us -> 3.16 us  [local(): sums[:, :, split:used]]
    all_to_all x0 -> x1, blocking collectives: none -> 21.9 us  [local(): lax.all_to_all(jnp.concatenate(terms + [label], axis=1), ('fsdp', 'seq'),...]
    all_to_all x4 -> x1, starting transfers between devices: 19.8 us -> 3.33 us  [local(): lax.all_to_all(jnp.concatenate(terms + [label], axis=1), ('fsdp', 'seq'),...]
    ppermute x2, waiting for transfers between devices: 18 us -> 33.8 us  [to_tokens(): other = lax.ppermute(other, 'seq', [(0, 1), (1, 0)])]
    convert_element_type x0 -> x2, local copies, waits for them, and re-layouts: none -> 15 us  [table(): part.reshape(adapters, count, R, width).transpose(1, 0, 2, 3).astype(F32)]
  transfers between devices with their start and end apart: 14 -> 7, of which waited for: 5 -> 3; matrix products, arithmetic and copies ran while one was open for 16% -> 23% of each run, Pallas kernels for 4% -> 42%
where the time goes in v2:
time: 1110 us; the launch traced here: 1100 us
  Pallas kernels  510 us (46%)
  matrix products  332 us (30%)
  local copies, waits for them, and re-layouts  121 us (11%)
  waiting for transfers between devices  45.8 us (4%)
  other arithmetic  44 us (4%)
  blocking collectives  21.9 us (2%)
  between operations  19.2 us (2%)
    pallas_call x2, Pallas kernels, gather_blocks(): pl.pallas_call(gather_kernel, in_specs=[pl.BlockSpec(memory_space=pl.ANY)...  261 us
    dot_general x28, matrix products, dot(): return jnp.dot(a, b, preferred_element_type=F32)  174 us
    dot_general x28, matrix products, dot_t(): lax.dot_general(a, b, (((1,), (1,)), ((), ())), preferred_element_type=F32)  127 us
    pallas_call x2, Pallas kernels, attn_bwd(): pl.pallas_call(kernel, in_specs=[pl.BlockSpec(memory_space=pltpu.SMEM)] +...  90.4 us
    pallas_call x2, Pallas kernels, attn_fwd(): pl.pallas_call(kernel, in_specs=[pl.BlockSpec(memory_space=pltpu.SMEM)] +...  66.3 us
    pallas_call x6, Pallas kernels, rows_aligned(): pl.pallas_call(functools.partial(rows_aligned_kernel, panels, rows), grid...  64.9 us
    unnamed x248, local copies, waits for them, and re-layouts  56.2 us
    ppermute x2, waiting for transfers between devices, to_tokens(): other = lax.ppermute(other, 'seq', [(0, 1), (1, 0)])  33.8 us
  transfers between devices with their start and end apart: 7, of which 3 were waited for; matrix products, arithmetic and copies ran while one was open for 23% of the time, Pallas kernels for 42%

profile of v2, /device:TPU:0, one launch (start us, length us, event | category | flops | bytes accessed | tf_op | source)
XLA Modules:
  0.0 1102.5 jit_solution(5696991301299216766)
XLA Ops:
  18.9 140.7 %gather_blocks.3.in_ref = bf16[119296,128]{1,0:T(8,128)(2,1)S(1)} custom-call(bf16[7456,128]{1,0:T(8,128)(2,1)S(1)} %get-tuple-element.40.src), custom_call_target="tpu_custom_call" | custom-call | tf_op jit(solution)/shard_map/gather_blocks/pallas_call | solution.py:485
  159.6 10.0 copy-done
  169.6 5.4 weight_rows.10
  175.0 13.4 %weight_rows.9 = bf16[1152,3456]{1,0:T(8,128)(2,1)} custom-call(bf16[119296,128]{1,0:T(8,128)(2,1)} %copy-done), custom_call_target="tpu_custom_call" | custom-call | bytes 15925248 | tf_op jit(solution)/shard_map/weight_rows/pallas_call | solution.py:51
  188.4 13.6 %weight_rows.11 = bf16[4304,1152]{1,0:T(8,128)(2,1)} custom-call(bf16[119296,128]{1,0:T(8,128)(2,1)} %copy-done), custom_call_target="tpu_custom_call" | custom-call | bytes 19832832 | tf_op jit(solution)/shard_map/weight_rows/pallas_call | solution.py:51
  202.0 13.6 %weight_rows_odd.3 = bf16[1152,4304]{1,0:T(8,128)(2,1)} custom-call(bf16[119296,128]{1,0:T(8,128)(2,1)} %copy-done), custom_call_target="tpu_custom_call" | custom-call | bytes 19832832 | tf_op jit(solution)/shard_map/weight_rows_odd/pallas_call | solution.py:102
  215.6 120.6 %gather_blocks.2.in_ref = bf16[119296,128]{1,0:T(8,128)(2,1)S(1)} custom-call(bf16[7456,128]{1,0:T(8,128)(2,1)S(1)} %get-tuple-element.41.src), custom_call_target="tpu_custom_call" | custom-call | tf_op jit(solution)/shard_map/gather_blocks/pallas_call | solution.py:485
  336.2 10.0 copy-done.1
  346.3 5.3 weight_rows.7
  351.6 13.4 %weight_rows.6 = bf16[1152,3456]{1,0:T(8,128)(2,1)} custom-call(bf16[119296,128]{1,0:T(8,128)(2,1)} %copy-done.1), custom_call_target="tpu_custom_call" | custom-call | bytes 15925248 | tf_op jit(solution)/shard_map/weight_rows/pallas_call | solution.py:51
  365.0 13.7 %weight_rows.8 = bf16[4304,1152]{1,0:T(8,128)(2,1)} custom-call(bf16[119296,128]{1,0:T(8,128)(2,1)} %copy-done.1), custom_call_target="tpu_custom_call" | custom-call | bytes 19832832 | tf_op jit(solution)/shard_map/weight_rows/pallas_call | solution.py:51
  378.8 13.6 %weight_rows_odd.2 = bf16[1152,4304]{1,0:T(8,128)(2,1)} custom-call(bf16[119296,128]{1,0:T(8,128)(2,1)} %copy-done.1), custom_call_target="tpu_custom_call" | custom-call | bytes 19832832 | tf_op jit(solution)/shard_map/weight_rows_odd/pallas_call | solution.py:102
  399.0 5.1 fusion.164
  423.1 11.7 %fusion.12.b = bf16[736,3456]{1,0:T(8,128)(2,1)} fusion(f32[736,1152]{1,0:T(8,128)} %fusion.86, f32[736,1152]{1,0:T(8,128)} %fusion.85, f32[736,1152]{1,0:T(8,128)} %fusion.84, bf16[736,1152]{1,0:T(8,128)(2,1)S(1)} %add_convert_fusion.3, bf16[1152,3456]{1,0:T(8,128)(2,1)S(1)} %bitcast.302, f32[3456]{0:T(1024)S(1)} %get-tuple-element.69), kind=kOutput, calls=%fused_computation.27 | convolution fusion | flops 5873209344 | bytes 24933888 | tf_op jit(solution)/shard_map/dot_general | solution.py:32
  434.8 33.0 %attention_forward.2 = (bf16[736,1152]{1,0:T(8,128)(2,1)}, f32[736,128]{1,0:T(8,128)}) custom-call(s32[1]{0:T(128)} %dynamic_slice.55.a, bf16[736,3456]{1,0:T(8,128)(2,1)} %fusion.12.b), custom_call_target="tpu_custom_call" | custom-call | flops 8875147264 | bytes 6782976 | tf_op jit(solution)/shard_map/attention_forward/pallas_call | solution.py:186
  469.8 5.0 convolution_add_fusion.11
  479.8 11.6 %fusion.170 = f32[736,4304]{1,0:T(8,128)} fusion(bf16[736,1152]{1,0:T(8,128)(2,1)S(1)} %add_convert_fusion.2, bf16[1152,4304]{1,0:T(8,128)(2,1)S(1)} %bitcast.294), kind=kOutput, calls=%fused_computation.342 | convolution fusion | flops 7298482176 | bytes 24283136 | tf_op jit(solution)/shard_map/dot_general | solution.py:32
  491.4 11.4 %multiply_convert_fusion.1 = (bf16[736,4304]{1,0:T(8,128)(2,1)S(1)}, f32[736,4304]{1,0:T(8,128)}) fusion(bf16[736,16]{0,1:T(8,128)(2,1)S(1)} %convolution_convert_fusion.34, bf16[1,2,8,16,4304]{4,3,2,1,0:T(8,128)(2,1)} %get-tuple-element.39, s32[]{:T(128)S(6)} %select_n.67, f32[736,4304]{1,0:T(8,128)} %fusion.170, f32[4304]{0:T(1024)S(1)} %slice_convert_fusion.5), kind=kOutput, calls=%fused_computation.22 | convolution fusion | flops 136212992 | bytes 31998788 | tf_op jit(solution)/shard_map/dot_general | solution.py:32
  505.6 8.4 convolution_add_fusion.13
  528.4 11.5 %fusion.13.b = bf16[736,3456]{1,0:T(8,128)(2,1)} fusion(f32[736,1152]{1,0:T(8,128)} %fusion.89, f32[736,1152]{1,0:T(8,128)} %fusion.88, f32[736,1152]{1,0:T(8,128)} %fusion.87, bf16[736,1152]{1,0:T(8,128)(2,1)S(1)} %add_convert_fusion.1, bf16[1152,3456]{1,0:T(8,128)(2,1)S(1)} %bitcast.304, f32[3456]{0:T(1024)S(1)} %get-tuple-element.68), kind=kOutput, calls=%fused_computation.29 | convolution fusion | flops 5873209344 | bytes 24933888 | tf_op jit(solution)/shard_map/dot_general | solution.py:32
  539.9 33.4 %attention_forward.3 = (bf16[736,1152]{1,0:T(8,128)(2,1)}, f32[736,128]{1,0:T(8,128)}) custom-call(s32[1]{0:T(128)} %dynamic_slice.55.a, bf16[736,3456]{1,0:T(8,128)(2,1)} %fusion.13.b), custom_call_target="tpu_custom_call" | custom-call | flops 8875147264 | bytes 6782976 | tf_op jit(solution)/shard_map/attention_forward/pallas_call | solution.py:186
  575.4 5.0 convolution_add_fusion.10
  584.8 11.4 %fusion.171 = f32[736,4304]{1,0:T(8,128)} fusion(bf16[736,1152]{1,0:T(8,128)(2,1)S(1)} %add_convert_fusion, bf16[1152,4304]{1,0:T(8,128)(2,1)S(1)} %bitcast.296), kind=kOutput, calls=%fused_computation.343 | convolution fusion | flops 7298482176 | bytes 24283136 | tf_op jit(solution)/shard_map/dot_general | solution.py:32
  596.2 11.3 %multiply_convert_fusion = (bf16[736,4304]{1,0:T(8,128)(2,1)S(1)}, f32[736,4304]{1,0:T(8,128)}) fusion(bf16[736,16]{0,1:T(8,128)(2,1)S(1)} %convolution_convert_fusion.31, bf16[1,2,8,16,4304]{4,3,2,1,0:T(8,128)(2,1)} %get-tuple-element.38, s32[]{:T(128)S(6)} %select_n.67, f32[736,4304]{1,0:T(8,128)} %fusion.171, f32[4304]{0:T(1024)S(1)} %slice_convert_fusion.4), kind=kOutput, calls=%fused_computation.20 | convolution fusion | flops 136212992 | bytes 31998788 | tf_op jit(solution)/shard_map/dot_general | solution.py:32
  610.9 16.8 %fusion.158 = f32[736,4304]{1,0:T(8,128)} fusion(bf16[4304,1152]{1,0:T(8,128)(2,1)} %weight_rows.11, f32[736]{0:T(1024)S(1)} %fusion.141, bf16[368,1152]{1,0:T(8,128)(2,1)} %collective-permute-done.2, bf16[368,1152]{1,0:T(8,128)(2,1)S(1)} %copy-done.33, pred[]{:T(512)S(6)} %eq.16), kind=kOutput, calls=%fused_computation.331 | convolution fusion | flops 7308656640 | bytes 24286080 | tf_op jit(solution)/shard_map/dot_general | solution.py:36
  627.7 17.1 %fusion.7 = bf16[736,4304]{1,0:T(8,128)(2,1)} fusion(f32[736,4304]{1,0:T(8,128)} %get-tuple-element.79, f32[736,4304]{1,0:T(8,128)} %fusion.158, bf16[736,16]{0,1:T(8,128)(2,1)S(1)} %convolution_convert_fusion.29, bf16[1,2,8,16,4304]{4,3,2,1,0:T(8,128)(2,1)} %get-tuple-element.38, s32[]{:T(128)S(6)} %add.360, s32[]{:T(128)S(6)} %select_n.67), kind=kOutput, calls=%fused_computation.15 | convolution fusion | flops 180561408 | bytes 32122888 | tf_op jit(solution)/shard_map/dot_general | solution.py:32
  644.8 14.9 %fusion.172 = f32[736,1152]{1,0:T(8,128)} fusion(bf16[736,4304]{1,0:T(8,128)(2,1)} %fusion.7, bf16[1152,4304]{1,0:T(8,128)(2,1)} %weight_rows_odd.3), kind=kOutput, calls=%fused_computation.344 | convolution fusion | flops 7298482176 | bytes 19643392 | tf_op jit(solution)/shard_map/dot_general | solution.py:36
  659.7 4.7 convolution_convert_fusion.28
  683.7 45.3 %attention_backward.2 = bf16[736,3456]{1,0:T(8,128)(2,1)} custom-call(s32[1]{0:T(128)} %dynamic_slice.55.a, bf16[736,3456]{1,0:T(8,128)(2,1)} %fusion.13.b, bf16[736,1152]{1,0:T(8,128)(2,1)} %fusion.26.c, bf16[736,1152]{1,0:T(8,128)(2,1)} %get-tuple-element.10.d, f32[736,128]{1,0:T(8,128)} %get-tuple-element.11.e), custom_call_target="tpu_custom_call" | custom-call | flops 22187868160 | bytes 13565952 | tf_op jit(solution)/shard_map/attention_backward/pallas_call | solution.py:263
  729.0 10.5 fusion.174
  753.2 14.4 %fusion.154 = f32[736,4304]{1,0:T(8,128)} fusion(bf16[4304,1152]{1,0:T(8,128)(2,1)} %weight_rows.8, f32[736,1152]{1,0:T(8,128)S(1)} %add_add_fusion.7), kind=kOutput, calls=%fused_computation.329 | convolution fusion | flops 7299330048 | bytes 25978880 | tf_op jit(solution)/shard_map/dot_general | solution.py:36
  767.5 16.2 %fusion.3 = bf16[736,4304]{1,0:T(8,128)(2,1)S(1)} fusion(f32[736,4304]{1,0:T(8,128)} %get-tuple-element.73, f32[736,4304]{1,0:T(8,128)} %fusion.154, bf16[736,16]{0,1:T(8,128)(2,1)S(1)} %convolution_convert_fusion.26, bf16[1,2,8,16,4304]{4,3,2,1,0:T(8,128)(2,1)} %get-tuple-element.39, s32[]{:T(128)S(6)} %add.360, s32[]{:T(128)S(6)} %select_n.67), kind=kOutput, calls=%fused_computation.11 | convolution fusion | flops 180561408 | bytes 32122888 | tf_op jit(solution)/shard_map/dot_general | solution.py:32
  783.8 16.3 %fusion.175 = f32[736,1152]{1,0:T(8,128)} fusion(bf16[736,4304]{1,0:T(8,128)(2,1)S(1)} %fusion.3, bf16[1152,4304]{1,0:T(8,128)(2,1)} %weight_rows_odd.2), kind=kOutput, calls=%fused_computation.347 | convolution fusion | flops 7298482176 | bytes 19643392 | tf_op jit(solution)/shard_map/dot_general | solution.py:36
  830.8 12.0 %all-to-all-done.1 = bf16[32,2,5120]{2,1,0:T(2,128)(2,1)} async-done(((bf16[32,2,5120]{2,1,0:T(2,128)(2,1)}), bf16[32,2,5120]{2,1,0:T(2,128)(2,1)}, u32[]{:S(2)}, u32[]{:S(2)}) %all-to-all-start.1) | async-done | bytes 655392 | tf_op jit(solution)/shard_map/all_to_all | solution.py:708
  842.7 5.0 reshape.283
  859.9 45.1 %attention_backward.3 = bf16[736,3456]{1,0:T(8,128)(2,1)} custom-call(s32[1]{0:T(128)} %dynamic_slice.55.a, bf16[736,3456]{1,0:T(8,128)(2,1)} %fusion.12.b, bf16[736,1152]{1,0:T(8,128)(2,1)} %fusion.27.c, bf16[736,1152]{1,0:T(8,128)(2,1)} %get-tuple-element.9.d, f32[736,128]{1,0:T(8,128)} %get-tuple-element.12.e), custom_call_target="tpu_custom_call" | custom-call | flops 22187868160 | bytes 13565952 | tf_op jit(solution)/shard_map/attention_backward/pallas_call | solution.py:263
  938.4 21.9 %all_to_all.24 = bf16[32,2,5120]{2,1,0:T(2,128)(2,1)} all-to-all(bf16[32,2,5120]{2,1,0:T(2,128)(2,1)} %reshape.284), channel_id=1, replica_groups=mesh['fsdp'=16,'seq'=2] {'fsdp','seq'}, dimensions={0} | all-to-all | bytes 1310720 | tf_op jit(solution)/shard_map/all_to_all | solution.py:708
  960.3 5.0 reshape.285
  968.1 12.8 %convolution_add_fusion.12 = f32[736,1152]{1,0:T(8,128)S(1)} fusion(bf16[736,4304]{1,0:T(8,128)(2,1)} %copy-done.11, bf16[4304,1152]{1,0:T(8,128)(2,1)} %weight_rows.11, f32[1152]{0:T(1024)S(1)} %copy-done.102), kind=kOutput, calls=%fused_computation.66 | convolution fusion | flops 7299330048 | bytes 19648000 | tf_op jit(solution)/shard_map/dot_general | solution.py:32
  984.4 10.3 fusion.177
  1001.2 8.0 collective-permute-done.1
  1010.7 25.8 %collective-permute-done.3 = bf16[368,1152]{1,0:T(8,128)(2,1)S(1)} collective-permute-done((bf16[368,1152]{1,0:T(8,128)(2,1)S(1)}, bf16[368,1152]{1,0:T(8,128)(2,1)S(1)}, u32[]{:S(2)}, u32[]{:S(2)}) %collective-permute-start.3) | collective-permute-done | bytes 847904 | tf_op jit(solution)/shard_map/ppermute | solution.py:556
  1038.6 5.4 copy.47
  1048.6 5.4 copy.48
  1058.5 7.4 reshape.277
  1065.9 7.6 reshape.276
  1076.7 4.8 slice_bitcast_fusion
  1082.5 4.8 copy.36
  (399 shorter events, 213.7 us)
Async XLA Ops:
  9.8 465.0 %copy-start.15 = (bf16[368,1152]{1,0:T(8,128)(2,1)}, bf16[368,1152]{1,0:T(8,128)(2,1)S(1)}, u32[]{:S(2)}) copy-start(bf16[368,1152]{1,0:T(8,128)(2,1)S(1)} %get-tuple-element.49) | copy-start | bytes 2543620
  9.8 399.2 %collective-permute-start = (bf16[368,1152]{1,0:T(8,128)(2,1)}, bf16[368,1152]{1,0:T(8,128)(2,1)S(1)}, u32[]{:S(2)}, u32[]{:S(2)}) collective-permute-start(bf16[368,1152]{1,0:T(8,128)(2,1)} %get-tuple-element.48), channel_id=1, source_target_pairs={{0,1},{1,0},{2,3},{3,2},{4,5},{5,4},{6,7},{7,6},{8,9},{9,8},{10,11... | collective-permute-start | bytes 2543624 | tf_op jit(solution)/shard_map/ppermute | solution.py:542
  14.0 593.4 %collective-permute-start.2 = (bf16[368,1152]{1,0:T(8,128)(2,1)}, bf16[368,1152]{1,0:T(8,128)(2,1)}, u32[]{:S(2)}, u32[]{:S(2)}) collective-permute-start(bf16[368,1152]{1,0:T(8,128)(2,1)} %get-tuple-element.45), channel_id=1, source_target_pairs={{0,1},{1,0},{2,3},{3,2},{4,5},{5,4},{6,7},{7,6},{8,9},{9,8},{10,11... | collective-permute-start | bytes 2543624 | tf_op jit(solution)/shard_map/ppermute | solution.py:542
  378.8 14.3 %copy-start.104 = (s32[2]{0:T(128)S(1)}, s32[2]{0:T(128)}, u32[]{:S(2)}) copy-start(s32[2]{0:T(128)} %param.12) | copy-start | bytes 28
  404.7 111.7 %copy-start.74 = (f32[1152]{0:T(1024)}, f32[1152]{0:T(1024)S(1)}, u32[]{:S(2)}) copy-start(f32[1152]{0:T(1024)S(1)} %get-tuple-element.59) | copy-start | bytes 13828
  404.7 72.8 %copy-start.76 = (f32[1152]{0:T(1024)}, f32[1152]{0:T(1024)S(1)}, u32[]{:S(2)}) copy-start(f32[1152]{0:T(1024)S(1)} %get-tuple-element.62) | copy-start | bytes 13828
  406.3 110.9 %copy-start.48 = (bf16[1,3,1,16,1152]{4,3,2,1,0:T(8,128)(2,1)}, bf16[1,3,1,16,1152]{4,3,2,1,0:T(8,128)(2,1)S(1)}, u32[]{:S(2)}) copy-start(bf16[1,3,1,16,1152]{4,3,2,1,0:T(8,128)(2,1)S(1)} %constant_dynamic-slice_fusion) | copy-start | bytes 331780
  409.0 65.8 %copy-start.29 = (bf16[368,1152]{1,0:T(8,128)(2,1)}, bf16[368,1152]{1,0:T(8,128)(2,1)S(1)}, u32[]{:S(2)}) copy-start(bf16[368,1152]{1,0:T(8,128)(2,1)S(1)} %collective-permute-done) | copy-start | bytes 2543620
  410.6 12.4 %slice-start.9 = ((s8[7962624]{0:T(1024)(128)(4,1)}), s8[4194304]{0:T(1024)(128)(4,1)S(1)}, s32[]{:S(2)}) async-start(s8[7962624]{0:T(1024)(128)(4,1)} %bitcast.301), calls=%async_computation.13 | async-start | bytes 8388608
  477.0 37.1 %copy-start.6 = (f32[736,1152]{1,0:T(8,128)}, f32[736,1152]{1,0:T(8,128)S(1)}, u32[]{:S(2)}) copy-start(f32[736,1152]{1,0:T(8,128)S(1)} %get-tuple-element.71) | copy-start | bytes 10174468
  478.4 13.0 %copy-start.21 = (bf16[736,1152]{1,0:T(8,128)(2,1)}, bf16[736,1152]{1,0:T(8,128)(2,1)S(1)}, u32[]{:S(2)}) copy-start(bf16[736,1152]{1,0:T(8,128)(2,1)S(1)} %add_convert_fusion.2) | copy-start | bytes 5087236
  479.8 11.6 %copy-start.68 = (bf16[736,16]{0,1:T(8,128)(2,1)}, bf16[736,16]{0,1:T(8,128)(2,1)S(1)}, u32[]{:S(2)}) copy-start(bf16[736,16]{0,1:T(8,128)(2,1)S(1)} %convolution_convert_fusion.34) | copy-start | bytes 70660
  479.8 25.8 %slice-start.6 = ((s8[9916416]{0:T(1024)(128)(4,1)}), s8[1527808]{0:T(1024)(128)(4,1)S(1)}, s32[]{:S(2)}) async-start(s8[9916416]{0:T(1024)(128)(4,1)} %bitcast.297), calls=%async_computation.10 | async-start | bytes 3055616
  479.8 25.8 %slice-start.7 = ((s8[9916416]{0:T(1024)(128)(4,1)}), s8[4194304]{0:T(1024)(128)(4,1)S(1)}, s32[]{:S(2)}) async-start(s8[9916416]{0:T(1024)(128)(4,1)} %bitcast.297), calls=%async_computation.11 | async-start | bytes 8388608
  491.4 14.2 %slice-start.8 = ((s8[9916416]{0:T(1024)(128)(4,1)}), s8[4194304]{0:T(1024)(128)(4,1)S(1)}, s32[]{:S(2)}) async-start(s8[9916416]{0:T(1024)(128)(4,1)} %bitcast.297), calls=%async_computation.12 | async-start | bytes 8388608
  515.9 64.5 %copy-start.4 = (f32[736,1152]{1,0:T(8,128)}, f32[736,1152]{1,0:T(8,128)S(1)}, u32[]{:S(2)}) copy-start(f32[736,1152]{1,0:T(8,128)S(1)} %get-tuple-element.75) | copy-start | bytes 10174468
  516.4 12.0 %slice-start.11 = ((s8[7962624]{0:T(1024)(128)(4,1)}), s8[4194304]{0:T(1024)(128)(4,1)S(1)}, s32[]{:S(2)}) async-start(s8[7962624]{0:T(1024)(128)(4,1)} %bitcast.303), calls=%async_computation.15 | async-start | bytes 8388608
  517.2 11.2 %copy-start.17 = (bf16[736,1152]{1,0:T(8,128)(2,1)}, bf16[736,1152]{1,0:T(8,128)(2,1)S(1)}, u32[]{:S(2)}) copy-start(bf16[736,1152]{1,0:T(8,128)(2,1)S(1)} %add_convert_fusion.1) | copy-start | bytes 5087236
  582.2 91.3 %copy-start.2 = (f32[736,1152]{1,0:T(8,128)}, f32[736,1152]{1,0:T(8,128)S(1)}, u32[]{:S(2)}) copy-start(f32[736,1152]{1,0:T(8,128)S(1)} %get-tuple-element.77) | copy-start | bytes 10174468
  583.4 12.8 %copy-start.23 = (bf16[736,1152]{1,0:T(8,128)(2,1)}, bf16[736,1152]{1,0:T(8,128)(2,1)S(1)}, u32[]{:S(2)}) copy-start(bf16[736,1152]{1,0:T(8,128)(2,1)S(1)} %add_convert_fusion) | copy-start | bytes 5087236
  596.2 11.3 %copy-start.33 = (bf16[368,1152]{1,0:T(8,128)(2,1)S(1)}, bf16[368,1152]{1,0:T(8,128)(2,1)}, u32[]{:S(2)}) copy-start(bf16[368,1152]{1,0:T(8,128)(2,1)} %get-tuple-element.44) | copy-start | bytes 2543620
  607.5 61.9 %copy-start.11 = (bf16[736,4304]{1,0:T(8,128)(2,1)}, bf16[736,4304]{1,0:T(8,128)(2,1)S(1)}, u32[]{:S(2)}) copy-start(bf16[736,4304]{1,0:T(8,128)(2,1)S(1)} %get-tuple-element.78) | copy-start | bytes 19006468
  610.9 16.8 %copy-start.100 = (bf16[736,16]{0,1:T(8,128)(2,1)}, bf16[736,16]{0,1:T(8,128)(2,1)S(1)}, u32[]{:S(2)}) copy-start(bf16[736,16]{0,1:T(8,128)(2,1)S(1)} %convolution_convert_fusion.29) | copy-start | bytes 70660
  751.8 15.7 %copy-start.8 = (f32[736,1152]{1,0:T(8,128)}, f32[736,1152]{1,0:T(8,128)S(1)}, u32[]{:S(2)}) copy-start(f32[736,1152]{1,0:T(8,128)S(1)} %add_add_fusion.7) | copy-start | bytes 10174468
  753.2 14.4 %copy-start.66 = (bf16[736,16]{0,1:T(8,128)(2,1)}, bf16[736,16]{0,1:T(8,128)(2,1)S(1)}, u32[]{:S(2)}) copy-start(bf16[736,16]{0,1:T(8,128)(2,1)S(1)} %convolution_convert_fusion.26) | copy-start | bytes 70660
  783.7 16.3 %copy-start.13 = (bf16[736,4304]{1,0:T(8,128)(2,1)}, bf16[736,4304]{1,0:T(8,128)(2,1)S(1)}, u32[]{:S(2)}) copy-start(bf16[736,4304]{1,0:T(8,128)(2,1)S(1)} %fusion.3) | copy-start | bytes 19006468
  810.0 15.0 %copy-start.7 = (f32[736,1152]{1,0:T(8,128)S(1)}, f32[736,1152]{1,0:T(8,128)}, u32[]{:S(2)}) copy-start(f32[736,1152]{1,0:T(8,128)} %copy-done.6) | copy-start | bytes 10174468
  810.0 15.0 %copy-start.63 = (f32[736]{0:T(1024)S(1)}, f32[736]{0:T(1024)}, u32[]{:S(2)}) copy-start(f32[736]{0:T(1024)} %copy-done.62) | copy-start | bytes 8836
  810.0 15.1 %copy-start.77 = (f32[1152]{0:T(1024)S(1)}, f32[1152]{0:T(1024)}, u32[]{:S(2)}) copy-start(f32[1152]{0:T(1024)} %copy-done.76) | copy-start | bytes 13828
  813.8 11.2 %copy-start.59 = (bf16[736,16]{0,1:T(8,128)(2,1)S(1)}, bf16[736,16]{0,1:T(8,128)(2,1)}, u32[]{:S(2)}) copy-start(bf16[736,16]{0,1:T(8,128)(2,1)} %convolution_convert_fusion.25) | copy-start | bytes 70660
  821.6 21.1 %all-to-all-start.1 = ((bf16[32,2,5120]{2,1,0:T(2,128)(2,1)}), bf16[32,2,5120]{2,1,0:T(2,128)(2,1)}, u32[]{:S(2)}, u32[]{:S(2)}) async-start(bf16[32,2,5120]{2,1,0:T(2,128)(2,1)} %reshape.282), calls=%async_computation.1 | async-start | bytes 1310720 | tf_op jit(solution)/shard_map/all_to_all | solution.py:708
  825.0 213.6 %all-gather.7.cloned.1.call-start = ((), (), s32[]{:S(2)}) async-start(), calls=%async_computation.3 | async-start | bytes 5406720 | tf_op jit(solution)/shard_map/all_gather | solution.py:717
  830.7 20.0 %copy-start.9 = (f32[736,1152]{1,0:T(8,128)S(1)}, f32[736,1152]{1,0:T(8,128)}, u32[]{:S(2)}) copy-start(f32[736,1152]{1,0:T(8,128)} %copy-done.8) | copy-start | bytes 10174468
  850.5 198.1 %all-gather.5.cloned.1.call-start = ((), (), s32[]{:S(2)}) async-start(), calls=%async_computation.2 | async-start | bytes 5406720 | tf_op jit(solution)/shard_map/all_gather | solution.py:717
  859.9 45.1 %copy-start.51 = (bf16[736,48]{0,1:T(8,128)(2,1)S(1)}, bf16[736,48]{0,1:T(8,128)(2,1)}, u32[]{:S(2)}) copy-start(bf16[736,48]{0,1:T(8,128)(2,1)} %copy-done.50) | copy-start | bytes 211972
  938.4 29.7 %copy-start.102 = (f32[1152]{0:T(1024)S(1)}, f32[1152]{0:T(1024)}, u32[]{:S(2)}) copy-start(f32[1152]{0:T(1024)} %get-tuple-element.52) | copy-start | bytes 13828
  968.1 12.8 %copy-start.3 = (f32[736,1152]{1,0:T(8,128)S(1)}, f32[736,1152]{1,0:T(8,128)}, u32[]{:S(2)}) copy-start(f32[736,1152]{1,0:T(8,128)} %copy-done.2) | copy-start | bytes 10174468
  968.1 12.8 %copy-start.73 = (bf16[736,16]{0,1:T(8,128)(2,1)S(1)}, bf16[736,16]{0,1:T(8,128)(2,1)}, u32[]{:S(2)}) copy-start(bf16[736,16]{0,1:T(8,128)(2,1)} %convolution_convert_fusion.30) | copy-start | bytes 70660
  982.7 12.0 %copy-start.16 = (bf16[368,1152]{1,0:T(8,128)(2,1)S(1)}, bf16[368,1152]{1,0:T(8,128)(2,1)}, u32[]{:S(2)}) copy-start(bf16[368,1152]{1,0:T(8,128)(2,1)} %copy-done.15) | copy-start | bytes 2543620
  982.7 12.0 %copy-start.30 = (bf16[368,1152]{1,0:T(8,128)(2,1)S(1)}, bf16[368,1152]{1,0:T(8,128)(2,1)}, u32[]{:S(2)}) copy-start(bf16[368,1152]{1,0:T(8,128)(2,1)} %copy-done.29) | copy-start | bytes 2543620
  982.7 12.0 %copy-start.56 = (bf16[1,3,1,16,1152]{4,3,2,1,0:T(8,128)(2,1)S(1)}, bf16[1,3,1,16,1152]{4,3,2,1,0:T(8,128)(2,1)}, u32[]{:S(2)}) copy-start(bf16[1,3,1,16,1152]{4,3,2,1,0:T(8,128)(2,1)} %copy-done.55) | copy-start | bytes 331780
  982.7 12.0 %copy-start.79 = (f32[736]{0:T(1024)S(1)}, f32[736]{0:T(1024)}, u32[]{:S(2)}) copy-start(f32[736]{0:T(1024)} %copy-done.78) | copy-start | bytes 8836
  982.7 12.0 %copy-start.93 = (f32[1152]{0:T(1024)S(1)}, f32[1152]{0:T(1024)}, u32[]{:S(2)}) copy-start(f32[1152]{0:T(1024)} %copy-done.92) | copy-start | bytes 13828
  982.7 12.0 %copy-start.95 = (bf16[736,16]{0,1:T(8,128)(2,1)S(1)}, bf16[736,16]{0,1:T(8,128)(2,1)}, u32[]{:S(2)}) copy-start(bf16[736,16]{0,1:T(8,128)(2,1)} %copy-done.94) | copy-start | bytes 70660
  982.7 12.0 %copy-start.97 = (bf16[736,16]{0,1:T(8,128)(2,1)S(1)}, bf16[736,16]{0,1:T(8,128)(2,1)}, u32[]{:S(2)}) copy-start(bf16[736,16]{0,1:T(8,128)(2,1)} %copy-done.96) | copy-start | bytes 70660
  982.7 12.0 %copy-start.99 = (bf16[736,16]{0,1:T(8,128)(2,1)S(1)}, bf16[736,16]{0,1:T(8,128)(2,1)}, u32[]{:S(2)}) copy-start(bf16[736,16]{0,1:T(8,128)(2,1)} %copy-done.98) | copy-start | bytes 70660
  982.7 26.4 %collective-permute-start.1 = (bf16[368,1152]{1,0:T(8,128)(2,1)S(1)}, bf16[368,1152]{1,0:T(8,128)(2,1)S(1)}, u32[]{:S(2)}, u32[]{:S(2)}) collective-permute-start(bf16[368,1152]{1,0:T(8,128)(2,1)S(1)} %get-tuple-element.47), channel_id=1, source_target_pairs={{0,1},{1,0},{2,3},{3,2},{4,5},{5,4},{6,7},{7,6},{8,9},{9,8},{10,11... | collective-permute-start | bytes 2543624 | tf_op jit(solution)/shard_map/ppermute | solution.py:556
  1000.6 35.9 %collective-permute-start.3 = (bf16[368,1152]{1,0:T(8,128)(2,1)S(1)}, bf16[368,1152]{1,0:T(8,128)(2,1)S(1)}, u32[]{:S(2)}, u32[]{:S(2)}) collective-permute-start(bf16[368,1152]{1,0:T(8,128)(2,1)S(1)} %get-tuple-element.43), channel_id=1, source_target_pairs={{0,1},{1,0},{2,3},{3,2},{4,5},{5,4},{6,7},{7,6},{8,9},{9,8},{10,11... | collective-permute-start | bytes 2543624 | tf_op jit(solution)/shard_map/ppermute | solution.py:556
  (77 other events, 363.1 us)
Sparse Core Ops, SparseCore 0:
  850.6 64.3 all-gather.6
  968.2 77.2 all-gather.4

commit v3 on v2

--- a/solution.py
+++ b/solution.py
@@ -490,17 +490,14 @@
         scratch_shapes=[pltpu.VMEM((rows, LANES), BF16), dma((2,))]
         + [dma((4, 5)), dma((4, 3)), dma((4,)), dma((4, 3))] + core
         + [dma((4, 5)), dma((4, 5)), dma((4, 3)), dma((4,)), dma((4, 3))] + core,
-        compiler_params=pltpu.CompilerParams(collective_id=collective_id, has_side_effects=True, vmem_limit_bytes=16 << 20),
+        compiler_params=pltpu.CompilerParams(collective_id=collective_id, has_side_effects=True, vmem_limit_bytes=VMEM_LIMIT),
         name="gather_blocks",
     )(shard)
 
 
-def gelu_tanh(tensor):
-    return (
-        0.5
-        * tensor
-        * (1.0 + jnp.tanh(0.7978845608028654 * (tensor + 0.044715 * tensor * tensor * tensor)))
-    )
+def gelu_parts(x):
+    inner = 0.7978845608028654 * (x + 0.044715 * x * x * x)
+    return jnp.tanh(inner)
 
 
 def layer_norm(tensor, gain, offset):
@@ -508,6 +505,357 @@
     centred = tensor - average
     variance = jnp.mean(centred * centred, axis=-1, keepdims=True)
     return centred * lax.rsqrt(variance + epsilon) * gain + offset
+
+
+def layer_norm_back(d_out, tensor, gain):
+    average = jnp.mean(tensor, axis=-1, keepdims=True)
+    centred = tensor - average
+    variance = jnp.mean(centred * centred, axis=-1, keepdims=True)
+    scale = lax.rsqrt(variance + epsilon)
+    normal = centred * scale
+    d_normal = d_out * gain
+    mean_d = jnp.mean(d_normal, axis=-1, keepdims=True)
+    mean_dn = jnp.mean(d_normal * normal, axis=-1, keepdims=True)
+    return (d_normal - mean_d - normal * mean_dn) * scale
+
+
+def dot_both(x, w, inner, up):
+    cut = w.shape[0] // 256 * 256
+    tail = dot(
+        jnp.concatenate([x[:, cut:], inner], axis=1), jnp.concatenate([w[cut:], up], axis=0)
+    )
+    return dot(x[:, :cut], w[:cut]) + tail
+
+
+def dot_both_t(x, w, inner, up_t):
+    cut = w.shape[1] // 256 * 256
+    tail = dot_t(
+        jnp.concatenate([x[:, cut:], inner], axis=1), jnp.concatenate([w[:, cut:], up_t], axis=1)
+    )
+    return dot_t(x[:, :cut], w[:, :cut]) + tail
+
+
+def whole(shape):
+    return pl.BlockSpec(shape, lambda i: (0,) * len(shape), pipeline_mode=pl.Buffered(1))
+
+
+def columns(rows, width):
+    return pl.BlockSpec((rows, width), lambda i: (0, i))
+
+
+def struct(shape, dtype):
+    return jax.ShapeDtypeStruct(shape, dtype)
+
+
+def dense_params(flops, bytes_accessed):
+    return dict(
+        cost_estimate=pl.CostEstimate(
+            flops=flops, bytes_accessed=bytes_accessed, transcendentals=0
+        ),
+        compiler_params=pltpu.CompilerParams(vmem_limit_bytes=VMEM_LIMIT),
+    )
+
+
+def qkv_kernel(hidden, w, vec, down, up, normed, inner, qkv, parts):
+    c = pl.program_id(0)
+
+    @pl.when(c == 0)
+    def _():
+        value = layer_norm(hidden[...], vec[0:1], vec[1:2]).astype(BF16)
+        normed[...] = value
+        narrow = dot_t(value, down[...]).astype(BF16)
+        inner[...] = narrow
+        for part in range(3):
+            parts[part] = narrow[:, part * R : (part + 1) * R]
+
+    bias = vec[pl.ds(jnp.where(c == 2, 5, 4), 1), :] * jnp.where(c == 1, 0.0, 1.0)
+    qkv[...] = (dot_both(normed[...], w[...], parts[c], up[0]) + bias).astype(BF16)
+
+
+def qkv_forward(hidden, w_qkv, vectors, attn):
+    rows = hidden.shape[0]
+    return pl.pallas_call(
+        qkv_kernel,
+        grid=(3,),
+        in_specs=[
+            whole((rows, D)),
+            columns(D, D),
+            whole((8, D)),
+            whole((3 * R, D)),
+            pl.BlockSpec((1, R, D), lambda i: (i, 0, 0)),
+        ],
+        out_specs=[whole((rows, D)), whole((rows, 3 * R)), columns(rows, D)],
+        out_shape=[
+            struct((rows, D), BF16),
+            struct((rows, 3 * R), BF16),
+            struct((rows, 3 * D), BF16),
+        ],
+        scratch_shapes=[pltpu.VMEM((3, rows, R), BF16)],
+        name="qkv_forward",
+        **dense_params(6 * rows * D * D, 14 * rows * D + 6 * D * D),
+    )(hidden, w_qkv, vectors, attn[0:3].reshape(3 * R, D), attn[4:7])
+
+
+TILE = 512
+
+
+def up_kernel(
+    attended, hidden, w_o, vec, down_o, up_o, down_1, w_1, b_1, up_1,
+    inner_o, middle, normed, inner_up, gate, activated,
+):
+    @pl.when(pl.program_id(0) == 0)
+    def _():
+        narrow = dot_t(attended[...], down_o[...]).astype(BF16)
+        inner_o[...] = narrow
+        middle[...] = hidden[...] + (dot_both(attended[...], w_o[...], narrow, up_o[...]) + vec[6:7])
+        value = layer_norm(middle[...], vec[2:3], vec[3:4]).astype(BF16)
+        normed[...] = value
+        inner_up[...] = dot_t(value, down_1[...]).astype(BF16)
+
+    x = dot_both(normed[...], w_1[...], inner_up[...], up_1[...]) + b_1[...]
+    gate[...] = x.astype(BF16)
+    activated[...] = (0.5 * x * (1.0 + gelu_parts(x))).astype(BF16)
+
+
+def up_forward(attended, hidden, w_o, vectors, attn, narrow, w_1, b_1, wide):
+    rows = hidden.shape[0]
+    return pl.pallas_call(
+        up_kernel,
+        grid=(pl.cdiv(FF, TILE),),
+        in_specs=[
+            whole((rows, D)),
+            whole((rows, D)),
+            whole((D, D)),
+            whole((8, D)),
+            whole((R, D)),
+            whole((R, D)),
+            whole((R, D)),
+            columns(D, TILE),
+            columns(1, TILE),
+            columns(R, TILE),
+        ],
+        out_specs=[
+            whole((rows, R)),
+            whole((rows, D)),
+            whole((rows, D)),
+            whole((rows, R)),
+            columns(rows, TILE),
+            columns(rows, TILE),
+        ],
+        out_shape=[
+            struct((rows, R), BF16),
+            struct((rows, D), F32),
+            struct((rows, D), BF16),
+            struct((rows, R), BF16),
+            struct((rows, FF), BF16),
+            struct((rows, FF), BF16),
+        ],
+        name="up_forward",
+        **dense_params(2 * rows * D * (D + FF), 12 * rows * D + 4 * rows * FF + 2 * D * (D + FF)),
+    )(attended, hidden, w_o, vectors, attn[3], attn[7], narrow[0], w_1, b_1, wide[0])
+
+
+THIRD = D // 3
+
+
+def down_kernel(activated, middle, w_2, b_2, down_2, up_2, inner, hidden):
+    @pl.when(pl.program_id(0) == 0)
+    def _():
+        inner[...] = dot_t(activated[...], down_2[...]).astype(BF16)
+
+    hidden[...] = middle[...] + (
+        dot(activated[...], w_2[...]) + b_2[...] + dot(inner[...], up_2[...])
+    )
+
+
+def down_forward(activated, middle, w_2, b_2, narrow, wide):
+    rows = middle.shape[0]
+    return pl.pallas_call(
+        down_kernel,
+        grid=(3,),
+        in_specs=[
+            whole((rows, FF)),
+            columns(rows, THIRD),
+            columns(FF, THIRD),
+            columns(1, THIRD),
+            whole((R, FF)),
+            columns(R, THIRD),
+        ],
+        out_specs=[whole((rows, R)), columns(rows, THIRD)],
+        out_shape=[struct((rows, R), BF16), struct((rows, D), F32)],
+        name="down_forward",
+        **dense_params(2 * rows * D * FF, 8 * rows * D + 2 * rows * FF + 2 * D * FF),
+    )(activated, middle, w_2, b_2, wide[1], narrow[1])
+
+
+def gate_kernel(
+    gradient, w_2, gate, down_2, up_1, up_2, inner_down, inner_up, d_gate, g_wide, d_inner_up, g_up_2,
+    d_branch, d_inner_down, total,
+):
+    i = pl.program_id(0)
+
+    @pl.when(i == 0)
+    def _():
+        value = gradient[...].astype(BF16)
+        d_branch[...] = value
+        d_inner_down[...] = dot_t(value, up_2[...]).astype(BF16)
+        g_up_2[...] = dot_l(inner_down[...], value)
+        total[...] = jnp.zeros_like(total)
+
+    left = FF - i * TILE
+    down = down_2[...]
+    d_act = dot_t(d_branch[...], w_2[...]) + dot(d_inner_down[...], down)
+    x = gate[...].astype(F32)
+    t = gelu_parts(x)
+    half = 0.5 * (1.0 + t)
+    slope = half + 0.5 * x * (1.0 - t * t) * (
+        0.7978845608028654 * (1.0 + 3 * 0.044715 * x * x)
+    )
+    keep = lax.broadcasted_iota(jnp.int32, (1, TILE), 1) < left
+    value = jnp.where(keep, slope * d_act, 0.0).astype(BF16)
+    d_gate[...] = value
+    up = jnp.where(keep, up_1[...], jnp.zeros_like(up_1[...]))
+    total[...] += dot_t(value, up)
+    g_wide[0:R] = dot_l(inner_up[...], value)
+    g_wide[R : 2 * R] = dot_l(d_inner_down[...], (x * half).astype(BF16))
+
+    @pl.when(i == pl.num_programs(0) - 1)
+    def _():
+        d_inner_up[...] = total[...].astype(BF16)
+
+
+def gate_backward(gradient, w_2, gate, narrow, wide, inner_down, inner_up):
+    rows = gradient.shape[0]
+    return pl.pallas_call(
+        gate_kernel,
+        grid=(pl.cdiv(FF, TILE),),
+        in_specs=[
+            whole((rows, D)),
+            pl.BlockSpec((TILE, D), lambda i: (i, 0)),
+            columns(rows, TILE),
+            columns(R, TILE),
+            columns(R, TILE),
+            whole((R, D)),
+            whole((rows, R)),
+            whole((rows, R)),
+        ],
+        out_specs=[columns(rows, TILE), columns(2 * R, TILE), whole((rows, R)), whole((R, D))],
+        out_shape=[
+            struct((rows, FF), BF16),
+            struct((2 * R, FF), F32),
+            struct((rows, R), BF16),
+            struct((R, D), F32),
+        ],
+        scratch_shapes=[
+            pltpu.VMEM((rows, D), BF16),
+            pltpu.VMEM((rows, R), BF16),
+            pltpu.VMEM((rows, R), F32),
+        ],
+        name="gate_backward",
+        **dense_params(2 * rows * D * FF, 4 * rows * D + 4 * rows * FF + 2 * D * FF),
+    )(gradient, w_2, gate, wide[1], wide[0], narrow[1], inner_down, inner_up)
+
+
+def middle_kernel(
+    d_gate, w_1, d_inner_up, down_1, normed, middle, gradient, vec, w_o, down_o, up_o, inner_o, attended,
+    d_middle, d_attended, g_rows, d_normed,
+):
+    i = pl.program_id(0)
+    at = pl.ds(pl.multiple_of(i * THIRD, LANES), THIRD)
+    d_normed[:, at] = dot_t(d_gate[...], w_1[...]) + dot(d_inner_up[...], down_1[:, at])
+
+    @pl.when(i == pl.num_programs(0) - 1)
+    def _():
+        value = gradient[...] + layer_norm_back(d_normed[...], middle[...], vec[2:3])
+        d_middle[...] = value
+        d_out = value.astype(BF16)
+        d_inner_o = dot_t(d_out, up_o[...]).astype(BF16)
+        d_attended[...] = (dot_t(d_out, w_o[...]) + dot(d_inner_o, down_o[...])).astype(BF16)
+        g_rows[0:R] = dot_l(d_inner_o, attended[...])
+        g_rows[R : 2 * R] = dot_l(inner_o[...], d_out)
+        g_rows[2 * R : 3 * R] = dot_l(d_inner_up[...], normed[...])
+
+
+def middle_backward(
+    d_gate, w_1, d_inner_up, narrow, normed, middle, gradient, vectors, w_o, attn, inner_o, attended
+):
+    rows = gradient.shape[0]
+    return pl.pallas_call(
+        middle_kernel,
+        grid=(3,),
+        in_specs=[
+            whole((rows, FF)),
+            pl.BlockSpec((THIRD, FF), lambda i: (i, 0)),
+            whole((rows, R)),
+            whole((R, D)),
+            whole((rows, D)),
+            whole((rows, D)),
+            whole((rows, D)),
+            whole((8, D)),
+            whole((D, D)),
+            whole((R, D)),
+            whole((R, D)),
+            whole((rows, R)),
+            whole((rows, D)),
+        ],
+        out_specs=[whole((rows, D)), whole((rows, D)), whole((3 * R, D))],
+        out_shape=[
+            struct((rows, D), F32),
+            struct((rows, D), BF16),
+            struct((3 * R, D), F32),
+        ],
+        scratch_shapes=[pltpu.VMEM((rows, D), F32)],
+        name="middle_backward",
+        **dense_params(2 * rows * D * (D + FF), 18 * rows * D + 2 * rows * FF + 2 * D * (D + FF)),
+    )(
+        d_gate, w_1, d_inner_up, narrow[0], normed, middle, gradient, vectors, w_o, attn[3], attn[7],
+        inner_o, attended,
+    )
+
+
+def input_kernel(
+    d_qkv, w_qkv, down, up, normed, inner, hidden, d_middle, vec, gradient, g_rows, d_normed, d_inner
+):
+    i = pl.program_id(0)
+
+    @pl.when(i == 0)
+    def _():
+        for c in range(3):
+            part = d_qkv[:, c * D : (c + 1) * D]
+            d_inner[:, c * R : (c + 1) * R] = dot_t(part, up[c]).astype(BF16)
+            g_rows[(3 + c) * R : (4 + c) * R] = dot_l(inner[:, c * R : (c + 1) * R], part)
+        g_rows[0 : 3 * R] = dot_l(d_inner[...], normed[...])
+
+    at = pl.ds(pl.multiple_of(i * THIRD, LANES), THIRD)
+    d_normed[:, at] = dot_t(d_qkv[...], w_qkv[...]) + dot(d_inner[...], down[:, at])
+
+    @pl.when(i == pl.num_programs(0) - 1)
+    def _():
+        gradient[...] = d_middle[...] + layer_norm_back(d_normed[...], hidden[...], vec[0:1])
+
+
+def input_backward(d_qkv, w_qkv, attn, normed, inner, hidden, d_middle, vectors):
+    rows = hidden.shape[0]
+    return pl.pallas_call(
+        input_kernel,
+        grid=(3,),
+        in_specs=[
+            whole((rows, 3 * D)),
+            pl.BlockSpec((THIRD, 3 * D), lambda i: (i, 0)),
+            whole((3 * R, D)),
+            whole((3, R, D)),
+            whole((rows, D)),
+            whole((rows, 3 * R)),
+            whole((rows, D)),
+            whole((rows, D)),
+            whole((8, D)),
+        ],
+        out_specs=[whole((rows, D)), whole((6 * R, D))],
+        out_shape=[struct((rows, D), F32), struct((6 * R, D), F32)],
+        scratch_shapes=[pltpu.VMEM((rows, D), F32), pltpu.VMEM((rows, 3 * R), BF16)],
+        name="input_backward",
+        **dense_params(6 * rows * D * D, 20 * rows * D + 6 * D * D),
+    )(d_qkv, w_qkv, attn[0:3].reshape(3 * R, D), attn[4:7], normed, inner, hidden, d_middle, vectors)
 
 
 def local(
@@ -578,31 +926,24 @@
         w_qkv, w_o, w_1, w_2 = unpack(flat)
         vectors = lax.slice_in_dim(flat, CUT_VECTORS, CUT_VECTORS + 106, axis=0).reshape(-1)
         vectors, b_1 = vectors[: 8 * D].reshape(8, D).astype(F32), vectors[8 * D : 8 * D + FF]
-        b_1 = b_1.astype(F32)
+        b_1 = b_1.astype(F32)[None, :]
         attn = pick(attention_adapter_weights[layer])
         narrow = pick(narrow_adapter_weights[layer])
         wide = pick(broad_adapter_weights[layer])
         weights.append((w_qkv, w_o, w_1, w_2, vectors, attn, narrow, wide))
-        normed = layer_norm(hidden, vectors[0], vectors[1]).astype(BF16)
-        inner_qkv = dot_t(normed, attn[0:3].reshape(3 * R, D)).astype(BF16)
-        lifted = jnp.concatenate(
-            [dot(inner_qkv[:, c * R : (c + 1) * R], attn[4 + c]) for c in range(3)], axis=1
-        )
-        bias_qkv = jnp.concatenate([vectors[4], jnp.zeros((D,), F32), vectors[5]])
-        qkv = (dot(normed, w_qkv) + bias_qkv + lifted).astype(BF16)
+        normed, inner_qkv, qkv = qkv_forward(hidden, w_qkv, vectors, attn)
         keys = None
         if parts > 1:
             keys = lax.all_gather(
                 qkv[:, D:], "seq", axis=0, tiled=True, axis_index_groups=groups
             )
         attended, stats = attn_fwd(length, qkv, keys)
-        inner_o = dot_t(attended, attn[3]).astype(BF16)
-        middle = hidden + (dot(attended, w_o) + vectors[6] + dot(inner_o, attn[7]))
-        normed_two = layer_norm(middle, vectors[2], vectors[3]).astype(BF16)
-        inner_up = dot_t(normed_two, narrow[0]).astype(BF16)
-        gate = dot(normed_two, w_1) + b_1 + dot(inner_up, wide[0])
-        activated = gelu_tanh(gate).astype(BF16)
-        inner_down = dot_t(activated, wide[1]).astype(BF16)
+        inner_o, middle, normed_two, inner_up, gate, activated = up_forward(
+            attended, hidden, w_o, vectors, attn, narrow, w_1, b_1, wide
+        )
+        inner_down, next_hidden = down_forward(
+            activated, middle, w_2, vectors[7:8], narrow, wide
+        )
         stored.append(
             (
                 hidden,
@@ -617,11 +958,10 @@
                 normed_two,
                 inner_up,
                 gate,
-                activated,
                 inner_down,
             )
         )
-        hidden = middle + (dot(activated, w_2) + vectors[7] + dot(inner_down, narrow[1]))
+        hidden = next_hidden
     output = to_tokens((hidden * row_mask).astype(BF16))
     gradient = to_image(cotangent).astype(F32) * row_mask
     collected = [None] * layer_count
@@ -639,27 +979,16 @@
             normed_two,
             inner_up,
             gate,
-            activated,
             inner_down,
         ) = stored[layer]
         w_qkv, w_o, w_1, w_2, vectors, attn, narrow, wide = weights[layer]
-        d_branch = gradient.astype(BF16)
-        d_inner_down = dot_t(d_branch, narrow[1]).astype(BF16)
-        up_second = dot_l(inner_down, d_branch)
-        d_activated = dot_t(d_branch, w_2) + dot(d_inner_down, wide[1])
-        down_second = dot_l(d_inner_down, activated)
-        d_gate = jax.vjp(gelu_tanh, gate)[1](d_activated)[0].astype(BF16)
-        d_inner_up = dot_t(d_gate, wide[0]).astype(BF16)
-        up_first = dot_l(inner_up, d_gate)
-        d_normed_two = dot_t(d_gate, w_1) + dot(d_inner_up, narrow[0])
-        down_first = dot_l(d_inner_up, normed_two)
-        norm_two = jax.vjp(lambda t: layer_norm(t, vectors[2], vectors[3]), middle)[1]
-        d_middle = gradient + norm_two(d_normed_two)[0]
-        d_out = d_middle.astype(BF16)
-        d_inner_o = dot_t(d_out, attn[7]).astype(BF16)
-        up_o = dot_l(inner_o, d_out)
-        d_attended = (dot_t(d_out, w_o) + dot(d_inner_o, attn[3])).astype(BF16)
-        down_o = dot_l(d_inner_o, attended)
+        d_gate, g_wide, d_inner_up, g_up_2 = gate_backward(
+            gradient, w_2, gate, narrow, wide, inner_down, inner_up
+        )
+        d_middle, d_attended, g_middle = middle_backward(
+            d_gate, w_1, d_inner_up, narrow, normed_two, middle, gradient, vectors, w_o, attn,
+            inner_o, attended,
+        )
         d_qkv = attn_bwd(length, qkv, d_attended, attended, stats, keys)
         if parts > 1:
             d_keys = lax.psum_scatter(
@@ -672,30 +1001,19 @@
             d_qkv = jnp.concatenate([d_qkv[0], d_keys.astype(BF16)], axis=1)
         else:
             d_qkv = d_qkv[0]
-        d_inner_qkv = jnp.concatenate(
-            [dot_t(d_qkv[:, c * D : (c + 1) * D], attn[4 + c]) for c in range(3)], axis=1
-        ).astype(BF16)
-        up_qkv = jnp.stack(
-            [
-                dot_l(inner_qkv[:, c * R : (c + 1) * R], d_qkv[:, c * D : (c + 1) * D])
-                for c in range(3)
-            ]
+        gradient, g_input = input_backward(
+            d_qkv, w_qkv, attn, normed, inner_qkv, layer_input, d_middle, vectors
         )
-        d_normed = dot_t(d_qkv, w_qkv) + dot(d_inner_qkv, attn[0:3].reshape(3 * R, D))
-        down_qkv = dot_l(d_inner_qkv, normed).reshape(3, R, D)
-        norm_one = jax.vjp(lambda t: layer_norm(t, vectors[0], vectors[1]), layer_input)[1]
-        gradient = d_middle + norm_one(d_normed)[0]
         rows_narrow = jnp.concatenate(
             [
-                down_qkv.reshape(3 * R, D),
-                down_o,
-                up_qkv.reshape(3 * R, D),
-                up_o,
-                down_first,
-                up_second,
+                g_input[: 3 * R],
+                g_middle[:R],
+                g_input[3 * R :],
+                g_middle[R:],
+                g_up_2,
             ]
         ).astype(BF16)
-        rows_wide = jnp.concatenate([up_first, down_second]).astype(BF16)
+        rows_wide = g_wide.astype(BF16)
 
         def shares(rows):
             share = -(-rows.shape[0] // device_count)

time: 1110 us -> 1060 us (0.955)
  matrix products: 332 us -> 1.77 us
  Pallas kernels: 510 us -> 785 us
  waiting for transfers between devices: 45.8 us -> 80.8 us
  local copies, waits for them, and re-layouts: 121 us -> 86.6 us
  blocking collectives: 21.9 us -> 45.6 us
  other arithmetic: 44 us -> 29.9 us
    dot_general x76 -> x0, matrix products: 330 us -> none  [the longest x28 174 us: dot(): return jnp.dot(a, b, preferred_element_type=F32)]
    pallas_call x0 -> x12, Pallas kernels: none -> 270 us  [the longest x2 55.6 us: gate_backward(): pl.pallas_call(gate_kernel, grid=(pl.cdiv(FF, TILE),), in_specs=[whole((r...]
    unnamed x248 -> x68, local copies, waits for them, and re-layouts: 56.2 us -> 17.5 us
    all_gather x2, waiting for transfers between devices: 0.01 us -> 35.5 us  [local(): sums = lax.all_gather(sums.astype(BF16), ('fsdp', 'seq')).transpose(1, 0, 2)]
    all_to_all x1 -> x2, blocking collectives: 21.9 us -> 45.6 us  [local(): lax.all_to_all(jnp.concatenate(terms + [label], axis=1), ('fsdp', 'seq'),...]
    all_to_all x1 -> x0, waiting for transfers between devices: 12 us -> none  [local(): lax.all_to_all(jnp.concatenate(terms + [label], axis=1), ('fsdp', 'seq'),...]
    ppermute x2, waiting for transfers between devices: 33.8 us -> 45.2 us  [to_tokens(): other = lax.ppermute(other, 'seq', [(0, 1), (1, 0)])]
  transfers between devices with their start and end apart: 7 -> 6, of which waited for: 3 -> 3; matrix products, arithmetic and copies ran while one was open for 23% -> 6% of each run, Pallas kernels for 42% -> 34%
where the time goes in v3:
time: 1060 us; the launch traced here: 1050 us
  Pallas kernels  785 us (74%)
  local copies, waits for them, and re-layouts  86.6 us (8%)
  waiting for transfers between devices  80.8 us (8%)
  blocking collectives  45.6 us (4%)
  other arithmetic  29.9 us (3%)
  between operations  17.7 us (2%)
    pallas_call x2, Pallas kernels, gather_blocks(): pl.pallas_call(gather_kernel, in_specs=[pl.BlockSpec(memory_space=pl.ANY)...  267 us
    pallas_call x2, Pallas kernels, attn_bwd(): pl.pallas_call(kernel, in_specs=[pl.BlockSpec(memory_space=pltpu.SMEM)] +...  90.1 us
    pallas_call x2, Pallas kernels, attn_fwd(): pl.pallas_call(kernel, in_specs=[pl.BlockSpec(memory_space=pltpu.SMEM)] +...  66.6 us
    pallas_call x6, Pallas kernels, rows_aligned(): pl.pallas_call(functools.partial(rows_aligned_kernel, panels, rows), grid...  65.1 us
    pallas_call x2, Pallas kernels, gate_backward(): pl.pallas_call(gate_kernel, grid=(pl.cdiv(FF, TILE),), in_specs=[whole((r...  55.6 us
    pallas_call x2, Pallas kernels, middle_backward(): pl.pallas_call(middle_kernel, grid=(3,), in_specs=[whole((rows, FF)), pl....  54.1 us
    pallas_call x2, Pallas kernels, up_forward(): pl.pallas_call(up_kernel, grid=(pl.cdiv(FF, TILE),), in_specs=[whole((row...  51.6 us
    all_to_all x2, blocking collectives, local(): lax.all_to_all(jnp.concatenate(terms + [label], axis=1), ('fsdp', 'seq'),...  45.6 us
  transfers between devices with their start and end apart: 6, of which 3 were waited for; matrix products, arithmetic and copies ran while one was open for 6% of the time, Pallas kernels for 34%

profile of v3, /device:TPU:0, one launch (start us, length us, event | category | flops | bytes accessed | tf_op | source)
XLA Modules:
  0.0 1052.7 jit_solution(7421997327241136795)
XLA Ops:
  7.2 2.6 dynamic-slice_bitcast_fusion.5
  9.8 2.9 collective-permute-start
  16.5 144.2 %gather_blocks.3.in_ref = bf16[119296,128]{1,0:T(8,128)(2,1)} custom-call(bf16[7456,128]{1,0:T(8,128)(2,1)} %get-tuple-element.112.src), custom_call_target="tpu_custom_call" | custom-call | tf_op jit(solution)/shard_map/gather_blocks/pallas_call | solution.py:485
  162.8 122.3 %gather_blocks.2.in_ref = bf16[119296,128]{1,0:T(8,128)(2,1)} custom-call(bf16[7456,128]{1,0:T(8,128)(2,1)} %get-tuple-element.113.src), custom_call_target="tpu_custom_call" | custom-call | tf_op jit(solution)/shard_map/gather_blocks/pallas_call | solution.py:485
  293.8 4.4 fusion.6
  305.0 5.7 weight_rows.10.w_o
  310.7 13.4 %weight_rows.9.w.w_qkv = bf16[1152,3456]{1,0:T(8,128)(2,1)} custom-call(bf16[119296,128]{1,0:T(8,128)(2,1)} %gather_blocks.3.in_ref), custom_call_target="tpu_custom_call" | custom-call | bytes 15925248 | tf_op jit(solution)/shard_map/weight_rows/pallas_call | solution.py:51
  324.1 13.6 %weight_rows.11.w_2 = bf16[4304,1152]{1,0:T(8,128)(2,1)} custom-call(bf16[119296,128]{1,0:T(8,128)(2,1)} %gather_blocks.3.in_ref), custom_call_target="tpu_custom_call" | custom-call | bytes 19832832 | tf_op jit(solution)/shard_map/weight_rows/pallas_call | solution.py:51
  337.7 13.6 %weight_rows_odd.3.w_1 = bf16[1152,4304]{1,0:T(8,128)(2,1)} custom-call(bf16[119296,128]{1,0:T(8,128)(2,1)} %gather_blocks.3.in_ref), custom_call_target="tpu_custom_call" | custom-call | bytes 19832832 | tf_op jit(solution)/shard_map/weight_rows_odd/pallas_call | solution.py:102
  351.9 5.4 weight_rows.7.w_o
  357.3 13.4 %weight_rows.6.w.w_qkv = bf16[1152,3456]{1,0:T(8,128)(2,1)} custom-call(bf16[119296,128]{1,0:T(8,128)(2,1)} %gather_blocks.2.in_ref), custom_call_target="tpu_custom_call" | custom-call | bytes 15925248 | tf_op jit(solution)/shard_map/weight_rows/pallas_call | solution.py:51
  370.7 13.5 %weight_rows.8.w_2 = bf16[4304,1152]{1,0:T(8,128)(2,1)} custom-call(bf16[119296,128]{1,0:T(8,128)(2,1)} %gather_blocks.2.in_ref), custom_call_target="tpu_custom_call" | custom-call | bytes 19832832 | tf_op jit(solution)/shard_map/weight_rows/pallas_call | solution.py:51
  384.2 13.6 %weight_rows_odd.2.w_1 = bf16[1152,4304]{1,0:T(8,128)(2,1)} custom-call(bf16[119296,128]{1,0:T(8,128)(2,1)} %gather_blocks.2.in_ref), custom_call_target="tpu_custom_call" | custom-call | bytes 19832832 | tf_op jit(solution)/shard_map/weight_rows_odd/pallas_call | solution.py:102
  403.4 6.9 convert_multiply_fusion
  410.3 13.6 %qkv_forward.2 = (bf16[736,1152]{1,0:T(8,128)(2,1)}, bf16[736,48]{1,0:T(8,128)(2,1)}, bf16[736,3456]{1,0:T(8,128)(2,1)}) custom-call(f32[736,1152]{1,0:T(8,128)} %get-tuple-element.143.hidden, bf16[1152,3456]{1,0:T(8,128)(2,1)} %weight_rows.6.w.w_qkv, f32[8,1152]{1,0:T(8,128)} %convert_element_type.119.vec, bf16[48,1152]{1,0:T(8,128)(2,1)} %bitcast.154, ...), custom_call_target="tpu_custom_call" | custom-call | flops 5860491264 | bytes 19832832 | tf_op jit(solution)/shard_map/qkv_forward/pallas_call | solution.py:577
  423.9 33.6 %attention_forward.2 = (bf16[736,1152]{1,0:T(8,128)(2,1)}, f32[736,128]{1,0:T(8,128)}) custom-call(s32[1]{0:T(128)} %dynamic_slice.53.a, bf16[736,3456]{1,0:T(8,128)(2,1)} %get-tuple-element.49.b), custom_call_target="tpu_custom_call" | custom-call | flops 8875147264 | bytes 6782976 | tf_op jit(solution)/shard_map/attention_forward/pallas_call | solution.py:186
  457.5 25.7 %up_forward.2 = (bf16[736,16]{1,0:T(8,128)(2,1)}, f32[736,1152]{1,0:T(8,128)}, bf16[736,1152]{1,0:T(8,128)(2,1)}, bf16[736,16]{1,0:T(8,128)(2,1)}, bf16[736,4304]{1,0:T(8,128)(2,1)}, /*index=5*/bf16[736,4304]{1,0:T(8,128)(2,1)}) custom-call(bf16[736,1152]{1,0:T(8,128)(2,1)} %get-tuple-element.50.attended.d, f32[736,1152]{1,0:T(8,128)} %get-tuple-element.143.hidden, ...), custom_call_target="tpu_custom_call" | custom-call | flops 9251979264 | bytes 35416064 | tf_op jit(solution)/shard_map/up_forward/pallas_call | solution.py:622
  483.2 18.9 %down_forward.2 = (bf16[736,16]{1,0:T(8,128)(2,1)}, f32[736,1152]{1,0:T(8,128)}) custom-call(bf16[736,4304]{1,0:T(8,128)(2,1)} %get-tuple-element.51.activated, f32[736,1152]{1,0:T(8,128)} %get-tuple-element.52.middle, bf16[4304,1152]{1,0:T(8,128)(2,1)} %weight_rows.8.w_2, f32[1,1152]{1,0:T(1,128)} %bitcast.159, bf16[16,4304]{1,0:T(8,128)(2,1)} %get-tuple-element.124.down_2, ...), custom_call_target="tpu_custom_call" | custom-call | flops 7298482176 | bytes 23034880 | tf_op jit(solution)/shard_map/down_forward/pallas_call | solution.py:673
  502.1 13.8 %qkv_forward.3 = (bf16[736,1152]{1,0:T(8,128)(2,1)}, bf16[736,48]{1,0:T(8,128)(2,1)}, bf16[736,3456]{1,0:T(8,128)(2,1)}) custom-call(f32[736,1152]{1,0:T(8,128)} %get-tuple-element.53.hidden, bf16[1152,3456]{1,0:T(8,128)(2,1)} %weight_rows.9.w.w_qkv, f32[8,1152]{1,0:T(8,128)} %convert_element_type.121.vec, bf16[48,1152]{1,0:T(8,128)(2,1)} %bitcast.156, ...), custom_call_target="tpu_custom_call" | custom-call | flops 5860491264 | bytes 19832832 | tf_op jit(solution)/shard_map/qkv_forward/pallas_call | solution.py:577
  515.8 33.1 %attention_forward.3 = (bf16[736,1152]{1,0:T(8,128)(2,1)}, f32[736,128]{1,0:T(8,128)}) custom-call(s32[1]{0:T(128)} %dynamic_slice.53.a, bf16[736,3456]{1,0:T(8,128)(2,1)} %get-tuple-element.54.b), custom_call_target="tpu_custom_call" | custom-call | flops 8875147264 | bytes 6782976 | tf_op jit(solution)/shard_map/attention_forward/pallas_call | solution.py:186
  548.9 25.9 %up_forward.3 = (bf16[736,16]{1,0:T(8,128)(2,1)}, f32[736,1152]{1,0:T(8,128)}, bf16[736,1152]{1,0:T(8,128)(2,1)}, bf16[736,16]{1,0:T(8,128)(2,1)}, bf16[736,4304]{1,0:T(8,128)(2,1)}, /*index=5*/bf16[736,4304]{1,0:T(8,128)(2,1)}) custom-call(bf16[736,1152]{1,0:T(8,128)(2,1)} %get-tuple-element.55.attended.d, f32[736,1152]{1,0:T(8,128)} %get-tuple-element.53.hidden, ...), custom_call_target="tpu_custom_call" | custom-call | flops 9251979264 | bytes 35416064 | tf_op jit(solution)/shard_map/up_forward/pallas_call | solution.py:622
  574.8 19.0 %down_forward.3 = (bf16[736,16]{1,0:T(8,128)(2,1)}, f32[736,1152]{1,0:T(8,128)}) custom-call(bf16[736,4304]{1,0:T(8,128)(2,1)} %get-tuple-element.56.activated, f32[736,1152]{1,0:T(8,128)} %get-tuple-element.57.middle, bf16[4304,1152]{1,0:T(8,128)(2,1)} %weight_rows.11.w_2, f32[1,1152]{1,0:T(1,128)} %bitcast.158, ...), custom_call_target="tpu_custom_call" | custom-call | flops 7298482176 | bytes 23034880 | tf_op jit(solution)/shard_map/down_forward/pallas_call | solution.py:673
  593.8 27.7 %gate_backward.2 = (bf16[736,4304]{1,0:T(8,128)(2,1)}, f32[32,4304]{1,0:T(8,128)}, bf16[736,16]{1,0:T(8,128)(2,1)}, f32[16,1152]{1,0:T(8,128)}) custom-call(f32[736,1152]{1,0:T(8,128)} %get-tuple-element.142.gradient, bf16[4304,1152]{1,0:T(8,128)(2,1)} %weight_rows.11.w_2, bf16[736,4304]{1,0:T(8,128)(2,1)} %get-tuple-element.59.gate, ...), custom_call_target="tpu_custom_call" | custom-call | flops 7298482176 | bytes 25978880 | tf_op jit(solution)/shard_map/gate_backward/pallas_call | solution.py:729
  621.5 27.3 %middle_backward.2 = (f32[736,1152]{1,0:T(8,128)}, bf16[736,1152]{1,0:T(8,128)(2,1)}, f32[48,1152]{1,0:T(8,128)}) custom-call(bf16[736,4304]{1,0:T(8,128)(2,1)} %get-tuple-element.62.d_gate, bf16[1152,4304]{1,0:T(8,128)(2,1)} %weight_rows_odd.3.w_1, bf16[736,16]{1,0:T(8,128)(2,1)} %get-tuple-element.63.d_inner_up, ...), custom_call_target="tpu_custom_call" | custom-call | flops 9251979264 | bytes 34167808 | tf_op jit(solution)/shard_map/middle_backward/pallas_call | solution.py:783
  648.7 45.0 %attention_backward.2.d_qkv = bf16[736,3456]{1,0:T(8,128)(2,1)} custom-call(s32[1]{0:T(128)} %dynamic_slice.53.a, bf16[736,3456]{1,0:T(8,128)(2,1)} %get-tuple-element.54.b, bf16[736,1152]{1,0:T(8,128)(2,1)} %get-tuple-element.66.c, bf16[736,1152]{1,0:T(8,128)(2,1)} %get-tuple-element.55.attended.d, f32[736,128]{1,0:T(8,128)} %get-tuple-element.67.e), custom_call_target="tpu_custom_call" | custom-call | flops 22187868160 | bytes 13565952 | tf_op jit(solution)/shard_map/attention_backward/pallas_call | solution.py:263
  693.7 21.5 %input_backward.2 = (f32[736,1152]{1,0:T(8,128)}, f32[96,1152]{1,0:T(8,128)}) custom-call(bf16[736,3456]{1,0:T(8,128)(2,1)} %attention_backward.2.d_qkv, bf16[1152,3456]{1,0:T(8,128)(2,1)} %weight_rows.9.w.w_qkv, bf16[48,1152]{1,0:T(8,128)(2,1)} %bitcast.157, bf16[3,16,1152]{2,1,0:T(8,128)(2,1)} %get-tuple-element.116.up, ...), custom_call_target="tpu_custom_call" | custom-call | flops 5860491264 | bytes 24920064 | tf_op jit(solution)/shard_map/input_backward/pallas_call | solution.py:839
  715.2 28.0 %gate_backward.3 = (bf16[736,4304]{1,0:T(8,128)(2,1)}, f32[32,4304]{1,0:T(8,128)}, bf16[736,16]{1,0:T(8,128)(2,1)}, f32[16,1152]{1,0:T(8,128)}) custom-call(f32[736,1152]{1,0:T(8,128)} %get-tuple-element.71.gradient, bf16[4304,1152]{1,0:T(8,128)(2,1)} %weight_rows.8.w_2, bf16[736,4304]{1,0:T(8,128)(2,1)} %get-tuple-element.72.gate, ...), custom_call_target="tpu_custom_call" | custom-call | flops 7298482176 | bytes 25978880 | tf_op jit(solution)/shard_map/gate_backward/pallas_call | solution.py:729
  743.2 26.9 %middle_backward.3 = (f32[736,1152]{1,0:T(8,128)}, bf16[736,1152]{1,0:T(8,128)(2,1)}, f32[48,1152]{1,0:T(8,128)}) custom-call(bf16[736,4304]{1,0:T(8,128)(2,1)} %get-tuple-element.75.d_gate, bf16[1152,4304]{1,0:T(8,128)(2,1)} %weight_rows_odd.2.w_1, bf16[736,16]{1,0:T(8,128)(2,1)} %get-tuple-element.76.d_inner_up, ...), custom_call_target="tpu_custom_call" | custom-call | flops 9251979264 | bytes 34167808 | tf_op jit(solution)/shard_map/middle_backward/pallas_call | solution.py:783
  771.1 45.1 %attention_backward.3.d_qkv = bf16[736,3456]{1,0:T(8,128)(2,1)} custom-call(s32[1]{0:T(128)} %dynamic_slice.53.a, bf16[736,3456]{1,0:T(8,128)(2,1)} %get-tuple-element.49.b, bf16[736,1152]{1,0:T(8,128)(2,1)} %get-tuple-element.79.c, bf16[736,1152]{1,0:T(8,128)(2,1)} %get-tuple-element.50.attended.d, f32[736,128]{1,0:T(8,128)} %get-tuple-element.80.e), custom_call_target="tpu_custom_call" | custom-call | flops 22187868160 | bytes 13565952 | tf_op jit(solution)/shard_map/attention_backward/pallas_call | solution.py:263
  816.1 21.5 %input_backward.3 = (f32[736,1152]{1,0:T(8,128)}, f32[96,1152]{1,0:T(8,128)}) custom-call(bf16[736,3456]{1,0:T(8,128)(2,1)} %attention_backward.3.d_qkv, bf16[1152,3456]{1,0:T(8,128)(2,1)} %weight_rows.6.w.w_qkv, bf16[48,1152]{1,0:T(8,128)(2,1)} %bitcast.155, bf16[3,16,1152]{2,1,0:T(8,128)(2,1)} %get-tuple-element.120.up, ...), custom_call_target="tpu_custom_call" | custom-call | flops 5860491264 | bytes 24920064 | tf_op jit(solution)/shard_map/input_backward/pallas_call | solution.py:839
  841.6 20.9 %all_to_all.24 = bf16[32,2,5120]{2,1,0:T(2,128)(2,1)S(1)} all-to-all(bf16[32,2,5120]{2,1,0:T(2,128)(2,1)S(1)} %reshape.136), channel_id=1, replica_groups=mesh['fsdp'=16,'seq'=2] {'fsdp','seq'}, dimensions={0} | all-to-all | bytes 1310720 | tf_op jit(solution)/shard_map/all_to_all | solution.py:1026
  866.9 24.8 %all_to_all.25 = bf16[32,2,5120]{2,1,0:T(2,128)(2,1)S(1)} all-to-all(bf16[32,2,5120]{2,1,0:T(2,128)(2,1)S(1)} %reshape.134), channel_id=1, replica_groups=mesh['fsdp'=16,'seq'=2] {'fsdp','seq'}, dimensions={0} | all-to-all | bytes 1310720 | tf_op jit(solution)/shard_map/all_to_all | solution.py:1026
  893.7 3.5 multiply_convert_fusion
  899.6 26.2 %collective-permute-done.1 = bf16[368,1152]{1,0:T(8,128)(2,1)S(1)} collective-permute-done((bf16[368,1152]{1,0:T(8,128)(2,1)S(1)}, bf16[368,1152]{1,0:T(8,128)(2,1)S(1)}, u32[]{:S(2)}, u32[]{:S(2)}) %collective-permute-start.1) | collective-permute-done | bytes 847904 | tf_op jit(solution)/shard_map/ppermute | solution.py:904
  927.4 19.0 %collective-permute-done.3 = bf16[368,1152]{1,0:T(8,128)(2,1)S(1)} collective-permute-done((bf16[368,1152]{1,0:T(8,128)(2,1)S(1)}, bf16[368,1152]{1,0:T(8,128)(2,1)S(1)}, u32[]{:S(2)}, u32[]{:S(2)}) %collective-permute-start.3) | collective-permute-done | bytes 847904 | tf_op jit(solution)/shard_map/ppermute | solution.py:904
  948.5 5.4 copy.72
  955.5 3.0 slice_convert_fusion.1
  958.5 7.4 reshape.128
  966.0 2.4 slice_bitcast_fusion.5
  968.3 5.0 slice_bitcast_fusion.1
  973.4 35.5 %all-gather.7.cloned.1.call-done = bf16[256,10240]{1,0:T(8,128)(2,1)} async-done(((bf16[8,10240]{1,0:T(8,128)(2,1)}), bf16[256,10240]{1,0:T(8,128)(2,1)}) %all-gather.7.cloned.1.call-update) | async-done | bytes 5242896 | tf_op jit(solution)/shard_map/all_gather | solution.py:1035
  1008.8 5.4 copy.71
  1015.7 3.0 slice_convert_fusion
  1018.8 7.6 reshape.129
  1026.3 2.5 slice_bitcast_fusion.4
  1028.9 2.8 slice_bitcast_fusion
  1032.7 4.8 copy.44
  1041.4 4.3 copy.46
  (131 shorter events, 49.8 us)
Async XLA Ops:
  7.2 5.6 copy-start.7
  7.2 941.3 %all-gather.5.cloned.1.call-start = ((), (), s32[]{:S(2)}) async-start(), calls=%async_computation.2 | async-start | bytes 5406720 | tf_op jit(solution)/shard_map/all_gather | solution.py:1035
  7.2 6.6 copy-start.4
  9.8 393.6 %collective-permute-start = (bf16[368,1152]{1,0:T(8,128)(2,1)}, bf16[368,1152]{1,0:T(8,128)(2,1)}, u32[]{:S(2)}, u32[]{:S(2)}) collective-permute-start(bf16[368,1152]{1,0:T(8,128)(2,1)} %get-tuple-element.133), channel_id=1, source_target_pairs={{0,1},{1,0},{2,3},{3,2},{4,5},{5,4},{6,7},{7,6},{8,9},{9,8},{10,11... | collective-permute-start | bytes 2543624 | tf_op jit(solution)/shard_map/ppermute | solution.py:890
  13.8 389.6 %collective-permute-start.2 = (bf16[368,1152]{1,0:T(8,128)(2,1)}, bf16[368,1152]{1,0:T(8,128)(2,1)}, u32[]{:S(2)}, u32[]{:S(2)}) collective-permute-start(bf16[368,1152]{1,0:T(8,128)(2,1)} %get-tuple-element.129), channel_id=1, source_target_pairs={{0,1},{1,0},{2,3},{3,2},{4,5},{5,4},{6,7},{7,6},{8,9},{9,8},{10,11... | collective-permute-start | bytes 2543624 | tf_op jit(solution)/shard_map/ppermute | solution.py:890
  162.8 125.1 %copy-start.17 = (s32[2]{0:T(128)S(1)}, s32[2]{0:T(128)}, u32[]{:S(2)}) copy-start(s32[2]{0:T(128)} %param.12) | copy-start | bytes 28
  162.8 125.7 %copy-start.18 = (s32[2]{0:T(128)S(1)}, s32[2]{0:T(128)}, u32[]{:S(2)}) copy-start(s32[2]{0:T(128)} %param.11) | copy-start | bytes 28
  162.8 127.4 %copy-start.8 = (bf16[2,2,8,16,1152]{4,3,2,1,0:T(8,128)(2,1)S(1)}, bf16[2,2,8,16,1152]{4,3,2,1,0:T(8,128)(2,1)}, u32[]{:S(2)}) copy-start(bf16[2,2,8,16,1152]{4,3,2,1,0:T(8,128)(2,1)} %param.15) | copy-start | bytes 3538948
  293.1 5.8 slice-start.2
  293.8 5.1 slice-start.3
  299.4 1.5 copy-start.5
  299.4 2.3 copy-start.6
  303.8 99.6 %copy-start.15 = (f32[736]{0:T(1024)}, f32[736]{0:T(1024)S(1)}, u32[]{:S(2)}) copy-start(f32[736]{0:T(1024)S(1)} %fusion.2) | copy-start | bytes 8836
  816.1 22.6 %copy-start.10 = (f32[32,4304]{1,0:T(8,128)S(1)}, f32[32,4304]{1,0:T(8,128)}, u32[]{:S(2)}) copy-start(f32[32,4304]{1,0:T(8,128)} %get-tuple-element.88) | copy-start | bytes 1652740
  816.1 22.7 %copy-start.14 = (f32[16,1152]{1,0:T(8,128)S(1)}, f32[16,1152]{1,0:T(8,128)}, u32[]{:S(2)}) copy-start(f32[16,1152]{1,0:T(8,128)} %get-tuple-element.87) | copy-start | bytes 221188
  841.5 23.0 %copy-start.11 = (f32[96,1152]{1,0:T(8,128)S(1)}, f32[96,1152]{1,0:T(8,128)}, u32[]{:S(2)}) copy-start(f32[96,1152]{1,0:T(8,128)} %get-tuple-element.89) | copy-start | bytes 1327108
  841.6 23.0 %copy-start.12 = (f32[48,1152]{1,0:T(8,128)S(1)}, f32[48,1152]{1,0:T(8,128)}, u32[]{:S(2)}) copy-start(f32[48,1152]{1,0:T(8,128)} %get-tuple-element.90) | copy-start | bytes 663556
  841.6 23.0 %copy-start.9 = (f32[32,4304]{1,0:T(8,128)S(1)}, f32[32,4304]{1,0:T(8,128)}, u32[]{:S(2)}) copy-start(f32[32,4304]{1,0:T(8,128)} %get-tuple-element.92) | copy-start | bytes 1652740
  862.4 2.3 copy-start.13
  864.4 144.4 %all-gather.7.cloned.1.call-start = ((), (), s32[]{:S(2)}) async-start(), calls=%async_computation.3 | async-start | bytes 5406720 | tf_op jit(solution)/shard_map/all_gather | solution.py:1035
  866.9 26.8 %copy-start.16 = (f32[736]{0:T(1024)S(1)}, f32[736]{0:T(1024)}, u32[]{:S(2)}) copy-start(f32[736]{0:T(1024)} %copy-done.15) | copy-start | bytes 8836
  897.3 28.6 %collective-permute-start.1 = (bf16[368,1152]{1,0:T(8,128)(2,1)S(1)}, bf16[368,1152]{1,0:T(8,128)(2,1)S(1)}, u32[]{:S(2)}, u32[]{:S(2)}) collective-permute-start(bf16[368,1152]{1,0:T(8,128)(2,1)S(1)} %get-tuple-element.131), channel_id=1, source_target_pairs={{0,1},{1,0},{2,3},{3,2},{4,5},{5,4},{6,7},{7,6},{8,9},{9,8},{10,11... | collective-permute-start | bytes 2543624 | tf_op jit(solution)/shard_map/ppermute | solution.py:904
  899.1 47.3 %collective-permute-start.3 = (bf16[368,1152]{1,0:T(8,128)(2,1)S(1)}, bf16[368,1152]{1,0:T(8,128)(2,1)S(1)}, u32[]{:S(2)}, u32[]{:S(2)}) collective-permute-start(bf16[368,1152]{1,0:T(8,128)(2,1)S(1)} %get-tuple-element.127), channel_id=1, source_target_pairs={{0,1},{1,0},{2,3},{3,2},{4,5},{5,4},{6,7},{7,6},{8,9},{9,8},{10,11... | collective-permute-start | bytes 2543624 | tf_op jit(solution)/shard_map/ppermute | solution.py:904
  1026.3 5.4 slice-start
  1028.9 2.8 slice-start.1
  1032.7 4.8 copy-start.2
  1032.7 4.8 copy-start.3
  1037.6 2.5 copy-start
  1037.7 3.1 copy-start.1
Sparse Core Ops, SparseCore 0:
  864.6 76.5 all-gather.4
  944.6 64.1 all-gather.6

commit v4 on v3

--- a/solution.py
+++ b/solution.py
@@ -40,93 +40,99 @@
     return lax.dot_general(a, b, (((0,), (0,)), ((), ())), preferred_element_type=F32)
 
 
-def rows_aligned_kernel(panels, rows, in_ref, out_ref, wide):
-    wide[...] = in_ref[...].astype(F32)
-    for c in range(panels):
-        out_ref[:, c * LANES : (c + 1) * LANES] = wide[pl.ds(c, rows, stride=panels), :].astype(BF16)
-
-
-def rows_aligned(flat, start, count, panels, rows):
-    step = rows * panels
+PANELS = (3 * D // LANES, D // LANES, 36, D // LANES)
+UNITS = (D // 16, D // 16, D // 16, FF // 16)
+TILES_AT = (0, 1944, 2592, 5184)
+TILES_END = 7605
+TILES_VECTORS = 22
+TILES_HELD = 7776
+FLAT_AT = (0, CUT_OUT, CUT_UP, CUT_DOWN)
+WIDE = PANELS[2] * LANES
+UP_ROWS = 16 * FF // LANES
+HALO = 1600
+
+
+def lay_kernel(own_rows, tiles, index_ref, before, own, after, out, flat, held, turned):
+    d = index_ref[0]
+    margin = 16 * PANELS[2]
+    flat[0:HALO] = before[...].astype(F32)
+    flat[HALO : HALO + own_rows] = own[...].astype(F32)
+    flat[HALO + own_rows : 2 * HALO + own_rows] = after[...].astype(F32)
+    flat_base = d * own_rows - HALO
+    tile_base = d * tiles
+
+    def span(at, units, panels):
+        low = jnp.maximum(tile_base - at, 0) // panels
+        high = jnp.clip((tile_base + tiles - at + panels - 1) // panels, 0, units)
+        return low, jnp.maximum(high, low)
+
+    for at, start, units, panels in zip(
+        TILES_AT + (TILES_END,),
+        FLAT_AT + (CUT_VECTORS,),
+        UNITS + (TILES_VECTORS,),
+        PANELS + (1,),
+    ):
+        low, high = span(at, units, panels)
+        if start == CUT_UP:
+            lane = lax.broadcasted_iota(jnp.int32, (8, LANES), 1)
+
+            def up_units(b, carry):
+                u = low + 8 * b
+                source = pl.multiple_of(start + UP_ROWS * u - flat_base, 2)
+                for j in range(16):
+                    first, shift = (FF * j) // LANES, (FF * j) % LANES
+                    turn = LANES - shift
+                    now = flat[pl.ds(source + first, 8, stride=UP_ROWS), :]
+                    now = pltpu.roll(now, turn, 1) if shift else now
+                    for c in range(34):
+                        value = now
+                        if c < 33 or shift > LANES - FF % LANES:
+                            now = flat[pl.ds(source + first + c + 1, 8, stride=UP_ROWS), :]
+                            now = pltpu.roll(now, turn, 1) if shift else now
+                            if shift:
+                                value = jnp.where(lane < turn, value, now)
+                        if c == 33:
+                            value = jnp.where(lane < FF - 33 * LANES, value, 0.0)
+                        turned[pl.ds(16 * c + j, 8, stride=16 * PANELS[2]), :] = value
+                target = pl.multiple_of(16 * (at + PANELS[2] * u - tile_base) + margin, 16)
+                held[pl.ds(target, 8 * 16 * PANELS[2]), :] = turned[...].astype(BF16)
+                return carry
+
+            turned[...] = jnp.zeros_like(turned)
+            lax.fori_loop(0, (high - low + 7) // 8, up_units, 0)
+        else:
+
+            def unit(u, carry):
+                source = pl.multiple_of(start + 16 * panels * u - flat_base, 16)
+                target = pl.multiple_of(16 * (at + panels * u - tile_base) + margin, 16)
+                for c in range(panels):
+                    value = flat[pl.ds(source + c, 16, stride=panels), :]
+                    held[pl.ds(target + 16 * c, 16), :] = value.astype(BF16)
+                return carry
+
+            lax.fori_loop(low, high, unit, 0)
+    out[...] = held[margin : margin + 16 * tiles]
+
+
+def lay_shard(index, shard, tiles, perms):
+    own_rows = shard.shape[0]
+    before = lax.ppermute(shard[own_rows - HALO :], "fsdp", perms[0])
+    after = lax.ppermute(shard[:HALO], "fsdp", perms[1])
+    vm = pl.BlockSpec(memory_space=pltpu.VMEM)
+    margin = 16 * PANELS[2]
     return pl.pallas_call(
-        functools.partial(rows_aligned_kernel, panels, rows),
-        grid=(pl.cdiv(count, rows),),
-        in_specs=[
-            pl.BlockSpec(
-                (pl.Element(step), pl.Element(LANES)),
-                lambda i: (pl.multiple_of(start + i * step, 16), 0),
-            )
-        ],
-        out_specs=pl.BlockSpec((rows, panels * LANES), lambda i: (i, 0)),
-        out_shape=jax.ShapeDtypeStruct((count, panels * LANES), BF16),
-        scratch_shapes=[pltpu.VMEM((step, LANES), F32)],
-        cost_estimate=pl.CostEstimate(
-            flops=0, bytes_accessed=4 * count * panels * LANES, transcendentals=0
-        ),
+        functools.partial(lay_kernel, own_rows, tiles),
+        in_specs=[pl.BlockSpec(memory_space=pltpu.SMEM), vm, vm, vm],
+        out_specs=vm,
+        out_shape=jax.ShapeDtypeStruct((16 * tiles, LANES), BF16),
+        scratch_shapes=[
+            pltpu.VMEM((own_rows + 2 * HALO + 8 * UP_ROWS, LANES), F32),
+            pltpu.VMEM((16 * tiles + 10 * margin, LANES), BF16),
+            pltpu.VMEM((8 * margin, LANES), F32),
+        ],
         compiler_params=pltpu.CompilerParams(vmem_limit_bytes=VMEM_LIMIT),
-        name="weight_rows",
-    )(flat)
-
-
-PERIOD = 8
-PERIOD_ROWS = PERIOD * FF // LANES
-
-
-def rows_odd_kernel(rows, in_ref, out_ref, wide, turned):
-    groups = rows // PERIOD
-    panels = -(-FF // LANES)
-    wide[...] = in_ref[...].astype(F32)
-    lane = lax.broadcasted_iota(jnp.int32, (groups, LANES), 1)
-    for j in range(PERIOD):
-        first, shift = (FF * j) // LANES, (FF * j) % LANES
-        held = wide[pl.ds(first, groups, stride=PERIOD_ROWS), :]
-        for c in range(panels):
-            after = min(first + c + 1, PERIOD_ROWS - 1)
-            after = wide[pl.ds(after, groups, stride=PERIOD_ROWS), :]
-            value = held
-            if shift:
-                value = jnp.where(
-                    lane < LANES - shift,
-                    pltpu.roll(held, LANES - shift, 1),
-                    pltpu.roll(after, LANES - shift, 1),
-                )
-            held = after
-            turned[pl.ds(c * rows + j, groups, stride=PERIOD), :] = value
-    for c in range(panels):
-        width = min(LANES, FF - c * LANES)
-        out_ref[:, c * LANES : c * LANES + width] = turned[pl.ds(c * rows, rows), :][:, :width].astype(BF16)
-
-
-def rows_odd(flat, start, count, rows):
-    step = rows * FF // LANES
-    return pl.pallas_call(
-        functools.partial(rows_odd_kernel, rows),
-        grid=(count // rows,),
-        in_specs=[
-            pl.BlockSpec(
-                (pl.Element(step), pl.Element(LANES)),
-                lambda i: (pl.multiple_of(start + i * step, 16), 0),
-            )
-        ],
-        out_specs=pl.BlockSpec((rows, FF), lambda i: (i, 0)),
-        out_shape=jax.ShapeDtypeStruct((count, FF), BF16),
-        scratch_shapes=[
-            pltpu.VMEM((step, LANES), F32),
-            pltpu.VMEM((-(-FF // LANES) * rows, LANES), F32),
-        ],
-        cost_estimate=pl.CostEstimate(flops=0, bytes_accessed=4 * count * FF, transcendentals=0),
-        compiler_params=pltpu.CompilerParams(vmem_limit_bytes=VMEM_LIMIT),
-        name="weight_rows_odd",
-    )(flat)
-
-
-def unpack(flat):
-    return (
-        rows_aligned(flat, 0, D, 3 * D // LANES, 64),
-        rows_aligned(flat, CUT_OUT, D, D // LANES, 192),
-        rows_odd(flat, CUT_UP, D, 128),
-        rows_aligned(flat, CUT_DOWN, FF, D // LANES, 288),
-    )
+        name="lay_shard",
+    )(index, before, shard, after)
 
 
 def pad_lanes(x, extra=None):
@@ -478,7 +484,7 @@
                 copy(place(zb, y, j, x), down_send.at[zb, j], z_recv.at[zb, j], down).wait_send()
 
 
-def gather_blocks(shard, collective_id):
+def gather_blocks(shard, collective_id, held_rows):
     rows = shard.shape[0]
     dma = pltpu.SemaphoreType.DMA
     core = [dma((1,)), dma((4, 5)), dma((4, 3)), dma((4,)), dma((4, 3))]
@@ -486,7 +492,7 @@
         gather_kernel,
         in_specs=[pl.BlockSpec(memory_space=pl.ANY)],
         out_specs=pl.BlockSpec(memory_space=pl.ANY),
-        out_shape=jax.ShapeDtypeStruct((16 * rows, LANES), BF16),
+        out_shape=jax.ShapeDtypeStruct((held_rows, LANES), BF16),
         scratch_shapes=[pltpu.VMEM((rows, LANES), BF16), dma((2,))]
         + [dma((4, 5)), dma((4, 3)), dma((4,)), dma((4, 3))] + core
         + [dma((4, 5)), dma((4, 5)), dma((4, 3)), dma((4,)), dma((4, 3))] + core,
@@ -535,6 +541,17 @@
     return dot_t(x[:, :cut], w[:, :cut]) + tail
 
 
+def matrix(ref, count=None):
+    units, panels = ref.shape[:2]
+    return jnp.concatenate(
+        [ref[:, p].reshape(units * 16, LANES) for p in range(count or panels)], axis=1
+    )
+
+
+def unit_block(units, panels, place):
+    return pl.BlockSpec((units, panels, 16, LANES), place)
+
+
 def whole(shape):
     return pl.BlockSpec(shape, lambda i: (0,) * len(shape), pipeline_mode=pl.Buffered(1))
 
@@ -569,7 +586,7 @@
             parts[part] = narrow[:, part * R : (part + 1) * R]
 
     bias = vec[pl.ds(jnp.where(c == 2, 5, 4), 1), :] * jnp.where(c == 1, 0.0, 1.0)
-    qkv[...] = (dot_both(normed[...], w[...], parts[c], up[0]) + bias).astype(BF16)
+    qkv[...] = (dot_both(normed[...], matrix(w), parts[c], up[0]) + bias).astype(BF16)
 
 
 def qkv_forward(hidden, w_qkv, vectors, attn):
@@ -579,7 +596,7 @@
         grid=(3,),
         in_specs=[
             whole((rows, D)),
-            columns(D, D),
+            unit_block(72, 9, lambda i: (0, i, 0, 0)),
             whole((8, D)),
             whole((3 * R, D)),
             pl.BlockSpec((1, R, D), lambda i: (i, 0, 0)),
@@ -597,6 +614,9 @@
 
 
 TILE = 512
+OUT_BLOCK = pl.BlockSpec(
+    (72, 9, 16, LANES), lambda i: (3, 0, 0, 0), pipeline_mode=pl.Buffered(1)
+)
 
 
 def up_kernel(
@@ -607,12 +627,12 @@
     def _():
         narrow = dot_t(attended[...], down_o[...]).astype(BF16)
         inner_o[...] = narrow
-        middle[...] = hidden[...] + (dot_both(attended[...], w_o[...], narrow, up_o[...]) + vec[6:7])
+        middle[...] = hidden[...] + (dot_both(attended[...], matrix(w_o), narrow, up_o[...]) + vec[6:7])
         value = layer_norm(middle[...], vec[2:3], vec[3:4]).astype(BF16)
         normed[...] = value
         inner_up[...] = dot_t(value, down_1[...]).astype(BF16)
 
-    x = dot_both(normed[...], w_1[...], inner_up[...], up_1[...]) + b_1[...]
+    x = dot_both(normed[...], matrix(w_1), inner_up[...], up_1[...]) + b_1[...]
     gate[...] = x.astype(BF16)
     activated[...] = (0.5 * x * (1.0 + gelu_parts(x))).astype(BF16)
 
@@ -621,16 +641,16 @@
     rows = hidden.shape[0]
     return pl.pallas_call(
         up_kernel,
-        grid=(pl.cdiv(FF, TILE),),
+        grid=(WIDE // TILE,),
         in_specs=[
             whole((rows, D)),
             whole((rows, D)),
-            whole((D, D)),
+            OUT_BLOCK,
             whole((8, D)),
             whole((R, D)),
             whole((R, D)),
             whole((R, D)),
-            columns(D, TILE),
+            unit_block(72, 4, lambda i: (1, i, 0, 0)),
             columns(1, TILE),
             columns(R, TILE),
         ],
@@ -647,8 +667,8 @@
             struct((rows, D), F32),
             struct((rows, D), BF16),
             struct((rows, R), BF16),
-            struct((rows, FF), BF16),
-            struct((rows, FF), BF16),
+            struct((rows, WIDE), BF16),
+            struct((rows, WIDE), BF16),
         ],
         name="up_forward",
         **dense_params(2 * rows * D * (D + FF), 12 * rows * D + 4 * rows * FF + 2 * D * (D + FF)),
@@ -663,8 +683,10 @@
     def _():
         inner[...] = dot_t(activated[...], down_2[...]).astype(BF16)
 
+    value = activated[:, :FF]
+
     hidden[...] = middle[...] + (
-        dot(activated[...], w_2[...]) + b_2[...] + dot(inner[...], up_2[...])
+        dot(value, matrix(w_2)) + b_2[...] + dot(inner[...], up_2[...])
     )
 
 
@@ -674,11 +696,14 @@
         down_kernel,
         grid=(3,),
         in_specs=[
-            whole((rows, FF)),
+            whole((rows, WIDE)),
             columns(rows, THIRD),
-            columns(FF, THIRD),
+            pl.BlockSpec(
+                (pl.Element(UNITS[3]), pl.Element(3), pl.Element(16), pl.Element(LANES)),
+                lambda i: (TILES_AT[3] // 9, 3 * i, 0, 0),
+            ),
             columns(1, THIRD),
-            whole((R, FF)),
+            whole((R, WIDE)),
             columns(R, THIRD),
         ],
         out_specs=[whole((rows, R)), columns(rows, THIRD)],
@@ -704,7 +729,7 @@
 
     left = FF - i * TILE
     down = down_2[...]
-    d_act = dot_t(d_branch[...], w_2[...]) + dot(d_inner_down[...], down)
+    d_act = dot_t(d_branch[...], matrix(w_2)) + dot(d_inner_down[...], down)
     x = gate[...].astype(F32)
     t = gelu_parts(x)
     half = 0.5 * (1.0 + t)
@@ -714,8 +739,7 @@
     keep = lax.broadcasted_iota(jnp.int32, (1, TILE), 1) < left
     value = jnp.where(keep, slope * d_act, 0.0).astype(BF16)
     d_gate[...] = value
-    up = jnp.where(keep, up_1[...], jnp.zeros_like(up_1[...]))
-    total[...] += dot_t(value, up)
+    total[...] += dot_t(value, up_1[...])
     g_wide[0:R] = dot_l(inner_up[...], value)
     g_wide[R : 2 * R] = dot_l(d_inner_down[...], (x * half).astype(BF16))
 
@@ -728,10 +752,10 @@
     rows = gradient.shape[0]
     return pl.pallas_call(
         gate_kernel,
-        grid=(pl.cdiv(FF, TILE),),
+        grid=(WIDE // TILE,),
         in_specs=[
             whole((rows, D)),
-            pl.BlockSpec((TILE, D), lambda i: (i, 0)),
+            unit_block(TILE // 16, 9, lambda i: (TILES_AT[3] // 9 * 16 // TILE + i, 0, 0, 0)),
             columns(rows, TILE),
             columns(R, TILE),
             columns(R, TILE),
@@ -741,8 +765,8 @@
         ],
         out_specs=[columns(rows, TILE), columns(2 * R, TILE), whole((rows, R)), whole((R, D))],
         out_shape=[
-            struct((rows, FF), BF16),
-            struct((2 * R, FF), F32),
+            struct((rows, WIDE), BF16),
+            struct((2 * R, WIDE), F32),
             struct((rows, R), BF16),
             struct((R, D), F32),
         ],
@@ -762,7 +786,9 @@
 ):
     i = pl.program_id(0)
     at = pl.ds(pl.multiple_of(i * THIRD, LANES), THIRD)
-    d_normed[:, at] = dot_t(d_gate[...], w_1[...]) + dot(d_inner_up[...], down_1[:, at])
+    d_normed[:, at] = dot_t(d_gate[:, : 34 * LANES], matrix(w_1, 34)) + dot(
+        d_inner_up[...], down_1[:, at]
+    )
 
     @pl.when(i == pl.num_programs(0) - 1)
     def _():
@@ -770,7 +796,7 @@
         d_middle[...] = value
         d_out = value.astype(BF16)
         d_inner_o = dot_t(d_out, up_o[...]).astype(BF16)
-        d_attended[...] = (dot_t(d_out, w_o[...]) + dot(d_inner_o, down_o[...])).astype(BF16)
+        d_attended[...] = (dot_t(d_out, matrix(w_o)) + dot(d_inner_o, down_o[...])).astype(BF16)
         g_rows[0:R] = dot_l(d_inner_o, attended[...])
         g_rows[R : 2 * R] = dot_l(inner_o[...], d_out)
         g_rows[2 * R : 3 * R] = dot_l(d_inner_up[...], normed[...])
@@ -784,15 +810,15 @@
         middle_kernel,
         grid=(3,),
         in_specs=[
-            whole((rows, FF)),
-            pl.BlockSpec((THIRD, FF), lambda i: (i, 0)),
+            whole((rows, WIDE)),
+            unit_block(THIRD // 16, PANELS[2], lambda i: (3 + i, 0, 0, 0)),
             whole((rows, R)),
             whole((R, D)),
             whole((rows, D)),
             whole((rows, D)),
             whole((rows, D)),
             whole((8, D)),
-            whole((D, D)),
+            OUT_BLOCK,
             whole((R, D)),
             whole((R, D)),
             whole((rows, R)),
@@ -827,7 +853,7 @@
         g_rows[0 : 3 * R] = dot_l(d_inner[...], normed[...])
 
     at = pl.ds(pl.multiple_of(i * THIRD, LANES), THIRD)
-    d_normed[:, at] = dot_t(d_qkv[...], w_qkv[...]) + dot(d_inner[...], down[:, at])
+    d_normed[:, at] = dot_t(d_qkv[...], matrix(w_qkv)) + dot(d_inner[...], down[:, at])
 
     @pl.when(i == pl.num_programs(0) - 1)
     def _():
@@ -841,7 +867,7 @@
         grid=(3,),
         in_specs=[
             whole((rows, 3 * D)),
-            pl.BlockSpec((THIRD, 3 * D), lambda i: (i, 0)),
+            unit_block(THIRD // 16, 27, lambda i: (i, 0, 0, 0)),
             whole((3 * R, D)),
             whole((3, R, D)),
             whole((rows, D)),
@@ -856,6 +882,185 @@
         name="input_backward",
         **dense_params(6 * rows * D * D, 20 * rows * D + 6 * D * D),
     )(d_qkv, w_qkv, attn[0:3].reshape(3 * R, D), attn[4:7], normed, inner, hidden, d_middle, vectors)
+
+
+SHARE = 5
+SHARE_ROWS = SHARE * 16
+
+
+def share_kernel(
+    adapters, terms, label, out, held, labels, totals, sums, local_sem, send, recv, label_send, label_recv, pair_sem
+):
+    x = lax.axis_index("seq")
+    f = lax.axis_index("fsdp")
+    count = terms.shape[0]
+    me = f * 2 + x
+    barrier = pltpu.get_barrier_semaphore()
+
+    def device(k):
+        return (k // 2, k % 2)
+
+    def greet(k, carry):
+        to = (me + k) % count
+        pl.semaphore_signal(barrier, inc=1, device_id=device(to), device_id_type=MESH)
+        return carry
+
+    lax.fori_loop(1, count, greet, 0)
+    pl.semaphore_wait(barrier, count - 1)
+
+    def share_to(to, slot):
+        return pltpu.make_async_remote_copy(
+            src_ref=terms.at[to],
+            dst_ref=held.at[slot],
+            send_sem=send.at[to],
+            recv_sem=recv.at[slot],
+            device_id=device(to),
+            device_id_type=MESH,
+        )
+
+    def label_to(to, slot):
+        return pltpu.make_async_remote_copy(
+            src_ref=label,
+            dst_ref=labels.at[slot],
+            send_sem=label_send.at[to],
+            recv_sem=label_recv.at[slot],
+            device_id=device(to),
+            device_id_type=MESH,
+        )
+
+    def post(k, carry):
+        to = (me + k) % count
+        label_to(to, me).start()
+        share_to(to, me).start()
+        return carry
+
+    lax.fori_loop(1, count, post, 0)
+    mine = pltpu.make_async_copy(terms.at[me], held.at[me], local_sem.at[0])
+    named = pltpu.make_async_copy(label, labels.at[me], local_sem.at[1])
+    mine.start()
+    named.start()
+    totals[...] = jnp.zeros_like(totals)
+
+    def add(slot):
+        value = held[slot].reshape(SHARE_ROWS, LANES).astype(F32)
+        name = labels[slot][0:1]
+        for e in range(adapters):
+            totals[e] += jnp.where(name == float(e), value, 0.0)
+
+    mine.wait()
+    named.wait()
+    add(me)
+
+    def take(k, carry):
+        slot = (me + count - k) % count
+        label_to(slot, slot).wait_recv()
+        share_to(slot, slot).wait_recv()
+        add(slot)
+        return carry
+
+    lax.fori_loop(1, count, take, 0)
+    sums[...] = totals[...].reshape(adapters * SHARE_ROWS, LANES).astype(BF16)
+    rows = adapters * SHARE_ROWS
+    part = out.at[pl.ds(pl.multiple_of(x * rows, 16), rows), :]
+    keep = pltpu.make_async_copy(sums, part, local_sem.at[0])
+    keep.start()
+    keep.wait()
+    across = pltpu.make_async_remote_copy(
+        src_ref=part,
+        dst_ref=part,
+        send_sem=pair_sem.at[0],
+        recv_sem=pair_sem.at[1],
+        device_id=(f, 1 - x),
+        device_id_type=MESH,
+    )
+    across.start()
+
+    def sent(k, carry):
+        to = (me + k) % count
+        label_to(to, me).wait_send()
+        share_to(to, me).wait_send()
+        return carry
+
+    lax.fori_loop(1, count, sent, 0)
+    across.wait_send()
+    other = out.at[pl.ds(pl.multiple_of((1 - x) * rows, 16), rows), :]
+    pltpu.make_async_remote_copy(
+        src_ref=other,
+        dst_ref=other,
+        send_sem=pair_sem.at[0],
+        recv_sem=pair_sem.at[1],
+        device_id=(f, 1 - x),
+        device_id_type=MESH,
+    ).wait_recv()
+
+
+def share_terms(terms, label, adapters):
+    count = terms.shape[0]
+    dma = pltpu.SemaphoreType.DMA
+    rows = adapters * SHARE_ROWS
+    return pl.pallas_call(
+        functools.partial(share_kernel, adapters),
+        in_specs=[pl.BlockSpec(memory_space=pl.ANY)] * 2,
+        out_specs=pl.BlockSpec(memory_space=pl.ANY),
+        out_shape=jax.ShapeDtypeStruct((2 * rows, LANES), BF16),
+        scratch_shapes=[
+            pltpu.VMEM((count, SHARE, 16, LANES), BF16),
+            pltpu.VMEM((count, 8, LANES), F32),
+            pltpu.VMEM((adapters, SHARE_ROWS, LANES), F32),
+            pltpu.VMEM((rows, LANES), BF16),
+            dma((2,)),
+            dma((count,)),
+            dma((count,)),
+            dma((count,)),
+            dma((count,)),
+            dma((2,)),
+        ],
+        compiler_params=pltpu.CompilerParams(
+            collective_id=1, has_side_effects=True, vmem_limit_bytes=VMEM_LIMIT
+        ),
+        name="share_terms",
+    )(terms, label)
+
+
+def table_kernel(layers, *refs):
+    attn, narrow, wide = refs[layers:]
+    for layer in range(layers):
+        source = refs[layer]
+        for t in range(10 * 9 + 2 * 34):
+            tile = source[t // SHARE, 0, t % SHARE].astype(F32)
+            if t < 90:
+                at = slice(t % 9 * LANES, (t % 9 + 1) * LANES)
+                if t < 72:
+                    attn[layer, t // 9, 0, :, at] = tile
+                else:
+                    narrow[layer, t // 9 - 8, 0, :, at] = tile
+            else:
+                c, p = (t - 90) // 34, (t - 90) % 34
+                width = min(LANES, FF - p * LANES)
+                wide[layer, c, 0, :, p * LANES : p * LANES + width] = tile[:, :width]
+
+
+def gradient_tables(gathered, adapters):
+    layers = len(gathered)
+    count = gathered[0].shape[0] // (adapters * SHARE_ROWS)
+    gathered = [g.reshape(count, adapters, SHARE, 16, LANES) for g in gathered]
+
+    def out_block(kinds, width):
+        return pl.BlockSpec((layers, kinds, 1, R, width), lambda e: (0, 0, e, 0, 0))
+
+    return pl.pallas_call(
+        functools.partial(table_kernel, layers),
+        grid=(adapters,),
+        in_specs=[pl.BlockSpec((count, 1, SHARE, 16, LANES), lambda e: (0, e, 0, 0, 0))] * layers,
+        out_specs=[out_block(8, D), out_block(2, D), out_block(2, FF)],
+        out_shape=[
+            struct((layers, 8, adapters, R, D), F32),
+            struct((layers, 2, adapters, R, D), F32),
+            struct((layers, 2, adapters, R, FF), F32),
+        ],
+        compiler_params=pltpu.CompilerParams(vmem_limit_bytes=VMEM_LIMIT),
+        name="gradient_tables",
+    )(*gathered)
 
 
 def local(
@@ -878,6 +1083,7 @@
     layer_count = frozen.shape[0]
     adapters = attention_adapter_weights.shape[2]
     parts = seq_parts // slots
+    on_block = (fsdp_parts, seq_parts, slots) == (16, 2, 2)
     slot = me // parts
     part = me % parts
     tokens = seq_total // parts
@@ -915,21 +1121,31 @@
         return lax.dynamic_index_in_dim(table, adapter, 1, keepdims=False)
 
     shards = lax.optimization_barrier(frozen.reshape(layer_count, -1, LANES))
+    steps = [(d, d + 1) for d in range(fsdp_parts - 1)]
+    steps = (steps, [(b, a) for a, b in steps])
+    tiles = -(-(TILES_END + TILES_VECTORS) // (2 * fsdp_parts)) * 2
+    index = lax.axis_index("fsdp").astype(jnp.int32).reshape(1)
+    shards = [lay_shard(index, shards[layer], tiles, steps) for layer in range(layer_count)]
     hidden = to_image(activations).astype(F32) * row_mask
+    shards[0], hidden = lax.optimization_barrier((shards[0], hidden))
     stored = []
     weights = []
     for layer in range(layer_count):
-        if (fsdp_parts, seq_parts) == (16, 2):
-            flat = gather_blocks(shards[layer], 0)
+        if on_block:
+            flat = gather_blocks(shards[layer], 0, 16 * TILES_HELD)
         else:
             flat = lax.all_gather(shards[layer], "fsdp", axis=0, tiled=True)
-        w_qkv, w_o, w_1, w_2 = unpack(flat)
-        vectors = lax.slice_in_dim(flat, CUT_VECTORS, CUT_VECTORS + 106, axis=0).reshape(-1)
+            flat = jnp.pad(flat, ((0, 16 * TILES_HELD - flat.shape[0]), (0, 0)))
+        if layer == layer_count - 1:
+            cotangent, flat = lax.optimization_barrier((cotangent, flat))
+            d_output = to_image(cotangent)
+        w_qkv, w_o, w_1, w_2 = (flat.reshape(-1, panels, 16, LANES) for panels in PANELS)
+        vectors = lax.slice_in_dim(flat, 16 * TILES_END, 16 * TILES_END + 106, axis=0).reshape(-1)
         vectors, b_1 = vectors[: 8 * D].reshape(8, D).astype(F32), vectors[8 * D : 8 * D + FF]
-        b_1 = b_1.astype(F32)[None, :]
+        b_1 = jnp.pad(b_1.astype(F32), (0, WIDE - FF))[None, :]
         attn = pick(attention_adapter_weights[layer])
         narrow = pick(narrow_adapter_weights[layer])
-        wide = pick(broad_adapter_weights[layer])
+        wide = jnp.pad(pick(broad_adapter_weights[layer]), ((0, 0), (0, 0), (0, WIDE - FF)))
         weights.append((w_qkv, w_o, w_1, w_2, vectors, attn, narrow, wide))
         normed, inner_qkv, qkv = qkv_forward(hidden, w_qkv, vectors, attn)
         keys = None
@@ -963,9 +1179,11 @@
         )
         hidden = next_hidden
     output = to_tokens((hidden * row_mask).astype(BF16))
-    gradient = to_image(cotangent).astype(F32) * row_mask
+    gradient = d_output.astype(F32) * row_mask
     collected = [None] * layer_count
     for layer in reversed(range(layer_count)):
+        if layer == 0:
+            output, gradient = lax.optimization_barrier((output, gradient))
         (
             layer_input,
             normed,
@@ -1012,8 +1230,24 @@
                 g_middle[R:],
                 g_up_2,
             ]
-        ).astype(BF16)
-        rows_wide = g_wide.astype(BF16)
+        )
+        if on_block:
+            terms = jnp.concatenate(
+                [
+                    rows_narrow.reshape(10, R, 9, LANES).transpose(0, 2, 1, 3).reshape(90, R, LANES),
+                    g_wide.reshape(2, R, 36, LANES)
+                    .transpose(0, 2, 1, 3)[:, :34]
+                    .reshape(68, R, LANES),
+                    jnp.zeros((2, R, LANES), F32),
+                ]
+            )
+            terms = terms.astype(BF16).reshape(device_count, SHARE, R, LANES)
+            label = jnp.broadcast_to(adapter.astype(F32), (8, LANES))
+            sums = share_terms(terms, label, adapters)
+            collected[layer] = gather_blocks(sums, 2, 16 * sums.shape[0])
+            continue
+        rows_narrow = rows_narrow.astype(BF16)
+        rows_wide = g_wide[:, :FF].astype(BF16)
 
         def shares(rows):
             share = -(-rows.shape[0] // device_count)
@@ -1040,9 +1274,12 @@
             return part.reshape(adapters, count, R, width).transpose(1, 0, 2, 3).astype(F32)
 
         collected[layer] = (table(sums[:, :, :split], 10, D), table(sums[:, :, split:used], 2, FF))
-    grad_attn = jnp.stack([entry[0][0:8] for entry in collected], axis=0)
-    grad_narrow = jnp.stack([entry[0][8:10] for entry in collected], axis=0)
-    grad_wide = jnp.stack([entry[1] for entry in collected], axis=0)
+    if on_block:
+        grad_attn, grad_narrow, grad_wide = gradient_tables(collected, adapters)
+    else:
+        grad_attn = jnp.stack([entry[0][0:8] for entry in collected], axis=0)
+        grad_narrow = jnp.stack([entry[0][8:10] for entry in collected], axis=0)
+        grad_wide = jnp.stack([entry[1] for entry in collected], axis=0)
     input_grad = to_tokens((gradient * row_mask).astype(BF16)).astype(F32)
     return (output, input_grad, grad_attn, grad_narrow, grad_wide)
 

time: 1060 us -> 934 us (0.88)
  waiting for transfers between devices: 80.8 us -> 0.02 us
  Pallas kernels: 785 us -> 840 us
  blocking collectives: 45.6 us -> 0 us
  local copies, waits for them, and re-layouts: 86.6 us -> 41 us
  between operations: 17.7 us -> 4.72 us
    pallas_call x2 -> x4, Pallas kernels: 267 us -> 335 us  [gather_blocks(): pl.pallas_call(gather_kernel, in_specs=[pl.BlockSpec(memory_space=pl.ANY)...]
    all_to_all x2 -> x0, blocking collectives: 45.6 us -> none  [local(): lax.all_to_all(jnp.concatenate(terms + [label], axis=1), ('fsdp', 'seq'),...]
    ppermute x2, waiting for transfers between devices: 45.2 us -> 0.01 us  [to_tokens(): other = lax.ppermute(other, 'seq', [(0, 1), (1, 0)])]
    all_gather x2 -> x0, waiting for transfers between devices: 35.5 us -> none  [local(): sums = lax.all_gather(sums.astype(BF16), ('fsdp', 'seq')).transpose(1, 0, 2)]
    convert_element_type x4 -> x0, local copies, waits for them, and re-layouts: 15.6 us -> none  [the longest x2 15 us: table(): part.reshape(adapters, count, R, width).transpose(1, 0, 2, 3).astype(F32)]
    pallas_call x20 -> x17, Pallas kernels: 362 us -> 348 us  [the longest x2 58.1 us: share_terms(): pl.pallas_call(functools.partial(share_kernel, adapters), in_specs=[pl.Bl...]
    another operation x4 -> x1, local copies, waits for them, and re-layouts: 12.8 us -> 0.01 us  [the longest x2 7.83 us: local(): grad_attn = jnp.stack([entry[0][0:8] for entry in collected], axis=0)]
    unnamed x68 -> x41, local copies, waits for them, and re-layouts: 17.5 us -> 6.54 us
  transfers between devices with their start and end apart: 6 -> 8, of which waited for: 3 -> 0; matrix products, arithmetic and copies ran while one was open for 6% -> 5% of each run, Pallas kernels for 34% -> 78%
where the time goes in v4:
time: 934 us; the launch traced here: 924 us
  Pallas kernels  840 us (90%)
  local copies, waits for them, and re-layouts  41 us (4%)
  other arithmetic  23.1 us (2%)
  starting transfers between devices  15.3 us (2%)
    pallas_call x4, Pallas kernels, gather_blocks(): pl.pallas_call(gather_kernel, in_specs=[pl.BlockSpec(memory_space=pl.ANY)...  335 us
    pallas_call x2, Pallas kernels, attn_bwd(): pl.pallas_call(kernel, in_specs=[pl.BlockSpec(memory_space=pltpu.SMEM)] +...  90.1 us
    pallas_call x2, Pallas kernels, attn_fwd(): pl.pallas_call(kernel, in_specs=[pl.BlockSpec(memory_space=pltpu.SMEM)] +...  66.1 us
    pallas_call x2, Pallas kernels, share_terms(): pl.pallas_call(functools.partial(share_kernel, adapters), in_specs=[pl.Bl...  58.1 us
    pallas_call x2, Pallas kernels, gate_backward(): pl.pallas_call(gate_kernel, grid=(WIDE // TILE,), in_specs=[whole((rows,...  56.2 us
    pallas_call x2, Pallas kernels, middle_backward(): pl.pallas_call(middle_kernel, grid=(3,), in_specs=[whole((rows, WIDE)), u...  54.4 us
    pallas_call x2, Pallas kernels, up_forward(): pl.pallas_call(up_kernel, grid=(WIDE // TILE,), in_specs=[whole((rows, D)...  52.4 us
    pallas_call x2, Pallas kernels, input_backward(): pl.pallas_call(input_kernel, grid=(3,), in_specs=[whole((rows, 3 * D)), u...  43.1 us
  transfers between devices with their start and end apart: 8, of which 0 were waited for; matrix products, arithmetic and copies ran while one was open for 5% of the time, Pallas kernels for 78%

profile of v4, /device:TPU:0, one launch (start us, length us, event | category | flops | bytes accessed | tf_op | source)
XLA Modules:
  0.0 924.2 jit_solution(8970604998546328745)
XLA Ops:
  0.6 2.6 copy.46
  3.2 1.9 copy-done
  5.1 1.2 slice_bitcast_fusion.2
  6.3 3.1 collective-permute-start.3
  9.5 1.3 collective-permute-start.4
  10.7 5.2 collective-permute-start
  15.9 1.3 collective-permute-start.1
  18.3 1.5 collective-permute-start.2
  19.8 4.3 slice_bitcast_fusion
  27.3 5.2 fusion.7
  34.1 4.7 fusion.8
  41.2 1.8 dynamic-slice_bitcast_fusion.8
  43.1 1.5 dynamic-slice_bitcast_fusion.14
  44.5 1.5 dynamic-slice_bitcast_fusion.10
  48.0 4.3 lay_shard.3.src
  52.3 130.6 %gather_blocks.5 = bf16[124416,128]{1,0:T(8,128)(2,1)} custom-call(bf16[7648,128]{1,0:T(8,128)(2,1)} %lay_shard.3.src), custom_call_target="tpu_custom_call" | custom-call | tf_op jit(solution)/shard_map/gather_blocks/pallas_call | solution.py:491
  188.0 4.3 lay_shard.2.src
  192.2 3.7 convert_multiply_fusion.1.hidden
  196.0 124.9 %gather_blocks.4 = bf16[124416,128]{1,0:T(8,128)(2,1)} custom-call(bf16[7648,128]{1,0:T(8,128)(2,1)} %lay_shard.2.src), custom_call_target="tpu_custom_call" | custom-call | tf_op jit(solution)/shard_map/gather_blocks/pallas_call | solution.py:491
  322.9 13.4 %qkv_forward.2 = (bf16[736,1152]{1,0:T(8,128)(2,1)}, bf16[736,48]{1,0:T(8,128)(2,1)}, bf16[736,3456]{1,0:T(8,128)(2,1)}) custom-call(f32[736,1152]{1,0:T(8,128)} %convert_multiply_fusion.1.hidden, bf16[288,27,16,128]{3,2,1,0:T(8,128)(2,1)} %bitcast.123, f32[8,1152]{1,0:T(8,128)} %convert_element_type.57.vec, bf16[48,1152]{1,0:T(8,128)(2,1)} %bitcast.154, ...), custom_call_target="tpu_custom_call" | custom-call | flops 5860491264 | bytes 19832832 | tf_op jit(solution)/shard_map/qkv_forward/pallas_call | solution.py:594
  336.3 33.1 %attention_forward.2 = (bf16[736,1152]{1,0:T(8,128)(2,1)}, f32[736,128]{1,0:T(8,128)}) custom-call(s32[1]{0:T(128)} %dynamic_slice.53.a, bf16[736,3456]{1,0:T(8,128)(2,1)} %get-tuple-element.60.b), custom_call_target="tpu_custom_call" | custom-call | flops 8875147264 | bytes 6782976 | tf_op jit(solution)/shard_map/attention_forward/pallas_call | solution.py:192
  370.6 26.4 %up_forward.2 = (bf16[736,16]{1,0:T(8,128)(2,1)}, f32[736,1152]{1,0:T(8,128)}, bf16[736,1152]{1,0:T(8,128)(2,1)}, bf16[736,16]{1,0:T(8,128)(2,1)}, bf16[736,4608]{1,0:T(8,128)(2,1)}, /*index=5*/bf16[736,4608]{1,0:T(8,128)(2,1)}) custom-call(bf16[736,1152]{1,0:T(8,128)(2,1)} %get-tuple-element.61.attended.d, f32[736,1152]{1,0:T(8,128)} %convert_multiply_fusion.1.hidden, ...), custom_call_target="tpu_custom_call" | custom-call | flops 9251979264 | bytes 35416064 | tf_op jit(solution)/shard_map/up_forward/pallas_call | solution.py:642
  397.0 18.2 %down_forward.2 = (bf16[736,16]{1,0:T(8,128)(2,1)}, f32[736,1152]{1,0:T(8,128)}) custom-call(bf16[736,4608]{1,0:T(8,128)(2,1)} %get-tuple-element.62.activated, f32[736,1152]{1,0:T(8,128)} %get-tuple-element.63.middle, bf16[864,9,16,128]{3,2,1,0:T(8,128)(2,1)} %bitcast.126, f32[1,1152]{1,0:T(1,128)} %bitcast.159, ...), custom_call_target="tpu_custom_call" | custom-call | flops 7298482176 | bytes 23034880 | tf_op jit(solution)/shard_map/down_forward/pallas_call | solution.py:695
  415.2 13.5 %qkv_forward.3 = (bf16[736,1152]{1,0:T(8,128)(2,1)}, bf16[736,48]{1,0:T(8,128)(2,1)}, bf16[736,3456]{1,0:T(8,128)(2,1)}) custom-call(f32[736,1152]{1,0:T(8,128)} %get-tuple-element.64.hidden, bf16[288,27,16,128]{3,2,1,0:T(8,128)(2,1)} %bitcast.131, f32[8,1152]{1,0:T(8,128)} %convert_element_type.59.vec, bf16[48,1152]{1,0:T(8,128)(2,1)} %bitcast.156, ...), custom_call_target="tpu_custom_call" | custom-call | flops 5860491264 | bytes 19832832 | tf_op jit(solution)/shard_map/qkv_forward/pallas_call | solution.py:594
  428.7 33.1 %attention_forward.3 = (bf16[736,1152]{1,0:T(8,128)(2,1)}, f32[736,128]{1,0:T(8,128)}) custom-call(s32[1]{0:T(128)} %dynamic_slice.53.a, bf16[736,3456]{1,0:T(8,128)(2,1)} %get-tuple-element.66.b), custom_call_target="tpu_custom_call" | custom-call | flops 8875147264 | bytes 6782976 | tf_op jit(solution)/shard_map/attention_forward/pallas_call | solution.py:192
  461.8 26.0 %up_forward.3 = (bf16[736,16]{1,0:T(8,128)(2,1)}, f32[736,1152]{1,0:T(8,128)}, bf16[736,1152]{1,0:T(8,128)(2,1)}, bf16[736,16]{1,0:T(8,128)(2,1)}, bf16[736,4608]{1,0:T(8,128)(2,1)}, /*index=5*/bf16[736,4608]{1,0:T(8,128)(2,1)}) custom-call(bf16[736,1152]{1,0:T(8,128)(2,1)} %get-tuple-element.67.attended.d, f32[736,1152]{1,0:T(8,128)} %get-tuple-element.64.hidden, ...), custom_call_target="tpu_custom_call" | custom-call | flops 9251979264 | bytes 35416064 | tf_op jit(solution)/shard_map/up_forward/pallas_call | solution.py:642
  487.8 18.5 %down_forward.3 = (bf16[736,16]{1,0:T(8,128)(2,1)}, f32[736,1152]{1,0:T(8,128)}) custom-call(bf16[736,4608]{1,0:T(8,128)(2,1)} %get-tuple-element.68.activated, f32[736,1152]{1,0:T(8,128)} %get-tuple-element.69.middle, bf16[864,9,16,128]{3,2,1,0:T(8,128)(2,1)} %bitcast.134, f32[1,1152]{1,0:T(1,128)} %bitcast.158, ...), custom_call_target="tpu_custom_call" | custom-call | flops 7298482176 | bytes 23034880 | tf_op jit(solution)/shard_map/down_forward/pallas_call | solution.py:695
  506.3 4.5 convert_multiply_fusion
  511.0 1.2 collective-permute-start.5
  512.1 28.0 %gate_backward.2 = (bf16[736,4608]{1,0:T(8,128)(2,1)}, f32[32,4608]{1,0:T(8,128)}, bf16[736,16]{1,0:T(8,128)(2,1)}, f32[16,1152]{1,0:T(8,128)}) custom-call(f32[736,1152]{1,0:T(8,128)} %get-tuple-element.147.gradient, bf16[864,9,16,128]{3,2,1,0:T(8,128)(2,1)} %bitcast.135, bf16[736,4608]{1,0:T(8,128)(2,1)} %get-tuple-element.72.gate, ...), custom_call_target="tpu_custom_call" | custom-call | flops 7298482176 | bytes 25978880 | tf_op jit(solution)/shard_map/gate_backward/pallas_call | solution.py:753
  540.1 1.1 convert.69
  541.4 27.4 %middle_backward.2 = (f32[736,1152]{1,0:T(8,128)}, bf16[736,1152]{1,0:T(8,128)(2,1)}, f32[48,1152]{1,0:T(8,128)}) custom-call(bf16[736,4608]{1,0:T(8,128)(2,1)} %get-tuple-element.75.d_gate, bf16[216,36,16,128]{3,2,1,0:T(8,128)(2,1)} %bitcast.137, bf16[736,16]{1,0:T(8,128)(2,1)} %get-tuple-element.76.d_inner_up, bf16[16,1152]{1,0:T(8,128)(2,1)} %get-tuple-element.140.down_1, ...), custom_call_target="tpu_custom_call" | custom-call | flops 9251979264 | bytes 34167808 | tf_op jit(solution)/shard_map/middle_backward/pallas_call | solution.py:809
  568.8 45.1 %attention_backward.2.d_qkv = bf16[736,3456]{1,0:T(8,128)(2,1)} custom-call(s32[1]{0:T(128)} %dynamic_slice.53.a, bf16[736,3456]{1,0:T(8,128)(2,1)} %get-tuple-element.66.b, bf16[736,1152]{1,0:T(8,128)(2,1)} %get-tuple-element.79.c, bf16[736,1152]{1,0:T(8,128)(2,1)} %get-tuple-element.67.attended.d, f32[736,128]{1,0:T(8,128)} %get-tuple-element.80.e), custom_call_target="tpu_custom_call" | custom-call | flops 22187868160 | bytes 13565952 | tf_op jit(solution)/shard_map/attention_backward/pallas_call | solution.py:269
  613.9 21.6 %input_backward.2 = (f32[736,1152]{1,0:T(8,128)}, f32[96,1152]{1,0:T(8,128)}) custom-call(bf16[736,3456]{1,0:T(8,128)(2,1)} %attention_backward.2.d_qkv, bf16[288,27,16,128]{3,2,1,0:T(8,128)(2,1)} %bitcast.138, bf16[48,1152]{1,0:T(8,128)(2,1)} %bitcast.157, bf16[3,16,1152]{2,1,0:T(8,128)(2,1)} %get-tuple-element.123.up, ...), custom_call_target="tpu_custom_call" | custom-call | flops 5860491264 | bytes 24920064 | tf_op jit(solution)/shard_map/input_backward/pallas_call | solution.py:865
  637.0 2.9 maximum_select_fusion.1
  639.9 28.2 %gate_backward.3 = (bf16[736,4608]{1,0:T(8,128)(2,1)}, f32[32,4608]{1,0:T(8,128)}, bf16[736,16]{1,0:T(8,128)(2,1)}, f32[16,1152]{1,0:T(8,128)}) custom-call(f32[736,1152]{1,0:T(8,128)} %get-tuple-element.86.gradient, bf16[864,9,16,128]{3,2,1,0:T(8,128)(2,1)} %bitcast.127, bf16[736,4608]{1,0:T(8,128)(2,1)} %get-tuple-element.87.gate, ...), custom_call_target="tpu_custom_call" | custom-call | flops 7298482176 | bytes 25978880 | tf_op jit(solution)/shard_map/gate_backward/pallas_call | solution.py:753
  668.1 27.1 %middle_backward.3 = (f32[736,1152]{1,0:T(8,128)}, bf16[736,1152]{1,0:T(8,128)(2,1)}, f32[48,1152]{1,0:T(8,128)}) custom-call(bf16[736,4608]{1,0:T(8,128)(2,1)} %get-tuple-element.90.d_gate, bf16[216,36,16,128]{3,2,1,0:T(8,128)(2,1)} %bitcast.129, bf16[736,16]{1,0:T(8,128)(2,1)} %get-tuple-element.91.d_inner_up, bf16[16,1152]{1,0:T(8,128)(2,1)} %get-tuple-element.142.down_1, ...), custom_call_target="tpu_custom_call" | custom-call | flops 9251979264 | bytes 34167808 | tf_op jit(solution)/shard_map/middle_backward/pallas_call | solution.py:809
  695.2 45.1 %attention_backward.3.d_qkv = bf16[736,3456]{1,0:T(8,128)(2,1)} custom-call(s32[1]{0:T(128)} %dynamic_slice.53.a, bf16[736,3456]{1,0:T(8,128)(2,1)} %get-tuple-element.60.b, bf16[736,1152]{1,0:T(8,128)(2,1)} %get-tuple-element.94.c, bf16[736,1152]{1,0:T(8,128)(2,1)} %get-tuple-element.61.attended.d, f32[736,128]{1,0:T(8,128)} %get-tuple-element.95.e), custom_call_target="tpu_custom_call" | custom-call | flops 22187868160 | bytes 13565952 | tf_op jit(solution)/shard_map/attention_backward/pallas_call | solution.py:269
  740.2 21.5 %input_backward.3 = (f32[736,1152]{1,0:T(8,128)}, f32[96,1152]{1,0:T(8,128)}) custom-call(bf16[736,3456]{1,0:T(8,128)(2,1)} %attention_backward.3.d_qkv, bf16[288,27,16,128]{3,2,1,0:T(8,128)(2,1)} %bitcast.130, bf16[48,1152]{1,0:T(8,128)(2,1)} %bitcast.155, bf16[3,16,1152]{2,1,0:T(8,128)(2,1)} %get-tuple-element.152.up, ...), custom_call_target="tpu_custom_call" | custom-call | flops 5860491264 | bytes 24920064 | tf_op jit(solution)/shard_map/input_backward/pallas_call | solution.py:865
  761.7 2.2 multiply_convert_fusion
  767.0 1.2 reshape.160
  768.3 1.3 maximum_maximum_fusion.1
  770.2 31.5 %share_terms.2.src = bf16[1280,128]{1,0:T(8,128)(2,1)} custom-call(bf16[32,5,16,128]{3,2,1,0:T(8,128)(2,1)} %bitcast.147, f32[8,128]{1,0:T(8,128)} %broadcast_in_dim.19.label), custom_call_target="tpu_custom_call" | custom-call | tf_op jit(solution)/shard_map/share_terms/pallas_call | solution.py:1001
  801.7 37.5 %gather_blocks.6 = bf16[20480,128]{1,0:T(8,128)(2,1)} custom-call(bf16[1280,128]{1,0:T(8,128)(2,1)} %share_terms.2.src), custom_call_target="tpu_custom_call" | custom-call | tf_op jit(solution)/shard_map/gather_blocks/pallas_call | solution.py:491
  839.2 26.6 %share_terms.3.src = bf16[1280,128]{1,0:T(8,128)(2,1)} custom-call(bf16[32,5,16,128]{3,2,1,0:T(8,128)(2,1)} %bitcast.146, f32[8,128]{1,0:T(8,128)} %broadcast_in_dim.19.label), custom_call_target="tpu_custom_call" | custom-call | tf_op jit(solution)/shard_map/share_terms/pallas_call | solution.py:1001
  865.8 42.5 %gather_blocks.7 = bf16[20480,128]{1,0:T(8,128)(2,1)} custom-call(bf16[1280,128]{1,0:T(8,128)(2,1)} %share_terms.3.src), custom_call_target="tpu_custom_call" | custom-call | tf_op jit(solution)/shard_map/gather_blocks/pallas_call | solution.py:491
  908.3 12.0 %gradient_tables.1 = (f32[2,8,8,16,1152]{4,3,2,1,0:T(8,128)}, f32[2,2,8,16,1152]{4,3,2,1,0:T(8,128)}, f32[2,2,8,16,4304]{4,3,2,1,0:T(8,128)}) custom-call(bf16[32,8,5,16,128]{4,3,2,1,0:T(8,128)(2,1)} %bitcast.141, bf16[32,8,5,16,128]{4,3,2,1,0:T(8,128)(2,1)} %bitcast.142), custom_call_target="tpu_custom_call" | custom-call | tf_op jit(solution)/shard_map/gradient_tables/pallas_call | solution.py:1051
  920.3 3.5 fusion
  (89 shorter events, 20.9 us)
Async XLA Ops:
  3.2 1.9 copy-start
  3.2 14.0 %copy-start.1 = (bf16[2,368,1152]{2,1,0:T(8,128)(2,1)S(1)}, bf16[2,368,1152]{2,1,0:T(8,128)(2,1)}, u32[]{:S(2)}) copy-start(bf16[2,368,1152]{2,1,0:T(8,128)(2,1)} %param.9) | copy-start | bytes 5087236
  6.3 41.7 %collective-permute-start.3 = (bf16[1600,128]{1,0:T(8,128)(2,1)}, bf16[1600,128]{1,0:T(8,128)(2,1)}, u32[]{:S(2)}, u32[]{:S(2)}) collective-permute-start(bf16[1600,128]{1,0:T(8,128)(2,1)} %get-tuple-element.116), channel_id=1, source_target_pairs={{0,2},{2,4},{4,6},{6,8},{8,10},{10,12},{12,14},{14,16},{16,18},{18... | collective-permute-start | bytes 1228808 | tf_op jit(solution)/shard_map/ppermute | solution.py:119
  9.5 38.5 %collective-permute-start.4 = (bf16[1600,128]{1,0:T(8,128)(2,1)}, bf16[1600,128]{1,0:T(8,128)(2,1)}, u32[]{:S(2)}, u32[]{:S(2)}) collective-permute-start(bf16[1600,128]{1,0:T(8,128)(2,1)} %get-tuple-element.115), channel_id=1, source_target_pairs={{2,0},{4,2},{6,4},{8,6},{10,8},{12,10},{14,12},{16,14},{18,16},{20... | collective-permute-start | bytes 1228808 | tf_op jit(solution)/shard_map/ppermute | solution.py:120
  10.7 177.2 %collective-permute-start = (bf16[1600,128]{1,0:T(8,128)(2,1)}, bf16[1600,128]{1,0:T(8,128)(2,1)}, u32[]{:S(2)}, u32[]{:S(2)}) collective-permute-start(bf16[1600,128]{1,0:T(8,128)(2,1)} %get-tuple-element.118), channel_id=1, source_target_pairs={{0,2},{2,4},{4,6},{6,8},{8,10},{10,12},{12,14},{14,16},{16,18},{18... | collective-permute-start | bytes 1228808 | tf_op jit(solution)/shard_map/ppermute | solution.py:119
  15.9 172.0 %collective-permute-start.1 = (bf16[1600,128]{1,0:T(8,128)(2,1)}, bf16[1600,128]{1,0:T(8,128)(2,1)}, u32[]{:S(2)}, u32[]{:S(2)}) collective-permute-start(bf16[1600,128]{1,0:T(8,128)(2,1)} %get-tuple-element.117), channel_id=1, source_target_pairs={{2,0},{4,2},{6,4},{8,6},{10,8},{12,10},{14,12},{16,14},{18,16},{20... | collective-permute-start | bytes 1228808 | tf_op jit(solution)/shard_map/ppermute | solution.py:120
  18.3 174.0 %collective-permute-start.2 = (bf16[368,1152]{1,0:T(8,128)(2,1)}, bf16[368,1152]{1,0:T(8,128)(2,1)}, u32[]{:S(2)}, u32[]{:S(2)}) collective-permute-start(bf16[368,1152]{1,0:T(8,128)(2,1)} %get-tuple-element.136), channel_id=1, source_target_pairs={{0,1},{1,0},{2,3},{3,2},{4,5},{5,4},{6,7},{7,6},{8,9},{9,8},{10,11... | collective-permute-start | bytes 2543624 | tf_op jit(solution)/shard_map/ppermute | solution.py:1096
  19.8 4.3 copy-start.12
  19.8 6.2 copy-start.13
  27.3 5.8 copy-start.3
  52.3 131.4 %copy-start.2 = (bf16[2,368,1152]{2,1,0:T(8,128)(2,1)S(1)}, bf16[2,368,1152]{2,1,0:T(8,128)(2,1)}, u32[]{:S(2)}) copy-start(bf16[2,368,1152]{2,1,0:T(8,128)(2,1)} %param.17) | copy-start | bytes 5087236
  185.4 320.9 %collective-permute-start.6 = (bf16[368,1152]{1,0:T(8,128)(2,1)}, bf16[368,1152]{1,0:T(8,128)(2,1)S(1)}, u32[]{:S(2)}, u32[]{:S(2)}) collective-permute-start(bf16[368,1152]{1,0:T(8,128)(2,1)} %get-tuple-element.132), channel_id=1, source_target_pairs={{0,1},{1,0},{2,3},{3,2},{4,5},{5,4},{6,7},{7,6},{8,9},{9,8},{10,11... | collective-permute-start | bytes 2543624 | tf_op jit(solution)/shard_map/ppermute | solution.py:1096
  511.0 126.0 %collective-permute-start.5 = (bf16[368,1152]{1,0:T(8,128)(2,1)S(1)}, bf16[368,1152]{1,0:T(8,128)(2,1)}, u32[]{:S(2)}, u32[]{:S(2)}) collective-permute-start(bf16[368,1152]{1,0:T(8,128)(2,1)S(1)} %get-tuple-element.134), channel_id=1, source_target_pairs={{0,1},{1,0},{2,3},{3,2},{4,5},{5,4},{6,7},{7,6},{8,9},{9,8},{10,11... | collective-permute-start | bytes 2543624 | tf_op jit(solution)/shard_map/ppermute | solution.py:1110
  613.9 22.6 %copy-start.8 = (f32[48,1152]{1,0:T(8,128)S(1)}, f32[48,1152]{1,0:T(8,128)}, u32[]{:S(2)}) copy-start(f32[48,1152]{1,0:T(8,128)} %get-tuple-element.105) | copy-start | bytes 663556
  613.9 22.7 %copy-start.10 = (f32[16,1152]{1,0:T(8,128)S(1)}, f32[16,1152]{1,0:T(8,128)}, u32[]{:S(2)}) copy-start(f32[16,1152]{1,0:T(8,128)} %get-tuple-element.106) | copy-start | bytes 221188
  763.9 1.3 copy-start.6
  764.0 1.3 copy-start.7
  764.0 2.1 copy-start.5
  764.1 2.2 copy-start.9
  764.1 156.1 %collective-permute-start.7 = (bf16[368,1152]{1,0:T(8,128)(2,1)S(1)}, bf16[368,1152]{1,0:T(8,128)(2,1)}, u32[]{:S(2)}, u32[]{:S(2)}) collective-permute-start(bf16[368,1152]{1,0:T(8,128)(2,1)S(1)} %get-tuple-element.130), channel_id=1, source_target_pairs={{0,1},{1,0},{2,3},{3,2},{4,5},{5,4},{6,7},{7,6},{8,9},{9,8},{10,11... | collective-permute-start | bytes 2543624 | tf_op jit(solution)/shard_map/ppermute | solution.py:1110
  765.3 3.0 copy-start.11
  765.4 0.7 copy-start.4

commit v5 on v4

--- a/solution.py
+++ b/solution.py
@@ -18,6 +18,7 @@
 F32 = jnp.float32
 MESH = pl.DeviceIdType.MESH
 VMEM_LIMIT = 60 << 20
+VMEM_MOST = 67043328
 C2 = math.log2(math.e) / math.sqrt(HD)
 SCALE = 1.0 / math.sqrt(HD)
 NEG = -1e30
@@ -287,7 +288,7 @@
     )(*operands)
 
 
-def gather_kernel(
+def gather_plan(
     src, out, stage, local_sem, z_recv, y_recv, b_recv, h_recv, c_recv_own, c_recv_z, c_recv_y, c_recv_b, c_recv_h,
     up_send, down_send, y_send, b_send, h_send, c_send_own, c_send_z, c_send_y, c_send_b, c_send_h,
 ):
@@ -326,44 +327,49 @@
     def arrived(spot, recv):
         copy(spot, local_sem.at[1], recv, mate).wait_recv()
 
-    barrier = pltpu.get_barrier_semaphore()
-    for to in (beside, across, mate):
-        pl.semaphore_signal(barrier, inc=1, device_id=to, device_id_type=MESH)
-
-    @pl.when(z < 3)
-    def _():
-        pl.semaphore_signal(barrier, inc=1, device_id=up, device_id_type=MESH)
-
-    @pl.when(z > 0)
-    def _():
-        pl.semaphore_signal(barrier, inc=1, device_id=down, device_id_type=MESH)
-
-    pl.semaphore_wait(barrier, 3 + jnp.where(z < 3, 1, 0) + jnp.where(z > 0, 1, 0))
-
     def own(j):
         begin = jnp.where(x == 0, begins[j], rows - begins[j] - sizes[j])
         return src.at[pl.ds(pl.multiple_of(begin, 16), sizes[j]), :]
 
     whole = (pl.multiple_of(f * rows, 16), rows)
-    for j in range(5):
-        spot = place(z, y, j, x)
+    keep = pltpu.make_async_copy(src if stage is None else stage, view(whole), local_sem.at[0])
+
+    def start():
+        barrier = pltpu.get_barrier_semaphore()
+        for to in (beside, across, mate):
+            pl.semaphore_signal(barrier, inc=1, device_id=to, device_id_type=MESH)
 
         @pl.when(z < 3)
         def _():
-            copy(spot, up_send.at[z, j], z_recv.at[z, j], up, own(j)).start()
+            pl.semaphore_signal(barrier, inc=1, device_id=up, device_id_type=MESH)
 
         @pl.when(z > 0)
         def _():
-            copy(spot, down_send.at[z, j], z_recv.at[z, j], down, own(j)).start()
-
-        if j < 3:
-            copy(spot, y_send.at[z, j], y_recv.at[z, j], beside, own(j)).start()
-    copy(whole, c_send_own.at[0], c_recv_own.at[0], mate, src).start()
-    fetch = pltpu.make_async_copy(src, stage, local_sem.at[0])
-    fetch.start()
-    fetch.wait()
-    keep = pltpu.make_async_copy(stage, view(whole), local_sem.at[0])
-    keep.start()
+            pl.semaphore_signal(barrier, inc=1, device_id=down, device_id_type=MESH)
+
+        pl.semaphore_wait(barrier, 3 + jnp.where(z < 3, 1, 0) + jnp.where(z > 0, 1, 0))
+
+        for j in range(5):
+            spot = place(z, y, j, x)
+
+            @pl.when(z < 3)
+            def _():
+                copy(spot, up_send.at[z, j], z_recv.at[z, j], up, own(j)).start()
+
+            @pl.when(z > 0)
+            def _():
+                copy(spot, down_send.at[z, j], z_recv.at[z, j], down, own(j)).start()
+
+            if j < 3:
+                copy(spot, y_send.at[z, j], y_recv.at[z, j], beside, own(j)).start()
+        copy(whole, c_send_own.at[0], c_recv_own.at[0], mate, src).start()
+        if stage is None:
+            keep.start()
+        else:
+            fetch = pltpu.make_async_copy(src, stage, local_sem.at[0])
+            fetch.start()
+            fetch.wait()
+            keep.start()
 
     def z_event(d, j):
         def flow(zb, onward, to, sends):
@@ -438,64 +444,76 @@
                 ready = at + 1.5 if d else j + 1
                 events.append((ready, functools.partial(y_event, d, j)))
                 events.append((ready + 2, functools.partial(h_event, d, j)))
-    for _, event in sorted(events, key=lambda e: e[0]):
+    def finish():
+        keep.wait()
+        other = 1 - c
+
+        def core_spot(zb, yb, j, side):
+            return place(zb, yb, j, side, other)
+
+        arrived((pl.multiple_of(((z * 2 + y) * 2 + other) * rows, 16), rows), c_recv_own.at[0])
+        copy(whole, c_send_own.at[0], c_recv_own.at[0], mate).wait_send()
+        for d in range(4):
+            def drain(zb, d=d):
+                for j in range(5):
+                    if d:
+                        arrived(core_spot(zb, y, j, x), c_recv_z.at[zb, j])
+                        copy(place(zb, y, j, x), c_send_z.at[zb, j], c_recv_z.at[zb, j], mate).wait_send()
+                    if j < 3:
+                        arrived(core_spot(zb, 1 - y, j, x), c_recv_y.at[zb, j])
+                        arrived(core_spot(zb, 1 - y, j, 1 - x), c_recv_h.at[zb, j])
+                        spot = place(zb, 1 - y, j, x)
+                        copy(spot, c_send_y.at[zb, j], c_recv_y.at[zb, j], mate).wait_send()
+                        copy(spot, h_send.at[zb, j], h_recv.at[zb, j], across).wait_send()
+                        spot = place(zb, 1 - y, j, 1 - x)
+                        copy(spot, c_send_h.at[zb, j], c_recv_h.at[zb, j], mate).wait_send()
+                        spot = place(zb, y, j, x)
+                        copy(spot, y_send.at[zb, j], y_recv.at[zb, j], beside).wait_send()
+                if d:
+                    arrived(core_spot(zb, y, 0, 1 - x), c_recv_b.at[zb])
+                    spot = place(zb, y, 0, 1 - x)
+                    copy(spot, c_send_b.at[zb], c_recv_b.at[zb], mate).wait_send()
+                    spot = place(zb, y, 0, x)
+                    copy(spot, b_send.at[zb], b_recv.at[zb], across).wait_send()
+
+            each(d, drain)
+            for j in range(5):
+                @pl.when(jnp.logical_and(z - d >= 0, z < 3))
+                def _():
+                    zb = z - d
+                    copy(place(zb, y, j, x), up_send.at[zb, j], z_recv.at[zb, j], up).wait_send()
+
+                @pl.when(jnp.logical_and(z + d <= 3, z > 0))
+                def _():
+                    zb = z + d
+                    copy(place(zb, y, j, x), down_send.at[zb, j], z_recv.at[zb, j], down).wait_send()
+
+    return start, sorted(events, key=lambda e: e[0]), finish
+
+
+def gather_kernel(*refs):
+    start, events, finish = gather_plan(*refs)
+    start()
+    for _, event in events:
         event()
-    keep.wait()
-    other = 1 - c
-
-    def core_spot(zb, yb, j, side):
-        return place(zb, yb, j, side, other)
-
-    arrived((pl.multiple_of(((z * 2 + y) * 2 + other) * rows, 16), rows), c_recv_own.at[0])
-    copy(whole, c_send_own.at[0], c_recv_own.at[0], mate).wait_send()
-    for d in range(4):
-        def drain(zb, d=d):
-            for j in range(5):
-                if d:
-                    arrived(core_spot(zb, y, j, x), c_recv_z.at[zb, j])
-                    copy(place(zb, y, j, x), c_send_z.at[zb, j], c_recv_z.at[zb, j], mate).wait_send()
-                if j < 3:
-                    arrived(core_spot(zb, 1 - y, j, x), c_recv_y.at[zb, j])
-                    arrived(core_spot(zb, 1 - y, j, 1 - x), c_recv_h.at[zb, j])
-                    spot = place(zb, 1 - y, j, x)
-                    copy(spot, c_send_y.at[zb, j], c_recv_y.at[zb, j], mate).wait_send()
-                    copy(spot, h_send.at[zb, j], h_recv.at[zb, j], across).wait_send()
-                    spot = place(zb, 1 - y, j, 1 - x)
-                    copy(spot, c_send_h.at[zb, j], c_recv_h.at[zb, j], mate).wait_send()
-                    spot = place(zb, y, j, x)
-                    copy(spot, y_send.at[zb, j], y_recv.at[zb, j], beside).wait_send()
-            if d:
-                arrived(core_spot(zb, y, 0, 1 - x), c_recv_b.at[zb])
-                spot = place(zb, y, 0, 1 - x)
-                copy(spot, c_send_b.at[zb], c_recv_b.at[zb], mate).wait_send()
-                spot = place(zb, y, 0, x)
-                copy(spot, b_send.at[zb], b_recv.at[zb], across).wait_send()
-
-        each(d, drain)
-        for j in range(5):
-            @pl.when(jnp.logical_and(z - d >= 0, z < 3))
-            def _():
-                zb = z - d
-                copy(place(zb, y, j, x), up_send.at[zb, j], z_recv.at[zb, j], up).wait_send()
-
-            @pl.when(jnp.logical_and(z + d <= 3, z > 0))
-            def _():
-                zb = z + d
-                copy(place(zb, y, j, x), down_send.at[zb, j], z_recv.at[zb, j], down).wait_send()
+    finish()
+
+
+def gather_semaphores():
+    dma = pltpu.SemaphoreType.DMA
+    core = [dma((1,)), dma((4, 5)), dma((4, 3)), dma((4,)), dma((4, 3))]
+    links = [dma((4, 5)), dma((4, 3)), dma((4,)), dma((4, 3))]
+    return [dma((2,))] + links + core + [dma((4, 5))] + links + core
 
 
 def gather_blocks(shard, collective_id, held_rows):
     rows = shard.shape[0]
-    dma = pltpu.SemaphoreType.DMA
-    core = [dma((1,)), dma((4, 5)), dma((4, 3)), dma((4,)), dma((4, 3))]
     return pl.pallas_call(
         gather_kernel,
         in_specs=[pl.BlockSpec(memory_space=pl.ANY)],
         out_specs=pl.BlockSpec(memory_space=pl.ANY),
         out_shape=jax.ShapeDtypeStruct((held_rows, LANES), BF16),
-        scratch_shapes=[pltpu.VMEM((rows, LANES), BF16), dma((2,))]
-        + [dma((4, 5)), dma((4, 3)), dma((4,)), dma((4, 3))] + core
-        + [dma((4, 5)), dma((4, 5)), dma((4, 3)), dma((4,)), dma((4, 3))] + core,
+        scratch_shapes=[pltpu.VMEM((rows, LANES), BF16)] + gather_semaphores(),
         compiler_params=pltpu.CompilerParams(collective_id=collective_id, has_side_effects=True, vmem_limit_bytes=VMEM_LIMIT),
         name="gather_blocks",
     )(shard)
@@ -882,6 +900,210 @@
         name="input_backward",
         **dense_params(6 * rows * D * D, 20 * rows * D + 6 * D * D),
     )(d_qkv, w_qkv, attn[0:3].reshape(3 * R, D), attn[4:7], normed, inner, hidden, d_middle, vectors)
+
+
+FORWARD_STEPS = (3, H, WIDE // TILE, 3)
+FORWARD_AT = (0, 3, 3 + H, 3 + H + WIDE // TILE)
+FORWARD_BEGINS = (
+    [4.5 * i for i in range(3)]
+    + [14 + 2 * i for i in range(H)]
+    + [46 + (5 if i else 0) + 2.6 * i for i in range(WIDE // TILE)]
+    + [76 + 5 * i for i in range(3)]
+)
+CHUNK_TIME = 7.0
+
+
+def forward_kernel(with_gather, *refs):
+    (
+        marks, hidden, w_qkv, vec, down, up, w_o, down_o, up_o, down_1, w_1, b_1, up_1, w_2, b_2, down_2, up_2,
+    ) = refs[:17]
+    refs = refs[17:]
+    if with_gather:
+        shard, refs = refs[0], refs[1:]
+    (
+        normed, inner_qkv, qkv, attended, stats, inner_o, middle, normed_two, inner_up, gate, inner_down,
+        next_hidden,
+    ) = refs[:12]
+    refs = refs[12:]
+    if with_gather:
+        flat, refs = refs[0], refs[1:]
+    heads, activated, parts = refs[:3]
+    i = pl.program_id(0)
+    rows = hidden.shape[0]
+    _, att_at, up_at, down_at = FORWARD_AT
+    last = down_at + 2
+
+    def at_step(k):
+        return pl.when(i == k)
+
+    if with_gather:
+        start, events, finish = gather_plan(shard, flat, None, *refs[3:])
+        at_step(0)(start)
+        steps = [[] for _ in FORWARD_BEGINS]
+        late = []
+        for when, event in events:
+            ready = [k for k, begin in enumerate(FORWARD_BEGINS) if begin >= CHUNK_TIME * when + 4]
+            (steps[ready[0]] if ready else late).append(event)
+        for k, due in enumerate(steps):
+            if due:
+
+                @at_step(k)
+                def _(due=due):
+                    for event in due:
+                        event()
+
+    @pl.when(i < att_at)
+    def _():
+        @at_step(0)
+        def _():
+            value = layer_norm(hidden[...], vec[0:1], vec[1:2]).astype(BF16)
+            normed[...] = value
+            narrow = dot_t(value, down[...]).astype(BF16)
+            inner_qkv[...] = narrow
+            for part in range(3):
+                parts[part] = narrow[:, part * R : (part + 1) * R]
+            stats[...] = jnp.zeros_like(stats)
+
+        bias = vec[pl.ds(jnp.where(i == 2, 5, 4), 1), :] * jnp.where(i == 1, 0.0, 1.0)
+        value = (dot_both(normed[...], matrix(w_qkv), parts[i], up[0]) + bias).astype(BF16)
+        qkv[...] = value
+        mark = marks[0]
+        for h in range(H):
+            heads[i, h] = pad_lanes(value[:, h * HD : (h + 1) * HD], mark)
+
+    @pl.when(jnp.logical_and(i >= att_at, i < up_at))
+    def _():
+        h = i - att_at
+        lane = lax.broadcasted_iota(jnp.int32, (rows, LANES), 1)
+        s = dot_t(heads[0, h], heads[1, h])
+        m = jnp.max(s, axis=1, keepdims=True)
+        p = jnp.exp2((s - m) * C2)
+        total = jnp.sum(p, axis=1, keepdims=True)
+        o = dot(p.astype(BF16), heads[2, h])
+        heads[0, h] = (o * (1.0 / total)).astype(BF16)
+        stats[...] = jnp.where(lane == h, m * C2 + jnp.log2(total), stats[...])
+
+    @pl.when(jnp.logical_and(i >= up_at, i < down_at))
+    def _():
+        t = i - up_at
+
+        @at_step(up_at)
+        def _():
+            for h in range(H):
+                attended[:, h * HD : (h + 1) * HD] = heads[0, h][:, :HD]
+            value = attended[...]
+            narrow = dot_t(value, down_o[...]).astype(BF16)
+            inner_o[...] = narrow
+            middle[...] = hidden[...] + (dot_both(value, matrix(w_o), narrow, up_o[...]) + vec[6:7])
+            value = layer_norm(middle[...], vec[2:3], vec[3:4]).astype(BF16)
+            normed_two[...] = value
+            inner_up[...] = dot_t(value, down_1[...]).astype(BF16)
+
+        x = dot_both(normed_two[...], matrix(w_1), inner_up[...], up_1[...]) + b_1[...]
+        gate[...] = x.astype(BF16)
+        value = (0.5 * x * (1.0 + gelu_parts(x))).astype(BF16)
+        activated[:, pl.ds(pl.multiple_of(t * TILE, LANES), TILE)] = value
+
+    @pl.when(i >= down_at)
+    def _():
+        @at_step(down_at)
+        def _():
+            inner_down[...] = dot_t(activated[...], down_2[...]).astype(BF16)
+
+        at = pl.ds(pl.multiple_of((i - down_at) * THIRD, LANES), THIRD)
+        next_hidden[...] = middle[:, at] + (
+            dot(activated[:, :FF], matrix(w_2.at[: UNITS[3]])) + b_2[...] + dot(inner_down[...], up_2[...])
+        )
+
+    if with_gather:
+
+        @at_step(last)
+        def _():
+            for event in late:
+                event()
+            finish()
+
+
+def layer_forward(length, hidden, w_qkv, w_o, w_1, w_2, vectors, b_1, attn, narrow, wide, shard=None):
+    rows = hidden.shape[0]
+    _, att_at, up_at, down_at = FORWARD_AT
+
+    def step(i, k):
+        return jnp.minimum(jnp.maximum(i - FORWARD_AT[k], 0), FORWARD_STEPS[k] - 1)
+
+    def cols(count, width, k):
+        return pl.BlockSpec((count, width), lambda i: (0, step(i, k)))
+
+    lane = lax.broadcasted_iota(jnp.int32, (rows, LANES - HD), 1)
+    key = lax.broadcasted_iota(jnp.int32, (rows, LANES - HD), 0)
+    marks = jnp.stack([jnp.ones_like(lane, F32), jnp.where(key < length[0], 0.0, NEG), jnp.zeros_like(lane, F32)])
+    marks = jnp.where(lane == 0, marks, 0.0).astype(BF16)
+    operands = [
+        marks, hidden, w_qkv, vectors, attn[0:3].reshape(3 * R, D), attn[4:7], w_o, attn[3], attn[7], narrow[0],
+        w_1, b_1, wide[0], w_2, vectors[7:8], wide[1], narrow[1],
+    ]
+    in_specs = [
+        pl.BlockSpec((1, rows, LANES - HD), lambda i: (step(i, 0), 0, 0)),
+        whole((rows, D)),
+        unit_block(72, 9, lambda i: (0, step(i, 0), 0, 0)),
+        whole((8, D)),
+        whole((3 * R, D)),
+        pl.BlockSpec((1, R, D), lambda i: (step(i, 0), 0, 0)),
+        OUT_BLOCK,
+        whole((R, D)),
+        whole((R, D)),
+        whole((R, D)),
+        unit_block(72, 4, lambda i: (1, step(i, 2), 0, 0)),
+        cols(1, TILE, 2),
+        cols(R, TILE, 2),
+        unit_block(288, 3, lambda i: (2, step(i, 3), 0, 0)),
+        cols(1, THIRD, 3),
+        whole((R, WIDE)),
+        cols(R, THIRD, 3),
+    ]
+    outs = [
+        (whole((rows, D)), struct((rows, D), BF16)),
+        (whole((rows, 3 * R)), struct((rows, 3 * R), BF16)),
+        (cols(rows, D, 0), struct((rows, 3 * D), BF16)),
+        (whole((rows, D)), struct((rows, D), BF16)),
+        (whole((rows, LANES)), struct((rows, LANES), F32)),
+        (whole((rows, R)), struct((rows, R), BF16)),
+        (whole((rows, D)), struct((rows, D), F32)),
+        (whole((rows, D)), struct((rows, D), BF16)),
+        (whole((rows, R)), struct((rows, R), BF16)),
+        (cols(rows, TILE, 2), struct((rows, WIDE), BF16)),
+        (whole((rows, R)), struct((rows, R), BF16)),
+        (cols(rows, THIRD, 3), struct((rows, D), F32)),
+    ]
+    scratch = [
+        pltpu.VMEM((3, H, rows, LANES), BF16),
+        pltpu.VMEM((rows, WIDE), BF16),
+        pltpu.VMEM((3, rows, R), BF16),
+    ]
+    params = dict(vmem_limit_bytes=VMEM_MOST)
+    if shard is not None:
+        operands.append(shard)
+        in_specs.append(pl.BlockSpec(memory_space=pl.ANY))
+        outs.append(
+            (pl.BlockSpec(memory_space=pl.ANY), struct((16 * TILES_HELD, LANES), BF16))
+        )
+        scratch += gather_semaphores()
+        params.update(collective_id=3, has_side_effects=True)
+    return pl.pallas_call(
+        functools.partial(forward_kernel, shard is not None),
+        grid=(sum(FORWARD_STEPS),),
+        in_specs=in_specs,
+        out_specs=[spec for spec, _ in outs],
+        out_shape=[shape for _, shape in outs],
+        scratch_shapes=scratch,
+        cost_estimate=pl.CostEstimate(
+            flops=2 * rows * D * (4 * D + 2 * FF) + 8 * rows * rows * D,
+            bytes_accessed=2 * D * (4 * D + 2 * FF) + 30 * rows * D,
+            transcendentals=H * rows * rows,
+        ),
+        compiler_params=pltpu.CompilerParams(**params),
+        name="layer_forward_gather" if shard is not None else "layer_forward",
+    )(*operands)
 
 
 SHARE = 5
@@ -1131,7 +1353,9 @@
     stored = []
     weights = []
     for layer in range(layer_count):
-        if on_block:
+        if on_block and layer > 0:
+            pass
+        elif on_block:
             flat = gather_blocks(shards[layer], 0, 16 * TILES_HELD)
         else:
             flat = lax.all_gather(shards[layer], "fsdp", axis=0, tiled=True)
@@ -1147,19 +1371,27 @@
         narrow = pick(narrow_adapter_weights[layer])
         wide = jnp.pad(pick(broad_adapter_weights[layer]), ((0, 0), (0, 0), (0, WIDE - FF)))
         weights.append((w_qkv, w_o, w_1, w_2, vectors, attn, narrow, wide))
-        normed, inner_qkv, qkv = qkv_forward(hidden, w_qkv, vectors, attn)
         keys = None
-        if parts > 1:
+        if parts == 1:
+            shard = shards[layer + 1] if on_block and layer + 1 < layer_count else None
+            made = layer_forward(
+                length, hidden, w_qkv, w_o, w_1, w_2, vectors, b_1, attn, narrow, wide, shard
+            )
+            normed, inner_qkv, qkv, attended, stats, inner_o, middle = made[:7]
+            normed_two, inner_up, gate, inner_down, next_hidden = made[7:12]
+            flat = made[12] if shard is not None else None
+        else:
+            normed, inner_qkv, qkv = qkv_forward(hidden, w_qkv, vectors, attn)
             keys = lax.all_gather(
                 qkv[:, D:], "seq", axis=0, tiled=True, axis_index_groups=groups
             )
-        attended, stats = attn_fwd(length, qkv, keys)
-        inner_o, middle, normed_two, inner_up, gate, activated = up_forward(
-            attended, hidden, w_o, vectors, attn, narrow, w_1, b_1, wide
-        )
-        inner_down, next_hidden = down_forward(
-            activated, middle, w_2, vectors[7:8], narrow, wide
-        )
+            attended, stats = attn_fwd(length, qkv, keys)
+            inner_o, middle, normed_two, inner_up, gate, activated = up_forward(
+                attended, hidden, w_o, vectors, attn, narrow, w_1, b_1, wide
+            )
+            inner_down, next_hidden = down_forward(
+                activated, middle, w_2, vectors[7:8], narrow, wide
+            )
         stored.append(
             (
                 hidden,

time: 934 us -> 861 us (0.922)
  Pallas kernels: 840 us -> 765 us
    pallas_call x4 -> x3, Pallas kernels: 335 us -> 214 us  [gather_blocks(): pl.pallas_call(gather_kernel, in_specs=[pl.BlockSpec(memory_space=pl.ANY)...]
    pallas_call x8 -> x2, Pallas kernels: 182 us -> 230 us  [layer_forward(): pl.pallas_call(functools.partial(forward_kernel, shard is not None), grid...]
  transfers between devices with their start and end apart: 8 -> 8, of which waited for: 0 -> 0; matrix products, arithmetic and copies ran while one was open for 5% -> 4% of each run, Pallas kernels for 78% -> 42%
where the time goes in v5:
time: 861 us; the launch traced here: 851 us
  Pallas kernels  765 us (89%)
  local copies, waits for them, and re-layouts  41.1 us (5%)
  other arithmetic  25.6 us (3%)
  starting transfers between devices  15.3 us (2%)
    pallas_call x2, Pallas kernels, layer_forward(): pl.pallas_call(functools.partial(forward_kernel, shard is not None), grid...  230 us
    pallas_call x3, Pallas kernels, gather_blocks(): pl.pallas_call(gather_kernel, in_specs=[pl.BlockSpec(memory_space=pl.ANY)...  214 us
    pallas_call x2, Pallas kernels, attn_bwd(): pl.pallas_call(kernel, in_specs=[pl.BlockSpec(memory_space=pltpu.SMEM)] +...  90.3 us
    pallas_call x2, Pallas kernels, share_terms(): pl.pallas_call(functools.partial(share_kernel, adapters), in_specs=[pl.Bl...  57.4 us
    pallas_call x2, Pallas kernels, gate_backward(): pl.pallas_call(gate_kernel, grid=(WIDE // TILE,), in_specs=[whole((rows,...  56.1 us
    pallas_call x2, Pallas kernels, middle_backward(): pl.pallas_call(middle_kernel, grid=(3,), in_specs=[whole((rows, WIDE)), u...  54.3 us
    pallas_call x2, Pallas kernels, input_backward(): pl.pallas_call(input_kernel, grid=(3,), in_specs=[whole((rows, 3 * D)), u...  43 us
  transfers between devices with their start and end apart: 8, of which 0 were waited for; matrix products, arithmetic and copies ran while one was open for 4% of the time, Pallas kernels for 42%

profile of v5, /device:TPU:0, one launch (start us, length us, event | category | flops | bytes accessed | tf_op | source)
XLA Modules:
  0.0 851.4 jit_solution(18227128482037759910)
XLA Ops:
  0.6 2.6 copy.53
  3.2 1.9 copy-done
  5.1 1.2 slice_bitcast_fusion.2
  6.3 3.1 collective-permute-start
  9.4 1.3 collective-permute-start.1
  10.7 1.0 dynamic-slice_bitcast_fusion.5
  11.8 2.4 collective-permute-start.2
  14.1 4.1 collective-permute-start.3
  18.2 1.4 collective-permute-start.4
  19.6 4.3 slice_bitcast_fusion
  25.4 1.8 fusion.8
  28.9 2.3 fusion.10
  31.3 4.7 fusion.9
  36.5 1.1 dynamic-slice_bitcast_fusion.6
  39.1 1.5 dynamic-slice_bitcast_fusion.14
  40.6 1.5 dynamic-slice_bitcast_fusion.10
  42.1 1.7 dynamic-slice_bitcast_fusion.8
  46.8 0.9 select_convert_fusion.refs_0_
  47.8 4.3 lay_shard.2.refs_0_
  52.0 4.3 lay_shard.3.refs_17_
  56.3 3.6 convert_multiply_fusion.1.refs_1_.hidden
  59.9 134.6 %gather_blocks.3 = bf16[124416,128]{1,0:T(8,128)(2,1)} custom-call(bf16[7648,128]{1,0:T(8,128)(2,1)} %lay_shard.2.refs_0_), custom_call_target="tpu_custom_call" | custom-call | tf_op jit(solution)/shard_map/gather_blocks/pallas_call | solution.py:511
  197.9 146.8 %layer_forward_gather.1 = (bf16[736,1152]{1,0:T(8,128)(2,1)}, bf16[736,48]{1,0:T(8,128)(2,1)}, bf16[736,3456]{1,0:T(8,128)(2,1)}, bf16[736,1152]{1,0:T(8,128)(2,...) custom-call(bf16[3,736,56]{2,1,0:T(8,128)(2,1)} %select_convert_fusi, ...), custom_call_target="tpu_custom_call" | custom-call | flops 27403223040 | bytes 55885824 | tf_op jit(solution)/shard_map/layer_forward_gather/pallas_call | solution.py:1092
  346.8 2.8 dynamic-slice_bitcast_fusion.2
  351.7 82.9 %layer_forward.1 = (bf16[736,1152]{1,0:T(8,128)(2,1)}, bf16[736,48]{1,0:T(8,128)(2,1)}, bf16[736,3456]{1,0:T(8,128)(2,1)}, bf16[736,1152]{1,0:T(8,128)(2,1)}, f3...) custom-call(bf16[3,736,56]{2,1,0:T(8,128)(2,1)} %select_convert_fusi, ...), custom_call_target="tpu_custom_call" | custom-call | flops 27403223040 | bytes 55885824 | tf_op jit(solution)/shard_map/layer_forward/pallas_call | solution.py:1092
  434.5 5.4 convert_multiply_fusion
  440.1 1.3 collective-permute-start.5
  441.4 27.8 %gate_backward.2 = (bf16[736,4608]{1,0:T(8,128)(2,1)}, f32[32,4608]{1,0:T(8,128)}, bf16[736,16]{1,0:T(8,128)(2,1)}, f32[16,1152]{1,0:T(8,128)}) custom-call(f32[736,1152]{1,0:T(8,128)} %get-tuple-element.145.gradient, bf16[864,9,16,128]{3,2,1,0:T(8,128)(2,1)} %bitcast.137, bf16[736,4608]{1,0:T(8,128)(2,1)} %get-tuple-element.65.gate, ...), custom_call_target="tpu_custom_call" | custom-call | flops 7298482176 | bytes 25978880 | tf_op jit(solution)/shard_map/gate_backward/pallas_call | solution.py:771
  469.2 1.1 convert.69
  470.5 27.2 %middle_backward.2 = (f32[736,1152]{1,0:T(8,128)}, bf16[736,1152]{1,0:T(8,128)(2,1)}, f32[48,1152]{1,0:T(8,128)}) custom-call(bf16[736,4608]{1,0:T(8,128)(2,1)} %get-tuple-element.68.d_gate, bf16[216,36,16,128]{3,2,1,0:T(8,128)(2,1)} %bitcast.139, bf16[736,16]{1,0:T(8,128)(2,1)} %get-tuple-element.69.d_inner_up, ...), custom_call_target="tpu_custom_call" | custom-call | flops 9251979264 | bytes 34167808 | tf_op jit(solution)/shard_map/middle_backward/pallas_call | solution.py:827
  497.8 45.2 %attention_backward.2.d_qkv = bf16[736,3456]{1,0:T(8,128)(2,1)} custom-call(s32[1]{0:T(128)} %dynamic_slice.53.a, bf16[736,3456]{1,0:T(8,128)(2,1)} %get-tuple-element.63.b, bf16[736,1152]{1,0:T(8,128)(2,1)} %get-tuple-element.74.c, bf16[736,1152]{1,0:T(8,128)(2,1)} %get-tuple-element.73.attended.d, f32[736,128]{1,0:T(8,128)} %get-tuple-element.75.e), custom_call_target="tpu_custom_call" | custom-call | flops 22187868160 | bytes 13565952 | tf_op jit(solution)/shard_map/attention_backward/pallas_call | solution.py:270
  543.0 21.5 %input_backward.2 = (f32[736,1152]{1,0:T(8,128)}, f32[96,1152]{1,0:T(8,128)}) custom-call(bf16[736,3456]{1,0:T(8,128)(2,1)} %attention_backward.2.d_qkv, bf16[288,27,16,128]{3,2,1,0:T(8,128)(2,1)} %bitcast.140, bf16[48,1152]{1,0:T(8,128)(2,1)} %bitcast.159, bf16[3,16,1152]{2,1,0:T(8,128)(2,1)} %get-tuple-element.121.refs_5_.up, ...), custom_call_target="tpu_custom_call" | custom-call | flops 5860491264 | bytes 24920064 | tf_op jit(solution)/shard_map/input_backward/pallas_call | solution.py:883
  564.5 1.0 convert.66
  566.0 2.9 maximum_select_fusion.1
  568.9 28.2 %gate_backward.3 = (bf16[736,4608]{1,0:T(8,128)(2,1)}, f32[32,4608]{1,0:T(8,128)}, bf16[736,16]{1,0:T(8,128)(2,1)}, f32[16,1152]{1,0:T(8,128)}) custom-call(f32[736,1152]{1,0:T(8,128)} %get-tuple-element.82.gradient, bf16[864,9,16,128]{3,2,1,0:T(8,128)(2,1)} %bitcast.129, bf16[736,4608]{1,0:T(8,128)(2,1)} %get-tuple-element.83.gate, ...), custom_call_target="tpu_custom_call" | custom-call | flops 7298482176 | bytes 25978880 | tf_op jit(solution)/shard_map/gate_backward/pallas_call | solution.py:771
  597.2 27.0 %middle_backward.3 = (f32[736,1152]{1,0:T(8,128)}, bf16[736,1152]{1,0:T(8,128)(2,1)}, f32[48,1152]{1,0:T(8,128)}) custom-call(bf16[736,4608]{1,0:T(8,128)(2,1)} %get-tuple-element.86.d_gate, bf16[216,36,16,128]{3,2,1,0:T(8,128)(2,1)} %bitcast.131, bf16[736,16]{1,0:T(8,128)(2,1)} %get-tuple-element.87.d_inner_up, ...), custom_call_target="tpu_custom_call" | custom-call | flops 9251979264 | bytes 34167808 | tf_op jit(solution)/shard_map/middle_backward/pallas_call | solution.py:827
  624.2 45.1 %attention_backward.3.d_qkv = bf16[736,3456]{1,0:T(8,128)(2,1)} custom-call(s32[1]{0:T(128)} %dynamic_slice.53.a, bf16[736,3456]{1,0:T(8,128)(2,1)} %get-tuple-element.81.b, bf16[736,1152]{1,0:T(8,128)(2,1)} %get-tuple-element.92.c, bf16[736,1152]{1,0:T(8,128)(2,1)} %get-tuple-element.91.attended.d, f32[736,128]{1,0:T(8,128)} %get-tuple-element.93.e), custom_call_target="tpu_custom_call" | custom-call | flops 22187868160 | bytes 13565952 | tf_op jit(solution)/shard_map/attention_backward/pallas_call | solution.py:270
  669.3 21.5 %input_backward.3 = (f32[736,1152]{1,0:T(8,128)}, f32[96,1152]{1,0:T(8,128)}) custom-call(bf16[736,3456]{1,0:T(8,128)(2,1)} %attention_backward.3.d_qkv, bf16[288,27,16,128]{3,2,1,0:T(8,128)(2,1)} %bitcast.132, bf16[48,1152]{1,0:T(8,128)(2,1)} %bitcast.161, bf16[3,16,1152]{2,1,0:T(8,128)(2,1)} %get-tuple-element.150.refs_5_.up, ...), custom_call_target="tpu_custom_call" | custom-call | flops 5860491264 | bytes 24920064 | tf_op jit(solution)/shard_map/input_backward/pallas_call | solution.py:883
  690.8 2.2 multiply_convert_fusion
  693.2 0.9 collective-permute-start.7
  695.9 1.2 reshape.164
  697.2 1.3 maximum_maximum_fusion.1
  699.1 31.1 %share_terms.2.refs_0_ = bf16[1280,128]{1,0:T(8,128)(2,1)} custom-call(bf16[32,5,16,128]{3,2,1,0:T(8,128)(2,1)} %bitcast.151, f32[8,128]{1,0:T(8,128)} %broadcast_in_dim.43.label), custom_call_target="tpu_custom_call" | custom-call | tf_op jit(solution)/shard_map/share_terms/pallas_call | solution.py:1223
  730.3 38.0 %gather_blocks.4 = bf16[20480,128]{1,0:T(8,128)(2,1)} custom-call(bf16[1280,128]{1,0:T(8,128)(2,1)} %share_terms.2.refs_0_), custom_call_target="tpu_custom_call" | custom-call | tf_op jit(solution)/shard_map/gather_blocks/pallas_call | solution.py:511
  768.3 26.3 %share_terms.3.refs_0_ = bf16[1280,128]{1,0:T(8,128)(2,1)} custom-call(bf16[32,5,16,128]{3,2,1,0:T(8,128)(2,1)} %bitcast.150, f32[8,128]{1,0:T(8,128)} %broadcast_in_dim.43.label), custom_call_target="tpu_custom_call" | custom-call | tf_op jit(solution)/shard_map/share_terms/pallas_call | solution.py:1223
  794.6 41.0 %gather_blocks.5 = bf16[20480,128]{1,0:T(8,128)(2,1)} custom-call(bf16[1280,128]{1,0:T(8,128)(2,1)} %share_terms.3.refs_0_), custom_call_target="tpu_custom_call" | custom-call | tf_op jit(solution)/shard_map/gather_blocks/pallas_call | solution.py:511
  835.6 12.0 %gradient_tables.1 = (f32[2,8,8,16,1152]{4,3,2,1,0:T(8,128)}, f32[2,2,8,16,1152]{4,3,2,1,0:T(8,128)}, f32[2,2,8,16,4304]{4,3,2,1,0:T(8,128)}) custom-call(bf16[32,8,5,16,128]{4,3,2,1,0:T(8,128)(2,1)} %bitcast.143, bf16[32,8,5,16,128]{4,3,2,1,0:T(8,128)(2,1)} %bitcast.144), custom_call_target="tpu_custom_call" | custom-call | tf_op jit(solution)/shard_map/gradient_tables/pallas_call | solution.py:1273
  847.5 3.5 fusion
  (95 shorter events, 16.1 us)
Async XLA Ops:
  3.2 1.9 copy-start
  3.2 7.5 copy-start.1
  6.3 41.5 %collective-permute-start = (bf16[1600,128]{1,0:T(8,128)(2,1)}, bf16[1600,128]{1,0:T(8,128)(2,1)}, u32[]{:S(2)}, u32[]{:S(2)}) collective-permute-start(bf16[1600,128]{1,0:T(8,128)(2,1)} %get-tuple-element.116), channel_id=1, source_target_pairs={{0,2},{2,4},{4,6},{6,8},{8,10},{10,12},{12,14},{14,16},{16,18},{18... | collective-permute-start | bytes 1228808 | tf_op jit(solution)/shard_map/ppermute | solution.py:120
  9.4 38.4 %collective-permute-start.1 = (bf16[1600,128]{1,0:T(8,128)(2,1)}, bf16[1600,128]{1,0:T(8,128)(2,1)}, u32[]{:S(2)}, u32[]{:S(2)}) collective-permute-start(bf16[1600,128]{1,0:T(8,128)(2,1)} %get-tuple-element.115), channel_id=1, source_target_pairs={{2,0},{4,2},{6,4},{8,6},{10,8},{12,10},{14,12},{16,14},{18,16},{20... | collective-permute-start | bytes 1228808 | tf_op jit(solution)/shard_map/ppermute | solution.py:121
  10.7 14.6 %slice-start = ((s8[4718592]{0:T(1024)(128)(4,1)}), s8[4194304]{0:T(1024)(128)(4,1)S(1)}, s32[]{:S(2)}) async-start(s8[4718592]{0:T(1024)(128)(4,1)} %bitcast.145), calls=%async_computation | async-start | bytes 8388608
  11.8 44.5 %collective-permute-start.2 = (bf16[368,1152]{1,0:T(8,128)(2,1)}, bf16[368,1152]{1,0:T(8,128)(2,1)}, u32[]{:S(2)}, u32[]{:S(2)}) collective-permute-start(bf16[368,1152]{1,0:T(8,128)(2,1)} %get-tuple-element.134), channel_id=1, source_target_pairs={{0,1},{1,0},{2,3},{3,2},{4,5},{5,4},{6,7},{7,6},{8,9},{9,8},{10,11... | collective-permute-start | bytes 2543624 | tf_op jit(solution)/shard_map/ppermute | solution.py:1318
  14.1 37.9 %collective-permute-start.3 = (bf16[1600,128]{1,0:T(8,128)(2,1)}, bf16[1600,128]{1,0:T(8,128)(2,1)}, u32[]{:S(2)}, u32[]{:S(2)}) collective-permute-start(bf16[1600,128]{1,0:T(8,128)(2,1)} %get-tuple-element.114), channel_id=1, source_target_pairs={{0,2},{2,4},{4,6},{6,8},{8,10},{10,12},{12,14},{14,16},{16,18},{18... | collective-permute-start | bytes 1228808 | tf_op jit(solution)/shard_map/ppermute | solution.py:120
  18.2 5.7 copy-start.12
  18.2 7.2 slice-start.1
  18.2 33.8 %collective-permute-start.4 = (bf16[1600,128]{1,0:T(8,128)(2,1)}, bf16[1600,128]{1,0:T(8,128)(2,1)}, u32[]{:S(2)}, u32[]{:S(2)}) collective-permute-start(bf16[1600,128]{1,0:T(8,128)(2,1)} %get-tuple-element.113), channel_id=1, source_target_pairs={{2,0},{4,2},{6,4},{8,6},{10,8},{12,10},{14,12},{16,14},{18,16},{20... | collective-permute-start | bytes 1228808 | tf_op jit(solution)/shard_map/ppermute | solution.py:121
  25.4 1.8 copy-start.13
  46.8 9.5 %copy-start.9 = (f32[736]{0:T(1024)}, f32[736]{0:T(1024)S(1)}, u32[]{:S(2)}) copy-start(f32[736]{0:T(1024)S(1)} %fusion.7) | copy-start | bytes 8836
  349.6 84.9 %collective-permute-start.6 = (bf16[368,1152]{1,0:T(8,128)(2,1)}, bf16[368,1152]{1,0:T(8,128)(2,1)}, u32[]{:S(2)}, u32[]{:S(2)}) collective-permute-start(bf16[368,1152]{1,0:T(8,128)(2,1)} %get-tuple-element.130), channel_id=1, source_target_pairs={{0,1},{1,0},{2,3},{3,2},{4,5},{5,4},{6,7},{7,6},{8,9},{9,8},{10,11... | collective-permute-start | bytes 2543624 | tf_op jit(solution)/shard_map/ppermute | solution.py:1318
  440.1 126.0 %collective-permute-start.5 = (bf16[368,1152]{1,0:T(8,128)(2,1)S(1)}, bf16[368,1152]{1,0:T(8,128)(2,1)}, u32[]{:S(2)}, u32[]{:S(2)}) collective-permute-start(bf16[368,1152]{1,0:T(8,128)(2,1)S(1)} %get-tuple-element.132), channel_id=1, source_target_pairs={{0,1},{1,0},{2,3},{3,2},{4,5},{5,4},{6,7},{7,6},{8,9},{9,8},{10,11... | collective-permute-start | bytes 2543624 | tf_op jit(solution)/shard_map/ppermute | solution.py:1332
  543.0 22.6 %copy-start.6 = (f32[48,1152]{1,0:T(8,128)S(1)}, f32[48,1152]{1,0:T(8,128)}, u32[]{:S(2)}) copy-start(f32[48,1152]{1,0:T(8,128)} %get-tuple-element.103) | copy-start | bytes 663556
  543.0 22.7 %copy-start.8 = (f32[16,1152]{1,0:T(8,128)S(1)}, f32[16,1152]{1,0:T(8,128)}, u32[]{:S(2)}) copy-start(f32[16,1152]{1,0:T(8,128)} %get-tuple-element.104) | copy-start | bytes 221188
  669.3 21.5 %copy-start.10 = (f32[736]{0:T(1024)S(1)}, f32[736]{0:T(1024)}, u32[]{:S(2)}) copy-start(f32[736]{0:T(1024)} %copy-done.9) | copy-start | bytes 8836
  693.1 1.1 copy-start.4
  693.1 1.1 copy-start.5
  693.1 1.9 copy-start.3
  693.2 2.0 copy-start.7
  693.2 154.3 %collective-permute-start.7 = (bf16[368,1152]{1,0:T(8,128)(2,1)S(1)}, bf16[368,1152]{1,0:T(8,128)(2,1)}, u32[]{:S(2)}, u32[]{:S(2)}) collective-permute-start(bf16[368,1152]{1,0:T(8,128)(2,1)S(1)} %get-tuple-element.128), channel_id=1, source_target_pairs={{0,1},{1,0},{2,3},{3,2},{4,5},{5,4},{6,7},{7,6},{8,9},{9,8},{10,11... | collective-permute-start | bytes 2543624 | tf_op jit(solution)/shard_map/ppermute | solution.py:1332
  694.2 3.0 copy-start.11
  694.3 0.7 copy-start.2

commit v6 on v5

--- a/solution.py
+++ b/solution.py
@@ -288,14 +288,23 @@
     )(*operands)
 
 
+LARGE_BLOCK = 4096
+
+
 def gather_plan(
     src, out, stage, local_sem, z_recv, y_recv, b_recv, h_recv, c_recv_own, c_recv_z, c_recv_y, c_recv_b, c_recv_h,
     up_send, down_send, y_send, b_send, h_send, c_send_own, c_send_z, c_send_y, c_send_b, c_send_h,
 ):
     rows = src.shape[0]
-    unit = rows // 6 // 16 * 16 + 16
-    sizes = [unit, unit, rows // 2 - 2 * unit, rows // 2 - 2 * unit, unit]
-    begins = [0, unit, 2 * unit, rows // 2, rows - 2 * unit]
+    if rows >= LARGE_BLOCK:
+        unit = rows // 6 // 16 * 16 + 16
+        sizes = [unit, unit, rows // 2 - 2 * unit, rows // 2 - 2 * unit, unit]
+        begins = [0, unit, 2 * unit, rows // 2, rows - 2 * unit]
+    else:
+        sizes = [rows // 2] * 2
+        begins = [0, rows // 2]
+    chunks, across_y = len(sizes), (len(sizes) + 1) // 2
+    lend = chunks == 5
     x = lax.axis_index("seq")
     f = lax.axis_index("fsdp")
     z, y, c = f // 4, (f // 2) % 2, f % 2
@@ -334,7 +343,7 @@
     whole = (pl.multiple_of(f * rows, 16), rows)
     keep = pltpu.make_async_copy(src if stage is None else stage, view(whole), local_sem.at[0])
 
-    def start():
+    def greet():
         barrier = pltpu.get_barrier_semaphore()
         for to in (beside, across, mate):
             pl.semaphore_signal(barrier, inc=1, device_id=to, device_id_type=MESH)
@@ -349,7 +358,10 @@
 
         pl.semaphore_wait(barrier, 3 + jnp.where(z < 3, 1, 0) + jnp.where(z > 0, 1, 0))
 
-        for j in range(5):
+    def start(first=True):
+        if first:
+            greet()
+        for j in range(chunks):
             spot = place(z, y, j, x)
 
             @pl.when(z < 3)
@@ -360,7 +372,7 @@
             def _():
                 copy(spot, down_send.at[z, j], z_recv.at[z, j], down, own(j)).start()
 
-            if j < 3:
+            if j < across_y:
                 copy(spot, y_send.at[z, j], y_recv.at[z, j], beside, own(j)).start()
         copy(whole, c_send_own.at[0], c_recv_own.at[0], mate, src).start()
         if stage is None:
@@ -380,9 +392,9 @@
             def _():
                 copy(spot, sends.at[zb, j], z_recv.at[zb, j], to).start()
 
-            if j == 0:
+            if j == 0 and lend:
                 copy(spot, b_send.at[zb], b_recv.at[zb], across).start()
-            if j < 3:
+            if j < across_y:
                 copy(spot, y_send.at[zb, j], y_recv.at[zb, j], beside).start()
             copy(spot, c_send_z.at[zb, j], c_recv_z.at[zb, j], mate).start()
 
@@ -434,13 +446,13 @@
 
     events = []
     for d in range(4):
-        for j in range(5):
-            at = (d - 1) * 5 + j + 1 if d else 0
+        for j in range(chunks):
+            at = (d - 1) * chunks + j + 1 if d else 0
             if d:
                 events.append((at, functools.partial(z_event, d, j)))
-                if j == 0:
+                if j == 0 and lend:
                     events.append((at + 2, functools.partial(b_event, d)))
-            if j < 3:
+            if j < across_y:
                 ready = at + 1.5 if d else j + 1
                 events.append((ready, functools.partial(y_event, d, j)))
                 events.append((ready + 2, functools.partial(h_event, d, j)))
@@ -455,11 +467,11 @@
         copy(whole, c_send_own.at[0], c_recv_own.at[0], mate).wait_send()
         for d in range(4):
             def drain(zb, d=d):
-                for j in range(5):
+                for j in range(chunks):
                     if d:
                         arrived(core_spot(zb, y, j, x), c_recv_z.at[zb, j])
                         copy(place(zb, y, j, x), c_send_z.at[zb, j], c_recv_z.at[zb, j], mate).wait_send()
-                    if j < 3:
+                    if j < across_y:
                         arrived(core_spot(zb, 1 - y, j, x), c_recv_y.at[zb, j])
                         arrived(core_spot(zb, 1 - y, j, 1 - x), c_recv_h.at[zb, j])
                         spot = place(zb, 1 - y, j, x)
@@ -469,7 +481,7 @@
                         copy(spot, c_send_h.at[zb, j], c_recv_h.at[zb, j], mate).wait_send()
                         spot = place(zb, y, j, x)
                         copy(spot, y_send.at[zb, j], y_recv.at[zb, j], beside).wait_send()
-                if d:
+                if d and lend:
                     arrived(core_spot(zb, y, 0, 1 - x), c_recv_b.at[zb])
                     spot = place(zb, y, 0, 1 - x)
                     copy(spot, c_send_b.at[zb], c_recv_b.at[zb], mate).wait_send()
@@ -477,7 +489,7 @@
                     copy(spot, b_send.at[zb], b_recv.at[zb], across).wait_send()
 
             each(d, drain)
-            for j in range(5):
+            for j in range(chunks):
                 @pl.when(jnp.logical_and(z - d >= 0, z < 3))
                 def _():
                     zb = z - d
@@ -902,22 +914,25 @@
     )(d_qkv, w_qkv, attn[0:3].reshape(3 * R, D), attn[4:7], normed, inner, hidden, d_middle, vectors)
 
 
-FORWARD_STEPS = (3, H, WIDE // TILE, 3)
+PAIR = 2 * LANES
+PAIRS = -(-D // PAIR)
+FORWARD_STEPS = (3, H, WIDE // TILE, PAIRS)
 FORWARD_AT = (0, 3, 3 + H, 3 + H + WIDE // TILE)
 FORWARD_BEGINS = (
     [4.5 * i for i in range(3)]
     + [14 + 2 * i for i in range(H)]
     + [46 + (5 if i else 0) + 2.6 * i for i in range(WIDE // TILE)]
-    + [76 + 5 * i for i in range(3)]
+    + [73 + 3 * i for i in range(PAIRS)]
 )
 CHUNK_TIME = 7.0
 
 
 def forward_kernel(with_gather, *refs):
     (
-        marks, hidden, w_qkv, vec, down, up, w_o, down_o, up_o, down_1, w_1, b_1, up_1, w_2, b_2, down_2, up_2,
-    ) = refs[:17]
-    refs = refs[17:]
+        bias_lane, hidden, w_qkv, vec, down, up, w_o, down_o, up_o, down_1, w_1, b_1, up_1, w_2, w_2_odd, b_2,
+        down_2, up_2,
+    ) = refs[:18]
+    refs = refs[18:]
     if with_gather:
         shard, refs = refs[0], refs[1:]
     (
@@ -931,7 +946,7 @@
     i = pl.program_id(0)
     rows = hidden.shape[0]
     _, att_at, up_at, down_at = FORWARD_AT
-    last = down_at + 2
+    last = down_at + PAIRS - 1
 
     def at_step(k):
         return pl.when(i == k)
@@ -967,7 +982,7 @@
         bias = vec[pl.ds(jnp.where(i == 2, 5, 4), 1), :] * jnp.where(i == 1, 0.0, 1.0)
         value = (dot_both(normed[...], matrix(w_qkv), parts[i], up[0]) + bias).astype(BF16)
         qkv[...] = value
-        mark = marks[0]
+        mark = jnp.where(i == 0, first_lane(rows, F32(1.0)), jnp.where(i == 1, bias_lane[...], jnp.zeros_like(bias_lane[...])))
         for h in range(H):
             heads[i, h] = pad_lanes(value[:, h * HD : (h + 1) * HD], mark)
 
@@ -1008,12 +1023,19 @@
     def _():
         @at_step(down_at)
         def _():
-            inner_down[...] = dot_t(activated[...], down_2[...]).astype(BF16)
-
-        at = pl.ds(pl.multiple_of((i - down_at) * THIRD, LANES), THIRD)
-        next_hidden[...] = middle[:, at] + (
-            dot(activated[:, :FF], matrix(w_2.at[: UNITS[3]])) + b_2[...] + dot(inner_down[...], up_2[...])
-        )
+            w = jnp.concatenate([matrix(w_2.at[: UNITS[3]]), down_2[...].T[:FF]], axis=1)
+            value = dot(activated[:, :FF], w)
+            narrow = value[:, LANES : LANES + R].astype(BF16)
+            inner_down[...] = narrow
+            value = value[:, :LANES] + b_2[:, :LANES] + dot(narrow, up_2[:, :LANES])
+            next_hidden[:, :LANES] = middle[:, D - LANES :] + value
+
+        @pl.when(i > down_at)
+        def _():
+            at = pl.ds(pl.multiple_of((i - down_at - 1) * PAIR, LANES), PAIR)
+            w = jnp.concatenate([matrix(w.at[: UNITS[3]]) for w in (w_2, w_2_odd)], axis=1)
+            value = dot(activated[:, :FF], w) + b_2[...] + dot(inner_down[...], up_2[...])
+            next_hidden[...] = middle[:, at] + value
 
     if with_gather:
 
@@ -1024,7 +1046,8 @@
             finish()
 
 
-def layer_forward(length, hidden, w_qkv, w_o, w_1, w_2, vectors, b_1, attn, narrow, wide, shard=None):
+def layer_forward(bias, hidden, weights, b_1, shard=None):
+    w_qkv, w_o, w_1, w_2, vectors, attn, narrow, wide, _ = weights
     rows = hidden.shape[0]
     _, att_at, up_at, down_at = FORWARD_AT
 
@@ -1034,16 +1057,18 @@
     def cols(count, width, k):
         return pl.BlockSpec((count, width), lambda i: (0, step(i, k)))
 
-    lane = lax.broadcasted_iota(jnp.int32, (rows, LANES - HD), 1)
-    key = lax.broadcasted_iota(jnp.int32, (rows, LANES - HD), 0)
-    marks = jnp.stack([jnp.ones_like(lane, F32), jnp.where(key < length[0], 0.0, NEG), jnp.zeros_like(lane, F32)])
-    marks = jnp.where(lane == 0, marks, 0.0).astype(BF16)
+    def pair(i):
+        return jnp.where(step(i, 3) == 0, PAIRS - 1, step(i, 3) - 1)
+
+    def pairs(count):
+        return pl.BlockSpec((count, PAIR), lambda i: (0, pair(i)))
+
     operands = [
-        marks, hidden, w_qkv, vectors, attn[0:3].reshape(3 * R, D), attn[4:7], w_o, attn[3], attn[7], narrow[0],
-        w_1, b_1, wide[0], w_2, vectors[7:8], wide[1], narrow[1],
+        bias, hidden, w_qkv, vectors, attn[0:3].reshape(3 * R, D), attn[4:7], w_o, attn[3], attn[7], narrow[0],
+        w_1, b_1, wide[0], w_2, w_2, vectors[7:8], wide[1], narrow[1],
     ]
     in_specs = [
-        pl.BlockSpec((1, rows, LANES - HD), lambda i: (step(i, 0), 0, 0)),
+        whole((rows, LANES - HD)),
         whole((rows, D)),
         unit_block(72, 9, lambda i: (0, step(i, 0), 0, 0)),
         whole((8, D)),
@@ -1056,10 +1081,11 @@
         unit_block(72, 4, lambda i: (1, step(i, 2), 0, 0)),
         cols(1, TILE, 2),
         cols(R, TILE, 2),
-        unit_block(288, 3, lambda i: (2, step(i, 3), 0, 0)),
-        cols(1, THIRD, 3),
+        unit_block(288, 1, lambda i: (2, 2 * pair(i), 0, 0)),
+        unit_block(288, 1, lambda i: (2, jnp.minimum(2 * pair(i) + 1, 8), 0, 0)),
+        pairs(1),
         whole((R, WIDE)),
-        cols(R, THIRD, 3),
+        pairs(R),
     ]
     outs = [
         (whole((rows, D)), struct((rows, D), BF16)),
@@ -1073,7 +1099,7 @@
         (whole((rows, R)), struct((rows, R), BF16)),
         (cols(rows, TILE, 2), struct((rows, WIDE), BF16)),
         (whole((rows, R)), struct((rows, R), BF16)),
-        (cols(rows, THIRD, 3), struct((rows, D), F32)),
+        (pairs(rows), struct((rows, D), F32)),
     ]
     scratch = [
         pltpu.VMEM((3, H, rows, LANES), BF16),
@@ -1110,25 +1136,17 @@
 SHARE_ROWS = SHARE * 16
 
 
-def share_kernel(
-    adapters, terms, label, out, held, labels, totals, sums, local_sem, send, recv, label_send, label_recv, pair_sem
+def share_plan(
+    adapters, named, terms, names, out, held, totals, sums, local_sem, send, recv, pair_sem
 ):
     x = lax.axis_index("seq")
     f = lax.axis_index("fsdp")
     count = terms.shape[0]
     me = f * 2 + x
-    barrier = pltpu.get_barrier_semaphore()
+    rows = adapters * SHARE_ROWS
 
     def device(k):
         return (k // 2, k % 2)
-
-    def greet(k, carry):
-        to = (me + k) % count
-        pl.semaphore_signal(barrier, inc=1, device_id=device(to), device_id_type=MESH)
-        return carry
-
-    lax.fori_loop(1, count, greet, 0)
-    pl.semaphore_wait(barrier, count - 1)
 
     def share_to(to, slot):
         return pltpu.make_async_remote_copy(
@@ -1140,108 +1158,114 @@
             device_id_type=MESH,
         )
 
-    def label_to(to, slot):
+    def own():
+        return pltpu.make_async_copy(terms.at[me], held.at[me], local_sem.at[0])
+
+    def across(side):
+        part = out.at[pl.ds(pl.multiple_of(side * rows, 16), rows), :]
         return pltpu.make_async_remote_copy(
-            src_ref=label,
-            dst_ref=labels.at[slot],
-            send_sem=label_send.at[to],
-            recv_sem=label_recv.at[slot],
-            device_id=device(to),
+            src_ref=part,
+            dst_ref=part,
+            send_sem=pair_sem.at[0],
+            recv_sem=pair_sem.at[1],
+            device_id=(f, 1 - x),
             device_id_type=MESH,
         )
 
-    def post(k, carry):
-        to = (me + k) % count
-        label_to(to, me).start()
-        share_to(to, me).start()
-        return carry
-
-    lax.fori_loop(1, count, post, 0)
-    mine = pltpu.make_async_copy(terms.at[me], held.at[me], local_sem.at[0])
-    named = pltpu.make_async_copy(label, labels.at[me], local_sem.at[1])
-    mine.start()
-    named.start()
-    totals[...] = jnp.zeros_like(totals)
-
-    def add(slot):
-        value = held[slot].reshape(SHARE_ROWS, LANES).astype(F32)
-        name = labels[slot][0:1]
-        for e in range(adapters):
-            totals[e] += jnp.where(name == float(e), value, 0.0)
-
-    mine.wait()
-    named.wait()
-    add(me)
-
-    def take(k, carry):
-        slot = (me + count - k) % count
-        label_to(slot, slot).wait_recv()
-        share_to(slot, slot).wait_recv()
-        add(slot)
-        return carry
-
-    lax.fori_loop(1, count, take, 0)
-    sums[...] = totals[...].reshape(adapters * SHARE_ROWS, LANES).astype(BF16)
+    def start():
+        barrier = pltpu.get_barrier_semaphore()
+
+        def greet(k, carry):
+            to = (me + k) % count
+            pl.semaphore_signal(barrier, inc=1, device_id=device(to), device_id_type=MESH)
+            return carry
+
+        lax.fori_loop(1, count, greet, 0)
+        pl.semaphore_wait(barrier, count - 1)
+
+        def post(k, carry):
+            to = (me + k) % count
+            share_to(to, me).start()
+            return carry
+
+        lax.fori_loop(1, count, post, 0)
+        own().start()
+
+    def add_up():
+        totals[...] = jnp.zeros_like(totals)
+
+        def add(slot):
+            value = held[slot, :SHARE].reshape(SHARE_ROWS, LANES).astype(F32)
+            if named:
+                name = names[pl.ds(slot, 1), :]
+            else:
+                name = held[slot, SHARE].astype(F32)[0:1]
+                names[pl.ds(slot, 1), :] = name
+            for e in range(adapters):
+                totals[e] += jnp.where(name == float(e), value, 0.0)
+
+        own().wait()
+        add(me)
+
+        def take(k, carry):
+            slot = (me + count - k) % count
+            share_to(slot, slot).wait_recv()
+            add(slot)
+            return carry
+
+        lax.fori_loop(1, count, take, 0)
+        sums[...] = totals[...].reshape(rows, LANES).astype(BF16)
+        part = out.at[pl.ds(pl.multiple_of(x * rows, 16), rows), :]
+        keep = pltpu.make_async_copy(sums, part, local_sem.at[0])
+        keep.start()
+        keep.wait()
+        across(x).start()
+
+    def finish():
+        def sent(k, carry):
+            to = (me + k) % count
+            share_to(to, me).wait_send()
+            return carry
+
+        lax.fori_loop(1, count, sent, 0)
+        across(x).wait_send()
+        across(1 - x).wait_recv()
+
+    return start, add_up, finish
+
+
+def share_kernel(adapters, *refs):
+    for part in share_plan(adapters, True, *refs):
+        part()
+
+
+def share_scratch(count, adapters, tiles):
+    dma = pltpu.SemaphoreType.DMA
     rows = adapters * SHARE_ROWS
-    part = out.at[pl.ds(pl.multiple_of(x * rows, 16), rows), :]
-    keep = pltpu.make_async_copy(sums, part, local_sem.at[0])
-    keep.start()
-    keep.wait()
-    across = pltpu.make_async_remote_copy(
-        src_ref=part,
-        dst_ref=part,
-        send_sem=pair_sem.at[0],
-        recv_sem=pair_sem.at[1],
-        device_id=(f, 1 - x),
-        device_id_type=MESH,
-    )
-    across.start()
-
-    def sent(k, carry):
-        to = (me + k) % count
-        label_to(to, me).wait_send()
-        share_to(to, me).wait_send()
-        return carry
-
-    lax.fori_loop(1, count, sent, 0)
-    across.wait_send()
-    other = out.at[pl.ds(pl.multiple_of((1 - x) * rows, 16), rows), :]
-    pltpu.make_async_remote_copy(
-        src_ref=other,
-        dst_ref=other,
-        send_sem=pair_sem.at[0],
-        recv_sem=pair_sem.at[1],
-        device_id=(f, 1 - x),
-        device_id_type=MESH,
-    ).wait_recv()
-
-
-def share_terms(terms, label, adapters):
-    count = terms.shape[0]
-    dma = pltpu.SemaphoreType.DMA
+    return [
+        pltpu.VMEM((count, tiles, 16, LANES), BF16),
+        pltpu.VMEM((adapters, SHARE_ROWS, LANES), F32),
+        pltpu.VMEM((rows, LANES), BF16),
+        dma((1,)),
+        dma((count,)),
+        dma((count,)),
+        dma((2,)),
+    ]
+
+
+def share_terms(terms, names, adapters):
     rows = adapters * SHARE_ROWS
     return pl.pallas_call(
         functools.partial(share_kernel, adapters),
-        in_specs=[pl.BlockSpec(memory_space=pl.ANY)] * 2,
+        in_specs=[pl.BlockSpec(memory_space=pl.ANY), pl.BlockSpec(memory_space=pltpu.VMEM)],
         out_specs=pl.BlockSpec(memory_space=pl.ANY),
         out_shape=jax.ShapeDtypeStruct((2 * rows, LANES), BF16),
-        scratch_shapes=[
-            pltpu.VMEM((count, SHARE, 16, LANES), BF16),
-            pltpu.VMEM((count, 8, LANES), F32),
-            pltpu.VMEM((adapters, SHARE_ROWS, LANES), F32),
-            pltpu.VMEM((rows, LANES), BF16),
-            dma((2,)),
-            dma((count,)),
-            dma((count,)),
-            dma((count,)),
-            dma((count,)),
-            dma((2,)),
-        ],
+        scratch_shapes=share_scratch(terms.shape[0], adapters, SHARE),
         compiler_params=pltpu.CompilerParams(
             collective_id=1, has_side_effects=True, vmem_limit_bytes=VMEM_LIMIT
         ),
         name="share_terms",
-    )(terms, label)
+    )(terms, names)
 
 
 def table_kernel(layers, *refs):
@@ -1283,6 +1307,300 @@
         compiler_params=pltpu.CompilerParams(vmem_limit_bytes=VMEM_LIMIT),
         name="gradient_tables",
     )(*gathered)
+
+
+BACKWARD_STEPS = (WIDE // TILE, PAIRS, 1, H, PAIRS)
+BACKWARD_AT = (0, 9, 14, 15, 31)
+SHARE_AT, PASS_AT, GATHER_AT = 7, 9, 10
+
+
+def backward_kernel(adapters, *refs):
+    (
+        gradient, w_2, gate, down_2, up_2, inner_down, inner_up, w_1, w_1_odd, up_1, down_1, normed_two_in, vec, w_o, down_o,
+        up_o, inner_o, attended, bias, stats, w_qkv, w_qkv_odd, up, down, inner_qkv, middle_in, qkv_in, hidden_in, normed_in,
+    ) = refs[:29]
+    refs = refs[29:]
+    if adapters:
+        terms, half, refs = refs[0], refs[1], refs[2:]
+    new_gradient, g_wide, g_up_2, g_middle, g_input = refs[:5]
+    refs = refs[5:]
+    if adapters:
+        pair, gathered, other_half, names, refs = refs[0], refs[1], refs[2], refs[3], refs[4:]
+    (
+        d_branch, d_inner_down, d_inner_up, wide, residual, d_normed, heads, stat_t, delta_t, load_sem,
+    ) = refs[:10]
+    refs = refs[10:]
+    i = pl.program_id(0)
+    _, middle_at, turn_at, att_at, input_at = BACKWARD_AT
+    last = input_at + PAIRS - 1
+
+    def at_step(k):
+        return pl.when(i == k)
+
+    def load_middle():
+        return pltpu.make_async_copy(middle_in, residual, load_sem.at[0])
+
+    def load_qkv():
+        return pltpu.make_async_copy(qkv_in, wide.at[:, : 3 * D], load_sem.at[1])
+
+    def load_hidden():
+        return pltpu.make_async_copy(hidden_in, residual, load_sem.at[0])
+
+    def load_normed_two():
+        return pltpu.make_async_copy(normed_two_in, d_branch, load_sem.at[2])
+
+    def load_normed():
+        return pltpu.make_async_copy(normed_in, d_branch, load_sem.at[2])
+
+    if adapters:
+        share_start, share_sum, share_finish = share_plan(
+            adapters, False, terms, names, pair, *refs[:7]
+        )
+        swap_sem = refs[7]
+        start, events, finish = gather_plan(pair, gathered, None, *refs[8:])
+        swap = pltpu.make_async_remote_copy(
+            src_ref=half,
+            dst_ref=other_half,
+            send_sem=swap_sem.at[0],
+            recv_sem=swap_sem.at[1],
+            device_id=(lax.axis_index("fsdp"), 1 - lax.axis_index("seq")),
+            device_id_type=MESH,
+        )
+        at_step(0)(share_start)
+        at_step(GATHER_AT + 12)(swap.start)
+        at_step(SHARE_AT)(share_sum)
+        at_step(PASS_AT)(share_finish)
+
+        @at_step(GATHER_AT)
+        def _():
+            start(False)
+
+        steps = {}
+        for when, event in events:
+            steps.setdefault(min(GATHER_AT + 1 + int(when), last), []).append(event)
+        for k, due in steps.items():
+
+            @at_step(k)
+            def _(due=due):
+                for event in due:
+                    event()
+
+    @pl.when(i < middle_at)
+    def _():
+        @at_step(0)
+        def _():
+            load_middle().start()
+            value = gradient[...].astype(BF16)
+            d_branch[...] = value
+            d_inner_down[...] = dot_t(value, up_2[...]).astype(BF16)
+            g_up_2[...] = dot_l(inner_down[...], value)
+
+        left = FF - i * TILE
+        d_act = dot_both_t(d_branch[...], matrix(w_2), d_inner_down[...], down_2[...].T)
+        x = gate[...].astype(F32)
+        t = gelu_parts(x)
+        half = 0.5 * (1.0 + t)
+        slope = half + 0.5 * x * (1.0 - t * t) * (
+            0.7978845608028654 * (1.0 + 3 * 0.044715 * x * x)
+        )
+        keep = lax.broadcasted_iota(jnp.int32, (1, TILE), 1) < left
+        value = jnp.where(keep, slope * d_act, 0.0).astype(BF16)
+        wide[:, pl.ds(pl.multiple_of(i * TILE, LANES), TILE)] = value
+        g_wide[0:R] = dot_l(inner_up[...], value)
+        g_wide[R : 2 * R] = dot_l(d_inner_down[...], (x * half).astype(BF16))
+
+    @pl.when(jnp.logical_and(i >= middle_at, i < turn_at))
+    def _():
+        at_step(middle_at)(load_normed_two().start)
+
+        @pl.when(i < turn_at - 1)
+        def _():
+            w = jnp.concatenate([matrix(w_1, 34), matrix(w_1_odd, 34)], axis=0)
+            d_normed[i - middle_at] = dot_t(wide[:, : 34 * LANES], w)
+
+        @at_step(turn_at - 1)
+        def _():
+            w = jnp.concatenate([matrix(w_1, 34), up_1[:, : 34 * LANES]], axis=0)
+            value = dot_t(wide[:, : 34 * LANES], w)
+            d_normed[PAIRS - 1, :, :LANES] = value[:, :LANES]
+            d_inner_up[...] = value[:, LANES : LANES + R].astype(BF16)
+
+    def joined():
+        parts = [d_normed[k] for k in range(PAIRS - 1)]
+        return jnp.concatenate(parts + [d_normed[PAIRS - 1, :, :LANES]], axis=1)
+
+    @at_step(turn_at)
+    def _():
+        load_qkv().start()
+        load_middle().wait()
+        d_two = joined() + dot(d_inner_up[...], down_1[...])
+        value = gradient[...] + layer_norm_back(d_two, residual[...], vec[2:3])
+        load_hidden().start()
+        new_gradient[...] = value
+        d_out = value.astype(BF16)
+        d_inner_o = dot_t(d_out, up_o[...]).astype(BF16)
+        wide[:, 3 * D :] = (dot_t(d_out, matrix(w_o)) + dot(d_inner_o, down_o[...])).astype(BF16)
+        g_middle[0:R] = dot_l(d_inner_o, attended[...])
+        g_middle[R : 2 * R] = dot_l(inner_o[...], d_out)
+        load_normed_two().wait()
+        g_middle[2 * R : 3 * R] = dot_l(d_inner_up[...], d_branch[...])
+        load_normed().start()
+        load_qkv().wait()
+        rows = gradient.shape[0]
+        lane = lax.broadcasted_iota(jnp.int32, (rows, LANES), 1)
+        delta = jnp.zeros((rows, LANES), F32)
+        marked = (first_lane(rows, F32(1.0)), bias[...], None)
+        for h in range(H):
+            for c in range(3):
+                part = wide[:, c * D + h * HD : c * D + (h + 1) * HD]
+                heads[c, h] = pad_lanes(part, marked[c])
+            do = wide[:, 3 * D + h * HD : 3 * D + (h + 1) * HD]
+            heads[3, h] = pad_lanes(do)
+            o = attended[:, h * HD : (h + 1) * HD].astype(F32)
+            d = jnp.sum(do.astype(F32) * o, axis=1, keepdims=True)
+            delta = jnp.where(lane == h, d, delta)
+        stat_t[...] = stats[...].T
+        delta_t[...] = delta.T
+
+    @pl.when(jnp.logical_and(i >= att_at, i < input_at))
+    def _():
+        h = i - att_at
+        q, k, do = heads[0, h], heads[1, h], heads[3, h]
+        p = jnp.exp2(dot_t(k, q) * C2 - stat_t[pl.ds(h, 1), :])
+        dv = dot(p.astype(BF16), do)
+        dp = dot_t(heads[2, h], do)
+        ds = (p * (dp - delta_t[pl.ds(h, 1), :])).astype(BF16)
+        dk = dot(ds, q)
+        dq = dot(k.T, ds)
+        heads[2, h] = dv.astype(BF16)
+        heads[1, h] = (dk * SCALE).astype(BF16)
+        heads[0, h] = (dq * SCALE).astype(BF16).T
+
+    @pl.when(i >= input_at)
+    def _():
+        @at_step(input_at)
+        def _():
+            load_normed().wait()
+            for c in range(3):
+                for h in range(H):
+                    wide[:, c * D + h * HD : c * D + (h + 1) * HD] = heads[c, h][:, :HD]
+            for c in range(3):
+                part = wide[:, c * D : (c + 1) * D]
+                g_input[(3 + c) * R : (4 + c) * R] = dot_l(inner_qkv[:, c * R : (c + 1) * R], part)
+
+        @pl.when(i < last)
+        def _():
+            w = jnp.concatenate([matrix(w_qkv), matrix(w_qkv_odd)], axis=0)
+            d_normed[i - input_at] = dot_t(wide[:, : 3 * D], w)
+
+        @at_step(last)
+        def _():
+            w = jnp.concatenate([matrix(w_qkv), up[...]], axis=0)
+            value = dot_t(wide[:, : 3 * D], w)
+            d_normed[PAIRS - 1, :, :LANES] = value[:, :LANES]
+            narrow = value[:, LANES : LANES + 3 * R].astype(BF16)
+            g_input[0 : 3 * R] = dot_l(narrow, d_branch[...])
+            load_hidden().wait()
+            d_one = joined() + dot(narrow, down[...])
+            new_gradient[...] += layer_norm_back(d_one, residual[...], vec[0:1])
+
+    if adapters:
+
+        @at_step(last)
+        def _():
+            finish()
+            swap.wait()
+
+
+def layer_backward(
+    gradient, saved, weights, bias, adapters=0, terms=None, half=None
+):
+    hidden, normed, inner_qkv, qkv, stats, attended, inner_o, middle, normed_two, inner_up, gate, inner_down = saved
+    w_qkv, w_o, w_1, w_2, vectors, attn, narrow, wide, up_diagonal = weights
+    rows = gradient.shape[0]
+
+    def step(i, k):
+        return jnp.minimum(jnp.maximum(i - BACKWARD_AT[k], 0), BACKWARD_STEPS[k] - 1)
+
+    def cols(count, width, k):
+        return pl.BlockSpec((count, width), lambda i: (0, step(i, k)))
+
+    hbm = pl.BlockSpec(memory_space=pl.ANY)
+    operands = [
+        (whole((rows, D)), gradient),
+        (unit_block(TILE // 16, 9, lambda i: (TILES_AT[3] // 9 * 16 // TILE + step(i, 0), 0, 0, 0)), w_2),
+        (cols(rows, TILE, 0), gate),
+        (cols(R, TILE, 0), wide[1]),
+        (whole((R, D)), narrow[1]),
+        (whole((rows, R)), inner_down),
+        (whole((rows, R)), inner_up),
+        (unit_block(8, PANELS[2], lambda i: (9 + 2 * step(i, 1), 0, 0, 0)), w_1),
+        (unit_block(8, PANELS[2], lambda i: (10 + jnp.minimum(2 * step(i, 1), 7), 0, 0, 0)), w_1),
+        (whole((R, WIDE)), wide[0]),
+        (whole((R, D)), narrow[0]),
+        (hbm, normed_two),
+        (whole((8, D)), vectors),
+        (OUT_BLOCK, w_o),
+        (whole((R, D)), attn[3]),
+        (whole((R, D)), attn[7]),
+        (whole((rows, R)), inner_o),
+        (whole((rows, D)), attended),
+        (whole((rows, LANES - HD)), bias),
+        (whole((rows, LANES)), stats),
+        (unit_block(8, 27, lambda i: (2 * step(i, 4), 0, 0, 0)), w_qkv),
+        (unit_block(8, 27, lambda i: (jnp.minimum(2 * step(i, 4) + 1, 8), 0, 0, 0)), w_qkv),
+        (whole((3 * R, 3 * D)), up_diagonal),
+        (whole((3 * R, D)), attn[0:3].reshape(3 * R, D)),
+        (whole((rows, 3 * R)), inner_qkv),
+        (hbm, middle),
+        (hbm, qkv),
+        (hbm, hidden),
+        (hbm, normed),
+    ]
+    outs = [
+        (whole((rows, D)), struct((rows, D), F32)),
+        (cols(2 * R, TILE, 0), struct((2 * R, WIDE), F32)),
+        (whole((R, D)), struct((R, D), F32)),
+        (whole((3 * R, D)), struct((3 * R, D), F32)),
+        (whole((6 * R, D)), struct((6 * R, D), F32)),
+    ]
+    scratch = [
+        pltpu.VMEM((rows, D), BF16),
+        pltpu.VMEM((rows, R), BF16),
+        pltpu.VMEM((rows, R), BF16),
+        pltpu.VMEM((rows, WIDE), BF16),
+        pltpu.VMEM((rows, D), F32),
+        pltpu.VMEM((PAIRS, rows, PAIR), F32),
+        pltpu.VMEM((4, H, rows, LANES), BF16),
+        pltpu.VMEM((LANES, rows), F32),
+        pltpu.VMEM((LANES, rows), F32),
+        pltpu.SemaphoreType.DMA((3,)),
+    ]
+    params = dict(vmem_limit_bytes=VMEM_MOST)
+    if adapters:
+        operands += [(hbm, terms), (hbm, half)]
+        block = 2 * adapters * SHARE_ROWS
+        outs += [(hbm, struct((block, LANES), BF16)), (hbm, struct((16 * block, LANES), BF16))]
+        outs += [(hbm, struct(half.shape, BF16))]
+        outs += [(whole((terms.shape[0], LANES)), struct((terms.shape[0], LANES), F32))]
+        scratch += share_scratch(terms.shape[0], adapters, SHARE + 1) + [pltpu.SemaphoreType.DMA((2,))]
+        scratch += gather_semaphores()
+        params.update(collective_id=4, has_side_effects=True)
+    return pl.pallas_call(
+        functools.partial(backward_kernel, adapters),
+        grid=(sum(BACKWARD_STEPS),),
+        in_specs=[spec for spec, _ in operands],
+        out_specs=[spec for spec, _ in outs],
+        out_shape=[shape for _, shape in outs],
+        scratch_shapes=scratch,
+        cost_estimate=pl.CostEstimate(
+            flops=2 * rows * D * (4 * D + 2 * FF) + 20 * rows * rows * D,
+            bytes_accessed=2 * D * (4 * D + 2 * FF) + 40 * rows * D,
+            transcendentals=H * rows * rows,
+        ),
+        compiler_params=pltpu.CompilerParams(**params),
+        name="layer_backward_share" if adapters else "layer_backward",
+    )(*[operand for _, operand in operands])
 
 
 def local(
@@ -1305,7 +1623,7 @@
     layer_count = frozen.shape[0]
     adapters = attention_adapter_weights.shape[2]
     parts = seq_parts // slots
-    on_block = (fsdp_parts, seq_parts, slots) == (16, 2, 2)
+    on_block = (fsdp_parts, seq_parts, slots, layer_count) == (16, 2, 2, 2)
     slot = me // parts
     part = me % parts
     tokens = seq_total // parts
@@ -1325,11 +1643,14 @@
         whole = lax.dynamic_index_in_dim(whole, slot, 0, keepdims=False)
         return lax.dynamic_slice_in_dim(whole, part * tokens, tokens, 0)
 
-    def to_tokens(v):
+    def half_of(v, which):
+        return lax.dynamic_slice_in_dim(v, which * local_len, local_len, 0)
+
+    def to_tokens(v, other=None):
         if parts == 1 and slots == 2:
-            mine = lax.dynamic_slice_in_dim(v, slot * local_len, local_len, 0)
-            other = lax.dynamic_slice_in_dim(v, (1 - slot) * local_len, local_len, 0)
-            other = lax.ppermute(other, "seq", [(0, 1), (1, 0)])
+            mine = half_of(v, slot)
+            if other is None:
+                other = lax.ppermute(half_of(v, 1 - slot), "seq", [(0, 1), (1, 0)])
             return jnp.where(slot == 0, jnp.stack([mine, other]), jnp.stack([other, mine]))
         whole = lax.all_gather(v, "seq", axis=0, tiled=True).reshape(slots, seq_total, -1)
         return lax.dynamic_slice_in_dim(whole, me * local_len, local_len, 1)
@@ -1340,14 +1661,21 @@
     positions = part * tokens + jnp.arange(tokens, dtype=jnp.int32)
     row_mask = ((positions < length[0]) & is_live).astype(F32)[:, None]
     def pick(table):
-        return lax.dynamic_index_in_dim(table, adapter, 1, keepdims=False)
-
+        return lax.dynamic_index_in_dim(table, adapter, 2, keepdims=False)
+
+    attention_adapters = pick(attention_adapter_weights)
+    narrow_adapters = pick(narrow_adapter_weights)
+    wide_adapters = pick(broad_adapter_weights)
+    wide_adapters = jnp.pad(wide_adapters, ((0, 0), (0, 0), (0, 0), (0, WIDE - FF)))
     shards = lax.optimization_barrier(frozen.reshape(layer_count, -1, LANES))
     steps = [(d, d + 1) for d in range(fsdp_parts - 1)]
     steps = (steps, [(b, a) for a, b in steps])
     tiles = -(-(TILES_END + TILES_VECTORS) // (2 * fsdp_parts)) * 2
     index = lax.axis_index("fsdp").astype(jnp.int32).reshape(1)
     shards = [lay_shard(index, shards[layer], tiles, steps) for layer in range(layer_count)]
+    lane = lax.broadcasted_iota(jnp.int32, (tokens, LANES - HD), 1)
+    key = lax.broadcasted_iota(jnp.int32, (tokens, LANES - HD), 0)
+    bias = jnp.where((lane == 0) & (key >= length[0]), NEG, 0.0).astype(BF16)
     hidden = to_image(activations).astype(F32) * row_mask
     shards[0], hidden = lax.optimization_barrier((shards[0], hidden))
     stored = []
@@ -1367,16 +1695,15 @@
         vectors = lax.slice_in_dim(flat, 16 * TILES_END, 16 * TILES_END + 106, axis=0).reshape(-1)
         vectors, b_1 = vectors[: 8 * D].reshape(8, D).astype(F32), vectors[8 * D : 8 * D + FF]
         b_1 = jnp.pad(b_1.astype(F32), (0, WIDE - FF))[None, :]
-        attn = pick(attention_adapter_weights[layer])
-        narrow = pick(narrow_adapter_weights[layer])
-        wide = jnp.pad(pick(broad_adapter_weights[layer]), ((0, 0), (0, 0), (0, WIDE - FF)))
-        weights.append((w_qkv, w_o, w_1, w_2, vectors, attn, narrow, wide))
+        attn, narrow, wide = attention_adapters[layer], narrow_adapters[layer], wide_adapters[layer]
+        up_diagonal = jnp.concatenate(
+            [jnp.pad(attn[4 + c], ((0, 0), (c * D, (2 - c) * D))) for c in range(3)]
+        )
+        weights.append((w_qkv, w_o, w_1, w_2, vectors, attn, narrow, wide, up_diagonal))
         keys = None
         if parts == 1:
             shard = shards[layer + 1] if on_block and layer + 1 < layer_count else None
-            made = layer_forward(
-                length, hidden, w_qkv, w_o, w_1, w_2, vectors, b_1, attn, narrow, wide, shard
-            )
+            made = layer_forward(bias, hidden, weights[layer], b_1, shard)
             normed, inner_qkv, qkv, attended, stats, inner_o, middle = made[:7]
             normed_two, inner_up, gate, inner_down, next_hidden = made[7:12]
             flat = made[12] if shard is not None else None
@@ -1410,12 +1737,12 @@
             )
         )
         hidden = next_hidden
-    output = to_tokens((hidden * row_mask).astype(BF16))
+    output = (hidden * row_mask).astype(BF16)
+    other_half = None
     gradient = d_output.astype(F32) * row_mask
     collected = [None] * layer_count
+    terms = None
     for layer in reversed(range(layer_count)):
-        if layer == 0:
-            output, gradient = lax.optimization_barrier((output, gradient))
         (
             layer_input,
             normed,
@@ -1431,29 +1758,48 @@
             gate,
             inner_down,
         ) = stored[layer]
-        w_qkv, w_o, w_1, w_2, vectors, attn, narrow, wide = weights[layer]
-        d_gate, g_wide, d_inner_up, g_up_2 = gate_backward(
-            gradient, w_2, gate, narrow, wide, inner_down, inner_up
-        )
-        d_middle, d_attended, g_middle = middle_backward(
-            d_gate, w_1, d_inner_up, narrow, normed_two, middle, gradient, vectors, w_o, attn,
-            inner_o, attended,
-        )
-        d_qkv = attn_bwd(length, qkv, d_attended, attended, stats, keys)
-        if parts > 1:
-            d_keys = lax.psum_scatter(
-                d_qkv[1].astype(F32),
-                "seq",
-                scatter_dimension=0,
-                tiled=True,
-                axis_index_groups=groups,
+        w_qkv, w_o, w_1, w_2, vectors, attn, narrow, wide = weights[layer][:8]
+        if parts == 1:
+            saved = (
+                layer_input, normed, inner_qkv, qkv, stats, attended, inner_o, middle, normed_two, inner_up,
+                gate, inner_down,
             )
-            d_qkv = jnp.concatenate([d_qkv[0], d_keys.astype(BF16)], axis=1)
+            hosted = terms if on_block and layer + 1 < layer_count else None
+            made = layer_backward(
+                gradient,
+                saved,
+                weights[layer],
+                bias,
+                adapters if hosted is not None else 0,
+                hosted,
+                half_of(output, 1 - slot),
+            )
+            gradient, g_wide, g_up_2, g_middle, g_input = made[:5]
+            if hosted is not None:
+                collected[layer + 1], other_half, names = made[6:9]
         else:
-            d_qkv = d_qkv[0]
-        gradient, g_input = input_backward(
-            d_qkv, w_qkv, attn, normed, inner_qkv, layer_input, d_middle, vectors
-        )
+            d_gate, g_wide, d_inner_up, g_up_2 = gate_backward(
+                gradient, w_2, gate, narrow, wide, inner_down, inner_up
+            )
+            d_middle, d_attended, g_middle = middle_backward(
+                d_gate, w_1, d_inner_up, narrow, normed_two, middle, gradient, vectors, w_o, attn,
+                inner_o, attended,
+            )
+            d_qkv = attn_bwd(length, qkv, d_attended, attended, stats, keys)
+            if parts > 1:
+                d_keys = lax.psum_scatter(
+                    d_qkv[1].astype(F32),
+                    "seq",
+                    scatter_dimension=0,
+                    tiled=True,
+                    axis_index_groups=groups,
+                )
+                d_qkv = jnp.concatenate([d_qkv[0], d_keys.astype(BF16)], axis=1)
+            else:
+                d_qkv = d_qkv[0]
+            gradient, g_input = input_backward(
+                d_qkv, w_qkv, attn, normed, inner_qkv, layer_input, d_middle, vectors
+            )
         rows_narrow = jnp.concatenate(
             [
                 g_input[: 3 * R],
@@ -1474,9 +1820,12 @@
                 ]
             )
             terms = terms.astype(BF16).reshape(device_count, SHARE, R, LANES)
-            label = jnp.broadcast_to(adapter.astype(F32), (8, LANES))
-            sums = share_terms(terms, label, adapters)
-            collected[layer] = gather_blocks(sums, 2, 16 * sums.shape[0])
+            if layer == 0:
+                sums = share_terms(terms, names, adapters)
+                collected[layer] = gather_blocks(sums, 2, 16 * sums.shape[0])
+            else:
+                name = jnp.broadcast_to(adapter.astype(BF16), (device_count, 1, R, LANES))
+                terms = jnp.concatenate([terms, name], axis=1)
             continue
         rows_narrow = rows_narrow.astype(BF16)
         rows_wide = g_wide[:, :FF].astype(BF16)
@@ -1512,6 +1861,7 @@
         grad_attn = jnp.stack([entry[0][0:8] for entry in collected], axis=0)
         grad_narrow = jnp.stack([entry[0][8:10] for entry in collected], axis=0)
         grad_wide = jnp.stack([entry[1] for entry in collected], axis=0)
+    output = to_tokens(output, other_half)
     input_grad = to_tokens((gradient * row_mask).astype(BF16)).astype(F32)
     return (output, input_grad, grad_attn, grad_narrow, grad_wide)
 

time: 861 us -> 801 us (0.930)
  Pallas kernels: 765 us -> 715 us
  local copies, waits for them, and re-layouts: 41.1 us -> 30.2 us
    pallas_call x3 -> x2, Pallas kernels: 214 us -> 169 us  [gather_blocks(): pl.pallas_call(gather_kernel, in_specs=[pl.BlockSpec(memory_space=pl.ANY)...]
    pallas_call x2 -> x1, Pallas kernels: 57.4 us -> 28.3 us  [share_terms(): pl.pallas_call(functools.partial(share_kernel, adapters), in_specs=[pl.Bl...]
    pallas_call x8 -> x2, Pallas kernels: 244 us -> 269 us  [layer_backward(): pl.pallas_call(functools.partial(backward_kernel, adapters), grid=(sum(BA...]
    slice x3 -> x0, local copies, waits for them, and re-layouts: 8.82 us -> none  [the longest x1 4.68 us: local(): broad_adapter_weights[layer]]
  transfers between devices with their start and end apart: 8 -> 7, of which waited for: 0 -> 0; matrix products, arithmetic and copies ran while one was open for 4% -> 3% of each run, Pallas kernels for 42% -> 21%
where the time goes in v6:
time: 801 us; the launch traced here: 793 us
  Pallas kernels  715 us (89%)
  local copies, waits for them, and re-layouts  30.2 us (4%)
  other arithmetic  27.9 us (3%)
  starting transfers between devices  14.9 us (2%)
    pallas_call x2, Pallas kernels, layer_backward(): pl.pallas_call(functools.partial(backward_kernel, adapters), grid=(sum(BA...  269 us
    pallas_call x2, Pallas kernels, layer_forward(): pl.pallas_call(functools.partial(forward_kernel, shard is not None), grid...  228 us
    pallas_call x2, Pallas kernels, gather_blocks(): pl.pallas_call(gather_kernel, in_specs=[pl.BlockSpec(memory_space=pl.ANY)...  169 us
    pallas_call x1, Pallas kernels, share_terms(): pl.pallas_call(functools.partial(share_kernel, adapters), in_specs=[pl.Bl...  28.3 us
  transfers between devices with their start and end apart: 7, of which 0 were waited for; matrix products, arithmetic and copies ran while one was open for 3% of the time, Pallas kernels for 21%

profile of v6, /device:TPU:0, one launch (start us, length us, event | category | flops | bytes accessed | tf_op | source)
XLA Modules:
  0.0 792.7 jit_solution(13020482839704637157)
XLA Ops:
  0.6 1.5 dynamic-slice_bitcast_fusion.5
  2.2 3.0 collective-permute-start.2
  5.2 2.6 copy.28
  7.8 1.9 copy-done
  9.7 1.0 slice_bitcast_fusion.2
  10.6 2.2 collective-permute-start
  12.9 1.3 collective-permute-start.1
  14.1 4.7 collective-permute-start.3
  18.8 1.3 collective-permute-start.4
  20.1 4.2 slice_bitcast_fusion
  29.8 1.1 dynamic-slice_bitcast_fusion.6
  30.9 0.8 fusion.15
  31.8 0.8 select_convert_fusion.refs_0_.refs_18_
  33.3 1.9 dynamic-slice_bitcast_fusion.7
  35.1 1.7 dynamic-slice_bitcast_fusion.11
  36.9 0.7 fusion.9.refs_22_
  37.6 0.8 fusion.11.refs_22_
  38.3 4.3 lay_shard.2.refs_0_
  42.6 4.3 lay_shard.3.refs_18_
  46.9 2.2 convert_multiply_fusion.1.refs_1_.refs_27_
  49.1 134.3 %gather_blocks.2 = bf16[124416,128]{1,0:T(8,128)(2,1)} custom-call(bf16[7648,128]{1,0:T(8,128)(2,1)} %lay_shard.2.refs_0_), custom_call_target="tpu_custom_call" | custom-call | tf_op jit(solution)/shard_map/gather_blocks/pallas_call | solution.py:523
  183.4 0.7 slice_convert_fusion.1
  184.8 0.8 slice_bitcast_fusion.7
  186.8 147.4 %layer_forward_gather.1 = (bf16[736,1152]{1,0:T(8,128)(2,1)}, bf16[736,48]{1,0:T(8,128)(2,1)}, bf16[736,3456]{1,0:T(8,128)(2,1)}, bf16[736,1152]{1,0:T(8,128)(2,...) custom-call(bf16[736,56]{1,0:T(8,128)(2,1)} %select_convert_fusion.r, ...), custom_call_target="tpu_custom_call" | custom-call | flops 27403223040 | bytes 55885824 | tf_op jit(solution)/shard_map/layer_forward_gather/pallas_call | solution.py:1118
  334.2 0.8 slice_bitcast_fusion.6
  334.9 0.7 slice_convert_fusion
  337.5 2.7 dynamic-slice_bitcast_fusion.2
  340.2 1.0 collective-permute-start.5
  341.2 81.0 %layer_forward.1 = (bf16[736,1152]{1,0:T(8,128)(2,1)}, bf16[736,48]{1,0:T(8,128)(2,1)}, bf16[736,3456]{1,0:T(8,128)(2,1)}, bf16[736,1152]{1,0:T(8,128)(2,1)}, f3...) custom-call(bf16[736,56]{1,0:T(8,128)(2,1)} %select_convert_fusion.r, ...), custom_call_target="tpu_custom_call" | custom-call | flops 27403223040 | bytes 55885824 | tf_op jit(solution)/shard_map/layer_forward/pallas_call | solution.py:1118
  422.2 5.8 multiply_convert_fusion.1
  428.0 123.0 %layer_backward.1 = (f32[736,1152]{1,0:T(8,128)}, f32[32,4608]{1,0:T(8,128)}, f32[16,1152]{1,0:T(8,128)}, f32[48,1152]{1,0:T(8,128)}, f32[96,1152]{1,0:T(8,128)}) custom-call(f32[736,1152]{1,0:T(8,128)} %get-tuple-element.132.refs_0_, bf16[864,9,16,128]{3,2,1,0:T(8,128)(2,1)} %bitcast.133, bf16[736,4608]{1,0:T(8,128)(2,1)} %get-tuple-element.57.refs_2_, ...), custom_call_target="tpu_custom_call" | custom-call | flops 34891628544 | bytes 64364544 | tf_op jit(solution)/shard_map/layer_backward/pallas_call | solution.py:1589
  551.1 1.1 convert.62
  552.2 1.0 convert.63
  553.2 0.9 convert_dynamic-update-slice_fusion.1
  554.9 1.0 concatenate.45.refs_29_
  556.0 1.3 dynamic-slice_bitcast_fusion.3
  557.3 146.1 %layer_backward_share.1 = (f32[736,1152]{1,0:T(8,128)}, f32[32,4608]{1,0:T(8,128)}, f32[16,1152]{1,0:T(8,128)}, f32[48,1152]{1,0:T(8,128)}, f32[96,1152]{1,0:T(8...) custom-call(f32[736,1152]{1,0:T(8,128)} %get-tuple-element.68.refs_0, ...), custom_call_target="tpu_custom_call" | custom-call | flops 34891628544 | bytes 64364544 | tf_op jit(solution)/shard_map/layer_backward_share/pallas_call | solution.py:1589
  703.4 1.0 convert.66
  704.4 1.0 convert.67
  705.4 2.2 multiply_convert_fusion
  707.8 1.5 collective-permute-start.6
  709.6 1.1 convert.69
  711.0 1.1 maximum_maximum_fusion.1
  712.1 28.3 %share_terms.1.refs_0_ = bf16[1280,128]{1,0:T(8,128)(2,1)} custom-call(bf16[32,5,16,128]{3,2,1,0:T(8,128)(2,1)} %bitcast.142, f32[32,128]{1,0:T(8,128)} %get-tuple-element.90.refs_1_), custom_call_target="tpu_custom_call" | custom-call | tf_op jit(solution)/shard_map/share_terms/pallas_call | solution.py:1258
  740.3 34.8 %gather_blocks.3 = bf16[20480,128]{1,0:T(8,128)(2,1)} custom-call(bf16[1280,128]{1,0:T(8,128)(2,1)} %share_terms.1.refs_0_), custom_call_target="tpu_custom_call" | custom-call | tf_op jit(solution)/shard_map/gather_blocks/pallas_call | solution.py:523
  775.1 12.1 %gradient_tables.1 = (f32[2,8,8,16,1152]{4,3,2,1,0:T(8,128)}, f32[2,2,8,16,1152]{4,3,2,1,0:T(8,128)}, f32[2,2,8,16,4304]{4,3,2,1,0:T(8,128)}) custom-call(bf16[32,8,5,16,128]{4,3,2,1,0:T(8,128)(2,1)} %bitcast.139, bf16[32,8,5,16,128]{4,3,2,1,0:T(8,128)(2,1)} %bitcast.140), custom_call_target="tpu_custom_call" | custom-call | tf_op jit(solution)/shard_map/gradient_tables/pallas_call | solution.py:1297
  787.2 1.5 maximum_select_fusion.2
  788.7 3.5 fusion
  (67 shorter events, 8.5 us)
Async XLA Ops:
  2.2 44.7 %collective-permute-start.2 = (bf16[368,1152]{1,0:T(8,128)(2,1)S(1)}, bf16[368,1152]{1,0:T(8,128)(2,1)S(1)}, u32[]{:S(2)}, u32[]{:S(2)}) collective-permute-start(bf16[368,1152]{1,0:T(8,128)(2,1)S(1)} %get-tuple-element.122), channel_id=1, source_target_pairs={{0,1},{1,0},{2,3},{3,2},{4,5},{5,4},{6,7},{7,6},{8,9},{9,8},{10,11... | collective-permute-start | bytes 2543624 | tf_op jit(solution)/shard_map/ppermute | solution.py:1636
  7.8 1.9 copy-start
  10.6 27.7 %collective-permute-start = (bf16[1600,128]{1,0:T(8,128)(2,1)}, bf16[1600,128]{1,0:T(8,128)(2,1)}, u32[]{:S(2)}, u32[]{:S(2)}) collective-permute-start(bf16[1600,128]{1,0:T(8,128)(2,1)} %get-tuple-element.112), channel_id=1, source_target_pairs={{0,2},{2,4},{4,6},{6,8},{8,10},{10,12},{12,14},{14,16},{16,18},{18... | collective-permute-start | bytes 1228808 | tf_op jit(solution)/shard_map/ppermute | solution.py:120
  12.9 25.5 %collective-permute-start.1 = (bf16[1600,128]{1,0:T(8,128)(2,1)}, bf16[1600,128]{1,0:T(8,128)(2,1)}, u32[]{:S(2)}, u32[]{:S(2)}) collective-permute-start(bf16[1600,128]{1,0:T(8,128)(2,1)} %get-tuple-element.111), channel_id=1, source_target_pairs={{2,0},{4,2},{6,4},{8,6},{10,8},{12,10},{14,12},{16,14},{18,16},{20... | collective-permute-start | bytes 1228808 | tf_op jit(solution)/shard_map/ppermute | solution.py:121
  14.1 28.5 %collective-permute-start.3 = (bf16[1600,128]{1,0:T(8,128)(2,1)S(1)}, bf16[1600,128]{1,0:T(8,128)(2,1)}, u32[]{:S(2)}, u32[]{:S(2)}) collective-permute-start(bf16[1600,128]{1,0:T(8,128)(2,1)S(1)} %get-tuple-element.110), channel_id=1, source_target_pairs={{0,2},{2,4},{4,6},{6,8},{8,10},{10,12},{12,14},{14,16},{16,18},{18... | collective-permute-start | bytes 1228808 | tf_op jit(solution)/shard_map/ppermute | solution.py:120
  18.8 23.8 %collective-permute-start.4 = (bf16[1600,128]{1,0:T(8,128)(2,1)S(1)}, bf16[1600,128]{1,0:T(8,128)(2,1)}, u32[]{:S(2)}, u32[]{:S(2)}) collective-permute-start(bf16[1600,128]{1,0:T(8,128)(2,1)S(1)} %get-tuple-element.109), channel_id=1, source_target_pairs={{2,0},{4,2},{6,4},{8,6},{10,8},{12,10},{14,12},{16,14},{18,16},{20... | collective-permute-start | bytes 1228808 | tf_op jit(solution)/shard_map/ppermute | solution.py:121
  20.1 4.3 copy-start.9
  20.1 6.0 copy-start.10
  28.7 18.2 %copy-start.6 = (f32[736]{0:T(1024)}, f32[736]{0:T(1024)S(1)}, u32[]{:S(2)}) copy-start(f32[736]{0:T(1024)S(1)} %fusion.17) | copy-start | bytes 8836
  340.2 82.0 %collective-permute-start.5 = (bf16[368,1152]{1,0:T(8,128)(2,1)}, bf16[368,1152]{1,0:T(8,128)(2,1)}, u32[]{:S(2)}, u32[]{:S(2)}) collective-permute-start(bf16[368,1152]{1,0:T(8,128)(2,1)} %get-tuple-element.120), channel_id=1, source_target_pairs={{0,1},{1,0},{2,3},{3,2},{4,5},{5,4},{6,7},{7,6},{8,9},{9,8},{10,11... | collective-permute-start | bytes 2543624 | tf_op jit(solution)/shard_map/ppermute | solution.py:1636
  551.0 3.4 copy-start.4
  551.1 3.6 copy-start.7
  554.1 1.9 copy-start.1
  705.4 3.9 copy-start.5
  707.7 3.3 copy-start.8
  707.8 80.9 %collective-permute-start.6 = (bf16[368,1152]{1,0:T(8,128)(2,1)S(1)}, bf16[368,1152]{1,0:T(8,128)(2,1)}, u32[]{:S(2)}, u32[]{:S(2)}) collective-permute-start(bf16[368,1152]{1,0:T(8,128)(2,1)S(1)} %get-tuple-element.116), channel_id=1, source_target_pairs={{0,1},{1,0},{2,3},{3,2},{4,5},{5,4},{6,7},{7,6},{8,9},{9,8},{10,11... | collective-permute-start | bytes 2543624 | tf_op jit(solution)/shard_map/ppermute | solution.py:1653
  775.1 12.1 %copy-start.2 = (bf16[1,368,1152]{2,1,0:T(8,128)(2,1)S(1)}, bf16[1,368,1152]{2,1,0:T(8,128)(2,1)}, u32[]{:S(2)}) copy-start(bf16[1,368,1152]{2,1,0:T(8,128)(2,1)} %get-tuple-element.117) | copy-start | bytes 2543620
  775.1 12.1 %copy-start.3 = (bf16[368,1152]{1,0:T(8,128)(2,1)S(1)}, bf16[368,1152]{1,0:T(8,128)(2,1)}, u32[]{:S(2)}) copy-start(bf16[368,1152]{1,0:T(8,128)(2,1)} %get-tuple-element.84) | copy-start | bytes 2543620

commit v7 on v6

--- a/solution.py
+++ b/solution.py
@@ -53,18 +53,18 @@
 HALO = 1600
 
 
-def lay_kernel(own_rows, tiles, index_ref, before, own, after, out, flat, held, turned):
-    d = index_ref[0]
+def lay_rows(d, own_rows, tiles, before, own, after, flat, held, turned):
     margin = 16 * PANELS[2]
-    flat[0:HALO] = before[...].astype(F32)
-    flat[HALO : HALO + own_rows] = own[...].astype(F32)
-    flat[HALO + own_rows : 2 * HALO + own_rows] = after[...].astype(F32)
+    flat[0:HALO] = before.astype(F32)
+    flat[HALO : HALO + own_rows] = own.astype(F32)
+    flat[HALO + own_rows : 2 * HALO + own_rows] = after.astype(F32)
     flat_base = d * own_rows - HALO
     tile_base = d * tiles
 
     def span(at, units, panels):
         low = jnp.maximum(tile_base - at, 0) // panels
-        high = jnp.clip((tile_base + tiles - at + panels - 1) // panels, 0, units)
+        high = jnp.maximum(tile_base + tiles - at + panels - 1, 0) // panels
+        high = jnp.minimum(high, units)
         return low, jnp.maximum(high, low)
 
     for at, start, units, panels in zip(
@@ -112,7 +112,21 @@
                 return carry
 
             lax.fori_loop(low, high, unit, 0)
+
+
+def lay_kernel(own_rows, tiles, index_ref, before, own, after, out, flat, held, turned):
+    margin = 16 * PANELS[2]
+    lay_rows(index_ref[0], own_rows, tiles, before[...], own[...], after[...], flat, held, turned)
     out[...] = held[margin : margin + 16 * tiles]
+
+
+def lay_scratch(own_rows, tiles):
+    margin = 16 * PANELS[2]
+    return [
+        pltpu.VMEM((own_rows + 2 * HALO + 8 * UP_ROWS, LANES), F32),
+        pltpu.VMEM((16 * tiles + 10 * margin, LANES), BF16),
+        pltpu.VMEM((8 * margin, LANES), F32),
+    ]
 
 
 def lay_shard(index, shard, tiles, perms):
@@ -120,17 +134,12 @@
     before = lax.ppermute(shard[own_rows - HALO :], "fsdp", perms[0])
     after = lax.ppermute(shard[:HALO], "fsdp", perms[1])
     vm = pl.BlockSpec(memory_space=pltpu.VMEM)
-    margin = 16 * PANELS[2]
     return pl.pallas_call(
         functools.partial(lay_kernel, own_rows, tiles),
         in_specs=[pl.BlockSpec(memory_space=pltpu.SMEM), vm, vm, vm],
         out_specs=vm,
         out_shape=jax.ShapeDtypeStruct((16 * tiles, LANES), BF16),
-        scratch_shapes=[
-            pltpu.VMEM((own_rows + 2 * HALO + 8 * UP_ROWS, LANES), F32),
-            pltpu.VMEM((16 * tiles + 10 * margin, LANES), BF16),
-            pltpu.VMEM((8 * margin, LANES), F32),
-        ],
+        scratch_shapes=lay_scratch(own_rows, tiles),
         compiler_params=pltpu.CompilerParams(vmem_limit_bytes=VMEM_LIMIT),
         name="lay_shard",
     )(index, before, shard, after)
@@ -1130,6 +1139,112 @@
         compiler_params=pltpu.CompilerParams(**params),
         name="layer_forward_gather" if shard is not None else "layer_forward",
     )(*operands)
+
+
+def first_gather_kernel(tiles, shard_a, shard_b, gathered, laid_a, laid_b, own, halo, flat, held, turned, *sems):
+    own_sem, halo_send, halo_recv = sems[:3]
+    f = lax.axis_index("fsdp")
+    x = lax.axis_index("seq")
+    z = f // 4
+    rows = shard_a.shape[0]
+    last = lax.axis_size("fsdp") - 1
+    margin = 16 * PANELS[2]
+    barrier = pltpu.get_barrier_semaphore()
+    start, events, finish = gather_plan(laid_a, gathered, None, *sems[3:])
+
+    def greet(to):
+        pl.semaphore_signal(barrier, inc=1, device_id=to, device_id_type=MESH)
+
+    y, c = (f // 2) % 2, f % 2
+    for to in ((f + 2 - 4 * y, x), (f, 1 - x), (f + 1 - 2 * c, x)):
+        greet(to)
+    for there, step in ((z < 3, 4), (z > 0, -4), (f < last, 1), (f > 0, -1)):
+
+        @pl.when(there)
+        def _(step=step):
+            greet((f + step, x))
+
+    expected = 3
+    for there in (z < 3, z > 0, f < last, f > 0):
+        expected = expected + jnp.where(there, 1, 0)
+    pl.semaphore_wait(barrier, expected)
+
+    def halo_copy(layer, side):
+        source = (shard_a, shard_b)[layer].at[pl.ds((rows - HALO) * (1 - side), HALO), :]
+        return pltpu.make_async_remote_copy(
+            src_ref=source,
+            dst_ref=halo.at[layer, side],
+            send_sem=halo_send.at[layer, side],
+            recv_sem=halo_recv.at[layer, side],
+            device_id=(f + 1 - 2 * side, x),
+            device_id_type=MESH,
+        )
+
+    def sends(side):
+        return f < last if side == 0 else f > 0
+
+    def takes(side):
+        return sends(1 - side)
+
+    for layer in range(2):
+        for side in range(2):
+
+            @pl.when(sends(side))
+            def _(layer=layer, side=side):
+                halo_copy(layer, side).start()
+
+    def lay(layer, source, laid):
+        fetch = pltpu.make_async_copy(source, own, own_sem.at[0])
+        fetch.start()
+        fetch.wait()
+        for side in range(2):
+
+            @pl.when(takes(side))
+            def _(side=side):
+                halo_copy(layer, side).wait_recv()
+
+            @pl.when(jnp.logical_not(takes(side)))
+            def _(side=side):
+                halo[layer, side] = jnp.zeros((HALO, LANES), BF16)
+
+        lay_rows(f, rows, tiles, halo[layer, 0], own[...], halo[layer, 1], flat, held, turned)
+        keep = pltpu.make_async_copy(held.at[pl.ds(margin, 16 * tiles), :], laid, own_sem.at[0])
+        keep.start()
+        keep.wait()
+
+    lay(0, shard_a, laid_a)
+    start(False)
+    lay(1, shard_b, laid_b)
+    for _, event in events:
+        event()
+    finish()
+    for layer in range(2):
+        for side in range(2):
+
+            @pl.when(sends(side))
+            def _(layer=layer, side=side):
+                halo_copy(layer, side).wait_send()
+
+
+def first_gather(shards, tiles):
+    rows = shards[0].shape[0]
+    dma = pltpu.SemaphoreType.DMA
+    hbm = pl.BlockSpec(memory_space=pl.ANY)
+    laid = jax.ShapeDtypeStruct((16 * tiles, LANES), BF16)
+    return pl.pallas_call(
+        functools.partial(first_gather_kernel, tiles),
+        in_specs=[hbm, hbm],
+        out_specs=[hbm, hbm, hbm],
+        out_shape=[jax.ShapeDtypeStruct((16 * TILES_HELD, LANES), BF16), laid, laid],
+        scratch_shapes=[pltpu.VMEM((rows, LANES), BF16), pltpu.VMEM((2, 2, HALO, LANES), BF16)]
+        + lay_scratch(rows, tiles)
+        + [dma((1,)), dma((2, 2)), dma((2, 2))]
+        + gather_semaphores(),
+        compiler_params=pltpu.CompilerParams(
+            collective_id=0, has_side_effects=True, vmem_limit_bytes=VMEM_MOST
+        ),
+        name="first_gather",
+    )(*shards)
 
 
 SHARE = 5
@@ -1603,6 +1718,70 @@
     )(*[operand for _, operand in operands])
 
 
+def prepare_kernel(scalars, attn_in, narrow_in, wide_in, mine, other, attn, narrow, wide, diagonal, bias, hidden):
+    length, live, slot = scalars[1], scalars[2], scalars[3]
+    attn[...] = attn_in[:, :, 0]
+    narrow[...] = narrow_in[:, :, 0]
+    wide[...] = jnp.zeros_like(wide)
+    wide[:, :, :, :FF] = wide_in[:, :, 0]
+    diagonal[...] = jnp.zeros_like(diagonal)
+    for layer in range(attn.shape[0]):
+        for c in range(3):
+            diagonal[layer, c * R : (c + 1) * R, c * D : (c + 1) * D] = attn_in[layer, 4 + c, 0]
+    bias[...] = key_bias(bias.shape[0], length)
+    half = mine.shape[1]
+    row = lax.broadcasted_iota(jnp.int32, (half, 1), 0)
+
+    def place(at, value):
+        keep = jnp.where(row + at < length, live, 0) > 0
+        hidden[at : at + half] = jnp.where(keep, value.astype(F32), 0.0)
+
+    for first in range(2):
+
+        @pl.when(slot == first)
+        def _(first=first):
+            place(first * half, mine[0])
+            place((1 - first) * half, other[...])
+
+
+def prepare(scalars, attention_table, narrow_table, wide_table, activations, other):
+    layers = attention_table.shape[0]
+    rows = 2 * other.shape[0]
+
+    def picked(kinds, width):
+        return pl.BlockSpec((layers, kinds, 1, R, width), lambda i, k: (0, 0, k[0], 0, 0))
+
+    def full(*shape):
+        return pl.BlockSpec(shape, lambda i, k: (0,) * len(shape))
+
+    shapes = [
+        ((layers, 8, R, D), BF16),
+        ((layers, 2, R, D), BF16),
+        ((layers, 2, R, WIDE), BF16),
+        ((layers, 3 * R, 3 * D), BF16),
+        ((rows, LANES - HD), BF16),
+        ((rows, D), F32),
+    ]
+    return pl.pallas_call(
+        prepare_kernel,
+        grid_spec=pltpu.PrefetchScalarGridSpec(
+            num_scalar_prefetch=1,
+            grid=(1,),
+            in_specs=[
+                picked(8, D),
+                picked(2, D),
+                picked(2, FF),
+                pl.BlockSpec((1,) + other.shape, lambda i, k: (k[3], 0, 0)),
+                full(*other.shape),
+            ],
+            out_specs=[full(*shape) for shape, _ in shapes],
+        ),
+        out_shape=[struct(*shape) for shape in shapes],
+        compiler_params=pltpu.CompilerParams(vmem_limit_bytes=VMEM_LIMIT),
+        name="prepare",
+    )(scalars, attention_table, narrow_table, wide_table, activations, other)
+
+
 def local(
     activations,
     group_image_count,
@@ -1660,32 +1839,50 @@
     is_live = slot < group_image_count[0]
     positions = part * tokens + jnp.arange(tokens, dtype=jnp.int32)
     row_mask = ((positions < length[0]) & is_live).astype(F32)[:, None]
-    def pick(table):
-        return lax.dynamic_index_in_dim(table, adapter, 2, keepdims=False)
-
-    attention_adapters = pick(attention_adapter_weights)
-    narrow_adapters = pick(narrow_adapter_weights)
-    wide_adapters = pick(broad_adapter_weights)
-    wide_adapters = jnp.pad(wide_adapters, ((0, 0), (0, 0), (0, 0), (0, WIDE - FF)))
     shards = lax.optimization_barrier(frozen.reshape(layer_count, -1, LANES))
-    steps = [(d, d + 1) for d in range(fsdp_parts - 1)]
-    steps = (steps, [(b, a) for a, b in steps])
     tiles = -(-(TILES_END + TILES_VECTORS) // (2 * fsdp_parts)) * 2
-    index = lax.axis_index("fsdp").astype(jnp.int32).reshape(1)
-    shards = [lay_shard(index, shards[layer], tiles, steps) for layer in range(layer_count)]
-    lane = lax.broadcasted_iota(jnp.int32, (tokens, LANES - HD), 1)
-    key = lax.broadcasted_iota(jnp.int32, (tokens, LANES - HD), 0)
-    bias = jnp.where((lane == 0) & (key >= length[0]), NEG, 0.0).astype(BF16)
-    hidden = to_image(activations).astype(F32) * row_mask
-    shards[0], hidden = lax.optimization_barrier((shards[0], hidden))
+    if on_block:
+        flat, *shards = first_gather([shards[layer] for layer in range(layer_count)], tiles)
+    else:
+        steps = [(d, d + 1) for d in range(fsdp_parts - 1)]
+        steps = (steps, [(b, a) for a, b in steps])
+        index = lax.axis_index("fsdp").astype(jnp.int32).reshape(1)
+        shards = [lay_shard(index, shards[layer], tiles, steps) for layer in range(layer_count)]
+    if parts == 1 and slots == 2:
+        other = lax.dynamic_index_in_dim(activations, 1 - slot, 0, keepdims=False)
+        other = lax.ppermute(other, "seq", [(0, 1), (1, 0)])
+        scalars = jnp.stack([adapter, length[0], is_live.astype(jnp.int32), slot.astype(jnp.int32)])
+        prepared = prepare(
+            scalars, attention_adapter_weights, narrow_adapter_weights, broad_adapter_weights, activations, other
+        )
+        attention_adapters, narrow_adapters, wide_adapters, up_diagonals, bias, hidden = prepared
+    else:
+        def pick(table):
+            return lax.dynamic_index_in_dim(table, adapter, 2, keepdims=False)
+
+        attention_adapters = pick(attention_adapter_weights)
+        narrow_adapters = pick(narrow_adapter_weights)
+        wide_adapters = pick(broad_adapter_weights)
+        wide_adapters = jnp.pad(wide_adapters, ((0, 0), (0, 0), (0, 0), (0, WIDE - FF)))
+        lane = lax.broadcasted_iota(jnp.int32, (tokens, LANES - HD), 1)
+        key = lax.broadcasted_iota(jnp.int32, (tokens, LANES - HD), 0)
+        bias = jnp.where((lane == 0) & (key >= length[0]), NEG, 0.0).astype(BF16)
+        hidden = to_image(activations).astype(F32) * row_mask
+        up_diagonals = jnp.stack(
+            [
+                jnp.concatenate(
+                    [
+                        jnp.pad(attention_adapters[layer, 4 + c], ((0, 0), (c * D, (2 - c) * D)))
+                        for c in range(3)
+                    ]
+                )
+                for layer in range(layer_count)
+            ]
+        )
     stored = []
     weights = []
     for layer in range(layer_count):
-        if on_block and layer > 0:
-            pass
-        elif on_block:
-            flat = gather_blocks(shards[layer], 0, 16 * TILES_HELD)
-        else:
+        if not on_block:
             flat = lax.all_gather(shards[layer], "fsdp", axis=0, tiled=True)
             flat = jnp.pad(flat, ((0, 16 * TILES_HELD - flat.shape[0]), (0, 0)))
         if layer == layer_count - 1:
@@ -1696,10 +1893,7 @@
         vectors, b_1 = vectors[: 8 * D].reshape(8, D).astype(F32), vectors[8 * D : 8 * D + FF]
         b_1 = jnp.pad(b_1.astype(F32), (0, WIDE - FF))[None, :]
         attn, narrow, wide = attention_adapters[layer], narrow_adapters[layer], wide_adapters[layer]
-        up_diagonal = jnp.concatenate(
-            [jnp.pad(attn[4 + c], ((0, 0), (c * D, (2 - c) * D))) for c in range(3)]
-        )
-        weights.append((w_qkv, w_o, w_1, w_2, vectors, attn, narrow, wide, up_diagonal))
+        weights.append((w_qkv, w_o, w_1, w_2, vectors, attn, narrow, wide, up_diagonals[layer]))
         keys = None
         if parts == 1:
             shard = shards[layer + 1] if on_block and layer + 1 < layer_count else None

time: 801 us -> 800 us (level)
  Pallas kernels: 715 us -> 731 us
  starting transfers between devices: 14.9 us -> 4.62 us
    pallas_call x2, Pallas kernels: 8.54 us -> 155 us  [the longest x1 150 us: first_gather(): pl.pallas_call(functools.partial(first_gather_kernel, tiles), in_specs=[h...]
    pallas_call x2 -> x1, Pallas kernels: 169 us -> 34.8 us  [gather_blocks(): pl.pallas_call(gather_kernel, in_specs=[pl.BlockSpec(memory_space=pl.ANY)...]
  transfers between devices with their start and end apart: 7 -> 3, of which waited for: 0 -> 0; matrix products, arithmetic and copies ran while one was open for 3% -> 2% of each run, Pallas kernels for 21% -> 39%
where the time goes in v7:
time: 800 us; the launch traced here: 792 us
  Pallas kernels  731 us (91%)
  local copies, waits for them, and re-layouts  29.3 us (4%)
  other arithmetic  24 us (3%)
    pallas_call x2, Pallas kernels, layer_backward(): pl.pallas_call(functools.partial(backward_kernel, adapters), grid=(sum(BA...  271 us
    pallas_call x2, Pallas kernels, layer_forward(): pl.pallas_call(functools.partial(forward_kernel, shard is not None), grid...  228 us
    pallas_call x1, Pallas kernels, first_gather(): pl.pallas_call(functools.partial(first_gather_kernel, tiles), in_specs=[h...  150 us
    pallas_call x1, Pallas kernels, gather_blocks(): pl.pallas_call(gather_kernel, in_specs=[pl.BlockSpec(memory_space=pl.ANY)...  34.8 us
    pallas_call x1, Pallas kernels, share_terms(): pl.pallas_call(functools.partial(share_kernel, adapters), in_specs=[pl.Bl...  30.2 us
  transfers between devices with their start and end apart: 3, of which 0 were waited for; matrix products, arithmetic and copies ran while one was open for 2% of the time, Pallas kernels for 39%

profile of v7, /device:TPU:0, one launch (start us, length us, event | category | flops | bytes accessed | tf_op | source)
XLA Modules:
  0.0 791.8 jit_solution(11209872562404049642)
XLA Ops:
  0.6 2.1 dynamic-slice_bitcast_fusion.4
  2.8 2.9 collective-permute-start
  5.7 2.6 copy.28
  8.3 2.1 slice_bitcast_fusion
  10.4 149.7 %first_gather.1 = (bf16[124416,128]{1,0:T(8,128)(2,1)}, bf16[7648,128]{1,0:T(8,128)(2,1)}, bf16[7648,128]{1,0:T(8,128)(2,1)}) custom-call(bf16[7456,128]{1,0:T(8,128)(2,1)} %get-tuple-element.108.shard_a, bf16[7456,128]{1,0:T(8,128)(2,1)} %get-tuple-element.107.shard_b), custom_call_target="tpu_custom_call" | custom-call | tf_op jit(solution)/shard_map/first_gather/pallas_call | solution.py:1234
  160.1 0.7 slice_convert_fusion.1
  160.8 0.6 convert_element_type.52.refs_3_.refs_12_
  161.5 1.2 dynamic_slice.29
  162.7 1.2 dynamic_slice.30
  164.6 0.6 copy.30
  165.2 0.8 slice_bitcast_fusion.19
  166.0 0.6 reshape.160.refs_11_
  167.2 0.7 pad.25.clone
  167.9 1.9 pad_add_fusion.scalars
  169.8 1.2 fusion.2
  171.0 5.4 prepare.1
  176.4 1.8 slice_bitcast_fusion.8
  178.3 1.6 slice_bitcast_fusion.10
  179.9 2.0 slice_bitcast_fusion.4
  181.9 146.8 %layer_forward_gather.1 = (bf16[736,1152]{1,0:T(8,128)(2,1)}, bf16[736,48]{1,0:T(8,128)(2,1)}, bf16[736,3456]{1,0:T(8,128)(2,1)}, bf16[736,1152]{1,0:T(8,128)(2,...) custom-call(bf16[736,56]{1,0:T(8,128)(2,1)} %get-tuple-element.56.re, ...), custom_call_target="tpu_custom_call" | custom-call | flops 27403223040 | bytes 55885824 | tf_op jit(solution)/shard_map/layer_forward_gather/pallas_call | solution.py:1127
  328.7 0.8 slice_bitcast_fusion.18
  329.4 0.7 slice_convert_fusion
  330.1 0.6 convert_element_type.54.refs_3_.refs_12_
  330.8 0.6 reshape.161.refs_11_
  331.4 0.6 copy.29
  332.0 2.7 dynamic-slice_bitcast_fusion.2
  334.7 1.2 collective-permute-start.1
  335.9 81.1 %layer_forward.1 = (bf16[736,1152]{1,0:T(8,128)(2,1)}, bf16[736,48]{1,0:T(8,128)(2,1)}, bf16[736,3456]{1,0:T(8,128)(2,1)}, bf16[736,1152]{1,0:T(8,128)(2,1)}, f3...) custom-call(bf16[736,56]{1,0:T(8,128)(2,1)} %get-tuple-element.56.re, ...), custom_call_target="tpu_custom_call" | custom-call | flops 27403223040 | bytes 55885824 | tf_op jit(solution)/shard_map/layer_forward/pallas_call | solution.py:1127
  417.0 2.0 slice_bitcast_fusion.2
  419.0 5.9 multiply_convert_fusion.1
  424.9 123.0 %layer_backward.1 = (f32[736,1152]{1,0:T(8,128)}, f32[32,4608]{1,0:T(8,128)}, f32[16,1152]{1,0:T(8,128)}, f32[48,1152]{1,0:T(8,128)}, f32[96,1152]{1,0:T(8,128)}) custom-call(f32[736,1152]{1,0:T(8,128)} %get-tuple-element.134.refs_0_, bf16[864,9,16,128]{3,2,1,0:T(8,128)(2,1)} %bitcast.103, bf16[736,4608]{1,0:T(8,128)(2,1)} %get-tuple-element.68.refs_2_, ...), custom_call_target="tpu_custom_call" | custom-call | flops 34891628544 | bytes 64364544 | tf_op jit(solution)/shard_map/layer_backward/pallas_call | solution.py:1704
  547.9 1.1 convert.63
  549.0 1.0 convert.64
  550.1 0.9 convert_dynamic-update-slice_fusion.1
  551.9 1.0 concatenate.29.refs_29_
  552.9 1.3 dynamic-slice_bitcast_fusion.3
  554.2 148.1 %layer_backward_share.1 = (f32[736,1152]{1,0:T(8,128)}, f32[32,4608]{1,0:T(8,128)}, f32[16,1152]{1,0:T(8,128)}, f32[48,1152]{1,0:T(8,128)}, f32[96,1152]{1,0:T(8...) custom-call(f32[736,1152]{1,0:T(8,128)} %get-tuple-element.80.refs_0, ...), custom_call_target="tpu_custom_call" | custom-call | flops 34891628544 | bytes 64364544 | tf_op jit(solution)/shard_map/layer_backward_share/pallas_call | solution.py:1704
  702.3 1.0 convert.67
  703.3 1.0 convert.68
  704.3 2.2 multiply_convert_fusion
  706.7 0.5 collective-permute-start.2
  707.2 0.2 copy-done.5
  708.2 1.1 maximum_maximum_fusion.1
  709.2 30.2 %share_terms.1.refs_0_ = bf16[1280,128]{1,0:T(8,128)(2,1)} custom-call(bf16[32,5,16,128]{3,2,1,0:T(8,128)(2,1)} %bitcast.122, f32[32,128]{1,0:T(8,128)} %get-tuple-element.102.refs_1_), custom_call_target="tpu_custom_call" | custom-call | tf_op jit(solution)/shard_map/share_terms/pallas_call | solution.py:1373
  739.5 34.8 %gather_blocks.1 = bf16[20480,128]{1,0:T(8,128)(2,1)} custom-call(bf16[1280,128]{1,0:T(8,128)(2,1)} %share_terms.1.refs_0_), custom_call_target="tpu_custom_call" | custom-call | tf_op jit(solution)/shard_map/gather_blocks/pallas_call | solution.py:532
  774.4 12.1 %gradient_tables.1 = (f32[2,8,8,16,1152]{4,3,2,1,0:T(8,128)}, f32[2,2,8,16,1152]{4,3,2,1,0:T(8,128)}, f32[2,2,8,16,4304]{4,3,2,1,0:T(8,128)}) custom-call(bf16[32,8,5,16,128]{4,3,2,1,0:T(8,128)(2,1)} %bitcast.118, bf16[32,8,5,16,128]{4,3,2,1,0:T(8,128)(2,1)} %bitcast.120), custom_call_target="tpu_custom_call" | custom-call | tf_op jit(solution)/shard_map/gradient_tables/pallas_call | solution.py:1412
  786.4 1.5 maximum_select_fusion.1
  788.0 3.5 fusion
  (46 shorter events, 1.8 us)
Async XLA Ops:
  2.8 168.3 %collective-permute-start = (bf16[368,1152]{1,0:T(8,128)(2,1)}, bf16[368,1152]{1,0:T(8,128)(2,1)}, u32[]{:S(2)}, u32[]{:S(2)}) collective-permute-start(bf16[368,1152]{1,0:T(8,128)(2,1)} %dynamic-slice_bitcast_fusion.4), channel_id=1, source_target_pairs={{0,1},{1,0},{2,3},{3,2},{4,5},{5,4},{6,7},{7,6},{8,9},{9,8},{10,11... | collective-permute-start | bytes 2543624 | tf_op jit(solution)/shard_map/ppermute | solution.py:1853
  334.7 84.3 %collective-permute-start.1 = (bf16[368,1152]{1,0:T(8,128)(2,1)}, bf16[368,1152]{1,0:T(8,128)(2,1)}, u32[]{:S(2)}, u32[]{:S(2)}) collective-permute-start(bf16[368,1152]{1,0:T(8,128)(2,1)} %get-tuple-element.114), channel_id=1, source_target_pairs={{0,1},{1,0},{2,3},{3,2},{4,5},{5,4},{6,7},{7,6},{8,9},{9,8},{10,11... | collective-permute-start | bytes 2543624 | tf_op jit(solution)/shard_map/ppermute | solution.py:1815
  547.9 3.4 copy-start.4
  551.0 0.7 copy-start.6
  551.3 1.5 copy-start
  706.6 0.9 copy-start.5
  706.6 1.2 copy-start.3
  706.7 81.3 %collective-permute-start.2 = (bf16[368,1152]{1,0:T(8,128)(2,1)S(1)}, bf16[368,1152]{1,0:T(8,128)(2,1)}, u32[]{:S(2)}, u32[]{:S(2)}) collective-permute-start(bf16[368,1152]{1,0:T(8,128)(2,1)S(1)} %get-tuple-element.110), channel_id=1, source_target_pairs={{0,1},{1,0},{2,3},{3,2},{4,5},{5,4},{6,7},{7,6},{8,9},{9,8},{10,11... | collective-permute-start | bytes 2543624 | tf_op jit(solution)/shard_map/ppermute | solution.py:1832
  707.5 0.7 copy-start.7
  774.3 12.1 %copy-start.1 = (bf16[1,368,1152]{2,1,0:T(8,128)(2,1)S(1)}, bf16[1,368,1152]{2,1,0:T(8,128)(2,1)}, u32[]{:S(2)}) copy-start(bf16[1,368,1152]{2,1,0:T(8,128)(2,1)} %get-tuple-element.111) | copy-start | bytes 2543620
  774.3 12.1 %copy-start.2 = (bf16[368,1152]{1,0:T(8,128)(2,1)S(1)}, bf16[368,1152]{1,0:T(8,128)(2,1)}, u32[]{:S(2)}) copy-start(bf16[368,1152]{1,0:T(8,128)(2,1)} %get-tuple-element.96) | copy-start | bytes 2543620

commit v8 on v7

--- a/solution.py
+++ b/solution.py
@@ -936,12 +936,17 @@
 CHUNK_TIME = 7.0
 
 
+def of_layer(layer, *shape):
+    return pl.BlockSpec(
+        (1,) + shape, lambda i: (layer,) + (0,) * len(shape), pipeline_mode=pl.Buffered(1)
+    )
+
+
 def forward_kernel(with_gather, *refs):
     (
-        bias_lane, hidden, w_qkv, vec, down, up, w_o, down_o, up_o, down_1, w_1, b_1, up_1, w_2, w_2_odd, b_2,
-        down_2, up_2,
-    ) = refs[:18]
-    refs = refs[18:]
+        bias_lane, hidden, w_qkv, vec, attn, w_o, narrow_in, w_1, b_1, up_1, w_2, w_2_odd, b_2, down_2, up_2,
+    ) = refs[:15]
+    refs = refs[15:]
     if with_gather:
         shard, refs = refs[0], refs[1:]
     (
@@ -982,14 +987,14 @@
         def _():
             value = layer_norm(hidden[...], vec[0:1], vec[1:2]).astype(BF16)
             normed[...] = value
-            narrow = dot_t(value, down[...]).astype(BF16)
+            narrow = dot_t(value, attn[0, 0:3].reshape(3 * R, D)).astype(BF16)
             inner_qkv[...] = narrow
             for part in range(3):
                 parts[part] = narrow[:, part * R : (part + 1) * R]
             stats[...] = jnp.zeros_like(stats)
 
         bias = vec[pl.ds(jnp.where(i == 2, 5, 4), 1), :] * jnp.where(i == 1, 0.0, 1.0)
-        value = (dot_both(normed[...], matrix(w_qkv), parts[i], up[0]) + bias).astype(BF16)
+        value = (dot_both(normed[...], matrix(w_qkv), parts[i], attn[0, 4 + i]) + bias).astype(BF16)
         qkv[...] = value
         mark = jnp.where(i == 0, first_lane(rows, F32(1.0)), jnp.where(i == 1, bias_lane[...], jnp.zeros_like(bias_lane[...])))
         for h in range(H):
@@ -1016,14 +1021,14 @@
             for h in range(H):
                 attended[:, h * HD : (h + 1) * HD] = heads[0, h][:, :HD]
             value = attended[...]
-            narrow = dot_t(value, down_o[...]).astype(BF16)
+            narrow = dot_t(value, attn[0, 3]).astype(BF16)
             inner_o[...] = narrow
-            middle[...] = hidden[...] + (dot_both(value, matrix(w_o), narrow, up_o[...]) + vec[6:7])
+            middle[...] = hidden[...] + (dot_both(value, matrix(w_o), narrow, attn[0, 7]) + vec[6:7])
             value = layer_norm(middle[...], vec[2:3], vec[3:4]).astype(BF16)
             normed_two[...] = value
-            inner_up[...] = dot_t(value, down_1[...]).astype(BF16)
-
-        x = dot_both(normed_two[...], matrix(w_1), inner_up[...], up_1[...]) + b_1[...]
+            inner_up[...] = dot_t(value, narrow_in[0, 0]).astype(BF16)
+
+        x = dot_both(normed_two[...], matrix(w_1), inner_up[...], up_1[0, 0]) + b_1[...]
         gate[...] = x.astype(BF16)
         value = (0.5 * x * (1.0 + gelu_parts(x))).astype(BF16)
         activated[:, pl.ds(pl.multiple_of(t * TILE, LANES), TILE)] = value
@@ -1032,18 +1037,18 @@
     def _():
         @at_step(down_at)
         def _():
-            w = jnp.concatenate([matrix(w_2.at[: UNITS[3]]), down_2[...].T[:FF]], axis=1)
+            w = jnp.concatenate([matrix(w_2.at[: UNITS[3]]), down_2[0, 0].T[:FF]], axis=1)
             value = dot(activated[:, :FF], w)
             narrow = value[:, LANES : LANES + R].astype(BF16)
             inner_down[...] = narrow
-            value = value[:, :LANES] + b_2[:, :LANES] + dot(narrow, up_2[:, :LANES])
+            value = value[:, :LANES] + b_2[:, :LANES] + dot(narrow, up_2[0, 0, :, :LANES])
             next_hidden[:, :LANES] = middle[:, D - LANES :] + value
 
         @pl.when(i > down_at)
         def _():
             at = pl.ds(pl.multiple_of((i - down_at - 1) * PAIR, LANES), PAIR)
             w = jnp.concatenate([matrix(w.at[: UNITS[3]]) for w in (w_2, w_2_odd)], axis=1)
-            value = dot(activated[:, :FF], w) + b_2[...] + dot(inner_down[...], up_2[...])
+            value = dot(activated[:, :FF], w) + b_2[...] + dot(inner_down[...], up_2[0, 0])
             next_hidden[...] = middle[:, at] + value
 
     if with_gather:
@@ -1055,8 +1060,9 @@
             finish()
 
 
-def layer_forward(bias, hidden, weights, b_1, shard=None):
-    w_qkv, w_o, w_1, w_2, vectors, attn, narrow, wide, _ = weights
+def layer_forward(layer, bias, hidden, weights, tables, shard=None):
+    w_qkv, w_o, w_1, w_2, vectors, b_1 = weights
+    attn, narrow, wide, _ = tables
     rows = hidden.shape[0]
     _, att_at, up_at, down_at = FORWARD_AT
 
@@ -1073,28 +1079,24 @@
         return pl.BlockSpec((count, PAIR), lambda i: (0, pair(i)))
 
     operands = [
-        bias, hidden, w_qkv, vectors, attn[0:3].reshape(3 * R, D), attn[4:7], w_o, attn[3], attn[7], narrow[0],
-        w_1, b_1, wide[0], w_2, w_2, vectors[7:8], wide[1], narrow[1],
+        bias, hidden, w_qkv, vectors, attn, w_o, narrow, w_1, b_1, wide, w_2, w_2, vectors[7:8], wide, narrow,
     ]
     in_specs = [
         whole((rows, LANES - HD)),
         whole((rows, D)),
         unit_block(72, 9, lambda i: (0, step(i, 0), 0, 0)),
         whole((8, D)),
-        whole((3 * R, D)),
-        pl.BlockSpec((1, R, D), lambda i: (step(i, 0), 0, 0)),
+        of_layer(layer, 8, R, D),
         OUT_BLOCK,
-        whole((R, D)),
-        whole((R, D)),
-        whole((R, D)),
+        of_layer(layer, 2, R, D),
         unit_block(72, 4, lambda i: (1, step(i, 2), 0, 0)),
         cols(1, TILE, 2),
-        cols(R, TILE, 2),
+        pl.BlockSpec((1, 1, R, TILE), lambda i: (layer, 0, 0, step(i, 2))),
         unit_block(288, 1, lambda i: (2, 2 * pair(i), 0, 0)),
         unit_block(288, 1, lambda i: (2, jnp.minimum(2 * pair(i) + 1, 8), 0, 0)),
         pairs(1),
-        whole((R, WIDE)),
-        pairs(R),
+        pl.BlockSpec((1, 1, R, WIDE), lambda i: (layer, 1, 0, 0), pipeline_mode=pl.Buffered(1)),
+        pl.BlockSpec((1, 1, R, PAIR), lambda i: (layer, 1, 0, pair(i))),
     ]
     outs = [
         (whole((rows, D)), struct((rows, D), BF16)),
@@ -1429,16 +1431,16 @@
 SHARE_AT, PASS_AT, GATHER_AT = 7, 9, 10
 
 
-def backward_kernel(adapters, *refs):
+def backward_kernel(adapters, spread, *refs):
     (
-        gradient, w_2, gate, down_2, up_2, inner_down, inner_up, w_1, w_1_odd, up_1, down_1, normed_two_in, vec, w_o, down_o,
-        up_o, inner_o, attended, bias, stats, w_qkv, w_qkv_odd, up, down, inner_qkv, middle_in, qkv_in, hidden_in, normed_in,
-    ) = refs[:29]
-    refs = refs[29:]
+        gradient, w_2, gate, down_2, inner_down, inner_up, w_1, w_1_odd, up_1, narrow, normed_two_in, vec, w_o, attn,
+        label, inner_o, attended, bias, stats, w_qkv, w_qkv_odd, up, inner_qkv, middle_in, qkv_in, hidden_in, normed_in,
+    ) = refs[:27]
+    refs = refs[27:]
     if adapters:
         terms, half, refs = refs[0], refs[1], refs[2:]
-    new_gradient, g_wide, g_up_2, g_middle, g_input = refs[:5]
-    refs = refs[5:]
+    new_gradient, new_terms = refs[:2]
+    refs = refs[2:]
     if adapters:
         pair, gathered, other_half, names, refs = refs[0], refs[1], refs[2], refs[3], refs[4:]
     (
@@ -1451,6 +1453,14 @@
 
     def at_step(k):
         return pl.when(i == k)
+
+    def place(t):
+        return t if spread == SHARE else t // SHARE * spread + t % SHARE
+
+    def put(table, value):
+        for p in range(D // LANES):
+            tile = value[:, p * LANES : (p + 1) * LANES]
+            new_terms[place(table * (D // LANES) + p)] = tile.astype(BF16)
 
     def load_middle():
         return pltpu.make_async_copy(middle_in, residual, load_sem.at[0])
@@ -1507,11 +1517,16 @@
             load_middle().start()
             value = gradient[...].astype(BF16)
             d_branch[...] = value
-            d_inner_down[...] = dot_t(value, up_2[...]).astype(BF16)
-            g_up_2[...] = dot_l(inner_down[...], value)
+            d_inner_down[...] = dot_t(value, narrow[0, 1]).astype(BF16)
+            put(9, dot_l(inner_down[...], value))
+            for t in (158, 159):
+                new_terms[place(t)] = jnp.zeros((R, LANES), BF16)
+            if spread > SHARE:
+                for k in range(SHARE, new_terms.shape[0], spread):
+                    new_terms[k] = label[...]
 
         left = FF - i * TILE
-        d_act = dot_both_t(d_branch[...], matrix(w_2), d_inner_down[...], down_2[...].T)
+        d_act = dot_both_t(d_branch[...], matrix(w_2), d_inner_down[...], down_2[0, 0].T)
         x = gate[...].astype(F32)
         t = gelu_parts(x)
         half = 0.5 * (1.0 + t)
@@ -1521,8 +1536,23 @@
         keep = lax.broadcasted_iota(jnp.int32, (1, TILE), 1) < left
         value = jnp.where(keep, slope * d_act, 0.0).astype(BF16)
         wide[:, pl.ds(pl.multiple_of(i * TILE, LANES), TILE)] = value
-        g_wide[0:R] = dot_l(inner_up[...], value)
-        g_wide[R : 2 * R] = dot_l(d_inner_down[...], (x * half).astype(BF16))
+        made = (
+            dot_l(inner_up[...], value).astype(BF16),
+            dot_l(d_inner_down[...], (x * half).astype(BF16)).astype(BF16),
+        )
+
+        def put_wide(panels):
+            for kind in range(2):
+                for p in panels:
+                    tile = made[kind][:, p * LANES : (p + 1) * LANES]
+                    new_terms[place(90 + 34 * kind + 4 * i + p)] = tile
+
+        put_wide(range(2))
+
+        @pl.when(i < middle_at - 1)
+        def _():
+            put_wide(range(2, 4))
+
 
     @pl.when(jnp.logical_and(i >= middle_at, i < turn_at))
     def _():
@@ -1535,7 +1565,7 @@
 
         @at_step(turn_at - 1)
         def _():
-            w = jnp.concatenate([matrix(w_1, 34), up_1[:, : 34 * LANES]], axis=0)
+            w = jnp.concatenate([matrix(w_1, 34), up_1[0, 0, :, : 34 * LANES]], axis=0)
             value = dot_t(wide[:, : 34 * LANES], w)
             d_normed[PAIRS - 1, :, :LANES] = value[:, :LANES]
             d_inner_up[...] = value[:, LANES : LANES + R].astype(BF16)
@@ -1548,17 +1578,17 @@
     def _():
         load_qkv().start()
         load_middle().wait()
-        d_two = joined() + dot(d_inner_up[...], down_1[...])
+        d_two = joined() + dot(d_inner_up[...], narrow[0, 0])
         value = gradient[...] + layer_norm_back(d_two, residual[...], vec[2:3])
         load_hidden().start()
         new_gradient[...] = value
         d_out = value.astype(BF16)
-        d_inner_o = dot_t(d_out, up_o[...]).astype(BF16)
-        wide[:, 3 * D :] = (dot_t(d_out, matrix(w_o)) + dot(d_inner_o, down_o[...])).astype(BF16)
-        g_middle[0:R] = dot_l(d_inner_o, attended[...])
-        g_middle[R : 2 * R] = dot_l(inner_o[...], d_out)
+        d_inner_o = dot_t(d_out, attn[0, 7]).astype(BF16)
+        wide[:, 3 * D :] = (dot_t(d_out, matrix(w_o)) + dot(d_inner_o, attn[0, 3])).astype(BF16)
+        put(3, dot_l(d_inner_o, attended[...]))
+        put(7, dot_l(inner_o[...], d_out))
         load_normed_two().wait()
-        g_middle[2 * R : 3 * R] = dot_l(d_inner_up[...], d_branch[...])
+        put(8, dot_l(d_inner_up[...], d_branch[...]))
         load_normed().start()
         load_qkv().wait()
         rows = gradient.shape[0]
@@ -1601,7 +1631,7 @@
                     wide[:, c * D + h * HD : c * D + (h + 1) * HD] = heads[c, h][:, :HD]
             for c in range(3):
                 part = wide[:, c * D : (c + 1) * D]
-                g_input[(3 + c) * R : (4 + c) * R] = dot_l(inner_qkv[:, c * R : (c + 1) * R], part)
+                put(4 + c, dot_l(inner_qkv[:, c * R : (c + 1) * R], part))
 
         @pl.when(i < last)
         def _():
@@ -1610,13 +1640,15 @@
 
         @at_step(last)
         def _():
-            w = jnp.concatenate([matrix(w_qkv), up[...]], axis=0)
+            w = jnp.concatenate([matrix(w_qkv), up[0]], axis=0)
             value = dot_t(wide[:, : 3 * D], w)
             d_normed[PAIRS - 1, :, :LANES] = value[:, :LANES]
-            narrow = value[:, LANES : LANES + 3 * R].astype(BF16)
-            g_input[0 : 3 * R] = dot_l(narrow, d_branch[...])
+            inner = value[:, LANES : LANES + 3 * R].astype(BF16)
+            made = dot_l(inner, d_branch[...])
+            for c in range(3):
+                put(c, made[c * R : (c + 1) * R])
             load_hidden().wait()
-            d_one = joined() + dot(narrow, down[...])
+            d_one = joined() + dot(inner, attn[0, 0:3].reshape(3 * R, D))
             new_gradient[...] += layer_norm_back(d_one, residual[...], vec[0:1])
 
     if adapters:
@@ -1628,10 +1660,11 @@
 
 
 def layer_backward(
-    gradient, saved, weights, bias, adapters=0, terms=None, half=None
+    layer, gradient, saved, weights, tables, bias, label, spread, adapters=0, terms=None, half=None
 ):
     hidden, normed, inner_qkv, qkv, stats, attended, inner_o, middle, normed_two, inner_up, gate, inner_down = saved
-    w_qkv, w_o, w_1, w_2, vectors, attn, narrow, wide, up_diagonal = weights
+    w_qkv, w_o, w_1, w_2, vectors, _ = weights
+    attn, narrow, wide, up_diagonal = tables
     rows = gradient.shape[0]
 
     def step(i, k):
@@ -1645,27 +1678,25 @@
         (whole((rows, D)), gradient),
         (unit_block(TILE // 16, 9, lambda i: (TILES_AT[3] // 9 * 16 // TILE + step(i, 0), 0, 0, 0)), w_2),
         (cols(rows, TILE, 0), gate),
-        (cols(R, TILE, 0), wide[1]),
-        (whole((R, D)), narrow[1]),
+        (pl.BlockSpec((1, 1, R, TILE), lambda i: (layer, 1, 0, step(i, 0))), wide),
         (whole((rows, R)), inner_down),
         (whole((rows, R)), inner_up),
         (unit_block(8, PANELS[2], lambda i: (9 + 2 * step(i, 1), 0, 0, 0)), w_1),
         (unit_block(8, PANELS[2], lambda i: (10 + jnp.minimum(2 * step(i, 1), 7), 0, 0, 0)), w_1),
-        (whole((R, WIDE)), wide[0]),
-        (whole((R, D)), narrow[0]),
+        (of_layer(layer, 1, R, WIDE), wide),
+        (of_layer(layer, 2, R, D), narrow),
         (hbm, normed_two),
         (whole((8, D)), vectors),
         (OUT_BLOCK, w_o),
-        (whole((R, D)), attn[3]),
-        (whole((R, D)), attn[7]),
+        (of_layer(layer, 8, R, D), attn),
+        (whole((R, LANES)), label),
         (whole((rows, R)), inner_o),
         (whole((rows, D)), attended),
         (whole((rows, LANES - HD)), bias),
         (whole((rows, LANES)), stats),
         (unit_block(8, 27, lambda i: (2 * step(i, 4), 0, 0, 0)), w_qkv),
         (unit_block(8, 27, lambda i: (jnp.minimum(2 * step(i, 4) + 1, 8), 0, 0, 0)), w_qkv),
-        (whole((3 * R, 3 * D)), up_diagonal),
-        (whole((3 * R, D)), attn[0:3].reshape(3 * R, D)),
+        (of_layer(layer, 3 * R, 3 * D), up_diagonal),
         (whole((rows, 3 * R)), inner_qkv),
         (hbm, middle),
         (hbm, qkv),
@@ -1674,10 +1705,7 @@
     ]
     outs = [
         (whole((rows, D)), struct((rows, D), F32)),
-        (cols(2 * R, TILE, 0), struct((2 * R, WIDE), F32)),
-        (whole((R, D)), struct((R, D), F32)),
-        (whole((3 * R, D)), struct((3 * R, D), F32)),
-        (whole((6 * R, D)), struct((6 * R, D), F32)),
+        (whole((32 * spread, R, LANES)), struct((32 * spread, R, LANES), BF16)),
     ]
     scratch = [
         pltpu.VMEM((rows, D), BF16),
@@ -1702,7 +1730,7 @@
         scratch += gather_semaphores()
         params.update(collective_id=4, has_side_effects=True)
     return pl.pallas_call(
-        functools.partial(backward_kernel, adapters),
+        functools.partial(backward_kernel, adapters, spread),
         grid=(sum(BACKWARD_STEPS),),
         in_specs=[spec for spec, _ in operands],
         out_specs=[spec for spec, _ in outs],
@@ -1718,8 +1746,40 @@
     )(*[operand for _, operand in operands])
 
 
-def prepare_kernel(scalars, attn_in, narrow_in, wide_in, mine, other, attn, narrow, wide, diagonal, bias, hidden):
-    length, live, slot = scalars[1], scalars[2], scalars[3]
+VECTOR_ROWS = 240
+
+
+def read_vectors(block, vectors, b_1, rows):
+    rows[...] = block[...].astype(F32)
+    for p in range(D // LANES):
+        vectors[:, p * LANES : (p + 1) * LANES] = rows[pl.ds(p, 8, stride=D // LANES), :]
+    b_1[...] = jnp.zeros_like(b_1)
+    first = 8 * D // LANES
+    for p in range(-(-FF // LANES)):
+        width = min(LANES, FF - p * LANES)
+        b_1[:, p * LANES : p * LANES + width] = rows[first + p : first + p + 1, :width]
+
+
+def layer_vectors(flat):
+    return pl.pallas_call(
+        read_vectors,
+        grid=(1,),
+        in_specs=[pl.BlockSpec((VECTOR_ROWS, LANES), lambda i: (16 * TILES_END // VECTOR_ROWS, 0))],
+        out_specs=[whole((8, D)), whole((1, WIDE))],
+        out_shape=[struct((8, D), F32), struct((1, WIDE), F32)],
+        scratch_shapes=[pltpu.VMEM((VECTOR_ROWS, LANES), F32)],
+        name="layer_vectors",
+    )(flat)
+
+
+def prepare_kernel(
+    scalars, attn_in, narrow_in, wide_in, mine, other, block, attn, narrow, wide, diagonal, bias, hidden, label,
+    vectors, b_1, rows,
+):
+    slot = scalars[5]
+    length, live = scalars[2 + slot], jnp.where(slot < scalars[4], 1, 0)
+    read_vectors(block, vectors, b_1, rows)
+    label[...] = jnp.full(label.shape, scalars[slot], jnp.int32).astype(F32).astype(BF16)
     attn[...] = attn_in[:, :, 0]
     narrow[...] = narrow_in[:, :, 0]
     wide[...] = jnp.zeros_like(wide)
@@ -1744,12 +1804,12 @@
             place((1 - first) * half, other[...])
 
 
-def prepare(scalars, attention_table, narrow_table, wide_table, activations, other):
+def prepare(scalars, attention_table, narrow_table, wide_table, activations, other, flat):
     layers = attention_table.shape[0]
     rows = 2 * other.shape[0]
 
     def picked(kinds, width):
-        return pl.BlockSpec((layers, kinds, 1, R, width), lambda i, k: (0, 0, k[0], 0, 0))
+        return pl.BlockSpec((layers, kinds, 1, R, width), lambda i, k: (0, 0, k[k[5]], 0, 0))
 
     def full(*shape):
         return pl.BlockSpec(shape, lambda i, k: (0,) * len(shape))
@@ -1761,6 +1821,9 @@
         ((layers, 3 * R, 3 * D), BF16),
         ((rows, LANES - HD), BF16),
         ((rows, D), F32),
+        ((R, LANES), BF16),
+        ((8, D), F32),
+        ((1, WIDE), F32),
     ]
     return pl.pallas_call(
         prepare_kernel,
@@ -1771,15 +1834,17 @@
                 picked(8, D),
                 picked(2, D),
                 picked(2, FF),
-                pl.BlockSpec((1,) + other.shape, lambda i, k: (k[3], 0, 0)),
+                pl.BlockSpec((1,) + other.shape, lambda i, k: (k[5], 0, 0)),
                 full(*other.shape),
+                pl.BlockSpec((VECTOR_ROWS, LANES), lambda i, k: (16 * TILES_END // VECTOR_ROWS, 0)),
             ],
             out_specs=[full(*shape) for shape, _ in shapes],
+            scratch_shapes=[pltpu.VMEM((VECTOR_ROWS, LANES), F32)],
         ),
         out_shape=[struct(*shape) for shape in shapes],
         compiler_params=pltpu.CompilerParams(vmem_limit_bytes=VMEM_LIMIT),
         name="prepare",
-    )(scalars, attention_table, narrow_table, wide_table, activations, other)
+    )(scalars, attention_table, narrow_table, wide_table, activations, other, flat)
 
 
 def local(
@@ -1848,14 +1913,22 @@
         steps = (steps, [(b, a) for a, b in steps])
         index = lax.axis_index("fsdp").astype(jnp.int32).reshape(1)
         shards = [lay_shard(index, shards[layer], tiles, steps) for layer in range(layer_count)]
-    if parts == 1 and slots == 2:
+    if on_block:
         other = lax.dynamic_index_in_dim(activations, 1 - slot, 0, keepdims=False)
         other = lax.ppermute(other, "seq", [(0, 1), (1, 0)])
-        scalars = jnp.stack([adapter, length[0], is_live.astype(jnp.int32), slot.astype(jnp.int32)])
+        scalars = jnp.concatenate(
+            [image_adapter_index, lengths, group_image_count, slot.astype(jnp.int32)[None]]
+        )
         prepared = prepare(
-            scalars, attention_adapter_weights, narrow_adapter_weights, broad_adapter_weights, activations, other
+            scalars,
+            attention_adapter_weights,
+            narrow_adapter_weights,
+            broad_adapter_weights,
+            activations,
+            other,
+            flat,
         )
-        attention_adapters, narrow_adapters, wide_adapters, up_diagonals, bias, hidden = prepared
+        tables, (bias, hidden, label) = prepared[:4], prepared[4:7]
     else:
         def pick(table):
             return lax.dynamic_index_in_dim(table, adapter, 2, keepdims=False)
@@ -1889,15 +1962,19 @@
             cotangent, flat = lax.optimization_barrier((cotangent, flat))
             d_output = to_image(cotangent)
         w_qkv, w_o, w_1, w_2 = (flat.reshape(-1, panels, 16, LANES) for panels in PANELS)
-        vectors = lax.slice_in_dim(flat, 16 * TILES_END, 16 * TILES_END + 106, axis=0).reshape(-1)
-        vectors, b_1 = vectors[: 8 * D].reshape(8, D).astype(F32), vectors[8 * D : 8 * D + FF]
-        b_1 = jnp.pad(b_1.astype(F32), (0, WIDE - FF))[None, :]
-        attn, narrow, wide = attention_adapters[layer], narrow_adapters[layer], wide_adapters[layer]
-        weights.append((w_qkv, w_o, w_1, w_2, vectors, attn, narrow, wide, up_diagonals[layer]))
+        if on_block:
+            vectors, b_1 = prepared[7:9] if layer == 0 else layer_vectors(flat)
+            weights.append((w_qkv, w_o, w_1, w_2, vectors, b_1))
+        else:
+            vectors = lax.slice_in_dim(flat, 16 * TILES_END, 16 * TILES_END + 106, axis=0).reshape(-1)
+            vectors, b_1 = vectors[: 8 * D].reshape(8, D).astype(F32), vectors[8 * D : 8 * D + FF]
+            b_1 = jnp.pad(b_1.astype(F32), (0, WIDE - FF))[None, :]
+            attn, narrow, wide = attention_adapters[layer], narrow_adapters[layer], wide_adapters[layer]
+            weights.append((w_qkv, w_o, w_1, w_2, vectors, attn, narrow, wide))
         keys = None
-        if parts == 1:
-            shard = shards[layer + 1] if on_block and layer + 1 < layer_count else None
-            made = layer_forward(bias, hidden, weights[layer], b_1, shard)
+        if on_block:
+            shard = shards[layer + 1] if layer + 1 < layer_count else None
+            made = layer_forward(layer, bias, hidden, weights[layer], tables, shard)
             normed, inner_qkv, qkv, attended, stats, inner_o, middle = made[:7]
             normed_two, inner_up, gate, inner_down, next_hidden = made[7:12]
             flat = made[12] if shard is not None else None
@@ -1952,26 +2029,37 @@
             gate,
             inner_down,
         ) = stored[layer]
-        w_qkv, w_o, w_1, w_2, vectors, attn, narrow, wide = weights[layer][:8]
-        if parts == 1:
+        if not on_block:
+            w_qkv, w_o, w_1, w_2, vectors, attn, narrow, wide = weights[layer]
+        if on_block:
             saved = (
                 layer_input, normed, inner_qkv, qkv, stats, attended, inner_o, middle, normed_two, inner_up,
                 gate, inner_down,
             )
-            hosted = terms if on_block and layer + 1 < layer_count else None
+            hosting = layer + 1 < layer_count
+            spread = SHARE if layer == 0 else SHARE + 1
             made = layer_backward(
+                layer,
                 gradient,
                 saved,
                 weights[layer],
+                tables,
                 bias,
-                adapters if hosted is not None else 0,
-                hosted,
+                label,
+                spread,
+                adapters if hosting else 0,
+                terms,
                 half_of(output, 1 - slot),
             )
-            gradient, g_wide, g_up_2, g_middle, g_input = made[:5]
-            if hosted is not None:
-                collected[layer + 1], other_half, names = made[6:9]
-        else:
+            gradient, terms = made[:2]
+            terms = terms.reshape(device_count, spread, R, LANES)
+            if hosting:
+                collected[layer + 1], other_half, names = made[3:6]
+            if layer == 0:
+                sums = share_terms(terms, names, adapters)
+                collected[layer] = gather_blocks(sums, 2, 16 * sums.shape[0])
+            continue
+        if True:
             d_gate, g_wide, d_inner_up, g_up_2 = gate_backward(
                 gradient, w_2, gate, narrow, wide, inner_down, inner_up
             )
@@ -2003,24 +2091,6 @@
                 g_up_2,
             ]
         )
-        if on_block:
-            terms = jnp.concatenate(
-                [
-                    rows_narrow.reshape(10, R, 9, LANES).transpose(0, 2, 1, 3).reshape(90, R, LANES),
-                    g_wide.reshape(2, R, 36, LANES)
-                    .transpose(0, 2, 1, 3)[:, :34]
-                    .reshape(68, R, LANES),
-                    jnp.zeros((2, R, LANES), F32),
-                ]
-            )
-            terms = terms.astype(BF16).reshape(device_count, SHARE, R, LANES)
-            if layer == 0:
-                sums = share_terms(terms, names, adapters)
-                collected[layer] = gather_blocks(sums, 2, 16 * sums.shape[0])
-            else:
-                name = jnp.broadcast_to(adapter.astype(BF16), (device_count, 1, R, LANES))
-                terms = jnp.concatenate([terms, name], axis=1)
-            continue
         rows_narrow = rows_narrow.astype(BF16)
         rows_wide = g_wide[:, :FF].astype(BF16)
 

time: 800 us -> 774 us (0.968)
  local copies, waits for them, and re-layouts: 29.3 us -> 13 us
  other arithmetic: 24 us -> 15 us
    pallas_call x2 -> x3, Pallas kernels: 271 us -> 271 us  [the longest x2 269 us: layer_backward(): pl.pallas_call(functools.partial(backward_kernel, adapters, spread), grid...]
  transfers between devices with their start and end apart: 3 -> 3, of which waited for: 0 -> 0; matrix products, arithmetic and copies ran while one was open for 2% -> 1% of each run, Pallas kernels for 39% -> 40%
where the time goes in v8:
time: 774 us; the launch traced here: 767 us
  Pallas kernels  732 us (95%)
  other arithmetic  15 us (2%)
  local copies, waits for them, and re-layouts  13 us (2%)
    pallas_call x2, Pallas kernels, layer_backward(): pl.pallas_call(functools.partial(backward_kernel, adapters, spread), grid...  269 us
    pallas_call x2, Pallas kernels, layer_forward(): pl.pallas_call(functools.partial(forward_kernel, shard is not None), grid...  228 us
    pallas_call x1, Pallas kernels, first_gather(): pl.pallas_call(functools.partial(first_gather_kernel, tiles), in_specs=[h...  149 us
    pallas_call x1, Pallas kernels, gather_blocks(): pl.pallas_call(gather_kernel, in_specs=[pl.BlockSpec(memory_space=pl.ANY)...  34.8 us
    pallas_call x1, Pallas kernels, share_terms(): pl.pallas_call(functools.partial(share_kernel, adapters), in_specs=[pl.Bl...  32.4 us
  transfers between devices with their start and end apart: 3, of which 0 were waited for; matrix products, arithmetic and copies ran while one was open for 1% of the time, Pallas kernels for 40%

profile of v8, /device:TPU:0, one launch (start us, length us, event | category | flops | bytes accessed | tf_op | source)
XLA Modules:
  0.0 766.6 jit_solution(15492814306141794548)
XLA Ops:
  0.6 2.1 dynamic-slice_bitcast_fusion.4
  2.8 2.9 collective-permute-start
  5.7 2.6 copy.16
  8.3 0.0 copy-start.3
  8.3 2.1 slice_bitcast_fusion
  11.1 0.0 copy-done.3
  11.1 0.6 dynamic_slice.26
  11.6 149.3 %first_gather.1 = (bf16[124416,128]{1,0:T(8,128)(2,1)}, bf16[7648,128]{1,0:T(8,128)(2,1)}, bf16[7648,128]{1,0:T(8,128)(2,1)}) custom-call(bf16[7456,128]{1,0:T(8,128)(2,1)} %get-tuple-element.106.shard_a, bf16[7456,128]{1,0:T(8,128)(2,1)} %get-tuple-element.105.shard_b), custom_call_target="tpu_custom_call" | custom-call | tf_op jit(solution)/shard_map/first_gather/pallas_call | solution.py:1236
  160.9 1.3 pad_add_fusion.scalars
  162.2 1.1 fusion.2
  163.3 0.0 collective-permute-done.other
  163.3 5.4 prepare.1
  168.8 1.4 slice.14.refs_12_
  170.1 146.3 %layer_forward_gather.1 = (bf16[736,1152]{1,0:T(8,128)(2,1)}, bf16[736,48]{1,0:T(8,128)(2,1)}, bf16[736,3456]{1,0:T(8,128)(2,1)}, bf16[736,1152]{1,0:T(8,128)(2,...) custom-call(bf16[736,56]{1,0:T(8,128)(2,1)} %get-tuple-element.56.re, ...), custom_call_target="tpu_custom_call" | custom-call | flops 27403223040 | bytes 55885824 | tf_op jit(solution)/shard_map/layer_forward_gather/pallas_call | solution.py:1129
  316.4 0.0 copy-start.1
  316.4 1.6 layer_vectors.1
  318.0 1.4 slice.15.refs_12_
  319.4 0.0 copy-done.1
  319.4 1.3 dynamic-slice_bitcast_fusion.2
  320.7 1.2 collective-permute-start.1
  321.9 81.3 %layer_forward.1 = (bf16[736,1152]{1,0:T(8,128)(2,1)}, bf16[736,48]{1,0:T(8,128)(2,1)}, bf16[736,3456]{1,0:T(8,128)(2,1)}, bf16[736,1152]{1,0:T(8,128)(2,1)}, f3...) custom-call(bf16[736,56]{1,0:T(8,128)(2,1)} %get-tuple-element.56.re, ...), custom_call_target="tpu_custom_call" | custom-call | flops 27403223040 | bytes 55885824 | tf_op jit(solution)/shard_map/layer_forward/pallas_call | solution.py:1129
  403.2 0.0 collective-permute-done.1
  403.2 5.3 multiply_convert_fusion.1
  408.5 1.4 dynamic-slice_bitcast_fusion.3
  409.9 121.0 %layer_backward.1 = (f32[736,1152]{1,0:T(8,128)}, bf16[192,16,128]{2,1,0:T(8,128)(2,1)}) custom-call(f32[736,1152]{1,0:T(8,128)} %get-tuple-element.114.refs_0_, bf16[864,9,16,128]{3,2,1,0:T(8,128)(2,1)} %bitcast.52, bf16[736,4608]{1,0:T(8,128)(2,1)} %get-tuple-element.71.refs_2_, ...), custom_call_target="tpu_custom_call" | custom-call | flops 34891628544 | bytes 64364544 | tf_op jit(solution)/shard_map/layer_backward/pallas_call | solution.py:1732
  530.9 148.3 %layer_backward_share.1 = (f32[736,1152]{1,0:T(8,128)}, bf16[160,16,128]{2,1,0:T(8,128)(2,1)}, bf16[1280,128]{1,0:T(8,128)(2,1)}, bf16[20480,128]{1,0:T(8,128)(2...) custom-call(f32[736,1152]{1,0:T(8,128)} %get-tuple-element.84.refs_0_, bf16[864,9,16,128]{3,2,1,0:T(8,128)(2,1)} %bitcast.41, ...), custom_call_target="tpu_custom_call" | custom-call | flops 34891628544 | bytes 64364544 | tf_op jit(solution)/shard_map/layer_backward_share/pallas_call | solution.py:1732
  679.2 2.2 multiply_convert_fusion
  681.4 0.1 dynamic-slice_bitcast_fusion
  681.5 0.5 collective-permute-start.2
  682.0 32.4 %share_terms.1.refs_0_ = bf16[1280,128]{1,0:T(8,128)(2,1)} custom-call(bf16[32,5,16,128]{3,2,1,0:T(8,128)(2,1)} %bitcast.62, f32[32,128]{1,0:T(8,128)} %get-tuple-element.100.refs_1_), custom_call_target="tpu_custom_call" | custom-call | tf_op jit(solution)/shard_map/share_terms/pallas_call | solution.py:1375
  714.3 34.8 %gather_blocks.1 = bf16[20480,128]{1,0:T(8,128)(2,1)} custom-call(bf16[1280,128]{1,0:T(8,128)(2,1)} %share_terms.1.refs_0_), custom_call_target="tpu_custom_call" | custom-call | tf_op jit(solution)/shard_map/gather_blocks/pallas_call | solution.py:532
  749.1 0.0 copy-start
  749.1 0.0 copy-start.2
  749.1 12.1 %gradient_tables.1 = (f32[2,8,8,16,1152]{4,3,2,1,0:T(8,128)}, f32[2,2,8,16,1152]{4,3,2,1,0:T(8,128)}, f32[2,2,8,16,4304]{4,3,2,1,0:T(8,128)}) custom-call(bf16[32,8,5,16,128]{4,3,2,1,0:T(8,128)(2,1)} %bitcast.56, bf16[32,8,5,16,128]{4,3,2,1,0:T(8,128)(2,1)} %bitcast.58), custom_call_target="tpu_custom_call" | custom-call | tf_op jit(solution)/shard_map/gradient_tables/pallas_call | solution.py:1414
  761.2 0.0 copy-done
  761.2 0.0 copy-done.2
  761.2 1.5 maximum_select_fusion.1
  762.8 0.0 collective-permute-done.2
  762.8 3.5 fusion
Async XLA Ops:
  2.8 160.6 %collective-permute-start = (bf16[368,1152]{1,0:T(8,128)(2,1)}, bf16[368,1152]{1,0:T(8,128)(2,1)}, u32[]{:S(2)}, u32[]{:S(2)}) collective-permute-start(bf16[368,1152]{1,0:T(8,128)(2,1)} %dynamic-slice_bitcast_fusion.4), channel_id=1, source_target_pairs={{0,1},{1,0},{2,3},{3,2},{4,5},{5,4},{6,7},{7,6},{8,9},{9,8},{10,11... | collective-permute-start | bytes 2543624 | tf_op jit(solution)/shard_map/ppermute | solution.py:1918
  8.3 2.8 copy-start.3
  316.4 3.0 copy-start.1
  320.7 82.5 %collective-permute-start.1 = (bf16[368,1152]{1,0:T(8,128)(2,1)}, bf16[368,1152]{1,0:T(8,128)(2,1)}, u32[]{:S(2)}, u32[]{:S(2)}) collective-permute-start(bf16[368,1152]{1,0:T(8,128)(2,1)} %get-tuple-element.112), channel_id=1, source_target_pairs={{0,1},{1,0},{2,3},{3,2},{4,5},{5,4},{6,7},{7,6},{8,9},{9,8},{10,11... | collective-permute-start | bytes 2543624 | tf_op jit(solution)/shard_map/ppermute | solution.py:1880
  681.5 81.2 %collective-permute-start.2 = (bf16[368,1152]{1,0:T(8,128)(2,1)S(1)}, bf16[368,1152]{1,0:T(8,128)(2,1)}, u32[]{:S(2)}, u32[]{:S(2)}) collective-permute-start(bf16[368,1152]{1,0:T(8,128)(2,1)S(1)} %get-tuple-element.108), channel_id=1, source_target_pairs={{0,1},{1,0},{2,3},{3,2},{4,5},{5,4},{6,7},{7,6},{8,9},{9,8},{10,11... | collective-permute-start | bytes 2543624 | tf_op jit(solution)/shard_map/ppermute | solution.py:1897
  749.1 12.1 %copy-start = (bf16[1,368,1152]{2,1,0:T(8,128)(2,1)S(1)}, bf16[1,368,1152]{2,1,0:T(8,128)(2,1)}, u32[]{:S(2)}) copy-start(bf16[1,368,1152]{2,1,0:T(8,128)(2,1)} %get-tuple-element.109) | copy-start | bytes 2543620
  749.1 12.1 %copy-start.2 = (bf16[368,1152]{1,0:T(8,128)(2,1)S(1)}, bf16[368,1152]{1,0:T(8,128)(2,1)}, u32[]{:S(2)}) copy-start(bf16[368,1152]{1,0:T(8,128)(2,1)} %get-tuple-element.97) | copy-start | bytes 2543620

commit v9 on v8

--- a/solution.py
+++ b/solution.py
@@ -925,15 +925,17 @@
 
 PAIR = 2 * LANES
 PAIRS = -(-D // PAIR)
-FORWARD_STEPS = (3, H, WIDE // TILE, PAIRS)
-FORWARD_AT = (0, 3, 3 + H, 3 + H + WIDE // TILE)
+TWIN = 2
+FOUR = 4
+FORWARD_STEPS = (3, H // FOUR, WIDE // TILE, PAIRS)
+FORWARD_AT = (0, 3, 3 + H // FOUR, 3 + H // FOUR + WIDE // TILE)
 FORWARD_BEGINS = (
     [4.5 * i for i in range(3)]
-    + [14 + 2 * i for i in range(H)]
-    + [46 + (5 if i else 0) + 2.6 * i for i in range(WIDE // TILE)]
-    + [73 + 3 * i for i in range(PAIRS)]
+    + [14 + 6 * i for i in range(H // FOUR)]
+    + [38 + (5 if i else 0) + 2.6 * i for i in range(WIDE // TILE)]
+    + [65 + 3 * i for i in range(PAIRS)]
 )
-CHUNK_TIME = 7.0
+CHUNK_TIME = 7.4
 
 
 def of_layer(layer, *shape):
@@ -1002,15 +1004,19 @@
 
     @pl.when(jnp.logical_and(i >= att_at, i < up_at))
     def _():
-        h = i - att_at
         lane = lax.broadcasted_iota(jnp.int32, (rows, LANES), 1)
-        s = dot_t(heads[0, h], heads[1, h])
-        m = jnp.max(s, axis=1, keepdims=True)
-        p = jnp.exp2((s - m) * C2)
-        total = jnp.sum(p, axis=1, keepdims=True)
-        o = dot(p.astype(BF16), heads[2, h])
-        heads[0, h] = (o * (1.0 / total)).astype(BF16)
-        stats[...] = jnp.where(lane == h, m * C2 + jnp.log2(total), stats[...])
+        pair_at = (i - att_at) * FOUR
+        scores = [dot_t(heads[0, pair_at + k], heads[1, pair_at + k]) for k in range(FOUR)]
+        kept = stats[...]
+        for k in range(FOUR):
+            h, s = pair_at + k, scores[k]
+            m = jnp.max(s, axis=1, keepdims=True)
+            p = jnp.exp2((s - m) * C2)
+            total = jnp.sum(p, axis=1, keepdims=True)
+            o = dot(p.astype(BF16), heads[2, h])
+            heads[0, h] = (o * (1.0 / total)).astype(BF16)
+            kept = jnp.where(lane == h, m * C2 + jnp.log2(total), kept)
+        stats[...] = kept
 
     @pl.when(jnp.logical_and(i >= up_at, i < down_at))
     def _():
@@ -1426,8 +1432,8 @@
     )(*gathered)
 
 
-BACKWARD_STEPS = (WIDE // TILE, PAIRS, 1, H, PAIRS)
-BACKWARD_AT = (0, 9, 14, 15, 31)
+BACKWARD_STEPS = (WIDE // TILE, PAIRS, 1, H // TWIN, PAIRS)
+BACKWARD_AT = (0, 9, 14, 15, 15 + H // TWIN)
 SHARE_AT, PASS_AT, GATHER_AT = 7, 9, 10
 
 
@@ -1609,17 +1615,18 @@
 
     @pl.when(jnp.logical_and(i >= att_at, i < input_at))
     def _():
-        h = i - att_at
-        q, k, do = heads[0, h], heads[1, h], heads[3, h]
-        p = jnp.exp2(dot_t(k, q) * C2 - stat_t[pl.ds(h, 1), :])
-        dv = dot(p.astype(BF16), do)
-        dp = dot_t(heads[2, h], do)
-        ds = (p * (dp - delta_t[pl.ds(h, 1), :])).astype(BF16)
-        dk = dot(ds, q)
-        dq = dot(k.T, ds)
-        heads[2, h] = dv.astype(BF16)
-        heads[1, h] = (dk * SCALE).astype(BF16)
-        heads[0, h] = (dq * SCALE).astype(BF16).T
+        for twin in range(TWIN):
+            h = (i - att_at) * TWIN + twin
+            q, k, do = heads[0, h], heads[1, h], heads[3, h]
+            p = jnp.exp2(dot_t(k, q) * C2 - stat_t[pl.ds(h, 1), :])
+            dv = dot(p.astype(BF16), do)
+            dp = dot_t(heads[2, h], do)
+            ds = (p * (dp - delta_t[pl.ds(h, 1), :])).astype(BF16)
+            dk = dot(ds, q)
+            dq = dot(k.T, ds)
+            heads[2, h] = dv.astype(BF16)
+            heads[1, h] = (dk * SCALE).astype(BF16)
+            heads[0, h] = (dq * SCALE).astype(BF16).T
 
     @pl.when(i >= input_at)
     def _():
@@ -2059,7 +2066,7 @@
                 sums = share_terms(terms, names, adapters)
                 collected[layer] = gather_blocks(sums, 2, 16 * sums.shape[0])
             continue
-        if True:
+        if not on_block:
             d_gate, g_wide, d_inner_up, g_up_2 = gate_backward(
                 gradient, w_2, gate, narrow, wide, inner_down, inner_up
             )

time: 774 us -> 757 us (0.978)
  Pallas kernels: 732 us -> 714 us
    pallas_call x2, Pallas kernels: 228 us -> 217 us  [layer_forward(): pl.pallas_call(functools.partial(forward_kernel, shard is not None), grid...]
    pallas_call x2, Pallas kernels: 269 us -> 259 us  [layer_backward(): pl.pallas_call(functools.partial(backward_kernel, adapters, spread), grid...]
where the time goes in v9:
time: 757 us; the launch traced here: 749 us
  Pallas kernels  714 us (94%)
  other arithmetic  15 us (2%)
  local copies, waits for them, and re-layouts  13 us (2%)
    pallas_call x2, Pallas kernels, layer_backward(): pl.pallas_call(functools.partial(backward_kernel, adapters, spread), grid...  259 us
    pallas_call x2, Pallas kernels, layer_forward(): pl.pallas_call(functools.partial(forward_kernel, shard is not None), grid...  217 us
    pallas_call x1, Pallas kernels, first_gather(): pl.pallas_call(functools.partial(first_gather_kernel, tiles), in_specs=[h...  149 us
    pallas_call x1, Pallas kernels, gather_blocks(): pl.pallas_call(gather_kernel, in_specs=[pl.BlockSpec(memory_space=pl.ANY)...  37.8 us
    pallas_call x1, Pallas kernels, share_terms(): pl.pallas_call(functools.partial(share_kernel, adapters), in_specs=[pl.Bl...  31.7 us
  transfers between devices with their start and end apart: 3, of which 0 were waited for; matrix products, arithmetic and copies ran while one was open for 1% of the time, Pallas kernels for 40%

profile of v9, /device:TPU:0, one launch (start us, length us, event | category | flops | bytes accessed | tf_op | source)
XLA Modules:
  0.0 749.3 jit_solution(12037753852180691200)
XLA Ops:
  0.6 2.1 dynamic-slice_bitcast_fusion.4
  2.8 2.9 collective-permute-start
  5.7 2.6 copy.16
  8.3 0.0 copy-start.3
  8.3 2.1 slice_bitcast_fusion
  11.1 0.0 copy-done.3
  11.1 0.6 dynamic_slice.26
  11.6 149.3 %first_gather.1 = (bf16[124416,128]{1,0:T(8,128)(2,1)}, bf16[7648,128]{1,0:T(8,128)(2,1)}, bf16[7648,128]{1,0:T(8,128)(2,1)}) custom-call(bf16[7456,128]{1,0:T(8,128)(2,1)} %get-tuple-element.106.shard_a, bf16[7456,128]{1,0:T(8,128)(2,1)} %get-tuple-element.105.shard_b), custom_call_target="tpu_custom_call" | custom-call | tf_op jit(solution)/shard_map/first_gather/pallas_call | solution.py:1242
  160.9 1.3 pad_add_fusion.scalars
  162.2 1.1 fusion.2
  163.3 0.0 collective-permute-done.other
  163.3 5.4 prepare.1
  168.8 1.4 slice.14.refs_12_
  170.1 149.2 %layer_forward_gather.1 = (bf16[736,1152]{1,0:T(8,128)(2,1)}, bf16[736,48]{1,0:T(8,128)(2,1)}, bf16[736,3456]{1,0:T(8,128)(2,1)}, bf16[736,1152]{1,0:T(8,128)(2,...) custom-call(bf16[736,56]{1,0:T(8,128)(2,1)} %get-tuple-element.56.re, ...), custom_call_target="tpu_custom_call" | custom-call | flops 27403223040 | bytes 55885824 | tf_op jit(solution)/shard_map/layer_forward_gather/pallas_call | solution.py:1135
  319.4 0.0 copy-start.1
  319.4 1.6 layer_vectors.1
  321.0 1.4 slice.15.refs_12_
  322.3 0.0 copy-done.1
  322.3 1.3 dynamic-slice_bitcast_fusion.2
  323.7 0.9 collective-permute-start.1
  324.6 68.1 %layer_forward.1 = (bf16[736,1152]{1,0:T(8,128)(2,1)}, bf16[736,48]{1,0:T(8,128)(2,1)}, bf16[736,3456]{1,0:T(8,128)(2,1)}, bf16[736,1152]{1,0:T(8,128)(2,1)}, f3...) custom-call(bf16[736,56]{1,0:T(8,128)(2,1)} %get-tuple-element.56.re, ...), custom_call_target="tpu_custom_call" | custom-call | flops 27403223040 | bytes 55885824 | tf_op jit(solution)/shard_map/layer_forward/pallas_call | solution.py:1135
  392.7 0.0 collective-permute-done.1
  392.7 5.3 multiply_convert_fusion.1
  398.0 1.4 dynamic-slice_bitcast_fusion.3
  399.4 118.7 %layer_backward.1 = (f32[736,1152]{1,0:T(8,128)}, bf16[192,16,128]{2,1,0:T(8,128)(2,1)}) custom-call(f32[736,1152]{1,0:T(8,128)} %get-tuple-element.114.refs_0_, bf16[864,9,16,128]{3,2,1,0:T(8,128)(2,1)} %bitcast.52, bf16[736,4608]{1,0:T(8,128)(2,1)} %get-tuple-element.71.refs_2_, ...), custom_call_target="tpu_custom_call" | custom-call | flops 34891628544 | bytes 64364544 | tf_op jit(solution)/shard_map/layer_backward/pallas_call | solution.py:1739
  518.1 140.4 %layer_backward_share.1 = (f32[736,1152]{1,0:T(8,128)}, bf16[160,16,128]{2,1,0:T(8,128)(2,1)}, bf16[1280,128]{1,0:T(8,128)(2,1)}, bf16[20480,128]{1,0:T(8,128)(2...) custom-call(f32[736,1152]{1,0:T(8,128)} %get-tuple-element.84.refs_0_, bf16[864,9,16,128]{3,2,1,0:T(8,128)(2,1)} %bitcast.41, ...), custom_call_target="tpu_custom_call" | custom-call | flops 34891628544 | bytes 64364544 | tf_op jit(solution)/shard_map/layer_backward_share/pallas_call | solution.py:1739
  658.5 2.2 multiply_convert_fusion
  660.7 0.1 dynamic-slice_bitcast_fusion
  660.9 1.4 collective-permute-start.2
  662.3 31.7 %share_terms.1.refs_0_ = bf16[1280,128]{1,0:T(8,128)(2,1)} custom-call(bf16[32,5,16,128]{3,2,1,0:T(8,128)(2,1)} %bitcast.62, f32[32,128]{1,0:T(8,128)} %get-tuple-element.100.refs_1_), custom_call_target="tpu_custom_call" | custom-call | tf_op jit(solution)/shard_map/share_terms/pallas_call | solution.py:1381
  694.0 37.8 %gather_blocks.1 = bf16[20480,128]{1,0:T(8,128)(2,1)} custom-call(bf16[1280,128]{1,0:T(8,128)(2,1)} %share_terms.1.refs_0_), custom_call_target="tpu_custom_call" | custom-call | tf_op jit(solution)/shard_map/gather_blocks/pallas_call | solution.py:532
  731.8 0.0 copy-start
  731.8 0.0 copy-start.2
  731.8 12.1 %gradient_tables.1 = (f32[2,8,8,16,1152]{4,3,2,1,0:T(8,128)}, f32[2,2,8,16,1152]{4,3,2,1,0:T(8,128)}, f32[2,2,8,16,4304]{4,3,2,1,0:T(8,128)}) custom-call(bf16[32,8,5,16,128]{4,3,2,1,0:T(8,128)(2,1)} %bitcast.56, bf16[32,8,5,16,128]{4,3,2,1,0:T(8,128)(2,1)} %bitcast.58), custom_call_target="tpu_custom_call" | custom-call | tf_op jit(solution)/shard_map/gradient_tables/pallas_call | solution.py:1420
  743.9 0.0 copy-done
  743.9 0.0 copy-done.2
  743.9 1.5 maximum_select_fusion.1
  745.4 0.0 collective-permute-done.2
  745.4 3.5 fusion
Async XLA Ops:
  2.8 160.6 %collective-permute-start = (bf16[368,1152]{1,0:T(8,128)(2,1)}, bf16[368,1152]{1,0:T(8,128)(2,1)}, u32[]{:S(2)}, u32[]{:S(2)}) collective-permute-start(bf16[368,1152]{1,0:T(8,128)(2,1)} %dynamic-slice_bitcast_fusion.4), channel_id=1, source_target_pairs={{0,1},{1,0},{2,3},{3,2},{4,5},{5,4},{6,7},{7,6},{8,9},{9,8},{10,11... | collective-permute-start | bytes 2543624 | tf_op jit(solution)/shard_map/ppermute | solution.py:1925
  8.3 2.8 copy-start.3
  319.4 3.0 copy-start.1
  323.7 69.0 %collective-permute-start.1 = (bf16[368,1152]{1,0:T(8,128)(2,1)}, bf16[368,1152]{1,0:T(8,128)(2,1)}, u32[]{:S(2)}, u32[]{:S(2)}) collective-permute-start(bf16[368,1152]{1,0:T(8,128)(2,1)} %get-tuple-element.112), channel_id=1, source_target_pairs={{0,1},{1,0},{2,3},{3,2},{4,5},{5,4},{6,7},{7,6},{8,9},{9,8},{10,11... | collective-permute-start | bytes 2543624 | tf_op jit(solution)/shard_map/ppermute | solution.py:1887
  660.9 84.5 %collective-permute-start.2 = (bf16[368,1152]{1,0:T(8,128)(2,1)S(1)}, bf16[368,1152]{1,0:T(8,128)(2,1)}, u32[]{:S(2)}, u32[]{:S(2)}) collective-permute-start(bf16[368,1152]{1,0:T(8,128)(2,1)S(1)} %get-tuple-element.108), channel_id=1, source_target_pairs={{0,1},{1,0},{2,3},{3,2},{4,5},{5,4},{6,7},{7,6},{8,9},{9,8},{10,11... | collective-permute-start | bytes 2543624 | tf_op jit(solution)/shard_map/ppermute | solution.py:1904
  731.8 12.1 %copy-start = (bf16[1,368,1152]{2,1,0:T(8,128)(2,1)S(1)}, bf16[1,368,1152]{2,1,0:T(8,128)(2,1)}, u32[]{:S(2)}) copy-start(bf16[1,368,1152]{2,1,0:T(8,128)(2,1)} %get-tuple-element.109) | copy-start | bytes 2543620
  731.8 12.1 %copy-start.2 = (bf16[368,1152]{1,0:T(8,128)(2,1)S(1)}, bf16[368,1152]{1,0:T(8,128)(2,1)}, u32[]{:S(2)}) copy-start(bf16[368,1152]{1,0:T(8,128)(2,1)} %get-tuple-element.97) | copy-start | bytes 2543620

commit v10 on v9

--- a/solution.py
+++ b/solution.py
@@ -302,7 +302,7 @@
 
 def gather_plan(
     src, out, stage, local_sem, z_recv, y_recv, b_recv, h_recv, c_recv_own, c_recv_z, c_recv_y, c_recv_b, c_recv_h,
-    up_send, down_send, y_send, b_send, h_send, c_send_own, c_send_z, c_send_y, c_send_b, c_send_h,
+    up_send, down_send, y_send, b_send, h_send, c_send_own, c_send_z, c_send_y, c_send_b, c_send_h, pieces=2,
 ):
     rows = src.shape[0]
     if rows >= LARGE_BLOCK:
@@ -310,8 +310,8 @@
         sizes = [unit, unit, rows // 2 - 2 * unit, rows // 2 - 2 * unit, unit]
         begins = [0, unit, 2 * unit, rows // 2, rows - 2 * unit]
     else:
-        sizes = [rows // 2] * 2
-        begins = [0, rows // 2]
+        sizes = [rows // pieces] * pieces
+        begins = [k * (rows // pieces) for k in range(pieces)]
     chunks, across_y = len(sizes), (len(sizes) + 1) // 2
     lend = chunks == 5
     x = lax.axis_index("seq")
@@ -513,7 +513,7 @@
 
 
 def gather_kernel(*refs):
-    start, events, finish = gather_plan(*refs)
+    start, events, finish = gather_plan(*refs, pieces=4)
     start()
     for _, event in events:
         event()

time: 757 us -> 755 us (level)
  no operation moved by 1% of the time
where the time goes in v10:
time: 755 us; the launch traced here: 748 us
  Pallas kernels  713 us (94%)
  other arithmetic  15 us (2%)
  local copies, waits for them, and re-layouts  13 us (2%)
    pallas_call x2, Pallas kernels, layer_backward(): pl.pallas_call(functools.partial(backward_kernel, adapters, spread), grid...  259 us
    pallas_call x2, Pallas kernels, layer_forward(): pl.pallas_call(functools.partial(forward_kernel, shard is not None), grid...  217 us
    pallas_call x1, Pallas kernels, first_gather(): pl.pallas_call(functools.partial(first_gather_kernel, tiles), in_specs=[h...  149 us
    pallas_call x1, Pallas kernels, gather_blocks(): pl.pallas_call(gather_kernel, in_specs=[pl.BlockSpec(memory_space=pl.ANY)...  36 us
    pallas_call x1, Pallas kernels, share_terms(): pl.pallas_call(functools.partial(share_kernel, adapters), in_specs=[pl.Bl...  31.7 us
  transfers between devices with their start and end apart: 3, of which 0 were waited for; matrix products, arithmetic and copies ran while one was open for 1% of the time, Pallas kernels for 40%

profile of v10, /device:TPU:0, one launch (start us, length us, event | category | flops | bytes accessed | tf_op | source)
XLA Modules:
  0.0 747.5 jit_solution(12881094699757183927)
XLA Ops:
  0.6 2.1 dynamic-slice_bitcast_fusion.4
  2.8 2.9 collective-permute-start
  5.7 2.6 copy.16
  8.3 0.0 copy-start.3
  8.3 2.1 slice_bitcast_fusion
  11.1 0.0 copy-done.3
  11.1 0.6 dynamic_slice.26
  11.6 149.3 %first_gather.1 = (bf16[124416,128]{1,0:T(8,128)(2,1)}, bf16[7648,128]{1,0:T(8,128)(2,1)}, bf16[7648,128]{1,0:T(8,128)(2,1)}) custom-call(bf16[7456,128]{1,0:T(8,128)(2,1)} %get-tuple-element.106.shard_a, bf16[7456,128]{1,0:T(8,128)(2,1)} %get-tuple-element.105.shard_b), custom_call_target="tpu_custom_call" | custom-call | tf_op jit(solution)/shard_map/first_gather/pallas_call | solution.py:1242
  160.9 1.3 pad_add_fusion.scalars
  162.2 1.1 fusion.2
  163.3 0.0 collective-permute-done.other
  163.3 5.4 prepare.1
  168.8 1.4 slice.14.refs_12_
  170.1 149.2 %layer_forward_gather.1 = (bf16[736,1152]{1,0:T(8,128)(2,1)}, bf16[736,48]{1,0:T(8,128)(2,1)}, bf16[736,3456]{1,0:T(8,128)(2,1)}, bf16[736,1152]{1,0:T(8,128)(2,...) custom-call(bf16[736,56]{1,0:T(8,128)(2,1)} %get-tuple-element.56.re, ...), custom_call_target="tpu_custom_call" | custom-call | flops 27403223040 | bytes 55885824 | tf_op jit(solution)/shard_map/layer_forward_gather/pallas_call | solution.py:1135
  319.4 0.0 copy-start.1
  319.4 1.6 layer_vectors.1
  321.0 1.4 slice.15.refs_12_
  322.3 0.0 copy-done.1
  322.3 1.3 dynamic-slice_bitcast_fusion.2
  323.7 0.9 collective-permute-start.1
  324.6 68.1 %layer_forward.1 = (bf16[736,1152]{1,0:T(8,128)(2,1)}, bf16[736,48]{1,0:T(8,128)(2,1)}, bf16[736,3456]{1,0:T(8,128)(2,1)}, bf16[736,1152]{1,0:T(8,128)(2,1)}, f3...) custom-call(bf16[736,56]{1,0:T(8,128)(2,1)} %get-tuple-element.56.re, ...), custom_call_target="tpu_custom_call" | custom-call | flops 27403223040 | bytes 55885824 | tf_op jit(solution)/shard_map/layer_forward/pallas_call | solution.py:1135
  392.7 0.0 collective-permute-done.1
  392.7 5.3 multiply_convert_fusion.1
  398.0 1.4 dynamic-slice_bitcast_fusion.3
  399.4 118.7 %layer_backward.1 = (f32[736,1152]{1,0:T(8,128)}, bf16[192,16,128]{2,1,0:T(8,128)(2,1)}) custom-call(f32[736,1152]{1,0:T(8,128)} %get-tuple-element.114.refs_0_, bf16[864,9,16,128]{3,2,1,0:T(8,128)(2,1)} %bitcast.52, bf16[736,4608]{1,0:T(8,128)(2,1)} %get-tuple-element.71.refs_2_, ...), custom_call_target="tpu_custom_call" | custom-call | flops 34891628544 | bytes 64364544 | tf_op jit(solution)/shard_map/layer_backward/pallas_call | solution.py:1739
  518.1 140.4 %layer_backward_share.1 = (f32[736,1152]{1,0:T(8,128)}, bf16[160,16,128]{2,1,0:T(8,128)(2,1)}, bf16[1280,128]{1,0:T(8,128)(2,1)}, bf16[20480,128]{1,0:T(8,128)(2...) custom-call(f32[736,1152]{1,0:T(8,128)} %get-tuple-element.84.refs_0_, bf16[864,9,16,128]{3,2,1,0:T(8,128)(2,1)} %bitcast.41, ...), custom_call_target="tpu_custom_call" | custom-call | flops 34891628544 | bytes 64364544 | tf_op jit(solution)/shard_map/layer_backward_share/pallas_call | solution.py:1739
  658.5 2.2 multiply_convert_fusion
  660.7 0.1 dynamic-slice_bitcast_fusion
  660.9 1.4 collective-permute-start.2
  662.3 31.7 %share_terms.1.refs_0_ = bf16[1280,128]{1,0:T(8,128)(2,1)} custom-call(bf16[32,5,16,128]{3,2,1,0:T(8,128)(2,1)} %bitcast.62, f32[32,128]{1,0:T(8,128)} %get-tuple-element.100.refs_1_), custom_call_target="tpu_custom_call" | custom-call | tf_op jit(solution)/shard_map/share_terms/pallas_call | solution.py:1381
  694.0 36.0 %gather_blocks.1 = bf16[20480,128]{1,0:T(8,128)(2,1)} custom-call(bf16[1280,128]{1,0:T(8,128)(2,1)} %share_terms.1.refs_0_), custom_call_target="tpu_custom_call" | custom-call | tf_op jit(solution)/shard_map/gather_blocks/pallas_call | solution.py:532
  730.0 0.0 copy-start
  730.0 0.0 copy-start.2
  730.0 12.1 %gradient_tables.1 = (f32[2,8,8,16,1152]{4,3,2,1,0:T(8,128)}, f32[2,2,8,16,1152]{4,3,2,1,0:T(8,128)}, f32[2,2,8,16,4304]{4,3,2,1,0:T(8,128)}) custom-call(bf16[32,8,5,16,128]{4,3,2,1,0:T(8,128)(2,1)} %bitcast.56, bf16[32,8,5,16,128]{4,3,2,1,0:T(8,128)(2,1)} %bitcast.58), custom_call_target="tpu_custom_call" | custom-call | tf_op jit(solution)/shard_map/gradient_tables/pallas_call | solution.py:1420
  742.1 0.0 copy-done
  742.1 0.0 copy-done.2
  742.1 1.5 maximum_select_fusion.1
  743.7 0.0 collective-permute-done.2
  743.7 3.5 fusion
Async XLA Ops:
  2.8 160.6 %collective-permute-start = (bf16[368,1152]{1,0:T(8,128)(2,1)}, bf16[368,1152]{1,0:T(8,128)(2,1)}, u32[]{:S(2)}, u32[]{:S(2)}) collective-permute-start(bf16[368,1152]{1,0:T(8,128)(2,1)} %dynamic-slice_bitcast_fusion.4), channel_id=1, source_target_pairs={{0,1},{1,0},{2,3},{3,2},{4,5},{5,4},{6,7},{7,6},{8,9},{9,8},{10,11... | collective-permute-start | bytes 2543624 | tf_op jit(solution)/shard_map/ppermute | solution.py:1925
  8.3 2.8 copy-start.3
  319.4 3.0 copy-start.1
  323.7 69.0 %collective-permute-start.1 = (bf16[368,1152]{1,0:T(8,128)(2,1)}, bf16[368,1152]{1,0:T(8,128)(2,1)}, u32[]{:S(2)}, u32[]{:S(2)}) collective-permute-start(bf16[368,1152]{1,0:T(8,128)(2,1)} %get-tuple-element.112), channel_id=1, source_target_pairs={{0,1},{1,0},{2,3},{3,2},{4,5},{5,4},{6,7},{7,6},{8,9},{9,8},{10,11... | collective-permute-start | bytes 2543624 | tf_op jit(solution)/shard_map/ppermute | solution.py:1887
  660.9 82.8 %collective-permute-start.2 = (bf16[368,1152]{1,0:T(8,128)(2,1)S(1)}, bf16[368,1152]{1,0:T(8,128)(2,1)}, u32[]{:S(2)}, u32[]{:S(2)}) collective-permute-start(bf16[368,1152]{1,0:T(8,128)(2,1)S(1)} %get-tuple-element.108), channel_id=1, source_target_pairs={{0,1},{1,0},{2,3},{3,2},{4,5},{5,4},{6,7},{7,6},{8,9},{9,8},{10,11... | collective-permute-start | bytes 2543624 | tf_op jit(solution)/shard_map/ppermute | solution.py:1904
  730.0 12.1 %copy-start = (bf16[1,368,1152]{2,1,0:T(8,128)(2,1)S(1)}, bf16[1,368,1152]{2,1,0:T(8,128)(2,1)}, u32[]{:S(2)}) copy-start(bf16[1,368,1152]{2,1,0:T(8,128)(2,1)} %get-tuple-element.109) | copy-start | bytes 2543620
  730.0 12.1 %copy-start.2 = (bf16[368,1152]{1,0:T(8,128)(2,1)S(1)}, bf16[368,1152]{1,0:T(8,128)(2,1)}, u32[]{:S(2)}) copy-start(bf16[368,1152]{1,0:T(8,128)(2,1)} %get-tuple-element.97) | copy-start | bytes 2543620

commit v11 on v10

--- a/solution.py
+++ b/solution.py
@@ -925,7 +925,6 @@
 
 PAIR = 2 * LANES
 PAIRS = -(-D // PAIR)
-TWIN = 2
 FOUR = 4
 FORWARD_STEPS = (3, H // FOUR, WIDE // TILE, PAIRS)
 FORWARD_AT = (0, 3, 3 + H // FOUR, 3 + H // FOUR + WIDE // TILE)
@@ -1432,8 +1431,8 @@
     )(*gathered)
 
 
-BACKWARD_STEPS = (WIDE // TILE, PAIRS, 1, H // TWIN, PAIRS)
-BACKWARD_AT = (0, 9, 14, 15, 15 + H // TWIN)
+BACKWARD_STEPS = (WIDE // TILE, PAIRS, 1, H // FOUR, PAIRS)
+BACKWARD_AT = (0, 9, 14, 15, 15 + H // FOUR)
 SHARE_AT, PASS_AT, GATHER_AT = 7, 9, 10
 
 
@@ -1498,7 +1497,7 @@
             device_id_type=MESH,
         )
         at_step(0)(share_start)
-        at_step(GATHER_AT + 12)(swap.start)
+        at_step(GATHER_AT + 9)(swap.start)
         at_step(SHARE_AT)(share_sum)
         at_step(PASS_AT)(share_finish)
 
@@ -1615,8 +1614,8 @@
 
     @pl.when(jnp.logical_and(i >= att_at, i < input_at))
     def _():
-        for twin in range(TWIN):
-            h = (i - att_at) * TWIN + twin
+        for twin in range(FOUR):
+            h = (i - att_at) * FOUR + twin
             q, k, do = heads[0, h], heads[1, h], heads[3, h]
             p = jnp.exp2(dot_t(k, q) * C2 - stat_t[pl.ds(h, 1), :])
             dv = dot(p.astype(BF16), do)

time: 755 us -> 758 us (level)
  no operation moved by 1% of the time
where the time goes in v11:
time: 758 us; the launch traced here: 751 us
  Pallas kernels  716 us (94%)
  other arithmetic  15 us (2%)
  local copies, waits for them, and re-layouts  13 us (2%)
    pallas_call x2, Pallas kernels, layer_backward(): pl.pallas_call(functools.partial(backward_kernel, adapters, spread), grid...  261 us
    pallas_call x2, Pallas kernels, layer_forward(): pl.pallas_call(functools.partial(forward_kernel, shard is not None), grid...  217 us
    pallas_call x1, Pallas kernels, first_gather(): pl.pallas_call(functools.partial(first_gather_kernel, tiles), in_specs=[h...  149 us
    pallas_call x1, Pallas kernels, gather_blocks(): pl.pallas_call(gather_kernel, in_specs=[pl.BlockSpec(memory_space=pl.ANY)...  36.2 us
    pallas_call x1, Pallas kernels, share_terms(): pl.pallas_call(functools.partial(share_kernel, adapters), in_specs=[pl.Bl...  32.7 us
  transfers between devices with their start and end apart: 3, of which 0 were waited for; matrix products, arithmetic and copies ran while one was open for 1% of the time, Pallas kernels for 40%

profile of v11, /device:TPU:0, one launch (start us, length us, event | category | flops | bytes accessed | tf_op | source)
XLA Modules:
  0.0 750.7 jit_solution(12073602590069880815)
XLA Ops:
  0.6 2.1 dynamic-slice_bitcast_fusion.4
  2.8 2.9 collective-permute-start
  5.7 2.6 copy.16
  8.3 0.0 copy-start.3
  8.3 2.1 slice_bitcast_fusion
  11.1 0.0 copy-done.3
  11.1 0.6 dynamic_slice.26
  11.6 149.3 %first_gather.1 = (bf16[124416,128]{1,0:T(8,128)(2,1)}, bf16[7648,128]{1,0:T(8,128)(2,1)}, bf16[7648,128]{1,0:T(8,128)(2,1)}) custom-call(bf16[7456,128]{1,0:T(8,128)(2,1)} %get-tuple-element.106.shard_a, bf16[7456,128]{1,0:T(8,128)(2,1)} %get-tuple-element.105.shard_b), custom_call_target="tpu_custom_call" | custom-call | tf_op jit(solution)/shard_map/first_gather/pallas_call | solution.py:1241
  160.9 1.3 pad_add_fusion.scalars
  162.2 1.1 fusion.2
  163.3 0.0 collective-permute-done.other
  163.3 5.4 prepare.1
  168.8 1.4 slice.14.refs_12_
  170.1 149.3 %layer_forward_gather.1 = (bf16[736,1152]{1,0:T(8,128)(2,1)}, bf16[736,48]{1,0:T(8,128)(2,1)}, bf16[736,3456]{1,0:T(8,128)(2,1)}, bf16[736,1152]{1,0:T(8,128)(2,...) custom-call(bf16[736,56]{1,0:T(8,128)(2,1)} %get-tuple-element.56.re, ...), custom_call_target="tpu_custom_call" | custom-call | flops 27403223040 | bytes 55885824 | tf_op jit(solution)/shard_map/layer_forward_gather/pallas_call | solution.py:1134
  319.5 0.0 copy-start.1
  319.5 1.6 layer_vectors.1
  321.1 1.4 slice.15.refs_12_
  322.5 0.0 copy-done.1
  322.5 1.3 dynamic-slice_bitcast_fusion.2
  323.8 0.9 collective-permute-start.1
  324.7 68.1 %layer_forward.1 = (bf16[736,1152]{1,0:T(8,128)(2,1)}, bf16[736,48]{1,0:T(8,128)(2,1)}, bf16[736,3456]{1,0:T(8,128)(2,1)}, bf16[736,1152]{1,0:T(8,128)(2,1)}, f3...) custom-call(bf16[736,56]{1,0:T(8,128)(2,1)} %get-tuple-element.56.re, ...), custom_call_target="tpu_custom_call" | custom-call | flops 27403223040 | bytes 55885824 | tf_op jit(solution)/shard_map/layer_forward/pallas_call | solution.py:1134
  392.8 0.0 collective-permute-done.1
  392.8 5.3 multiply_convert_fusion.1
  398.2 1.4 dynamic-slice_bitcast_fusion.3
  399.5 118.8 %layer_backward.1 = (f32[736,1152]{1,0:T(8,128)}, bf16[192,16,128]{2,1,0:T(8,128)(2,1)}) custom-call(f32[736,1152]{1,0:T(8,128)} %get-tuple-element.114.refs_0_, bf16[864,9,16,128]{3,2,1,0:T(8,128)(2,1)} %bitcast.52, bf16[736,4608]{1,0:T(8,128)(2,1)} %get-tuple-element.71.refs_2_, ...), custom_call_target="tpu_custom_call" | custom-call | flops 34891628544 | bytes 64364544 | tf_op jit(solution)/shard_map/layer_backward/pallas_call | solution.py:1738
  518.4 142.2 %layer_backward_share.1 = (f32[736,1152]{1,0:T(8,128)}, bf16[160,16,128]{2,1,0:T(8,128)(2,1)}, bf16[1280,128]{1,0:T(8,128)(2,1)}, bf16[20480,128]{1,0:T(8,128)(2...) custom-call(f32[736,1152]{1,0:T(8,128)} %get-tuple-element.84.refs_0_, bf16[864,9,16,128]{3,2,1,0:T(8,128)(2,1)} %bitcast.41, ...), custom_call_target="tpu_custom_call" | custom-call | flops 34891628544 | bytes 64364544 | tf_op jit(solution)/shard_map/layer_backward_share/pallas_call | solution.py:1738
  660.5 2.2 multiply_convert_fusion
  662.8 0.1 dynamic-slice_bitcast_fusion
  662.9 1.5 collective-permute-start.2
  664.5 32.7 %share_terms.1.refs_0_ = bf16[1280,128]{1,0:T(8,128)(2,1)} custom-call(bf16[32,5,16,128]{3,2,1,0:T(8,128)(2,1)} %bitcast.62, f32[32,128]{1,0:T(8,128)} %get-tuple-element.100.refs_1_), custom_call_target="tpu_custom_call" | custom-call | tf_op jit(solution)/shard_map/share_terms/pallas_call | solution.py:1380
  697.2 36.2 %gather_blocks.1 = bf16[20480,128]{1,0:T(8,128)(2,1)} custom-call(bf16[1280,128]{1,0:T(8,128)(2,1)} %share_terms.1.refs_0_), custom_call_target="tpu_custom_call" | custom-call | tf_op jit(solution)/shard_map/gather_blocks/pallas_call | solution.py:532
  733.4 0.0 copy-start
  733.4 0.0 copy-start.2
  733.4 12.1 %gradient_tables.1 = (f32[2,8,8,16,1152]{4,3,2,1,0:T(8,128)}, f32[2,2,8,16,1152]{4,3,2,1,0:T(8,128)}, f32[2,2,8,16,4304]{4,3,2,1,0:T(8,128)}) custom-call(bf16[32,8,5,16,128]{4,3,2,1,0:T(8,128)(2,1)} %bitcast.56, bf16[32,8,5,16,128]{4,3,2,1,0:T(8,128)(2,1)} %bitcast.58), custom_call_target="tpu_custom_call" | custom-call | tf_op jit(solution)/shard_map/gradient_tables/pallas_call | solution.py:1419
  745.5 0.0 copy-done
  745.5 0.0 copy-done.2
  745.5 1.5 maximum_select_fusion.1
  747.1 0.0 collective-permute-done.2
  747.1 3.5 fusion
Async XLA Ops:
  2.8 160.6 %collective-permute-start = (bf16[368,1152]{1,0:T(8,128)(2,1)}, bf16[368,1152]{1,0:T(8,128)(2,1)}, u32[]{:S(2)}, u32[]{:S(2)}) collective-permute-start(bf16[368,1152]{1,0:T(8,128)(2,1)} %dynamic-slice_bitcast_fusion.4), channel_id=1, source_target_pairs={{0,1},{1,0},{2,3},{3,2},{4,5},{5,4},{6,7},{7,6},{8,9},{9,8},{10,11... | collective-permute-start | bytes 2543624 | tf_op jit(solution)/shard_map/ppermute | solution.py:1924
  8.3 2.8 copy-start.3
  319.5 3.0 copy-start.1
  323.8 69.0 %collective-permute-start.1 = (bf16[368,1152]{1,0:T(8,128)(2,1)}, bf16[368,1152]{1,0:T(8,128)(2,1)}, u32[]{:S(2)}, u32[]{:S(2)}) collective-permute-start(bf16[368,1152]{1,0:T(8,128)(2,1)} %get-tuple-element.112), channel_id=1, source_target_pairs={{0,1},{1,0},{2,3},{3,2},{4,5},{5,4},{6,7},{7,6},{8,9},{9,8},{10,11... | collective-permute-start | bytes 2543624 | tf_op jit(solution)/shard_map/ppermute | solution.py:1886
  662.9 84.2 %collective-permute-start.2 = (bf16[368,1152]{1,0:T(8,128)(2,1)S(1)}, bf16[368,1152]{1,0:T(8,128)(2,1)}, u32[]{:S(2)}, u32[]{:S(2)}) collective-permute-start(bf16[368,1152]{1,0:T(8,128)(2,1)S(1)} %get-tuple-element.108), channel_id=1, source_target_pairs={{0,1},{1,0},{2,3},{3,2},{4,5},{5,4},{6,7},{7,6},{8,9},{9,8},{10,11... | collective-permute-start | bytes 2543624 | tf_op jit(solution)/shard_map/ppermute | solution.py:1903
  733.4 12.1 %copy-start = (bf16[1,368,1152]{2,1,0:T(8,128)(2,1)S(1)}, bf16[1,368,1152]{2,1,0:T(8,128)(2,1)}, u32[]{:S(2)}) copy-start(bf16[1,368,1152]{2,1,0:T(8,128)(2,1)} %get-tuple-element.109) | copy-start | bytes 2543620
  733.4 12.1 %copy-start.2 = (bf16[368,1152]{1,0:T(8,128)(2,1)S(1)}, bf16[368,1152]{1,0:T(8,128)(2,1)}, u32[]{:S(2)}) copy-start(bf16[368,1152]{1,0:T(8,128)(2,1)} %get-tuple-element.97) | copy-start | bytes 2543620
